TPU v7x, 32 devices: a whole 2x2x4 slice. The times are simulated.
32 devices in a mesh: row: 16 (over z, y, core), col: 2 (over x).
Axes of the slice: x: 2, y: 2, z: 4, core: 2. Of those that a mesh axis runs over, the one named last changes fastest.
Arguments:
- states: float32 [16384, 768], P(('row', 'col')), may hold values from -6 to 6
- upstream: float32 [16384, 768], P(('row', 'col')), may hold values from -6 to 6
- teacher: float32 [16384, 768], P(('row', 'col')), may hold values from -6 to 6
- validity: int32 [16384], P(('row', 'col')), may hold values from 0 to 1, as said below
- picture_start: int32 [32, 2], P(('row', 'col')), may hold values from 0 to 256, as said below
- first_gain: float32 [768], replicated, may hold values from 0.5 to 1.5
- query_weight: bfloat16 [768, 768], P('row', 'col'), may hold values from -0.21875 to 0.21875
- key_weight: bfloat16 [768, 768], P('row', 'col'), may hold values from -0.21875 to 0.21875
- value_weight: bfloat16 [768, 768], P('row', 'col'), may hold values from -0.21875 to 0.21875
- premix: float32 [12, 12], replicated, may hold values from -3 to 3
- postmix: float32 [12, 12], replicated, may hold values from -3 to 3
- output_weight: bfloat16 [768, 768], P('row', 'col'), may hold values from -0.875 to 0.875
- second_gain: float32 [768], replicated, may hold values from 0.5 to 1.5
- up_weight: bfloat16 [768, 3072], P('row', 'col'), may hold values from -0.21875 to 0.21875
- down_weight: bfloat16 [3072, 768], P('col', 'row'), may hold values from -0.109375 to 0.109375
Outputs:
- layer_out: float32 [16384, 768], P(('row', 'col'))
- distill_loss: float32 [], replicated
- task_loss: float32 [], replicated
- input_grad: float32 [16384, 768], P(('row', 'col'))
- first_grad: float32 [768], replicated
- query_grad: float32 [768, 768], P('row', 'col')
- key_grad: float32 [768, 768], P('row', 'col')
- value_grad: float32 [768, 768], P('row', 'col')
- premix_grad: float32 [12, 12], replicated
- postmix_grad: float32 [12, 12], replicated
- output_grad: float32 [768, 768], P('row', 'col')
- second_grad: float32 [768], replicated
- up_grad: float32 [768, 3072], P('row', 'col')
- down_grad: float32 [3072, 768], P('col', 'row')
Inputs may be any that keep to these rules, and one draw needn't show every extreme that they name: `validity`: the first token of every sequence is valid. `picture_start`: row s holds the starts of sequence s's two picture spans of 256 positions; the first span lies within positions 0 to 255, the second within 256 to 511.
All inputs are finite; a program needn't handle non-finite values.
Results may differ from a plain program's by a relative error of at most 0.03.
The roundings to bfloat16 on the way count: a program that leaves them out, or rounds other values in their place, can miss the bound.
Values may be sent and summed in bfloat16 or wider, within the bound.
No kernel may reach another device: no remote copies, remote signals or barrier semaphores. Data moves between devices by JAX's collectives and lax.ppermute only.
A program may use at most 256 MiB of HBM per device.

v0:
```python
import jax
import jax.numpy as jnp
from jax import lax
from jax.sharding import PartitionSpec as P

HEADS = 12
HEAD_DIM = 64
PIC = 256


EPSILON = 1e-06
HIGHEST = lax.Precision.HIGHEST


def permitted(positions, columns, starts):
    causal = columns[None, :] <= positions[:, None]
    first_rows = (positions >= starts[0]) & (positions < starts[0] + PIC)
    first_cols = (columns >= starts[0]) & (columns < starts[0] + PIC)
    second_rows = (positions >= starts[1]) & (positions < starts[1] + PIC)
    second_cols = (columns >= starts[1]) & (columns < starts[1] + PIC)
    return (
        causal
        | first_rows[:, None] & first_cols[None, :]
        | second_rows[:, None] & second_cols[None, :]
    )


def inverse_rms(values):
    return lax.rsqrt(jnp.mean(values * values, axis=-1, keepdims=True) + EPSILON)


def regroup(gathered, row_total, col_total):
    return tuple(
        (
            block_piece.reshape((row_total, col_total) + block_piece.shape[1:])
            for block_piece in gathered
        )
    )


def project(activations, weight_blocks):
    seq_len = activations.shape[0]
    row_total, col_total, inner_size, outer_size = weight_blocks.shape
    result = jnp.einsum(
        "srd,rcde->sce",
        activations.reshape(seq_len, row_total, inner_size),
        weight_blocks,
        preferred_element_type=jnp.float32,
    )
    return result.reshape(seq_len, col_total * outer_size)


def project_back(gradients, weight_blocks):
    seq_len = gradients.shape[0]
    row_total, col_total, inner_size, outer_size = weight_blocks.shape
    result = jnp.einsum(
        "sce,rcde->srd",
        gradients.reshape(seq_len, col_total, outer_size),
        weight_blocks,
        preferred_element_type=jnp.float32,
    )
    return result.reshape(seq_len, row_total * inner_size)


def weight_term(activations, gradients, weight_blocks):
    seq_len = activations.shape[0]
    row_total, col_total, inner_size, outer_size = weight_blocks.shape
    result = jnp.einsum(
        "srd,sce->rcde",
        activations.reshape(seq_len, row_total, inner_size),
        gradients.reshape(seq_len, col_total, outer_size),
        preferred_element_type=jnp.float32,
    )
    return result.reshape(row_total * col_total, inner_size, outer_size)


def attend(queries, keys_all, values_all, premix, postmix, starts):
    seq_len = queries.shape[0]
    block_rows = min(512, seq_len)
    block_total = seq_len // block_rows
    factor_scale = HEAD_DIM ** (-0.5)
    columns = jnp.arange(seq_len, dtype=jnp.int32)

    def one_block(scan_item):
        query_block, offset = scan_item
        positions = offset + jnp.arange(block_rows, dtype=jnp.int32)
        scores = (
            jnp.einsum("qgd,kgd->gqk", query_block, keys_all, preferred_element_type=jnp.float32)
            * factor_scale
        )
        mixed_scores = jnp.einsum("gh,gqk->hqk", premix, scores, precision=HIGHEST)
        mixed_scores = jnp.where(permitted(positions, columns, starts)[None], mixed_scores, -1e30)
        highest = jnp.max(mixed_scores, axis=-1, keepdims=True)
        exp_terms = jnp.exp(mixed_scores - highest)
        totals = jnp.sum(exp_terms, axis=-1, keepdims=True)
        softmax_probs = exp_terms / totals
        weights = jnp.einsum("hg,hqk->gqk", postmix, softmax_probs, precision=HIGHEST).astype(
            jnp.bfloat16
        )
        result = jnp.einsum("gqk,kgd->qgd", weights, values_all, preferred_element_type=jnp.float32)
        return (result, highest[:, :, 0] + jnp.log(totals[:, :, 0]))

    blocks = queries.reshape(block_total, block_rows, HEADS, HEAD_DIM)
    offsets = jnp.arange(block_total, dtype=jnp.int32) * block_rows
    results, logsums = lax.map(one_block, (blocks, offsets))
    return (results.reshape(seq_len, HEADS * HEAD_DIM), logsums)


def attend_back(queries, keys_all, values_all, grads_out, logsums, premix, postmix, starts):
    seq_len = queries.shape[0]
    block_rows = min(512, seq_len)
    block_total = seq_len // block_rows
    factor_scale = HEAD_DIM ** (-0.5)
    columns = jnp.arange(seq_len, dtype=jnp.int32)

    def one_block(carried, scan_item):
        key_acc, value_acc, premix_acc, postmix_acc = carried
        query_block, grad_block, logsum_block, offset = scan_item
        positions = offset + jnp.arange(block_rows, dtype=jnp.int32)
        scores = (
            jnp.einsum("qgd,kgd->gqk", query_block, keys_all, preferred_element_type=jnp.float32)
            * factor_scale
        )
        mixed_scores = jnp.einsum("gh,gqk->hqk", premix, scores, precision=HIGHEST)
        mixed_scores = jnp.where(permitted(positions, columns, starts)[None], mixed_scores, -1e30)
        softmax_probs = jnp.exp(mixed_scores - logsum_block[:, :, None])
        weights = jnp.einsum("hg,hqk->gqk", postmix, softmax_probs, precision=HIGHEST).astype(
            jnp.bfloat16
        )
        weight_grad = jnp.einsum(
            "qgd,kgd->gqk", grad_block, values_all, preferred_element_type=jnp.float32
        )
        value_acc = value_acc + jnp.einsum(
            "gqk,qgd->kgd", weights, grad_block, preferred_element_type=jnp.float32
        )
        postmix_acc = postmix_acc + jnp.einsum(
            "hqk,gqk->hg", softmax_probs, weight_grad, precision=HIGHEST
        )
        prob_grad = jnp.einsum("hg,gqk->hqk", postmix, weight_grad, precision=HIGHEST)
        mixed_grad = softmax_probs * (
            prob_grad - jnp.sum(softmax_probs * prob_grad, axis=-1, keepdims=True)
        )
        premix_acc = premix_acc + jnp.einsum("gqk,hqk->gh", scores, mixed_grad, precision=HIGHEST)
        score_grad = jnp.einsum("gh,hqk->gqk", premix, mixed_grad, precision=HIGHEST).astype(
            jnp.bfloat16
        )
        query_part = (
            jnp.einsum("gqk,kgd->qgd", score_grad, keys_all, preferred_element_type=jnp.float32)
            * factor_scale
        )
        key_acc = (
            key_acc
            + jnp.einsum(
                "gqk,qgd->kgd", score_grad, query_block, preferred_element_type=jnp.float32
            )
            * factor_scale
        )
        return ((key_acc, value_acc, premix_acc, postmix_acc), query_part)

    blocks = queries.reshape(block_total, block_rows, HEADS, HEAD_DIM)
    grad_blocks = grads_out.reshape(block_total, block_rows, HEADS, HEAD_DIM)
    offsets = jnp.arange(block_total, dtype=jnp.int32) * block_rows
    zero_heads = jnp.zeros((seq_len, HEADS, HEAD_DIM), jnp.float32)
    zero_mix = jnp.zeros((HEADS, HEADS), jnp.float32)
    (key_acc, value_acc, premix_acc, postmix_acc), query_parts = lax.scan(
        one_block,
        (zero_heads, zero_heads, zero_mix, zero_mix),
        (blocks, grad_blocks, logsums, offsets),
    )
    widths_all = HEADS * HEAD_DIM
    return (
        query_parts.reshape(seq_len, widths_all),
        key_acc.reshape(seq_len, widths_all),
        value_acc.reshape(seq_len, widths_all),
        premix_acc,
        postmix_acc,
    )


def shards(
    states,
    upstream,
    teacher,
    validity,
    picture_start,
    first_gain,
    query_weight,
    key_weight,
    value_weight,
    premix,
    postmix,
    output_weight,
    second_gain,
    up_weight,
    down_weight,
):
    row_total = lax.axis_size("row")
    col_total = lax.axis_size("col")
    seq_len, features = states.shape
    starts = picture_start[0]
    gathered = (
        lax.all_gather(query_weight[None], ("row", "col"), axis=0, tiled=True),
        lax.all_gather(key_weight[None], ("row", "col"), axis=0, tiled=True),
        lax.all_gather(value_weight[None], ("row", "col"), axis=0, tiled=True),
        lax.all_gather(output_weight[None], ("row", "col"), axis=0, tiled=True),
        lax.all_gather(up_weight[None], ("row", "col"), axis=0, tiled=True),
        lax.all_gather(down_weight[None], ("row", "col"), axis=0, tiled=True),
    )
    attn_blocks = regroup(gathered[:4], row_total, col_total)
    ffn_blocks = gathered[4:]
    first_scale = inverse_rms(states)
    normed = (states * first_scale * first_gain).astype(jnp.bfloat16)
    queries = project(normed, attn_blocks[0]).astype(jnp.bfloat16)
    keys_all = project(normed, attn_blocks[1]).astype(jnp.bfloat16)
    values_all = project(normed, attn_blocks[2]).astype(jnp.bfloat16)
    head_shape = (seq_len, HEADS, HEAD_DIM)
    attn_raw, logsums = attend(
        queries.reshape(head_shape),
        keys_all.reshape(head_shape),
        values_all.reshape(head_shape),
        premix,
        postmix,
        starts,
    )
    attended = attn_raw.astype(jnp.bfloat16)
    middle = states + project(attended, attn_blocks[3])
    second_scale = inverse_rms(middle)
    normed_two = (middle * second_scale * second_gain).astype(jnp.bfloat16)
    up_blocks, down_blocks = regroup(ffn_blocks, row_total, col_total)
    hidden_units = up_blocks.shape[3]
    hidden_pre = project(normed_two, up_blocks)
    hidden = jnp.maximum(hidden_pre, 0.0).astype(jnp.bfloat16)
    ffn_out = jnp.einsum(
        "scf,rcfd->srd",
        hidden.reshape(seq_len, col_total, hidden_units),
        down_blocks,
        preferred_element_type=jnp.float32,
    ).reshape(seq_len, features)
    layer_out = middle + ffn_out
    valid_marks = validity.astype(jnp.float32)
    differ = layer_out - teacher
    total_valid, distance, linear = lax.psum(
        (
            jnp.sum(valid_marks),
            jnp.sum(valid_marks * jnp.sum(differ * differ, axis=1)),
            jnp.sum(valid_marks * jnp.sum(upstream * layer_out, axis=1)),
        ),
        ("row", "col"),
    )
    distill_loss = distance / (total_valid * features)
    task_loss = linear / total_valid
    factor = seq_len * row_total * col_total / total_valid
    out_grad = factor * valid_marks[:, None] * (upstream + differ)
    out_low = out_grad.astype(jnp.bfloat16)
    regathered = (
        lax.all_gather(query_weight[None], ("row", "col"), axis=0, tiled=True),
        lax.all_gather(key_weight[None], ("row", "col"), axis=0, tiled=True),
        lax.all_gather(value_weight[None], ("row", "col"), axis=0, tiled=True),
        lax.all_gather(output_weight[None], ("row", "col"), axis=0, tiled=True),
        lax.all_gather(up_weight[None], ("row", "col"), axis=0, tiled=True),
        lax.all_gather(down_weight[None], ("row", "col"), axis=0, tiled=True),
    )
    attn_back = regroup(regathered[:4], row_total, col_total)
    ffn_back = regathered[4:]
    up_blocks, down_blocks = regroup(ffn_back, row_total, col_total)
    row_width = up_blocks.shape[2]
    hidden_units = up_blocks.shape[3]
    out_rows = out_low.reshape(seq_len, row_total, row_width)
    hidden_grad = jnp.einsum(
        "srd,rcfd->scf", out_rows, down_blocks, preferred_element_type=jnp.float32
    ).reshape(seq_len, col_total * hidden_units)
    pre_grad = jnp.where(hidden_pre > 0, hidden_grad, 0.0).astype(jnp.bfloat16)
    normed_two_grad = project_back(pre_grad, up_blocks)
    up_term = weight_term(normed_two, pre_grad, up_blocks)
    down_term = jnp.einsum(
        "scf,srd->rcfd",
        hidden.reshape(seq_len, col_total, hidden_units),
        out_rows,
        preferred_element_type=jnp.float32,
    ).reshape(row_total * col_total, hidden_units, row_width)
    second_term = second_gain * normed_two_grad
    second_part = jnp.sum(normed_two_grad * middle * second_scale, axis=0)
    second_cube = second_scale * second_scale * second_scale
    middle_grad = (
        out_grad
        + second_scale * second_term
        - middle * second_cube * jnp.mean(second_term * middle, axis=1, keepdims=True)
    )
    branch_low = middle_grad.astype(jnp.bfloat16)
    attended_grad = project_back(branch_low, attn_back[3]).astype(jnp.bfloat16)
    output_term = weight_term(attended, branch_low, attn_back[3])
    queries_grad, keys_grad, values_grad, premix_part, postmix_part = attend_back(
        queries.reshape(head_shape),
        keys_all.reshape(head_shape),
        values_all.reshape(head_shape),
        attended_grad.reshape(head_shape),
        logsums,
        premix,
        postmix,
        starts,
    )
    queries_low = queries_grad.astype(jnp.bfloat16)
    keys_low = keys_grad.astype(jnp.bfloat16)
    values_low = values_grad.astype(jnp.bfloat16)
    normed_grad = (
        project_back(queries_low, attn_back[0])
        + project_back(keys_low, attn_back[1])
        + project_back(values_low, attn_back[2])
    )
    query_term = weight_term(normed, queries_low, attn_back[0])
    key_term = weight_term(normed, keys_low, attn_back[1])
    value_term = weight_term(normed, values_low, attn_back[2])
    first_term = first_gain * normed_grad
    first_part = jnp.sum(normed_grad * states * first_scale, axis=0)
    first_cube = first_scale * first_scale * first_scale
    input_grad = (
        middle_grad
        + first_scale * first_term
        - states * first_cube * jnp.mean(first_term * states, axis=1, keepdims=True)
    )
    reduced = (
        lax.psum_scatter(query_term, ("row", "col"), scatter_dimension=0, tiled=True),
        lax.psum_scatter(key_term, ("row", "col"), scatter_dimension=0, tiled=True),
        lax.psum_scatter(value_term, ("row", "col"), scatter_dimension=0, tiled=True),
        lax.psum_scatter(output_term, ("row", "col"), scatter_dimension=0, tiled=True),
        lax.psum_scatter(up_term, ("row", "col"), scatter_dimension=0, tiled=True),
        lax.psum_scatter(down_term, ("row", "col"), scatter_dimension=0, tiled=True),
    )
    up_local = reduced[4][0]
    down_local = reduced[5][0]
    first_grad, second_grad, premix_grad, postmix_grad = lax.psum(
        (first_part, second_part, premix_part, postmix_part), ("row", "col")
    )
    return (
        layer_out,
        distill_loss,
        task_loss,
        input_grad,
        first_grad,
        reduced[0][0],
        reduced[1][0],
        reduced[2][0],
        premix_grad,
        postmix_grad,
        reduced[3][0],
        second_grad,
        up_local,
        down_local,
    )


def solution(mesh):
    placed = (
        P(("row", "col"), None),
        P(("row", "col"), None),
        P(("row", "col"), None),
        P(("row", "col")),
        P(("row", "col"), None),
        P(),
        P("row", "col"),
        P("row", "col"),
        P("row", "col"),
        P(),
        P(),
        P("row", "col"),
        P(),
        P("row", "col"),
        P("col", "row"),
    )
    return jax.shard_map(
        shards,
        mesh=mesh,
        in_specs=placed,
        out_specs=(
            P(("row", "col"), None),
            P(),
            P(),
            P(("row", "col"), None),
            P(),
            P("row", "col"),
            P("row", "col"),
            P("row", "col"),
            P(),
            P(),
            P("row", "col"),
            P(),
            P("row", "col"),
            P("col", "row"),
        ),
        check_vma=False,
    )
```

profile of v0, /device:TPU:0, one launch (start us, length us, event | category | flops | bytes accessed | tf_op | source)
XLA Modules:
  0.0 1282.0 jit_solution(15491567621112611410)
XLA Ops:
  20.1 47.6 %all-gather.19.cloned.1.call-done = bf16[1536,384]{1,0:T(8,128)(2,1)} async-done(((bf16[48,384]{1,0:T(8,128)(2,1)}), bf16[1536,384]{1,0:T(8,128)(2,1)}) %all-gather.19.cloned.1.call-update) | async-done | bytes 1179664 | tf_op jit(solution)/shard_map/all_gather | solution.py:205
  72.2 51.4 %all-gather.15.cloned.1.call-done = bf16[1536,384]{1,0:T(8,128)(2,1)} async-done(((bf16[48,384]{1,0:T(8,128)(2,1)}), bf16[1536,384]{1,0:T(8,128)(2,1)}) %all-gather.15.cloned.1.call-update) | async-done | bytes 1179664 | tf_op jit(solution)/shard_map/all_gather | solution.py:202
  129.8 49.8 %all-gather.17.cloned.1.call-done = bf16[1536,384]{1,0:T(8,128)(2,1)} async-done(((bf16[48,384]{1,0:T(8,128)(2,1)}), bf16[1536,384]{1,0:T(8,128)(2,1)}) %all-gather.17.cloned.1.call-update) | async-done | bytes 1179664 | tf_op jit(solution)/shard_map/all_gather | solution.py:203
  186.6 48.7 %all-gather.13.cloned.1.call-done = bf16[1536,384]{1,0:T(8,128)(2,1)} async-done(((bf16[48,384]{1,0:T(8,128)(2,1)}), bf16[1536,384]{1,0:T(8,128)(2,1)}) %all-gather.13.cloned.1.call-update) | async-done | bytes 1179664 | tf_op jit(solution)/shard_map/all_gather | solution.py:204
  252.5 44.9 %bitcast_reduce_fusion = (f32[12,512]{0,1:T(8,128)S(1)}, f32[512,512,12]{1,2,0:T(8,128)S(1)}) fusion(pred[512,512]{1,0:T(8,128)(4,1)S(1)} %fusion.72, f32[12,12]{1,0:T(8,128)S(1)} %copy-done.43, f32[12,512,512]{2,1,0:T(8,128)} %broadcast_multiply_fusion), kind=kOutput, calls=%fused_computation.14 | convolution fusion | flops 459270144 | bytes 25453120 | tf_op jit(solution)/shard_map/while/body/eval_jaxpr/gh,gqk->hqk/dot_general | solution.py:91
  303.5 22.6 %fusion.12 = bf16[512,512,12]{1,2,0:T(8,128)(2,1)} fusion(f32[512,512,12]{1,2,0:T(8,128)S(1)} %get-tuple-element.115, f32[12,512]{0,1:T(8,128)S(1)} %fusion.15, f32[12,512]{0,1:T(8,128)S(1)} %get-tuple-element.114, pred[512,512]{1,0:T(8,128)(4,1)S(1)} %fusion.72, f32[12,12]{1,0:T(8,128)S(1)} %copy-done), kind=kOutput, calls=%fused_computation.17 | convolution fusion | flops 462422016 | bytes 19186240 | tf_op jit(solution)/shard_map/while/body/eval_jaxpr/hg,hqk->gqk/dot_general | solution.py:97
  326.1 10.4 fusion.58
  379.3 11.7 dot_general.177
  406.3 39.3 %psum.50 = f32[]{:T(128)} all-reduce(f32[]{:T(128)} %get-tuple-element.81), channel_id=1, replica_groups=mesh['row'=16,'col'=2] {'row','col'}, use_global_device_ids=true, to_apply=%region_8.9 | all-reduce | flops 1 | bytes 8 | tf_op jit(solution)/shard_map/psum | solution.py:242
  451.8 11.8 dot_general.183
  483.1 51.5 %fusion.8 = (f32[12,512]{0,1:T(8,128)}, f32[512,512,12]{1,2,0:T(8,128)}) fusion(f32[12,512]{0,1:T(8,128)} %log_add_fusion, f32[512,512,12]{1,2,0:T(8,128)} %copy-done.1, pred[512,512]{1,0:T(8,128)(4,1)S(1)} %fusion.72, f32[12,12]{1,0:T(8,128)S(1)} %copy-done, f32[12,512,512]{2,1,0:T(8,128)S(1)} %fusion.91), kind=kOutput, calls=%fused_computation.10 | convolution fusion | flops 465561600 | bytes 38060608 | tf_op jit(solution)/shard_map/while/body/eval_jaxpr/hg,gqk->hqk/dot_general | solution.py:139
  534.6 28.6 %convert_bitcast_fusion = bf16[12,512,512]{2,0,1:T(8,128)(2,1)} fusion(f32[512,512,12]{1,2,0:T(8,128)} %get-tuple-element.123, f32[12,512]{0,1:T(8,128)} %get-tuple-element.122, f32[12,512]{0,1:T(8,128)} %log_add_fusion, f32[512,512,12]{1,2,0:T(8,128)} %copy-done.1, pred[512,512]{1,0:T(8,128)(4,1)S(1)} %fusion.72, f32[12,12]{1,0:T(8,128)S(1)} %copy-done.43), kind=kOutput, calls=%fused_computation.23 | convolution fusion | flops 468713472 | bytes 31769152 | tf_op jit(solution)/shard_map/while/body/eval_jaxpr/gh,hqk->gqk/dot_general | solution.py:144
  563.2 10.2 multiply_convert_fusion.1
  580.2 10.2 multiply_convert_fusion
  594.1 26.1 %fusion.22 = bf16[512,512,12]{1,2,0:T(8,128)(2,1)} fusion(f32[512,512,12]{1,2,0:T(8,128)} %copy-done.1, f32[12,512]{0,1:T(8,128)S(1)} %copy-done.8, pred[512,512]{1,0:T(8,128)(4,1)S(1)} %fusion.72, f32[12,12]{1,0:T(8,128)S(1)} %copy-done), kind=kOutput, calls=%fused_computation.28 | convolution fusion | flops 459276288 | bytes 19161664 | tf_op jit(solution)/shard_map/while/body/eval_jaxpr/hg,hqk->gqk/dot_general | solution.py:127
  620.2 10.1 fusion.55
  665.7 19.6 %fusion.135 = f32[12,512,512]{2,0,1:T(8,128)} fusion(f32[512,512,12]{1,2,0:T(8,128)} %get-tuple-element.123, f32[12,512]{0,1:T(8,128)S(1)} %copy-done.30, f32[12,512]{0,1:T(8,128)S(1)} %copy-done.8, f32[512,512,12]{1,2,0:T(8,128)} %copy-done.1, pred[512,512]{1,0:T(8,128)(4,1)S(1)} %fusion.72), kind=kLoop, calls=%fused_computation.11.clone.clone.clone.clone.1 | loop fusion | flops 12582912 | bytes 38060032 | tf_op jit(solution)/shard_map/while/body/eval_jaxpr/gqk,hqk->gh/dot_general | solution.py:143
  685.3 31.8 %fusion.61 = f32[12,12]{1,0:T(8,128)S(1)} fusion(f32[12,512,512]{2,1,0:T(8,128)} %broadcast_multiply_fusion, f32[12,512,512]{2,0,1:T(8,128)} %fusion.135), kind=kOutput, calls=%fused_computation.92 | convolution fusion | flops 452984832 | bytes 25166400 | tf_op jit(solution)/shard_map/while/body/eval_jaxpr/gqk,hqk->gh/dot_general | solution.py:143
  717.2 31.1 %fusion.66 = f32[12,12]{1,0:T(8,128)S(1)} fusion(f32[12,512,512]{2,1,0:T(8,128)} %copy-done.2, f32[512,512,12]{1,2,0:T(8,128)S(1)} %bitcast.306, f32[12,512]{0,1:T(8,128)S(1)} %copy-done.8, pred[512,512]{1,0:T(8,128)(4,1)S(1)} %fusion.72), kind=kOutput, calls=%fused_computation.93 | convolution fusion | flops 459276288 | bytes 25453120 | tf_op jit(solution)/shard_map/while/body/eval_jaxpr/hqk,gqk->hg/dot_general | solution.py:136
  748.4 41.2 %all-reduce = (f32[]{:T(128)}, f32[]{:T(128)}, f32[768]{0:T(1024)}, f32[12,12]{1,0:T(8,128)}, f32[12,12]{1,0:T(8,128)}, /*index=5*/f32[768]{0:T(1024)}) all-reduce(f32[]{:T(128)} %get-tuple-element.82, f32[]{:T(128)} %get-tuple-element.80, f32[768]{0:T(1024)S(1)} %get-tuple-element.76, ...), channel_id=1, replica_groups=mesh['row'=16,'col'=2] {'row','col'}, use_global_device_ids=true, to_apply=%region_6.7 | all-reduce | flops 1826 | bytes 14608 | tf_op jit(solution)/shard_map/psum | solution.py:242
  795.7 89.5 %reduce-scatter.9.cloned.1.call-done = f32[1,48,384]{2,1,0:T(8,128)} async-done(((f32[32,48,384]{2,1,0:T(8,128)}), f32[1,48,384]{2,1,0:T(8,128)}) %reduce-scatter.9.cloned.1.call-update) | async-done | bytes 73744 | tf_op jit(solution)/shard_map/reduce_scatter | solution.py:323
  885.2 104.3 %reduce-scatter.11.cloned.1.call-done = f32[1,48,384]{2,1,0:T(8,128)} async-done(((f32[32,48,384]{2,1,0:T(8,128)}), f32[1,48,384]{2,1,0:T(8,128)}) %reduce-scatter.11.cloned.1.call-update) | async-done | bytes 73744 | tf_op jit(solution)/shard_map/reduce_scatter | solution.py:324
  989.5 141.7 %reduce-scatter.15.cloned.1.call-done = f32[1,48,1536]{2,1,0:T(8,128)} async-done(((f32[32,48,1536]{2,1,0:T(8,128)}), f32[1,48,1536]{2,1,0:T(8,128)}) %reduce-scatter.15.cloned.1.call-update) | async-done | bytes 294928 | tf_op jit(solution)/shard_map/reduce_scatter | solution.py:326
  1131.2 141.5 %reduce-scatter.17.cloned.1.call-done = f32[1,1536,48]{1,2,0:T(8,128)} async-done(((f32[32,1536,48]{1,2,0:T(8,128)}), f32[1,1536,48]{1,2,0:T(8,128)}) %reduce-scatter.17.cloned.1.call-update) | async-done | bytes 294928 | tf_op jit(solution)/shard_map/reduce_scatter | solution.py:327
  (199 shorter events, 184.4 us)
Async XLA Ops:
  7.2 296.3 %copy-start = (f32[12,12]{1,0:T(8,128)S(1)}, f32[12,12]{1,0:T(8,128)}, u32[]{:S(2)}) copy-start(f32[12,12]{1,0:T(8,128)} %param.25) | copy-start | bytes 1732
  7.2 60.5 %all-gather.19.cloned.1.call-start = ((), (), s32[]{:S(2)}) async-start(), calls=%async_computation.15 | async-start | bytes 1216512 | tf_op jit(solution)/shard_map/all_gather | solution.py:205
  7.9 115.7 %all-gather.15.cloned.1.call-start = ((), (), s32[]{:S(2)}) async-start(), calls=%async_computation.13 | async-start | bytes 1216512 | tf_op jit(solution)/shard_map/all_gather | solution.py:202
  8.7 170.9 %all-gather.17.cloned.1.call-start = ((), (), s32[]{:S(2)}) async-start(), calls=%async_computation.14 | async-start | bytes 1216512 | tf_op jit(solution)/shard_map/all_gather | solution.py:203
  9.4 225.9 %all-gather.13.cloned.1.call-start = ((), (), s32[]{:S(2)}) async-start(), calls=%async_computation.12 | async-start | bytes 1216512 | tf_op jit(solution)/shard_map/all_gather | solution.py:204
  10.0 330.8 %all-gather.23.cloned.1.call-start = ((), (), s32[]{:S(2)}) async-start(), calls=%async_computation.17 | async-start | bytes 4866048 | tf_op jit(solution)/shard_map/all_gather | solution.py:207
  10.6 354.6 %all-gather.21.cloned.1.call-start = ((), (), s32[]{:S(2)}) async-start(), calls=%async_computation.16 | async-start | bytes 4866048 | tf_op jit(solution)/shard_map/all_gather | solution.py:206
  11.1 784.5 %reduce-scatter.7.cloned.1.call-start = ((), (), s32[]{:S(2)}) async-start(), calls=%async_computation.6 | async-start | bytes 2433024 | tf_op jit(solution)/shard_map/reduce_scatter | solution.py:322
  18.5 220.6 %copy-start.5 = (bf16[512,768]{0,1:T(8,128)(2,1)}, bf16[512,768]{0,1:T(8,128)(2,1)S(1)}, u32[]{:S(2)}) copy-start(bf16[512,768]{0,1:T(8,128)(2,1)S(1)} %copy.80) | copy-start | bytes 2359300
  129.8 116.4 %copy-start.22 = (bf16[512,768]{0,1:T(8,128)(2,1)}, bf16[512,768]{0,1:T(8,128)(2,1)S(1)}, u32[]{:S(2)}) copy-start(bf16[512,768]{0,1:T(8,128)(2,1)S(1)} %copy.84) | copy-start | bytes 2359300
  340.0 51.1 %copy-start.15 = (bf16[512,768]{0,1:T(8,128)(2,1)}, bf16[512,768]{0,1:T(8,128)(2,1)S(1)}, u32[]{:S(2)}) copy-start(bf16[512,768]{0,1:T(8,128)(2,1)S(1)} %copy.90) | copy-start | bytes 2359300
  483.1 51.5 %copy-start.2 = (f32[12,512,512]{2,1,0:T(8,128)}, f32[12,512,512]{2,1,0:T(8,128)S(1)}, u32[]{:S(2)}) copy-start(f32[12,512,512]{2,1,0:T(8,128)S(1)} %fusion.91) | copy-start | bytes 37748740
  534.6 28.6 %copy-start.25 = (bf16[512,768]{0,1:T(8,128)(2,1)S(1)}, bf16[512,768]{0,1:T(8,128)(2,1)}, u32[]{:S(2)}) copy-start(bf16[512,768]{0,1:T(8,128)(2,1)} %copy.86) | copy-start | bytes 2359300
  576.1 219.6 %reduce-scatter.13.cloned.1.call-start = ((), (), s32[]{:S(2)}) async-start(), calls=%async_computation.9 | async-start | bytes 2433024 | tf_op jit(solution)/shard_map/reduce_scatter | solution.py:325
  579.9 305.3 %reduce-scatter.9.cloned.1.call-start = ((), (), s32[]{:S(2)}) async-start(), calls=%async_computation.7 | async-start | bytes 2433024 | tf_op jit(solution)/shard_map/reduce_scatter | solution.py:323
  593.8 26.5 %copy-start.27 = (bf16[512,768]{0,1:T(8,128)(2,1)S(1)}, bf16[512,768]{0,1:T(8,128)(2,1)}, u32[]{:S(2)}) copy-start(bf16[512,768]{0,1:T(8,128)(2,1)} %copy.100) | copy-start | bytes 2359300
  593.8 395.8 %reduce-scatter.11.cloned.1.call-start = ((), (), s32[]{:S(2)}) async-start(), calls=%async_computation.8 | async-start | bytes 2433024 | tf_op jit(solution)/shard_map/reduce_scatter | solution.py:324
  632.8 498.4 %reduce-scatter.15.cloned.1.call-start = ((), (), s32[]{:S(2)}) async-start(), calls=%async_computation.10 | async-start | bytes 9732096 | tf_op jit(solution)/shard_map/reduce_scatter | solution.py:326
  650.3 622.4 %reduce-scatter.17.cloned.1.call-start = ((), (), s32[]{:S(2)}) async-start(), calls=%async_computation.11 | async-start | bytes 9732096 | tf_op jit(solution)/shard_map/reduce_scatter | solution.py:327
  665.7 51.5 %slice-start = ((s8[16777216]{0:T(1024)(128)(4,1)}), s8[4194304]{0:T(1024)(128)(4,1)S(1)}, s32[]{:S(2)}) async-start(s8[16777216]{0:T(1024)(128)(4,1)} %bitcast.305), calls=%async_computation.18 | async-start | bytes 8388608
  665.7 51.5 %slice-start.1 = ((s8[16777216]{0:T(1024)(128)(4,1)}), s8[4194304]{0:T(1024)(128)(4,1)S(1)}, s32[]{:S(2)}) async-start(s8[16777216]{0:T(1024)(128)(4,1)} %bitcast.305), calls=%async_computation.19 | async-start | bytes 8388608
  685.3 31.9 %slice-start.2 = ((s8[16777216]{0:T(1024)(128)(4,1)}), s8[4194304]{0:T(1024)(128)(4,1)S(1)}, s32[]{:S(2)}) async-start(s8[16777216]{0:T(1024)(128)(4,1)} %bitcast.305), calls=%async_computation.20 | async-start | bytes 8388608
  685.3 31.9 %slice-start.3 = ((s8[16777216]{0:T(1024)(128)(4,1)}), s8[4194304]{0:T(1024)(128)(4,1)S(1)}, s32[]{:S(2)}) async-start(s8[16777216]{0:T(1024)(128)(4,1)} %bitcast.305), calls=%async_computation.21 | async-start | bytes 8388608
  717.2 74.9 %copy-start.45 = (f32[512]{0:T(512)S(1)}, f32[512]{0:T(512)}, u32[]{:S(2)}) copy-start(f32[512]{0:T(512)} %get-tuple-element.108) | copy-start | bytes 6148
  (39 other events, 177.0 us)
Sparse Core Ops, SparseCore 0:
  10.9 56.7 all-gather.18
  70.6 52.9 all-gather.14
  126.6 52.9 all-gather.16
  182.3 52.9 all-gather.12
  238.0 62.4 all-gather.22
  303.3 61.8 all-gather.20
  576.2 99.9 reduce-scatter.6
  682.0 98.5 reduce-scatter.12
  786.5 98.6 reduce-scatter.8
  890.9 98.5 reduce-scatter.10
  996.0 135.1 reduce-scatter.14
  1137.5 135.1 reduce-scatter.16
where the time goes:
time: 1290 us; the launch traced here: 1280 us
  waiting for transfers between devices  679 us (53%)
  matrix products  343 us (27%)
  local copies, waits for them, and re-layouts  114 us (9%)
  blocking collectives  80.4 us (6%)
  other arithmetic  42.7 us (3%)
  between operations  22 us (2%)
    reduce_scatter x1, waiting for transfers between devices, shards(): lax.psum_scatter(up_term, ('row', 'col'), scatter_dimension=0, tiled=True)  142 us
    reduce_scatter x1, waiting for transfers between devices, shards(): lax.psum_scatter(down_term, ('row', 'col'), scatter_dimension=0, tiled=True)  141 us
    reduce_scatter x1, waiting for transfers between devices, shards(): lax.psum_scatter(value_term, ('row', 'col'), scatter_dimension=0, tiled=T...  104 us
    reduce_scatter x1, waiting for transfers between devices, shards(): lax.psum_scatter(key_term, ('row', 'col'), scatter_dimension=0, tiled=True)  89.5 us
    psum x2, blocking collectives, shards(): lax.psum((jnp.sum(valid_marks), jnp.sum(valid_marks * jnp.sum(differ * di...  80.4 us
    dot_general x1, matrix products, one_block(): jnp.einsum('hg,gqk->hqk', postmix, weight_grad, precision=HIGHEST)  51.5 us
    all_gather x1, waiting for transfers between devices, shards(): lax.all_gather(query_weight[None], ('row', 'col'), axis=0, tiled=True)  51.4 us
    all_gather x1, waiting for transfers between devices, shards(): lax.all_gather(key_weight[None], ('row', 'col'), axis=0, tiled=True)  49.8 us
  transfers between devices with their start and end apart: 12, of which 9 were waited for; matrix products, arithmetic and copies ran while one was open for 25% of the time, Pallas kernels for 0%

commit v1 on v0

v1 whole, which is shorter than its diff:
```python
import functools

import jax
import jax.numpy as jnp
from jax import lax
from jax.experimental import pallas as pl
from jax.experimental.pallas import tpu as pltpu
from jax.sharding import PartitionSpec as P

HEADS = 12
HEAD_DIM = 64
PIC = 256
EPSILON = 1e-06
F32 = jnp.float32
BF16 = jnp.bfloat16
AXES = ("row", "col")
X_BIT, CORE_BIT, Y_BIT, Z_BIT = 1, 2, 4, 8
PLANE = (X_BIT, Y_BIT, X_BIT | Y_BIT)
LINE = (Z_BIT, 2 * Z_BIT, 3 * Z_BIT)
EXTRA = 128
PARAMS = pltpu.CompilerParams(vmem_limit_bytes=60000 * 1024)
SMEM = pl.BlockSpec(memory_space=pltpu.SMEM)
ANY = pl.BlockSpec(memory_space=pl.ANY)
VMEM = pl.BlockSpec(memory_space=pltpu.VMEM)


def dot(a, b):
    return lax.dot_general(a, b, (((1,), (0,)), ((), ())), preferred_element_type=F32)


def dot_nt(a, b):
    return lax.dot_general(a, b, (((1,), (1,)), ((), ())), preferred_element_type=F32)


def place_copies(spot, pieces, wholes, rows_at, cols_at, widths, sems):
    if len(pieces) == len(wholes):
        return [
            pltpu.make_async_copy(piece, whole, sems.at[n])
            for n, (piece, whole) in enumerate(zip(pieces, wholes))
        ]
    copies = []
    for k, piece in enumerate(pieces):
        core, y, x = k // 4, (k // 2) % 2, k % 2
        for z in range(4):
            r = ((spot[0] ^ z) * 2 + (spot[1] ^ y)) * 2 + (spot[2] ^ core)
            c = spot[3] ^ x
            for whole, row, col, width in zip(wholes, rows_at, cols_at, widths):
                depth = whole.shape[0] // 16
                copies.append(
                    pltpu.make_async_copy(
                        piece.at[z, pl.ds(row, depth), pl.ds(col, width)],
                        whole.at[
                            pl.ds(pl.multiple_of(r * depth, 16), depth),
                            pl.ds(pl.multiple_of(c * width, 128), width),
                        ],
                        sems.at[len(copies)],
                    )
                )
    return copies


def send_copies(spot, source, keep, send, row, half, col, width, sems):
    depth = source.shape[0] // 16
    copies = []
    for j in range(8):
        z, y = j // 2, j % 2
        plane = (spot[1] ^ y) * 2 + (spot[3] ^ half)
        for n, (target, core) in enumerate(((keep, spot[2]), (send, 1 - spot[2]))):
            start = pl.multiple_of((2 * j + core) * depth, 16)
            copies.append(
                pltpu.make_async_copy(
                    source.at[pl.ds(start, depth), pl.ds(0, width)],
                    target.at[plane, spot[0] ^ z, pl.ds(row, depth), pl.ds(col, width)],
                    sems.at[2 * j + n],
                )
            )
    return copies


def attend_kernel(blocks, spot, starts, normed_ref, *rest):
    pieces, rest = rest[:blocks], rest[blocks:]
    pm_ref, po_ref, q_ref, k_ref, v_ref, out_ref, p_ref, wq, wk, wv, kt, bias, acc, sems = rest
    step = pl.program_id(0)
    half = normed_ref.shape[0] // 2

    @pl.when(step == 0)
    def _():
        width = wq.shape[1] // 2
        depth = wq.shape[0] // 16
        copies = place_copies(
            spot, pieces, (wq, wk, wv), (0, depth, 2 * depth), (0, 0, 0), (width,) * 3, sems
        )
        for copy in copies:
            copy.start()
        rows = lax.broadcasted_iota(jnp.int32, (half, half), 0)
        cols = lax.broadcasted_iota(jnp.int32, (half, half), 1)
        for b in range(2):
            i, j = rows + b * half, cols + b * half
            ok = j <= i
            for s in range(2):
                p = starts[0, s]
                ok = ok | ((i >= p) & (i < p + PIC) & (j >= p) & (j < p + PIC))
            bias[b] = jnp.where(ok, 0.0, -1e30)
        acc[...] = jnp.zeros_like(acc)
        for copy in copies:
            copy.wait()
        k_ref[...] = dot(normed_ref[...], wk[...]).astype(BF16)
        kt[...] = k_ref[...].T
        q_ref[...] = dot(normed_ref[...], wq[...]).astype(BF16)
        v_ref[...] = dot(normed_ref[...], wv[...]).astype(BF16)

    pm = pm_ref[0]
    po = po_ref[0]
    vs = (v_ref[...].astype(F32) * po).astype(BF16)
    top = (q_ref[:half].astype(F32) * pm).astype(BF16)
    low = (q_ref[half:].astype(F32) * pm).astype(BF16)
    s0 = dot(top, kt[:, :half]) + bias[0]
    s1 = dot(low, kt[:, :half])
    s2 = dot(low, kt[:, half:]) + bias[1]
    m0 = jnp.max(s0, axis=1, keepdims=True)
    e0 = jnp.exp(s0 - m0)
    p0 = (e0 / jnp.sum(e0, axis=1, keepdims=True)).astype(BF16)
    m1 = jnp.maximum(jnp.max(s1, axis=1, keepdims=True), jnp.max(s2, axis=1, keepdims=True))
    e1 = jnp.exp(s1 - m1)
    e2 = jnp.exp(s2 - m1)
    inv = 1.0 / (jnp.sum(e1, axis=1, keepdims=True) + jnp.sum(e2, axis=1, keepdims=True))
    p1 = (e1 * inv).astype(BF16)
    p2 = (e2 * inv).astype(BF16)
    p_ref[0, :, :half] = p0
    p_ref[0, :, half : 2 * half] = p1
    p_ref[0, :, 2 * half :] = p2
    acc[:half] += dot(p0, vs[:half])
    acc[half:] += dot(p1, vs[:half]) + dot(p2, vs[half:])

    @pl.when(step == HEADS - 1)
    def _():
        out_ref[...] = acc[...].astype(BF16)


def attend(spot, starts, normed, pieces, pm, po):
    seq, width = normed.shape
    half = seq // 2
    whole = pl.BlockSpec((seq, width), lambda h: (0, 0))
    row = pl.BlockSpec((1, 1, width), lambda h: (h, 0, 0))
    low = jax.ShapeDtypeStruct((seq, width), BF16)
    return pl.pallas_call(
        functools.partial(attend_kernel, len(pieces)),
        grid=(HEADS,),
        in_specs=[SMEM, SMEM, whole] + [ANY] * len(pieces) + [row, row],
        out_specs=[whole] * 4 + [pl.BlockSpec((1, half, 3 * half), lambda h: (h, 0, 0))],
        out_shape=[low] * 4 + [jax.ShapeDtypeStruct((HEADS, half, 3 * half), BF16)],
        scratch_shapes=[pltpu.VMEM((width, width), BF16)] * 3
        + [
            pltpu.VMEM((width, seq), BF16),
            pltpu.VMEM((2, half, half), F32),
            pltpu.VMEM((seq, width), F32),
            pltpu.SemaphoreType.DMA((96,)),
        ],
        compiler_params=PARAMS,
        name="attend",
    )(spot, starts, normed, *pieces, pm, po)


def middle_kernel(blocks, outs, spot, factor, *rest):
    pieces, rest = rest[:blocks], rest[blocks:]
    att_ref, states_ref, up_ref, teach_ref, valid_ref, gain_ref = rest[:6]
    layer_ref, mid_ref, agrad_ref, sums_ref = rest[6:10]
    grads, rest = rest[10 : 10 + outs], rest[10 + outs :]
    wo, wu, wd, hidden, pre, n2t, olt, slots, sems, out_sems = rest
    seq, width = att_ref.shape
    units = wu.shape[1]
    blocked = blocks == 8
    copies = place_copies(
        spot,
        pieces,
        (wo, wu, wd),
        (0, 0, 0),
        (units, 0, units // 2),
        (width // 2, units // 2, units // 2),
        sems,
    )
    for copy in copies:
        copy.start()
    for n, copy in enumerate(copies):
        if n % 3 == 0:
            copy.wait()
    mid_ref[...] = states_ref[...] + dot(att_ref[...], wo[...])
    middle = mid_ref[...]
    scale = lax.rsqrt(jnp.mean(middle * middle, axis=1, keepdims=True) + EPSILON)
    n2 = (middle * scale * gain_ref[...]).astype(BF16)
    n2t[...] = n2.T
    for n, copy in enumerate(copies):
        if n % 3 != 0:
            copy.wait()

    chunk = 512
    steps = units // chunk

    def up_step(j, _):
        at = pl.ds(pl.multiple_of(j * chunk, chunk), chunk)
        hidden[:, at] = jnp.maximum(dot(n2, wu[:, at]), 0.0).astype(BF16)
        return 0

    lax.fori_loop(0, steps, up_step, 0)
    layer_ref[...] = mid_ref[...] + dot_nt(hidden[...], wd[...])
    layer = layer_ref[...]
    valid = valid_ref[...].astype(F32)
    upstream = up_ref[...]
    differ = layer - teach_ref[...]
    sums_ref[1:2, :] = jnp.sum(valid * (differ * differ), axis=0, keepdims=True)
    sums_ref[2:3, :] = jnp.sum(valid * (upstream * layer), axis=0, keepdims=True)
    out_grad = (factor[0, 0] * valid) * (upstream + differ)
    out_low = out_grad.astype(BF16)
    olt[...] = out_low.T

    def down_step(j, _):
        at = pl.ds(pl.multiple_of(j * chunk, chunk), chunk)
        part = hidden[:, at]
        back = jnp.where(part > 0, dot(out_low, wd[:, at]), 0.0).astype(BF16)
        pre[:, at] = back
        for which, (left, right) in enumerate(((n2t, back), (olt, part))):
            slot = slots.at[which]

            @pl.when(j > 0)
            def _():
                for copy in grad_copies(which, j - 1):
                    copy.wait()

            slot[...] = dot(left[...], right).astype(BF16)
            for copy in grad_copies(which, j):
                copy.start()
        return 0

    def grad_copies(which, j):
        if not blocked:
            at = pl.ds(pl.multiple_of(j * chunk, chunk), chunk)
            return [pltpu.make_async_copy(slots.at[which], grads[which].at[:, at], out_sems.at[which, 0])]
        per = steps // 2
        return send_copies(
            spot,
            slots.at[which],
            grads[0],
            grads[1],
            0,
            j // per,
            pl.multiple_of(which * (units // 2) + (j % per) * chunk, 128),
            chunk,
            out_sems.at[which],
        )

    lax.fori_loop(0, steps, down_step, 0)
    grad = dot_nt(pre[...], wu[...])
    middle = mid_ref[...]
    scale = lax.rsqrt(jnp.mean(middle * middle, axis=1, keepdims=True) + EPSILON)
    sums_ref[0:1, :] = jnp.sum(grad * middle * scale, axis=0, keepdims=True)
    term = gain_ref[...] * grad
    inner = jnp.mean(term * middle, axis=1, keepdims=True)
    layer = layer_ref[...]
    out_grad = (factor[0, 0] * valid_ref[...].astype(F32)) * (
        up_ref[...] + (layer - teach_ref[...])
    )
    mid_grad = out_grad + scale * term - middle * (scale * scale * scale) * inner
    mid_ref[...] = mid_grad
    branch = mid_grad.astype(BF16)
    agrad_ref[...] = dot_nt(branch, wo[...]).astype(BF16)
    n2t[...] = att_ref[...].T
    for which in range(2):
        for copy in grad_copies(which, steps - 1):
            copy.wait()
    half = width // 2
    last = []
    for c in range(2):
        slots[c, :, :half] = dot(n2t[...], branch[:, c * half : (c + 1) * half]).astype(BF16)
        if blocked:
            made = send_copies(
                spot, slots.at[c], grads[0], grads[1], 0, c, units, half, out_sems.at[c]
            )
        else:
            made = [
                pltpu.make_async_copy(
                    slots.at[c, :, pl.ds(0, half)],
                    grads[2].at[:, pl.ds(c * half, half)],
                    out_sems.at[c, 0],
                )
            ]
        for copy in made:
            copy.start()
        last += made
    for copy in last:
        copy.wait()


def middle_block(spot, factor, pieces, attended, states, upstream, teacher, valid, gain, units):
    seq, width = attended.shape
    full = jax.ShapeDtypeStruct((seq, width), F32)
    if len(pieces) == 8:
        depth = width // 16
        grads = [jax.ShapeDtypeStruct((4, 4, depth, units + width // 2), BF16)] * 2
    else:
        grads = [
            jax.ShapeDtypeStruct((width, units), BF16),
            jax.ShapeDtypeStruct((width, units), BF16),
            jax.ShapeDtypeStruct((width, width), BF16),
        ]
    return pl.pallas_call(
        functools.partial(middle_kernel, len(pieces), len(grads)),
        in_specs=[SMEM, SMEM] + [ANY] * len(pieces) + [VMEM] * 6,
        out_specs=[VMEM] * 4 + [ANY] * len(grads),
        out_shape=[
            full,
            full,
            jax.ShapeDtypeStruct((seq, width), BF16),
            jax.ShapeDtypeStruct((8, width), F32),
        ]
        + grads,
        scratch_shapes=[
            pltpu.VMEM((width, width), BF16),
            pltpu.VMEM((width, units), BF16),
            pltpu.VMEM((width, units), BF16),
            pltpu.VMEM((seq, units), BF16),
            pltpu.VMEM((seq, units), BF16),
            pltpu.VMEM((width, seq), BF16),
            pltpu.VMEM((width, seq), BF16),
            pltpu.VMEM((2, width, 512), BF16),
            pltpu.SemaphoreType.DMA((96,)),
            pltpu.SemaphoreType.DMA((2, 16)),
        ],
        compiler_params=PARAMS,
        name="middle",
    )(spot, factor, *pieces, attended, states, upstream, teacher, valid, gain)


def attend_back_kernel(
    blocked, spot, pms, pos, nt_ref, q_ref, k_ref, v_ref, g_ref, p_ref, pm_ref, po_ref,
    dq_ref, dk_ref, dv_ref, pre_ref, post_ref, *rest,
):
    outs = 2 if blocked else 3
    grads = rest[:outs]
    vt, qt, gt, dq, dkt, dvt, slots, sems = rest[outs:]
    step = pl.program_id(0)
    seq, width = q_ref.shape
    half = seq // 2

    @pl.when(step == 0)
    def _():
        vt[...] = v_ref[...].T
        qt[...] = q_ref[...].T
        gt[...] = g_ref[...].T
        dq[...] = jnp.zeros_like(dq)
        dkt[...] = jnp.zeros_like(dkt)
        dvt[...] = jnp.zeros_like(dvt)

    pm = pm_ref[0]
    po = po_ref[0]
    p0, p1, p2 = (p_ref[0, :, b * half : (b + 1) * half] for b in range(3))
    top = (g_ref[:half].astype(F32) * po).astype(BF16)
    low = (g_ref[half:].astype(F32) * po).astype(BF16)
    g0 = dot(top, vt[:, :half])
    g1 = dot(low, vt[:, :half])
    g2 = dot(low, vt[:, half:])
    u0 = dot(gt[:, :half], p0) + dot(gt[:, half:], p1)
    u1 = dot(gt[:, half:], p2)
    f0, f1, f2 = p0.astype(F32), p1.astype(F32), p2.astype(F32)
    t0 = f0 * g0
    d0 = (t0 - f0 * jnp.sum(t0, axis=1, keepdims=True)).astype(BF16)
    t1, t2 = f1 * g1, f2 * g2
    r1 = jnp.sum(t1, axis=1, keepdims=True) + jnp.sum(t2, axis=1, keepdims=True)
    d1 = (t1 - f1 * r1).astype(BF16)
    d2 = (t2 - f2 * r1).astype(BF16)
    w0 = dot(d0, k_ref[:half])
    w1 = dot(d1, k_ref[:half]) + dot(d2, k_ref[half:])
    dq[:half] += pm * w0
    dq[half:] += pm * w1
    pre_ref[0] = jnp.sum(q_ref[:half].astype(F32) * w0, axis=0, keepdims=True) + jnp.sum(
        q_ref[half:].astype(F32) * w1, axis=0, keepdims=True
    )
    for g in range(HEADS):
        at = slice(g * HEAD_DIM, (g + 1) * HEAD_DIM)
        b = pos[step, g]
        u0g, u1g = u0[at], u1[at]
        dvt[at, :half] += b * u0g
        dvt[at, half:] += b * u1g
        both = u0g * vt[at, :half].astype(F32) + u1g * vt[at, half:].astype(F32)
        post_ref[0, g : g + 1, :] = jnp.sum(both, axis=0, keepdims=True)
    qs = jnp.concatenate(
        [
            (qt[g * HEAD_DIM : (g + 1) * HEAD_DIM].astype(F32) * pms[step, g]).astype(BF16)
            for g in range(HEADS)
        ],
        axis=0,
    )
    dkt[:, :half] += dot(qs[:, :half], d0) + dot(qs[:, half:], d1)
    dkt[:, half:] += dot(qs[:, half:], d2)

    @pl.when(step == HEADS - 1)
    def _():
        dq_ref[...] = dq[...].astype(BF16)
        dk_ref[...] = dkt[...].astype(BF16).T
        dv_ref[...] = dvt[...].astype(BF16).T
        made = []
        for n, ref in enumerate((dq_ref, dk_ref, dv_ref)):
            slots[n] = dot(nt_ref[...], ref[...]).astype(BF16)
            if blocked:
                part = width // 2
                for c in range(2):
                    made += send_copies(
                        spot,
                        slots.at[n, :, pl.ds(c * part, part)],
                        grads[0],
                        grads[1],
                        n * (width // 16),
                        c,
                        0,
                        part,
                        sems.at[2 * n + c],
                    )
            else:
                made.append(pltpu.make_async_copy(slots.at[n], grads[n], sems.at[n, 0]))
            for copy in made[-32 if blocked else -1 :]:
                copy.start()
        for copy in made:
            copy.wait()


def attend_back(spot, blocked, nt, q, k, v, g, p, pm, po, pms, pos):
    seq, width = q.shape
    half = seq // 2
    whole = pl.BlockSpec((seq, width), lambda h: (0, 0))
    row = pl.BlockSpec((1, 1, width), lambda h: (h, 0, 0))
    low = jax.ShapeDtypeStruct((seq, width), BF16)
    if blocked:
        grads = [jax.ShapeDtypeStruct((4, 4, 3 * (width // 16), width // 2), BF16)] * 2
    else:
        grads = [jax.ShapeDtypeStruct((width, width), BF16)] * 3
    return pl.pallas_call(
        functools.partial(attend_back_kernel, blocked),
        grid=(HEADS,),
        in_specs=[SMEM, SMEM, SMEM, pl.BlockSpec((width, seq), lambda h: (0, 0))]
        + [whole] * 4
        + [pl.BlockSpec((1, half, 3 * half), lambda h: (h, 0, 0)), row, row],
        out_specs=[whole] * 3
        + [row, pl.BlockSpec((1, HEADS, half), lambda h: (h, 0, 0))]
        + [ANY] * len(grads),
        out_shape=[low] * 3
        + [
            jax.ShapeDtypeStruct((HEADS, 1, width), F32),
            jax.ShapeDtypeStruct((HEADS, HEADS, half), F32),
        ]
        + grads,
        scratch_shapes=[pltpu.VMEM((width, seq), BF16)] * 3
        + [
            pltpu.VMEM((seq, width), F32),
            pltpu.VMEM((width, seq), F32),
            pltpu.VMEM((width, seq), F32),
            pltpu.VMEM((3, width, width), BF16),
            pltpu.SemaphoreType.DMA((6, 16)),
        ],
        compiler_params=PARAMS,
        name="attend_back",
    )(spot, pms, pos, nt, q, k, v, g, p, pm, po)


def input_kernel(blocks, spot, *rest):
    pieces, rest = rest[:blocks], rest[blocks:]
    dq_ref, dk_ref, dv_ref, states_ref, mid_ref, gain_ref, out_ref, first_ref = rest[:8]
    wq, wk, wv, sems = rest[8:]
    width = wq.shape[1] // 2
    depth = wq.shape[0] // 16
    copies = place_copies(
        spot, pieces, (wq, wk, wv), (0, depth, 2 * depth), (0, 0, 0), (width,) * 3, sems
    )
    for copy in copies:
        copy.start()
    states = states_ref[...]
    scale = lax.rsqrt(jnp.mean(states * states, axis=1, keepdims=True) + EPSILON)
    for copy in copies:
        copy.wait()
    grad = (
        dot_nt(dq_ref[...], wq[...]) + dot_nt(dk_ref[...], wk[...]) + dot_nt(dv_ref[...], wv[...])
    )
    first_ref[...] = jnp.broadcast_to(
        jnp.sum(grad * states * scale, axis=0, keepdims=True), first_ref.shape
    )
    term = gain_ref[...] * grad
    inner = jnp.mean(term * states, axis=1, keepdims=True)
    out_ref[...] = mid_ref[...] + scale * term - states * (scale * scale * scale) * inner


def input_block(spot, pieces, dq, dk, dv, states, mid_grad, gain):
    seq, width = dq.shape
    return pl.pallas_call(
        functools.partial(input_kernel, len(pieces)),
        in_specs=[SMEM] + [ANY] * len(pieces) + [VMEM] * 6,
        out_specs=[VMEM] * 2,
        out_shape=[
            jax.ShapeDtypeStruct((seq, width), F32),
            jax.ShapeDtypeStruct((8, width), F32),
        ],
        scratch_shapes=[pltpu.VMEM((width, width), BF16)] * 3 + [pltpu.SemaphoreType.DMA((96,))],
        compiler_params=PARAMS,
        name="input_grad",
    )(spot, *pieces, dq, dk, dv, states, mid_grad, gain)


def exchange(value, mask, total):
    return lax.ppermute(value, AXES, [(i, i ^ mask) for i in range(total)])


def gather_blocks(packet, total):
    line = jnp.stack([packet] + [exchange(packet, m, total) for m in LINE])
    plane = [line] + [exchange(line, m, total) for m in PLANE]
    return plane + [exchange(part, CORE_BIT, total) for part in plane]


def add_low(*terms):
    return functools.reduce(jnp.add, [t.astype(F32) for t in terms])


def reduce_blocks(keep, send, total):
    other = exchange(send, CORE_BIT, total)
    away = [
        exchange(add_low(keep[k], other[k]).astype(BF16), m, total) for k, m in enumerate(PLANE, 1)
    ]
    line = add_low(keep[0], other[0], *away)
    far = [exchange(line[k].astype(BF16), m, total) for k, m in enumerate(LINE, 1)]
    return add_low(line[0], *far)


def reduce_small(value, total):
    value = value + exchange(value, CORE_BIT, total)
    value = add_low(value, *[exchange(value, m, total) for m in PLANE])
    return add_low(value, *[exchange(value, m, total) for m in LINE])


def gather_whole(block):
    rows, cols = lax.axis_size("row"), lax.axis_size("col")
    depth, width = block.shape
    every = lax.all_gather(block[None], AXES, axis=0, tiled=True)
    every = every.reshape(rows, cols, depth, width).transpose(0, 2, 1, 3)
    return every.reshape(rows * depth, cols * width)


def scatter_whole(grad):
    rows, cols = lax.axis_size("row"), lax.axis_size("col")
    depth, width = grad.shape[0] // rows, grad.shape[1] // cols
    parts = grad.reshape(rows, depth, cols, width).transpose(0, 2, 1, 3)
    parts = parts.reshape(rows * cols, depth, width).astype(F32)
    return lax.psum_scatter(parts, AXES, scatter_dimension=0, tiled=True)[0]


def shards(
    states,
    upstream,
    teacher,
    validity,
    picture_start,
    first_gain,
    query_weight,
    key_weight,
    value_weight,
    premix,
    postmix,
    output_weight,
    second_gain,
    up_weight,
    down_weight,
):
    row_total = lax.axis_size("row")
    col_total = lax.axis_size("col")
    total = row_total * col_total
    seq_len, features = states.shape
    depth, width = query_weight.shape
    units = up_weight.shape[1] * col_total
    blocked = (row_total, col_total) == (16, 2)
    row = lax.axis_index("row")
    spot = jnp.stack([row // 4, (row // 2) % 2, row % 2, lax.axis_index("col")]).astype(jnp.int32)
    count = jnp.sum(validity)
    down_turned = down_weight.T
    if blocked:
        packet = jnp.concatenate([query_weight, key_weight, value_weight], axis=0)
        qkv = gather_blocks(packet, total)
        lanes = lax.broadcasted_iota(jnp.int32, (depth, EXTRA), 1)
        digits = jnp.where(lanes == 0, count // 256, jnp.where(lanes == 1, count % 256, 0))
        packet = jnp.concatenate(
            [up_weight, down_turned, output_weight, digits.astype(BF16)], axis=1
        )
        rest = gather_blocks(packet, total)
        at = 2 * up_weight.shape[1] + width
        marks = sum(jnp.sum(part[:, 0, at : at + 2].astype(F32), axis=0) for part in rest)
        total_valid = marks[0] * 256.0 + marks[1]
    else:
        qkv = [gather_whole(w) for w in (query_weight, key_weight, value_weight)]
        rest = [gather_whole(w) for w in (output_weight, up_weight, down_turned)]
        total_valid = lax.psum(count.astype(F32), AXES)
    first_scale = lax.rsqrt(jnp.mean(states * states, axis=-1, keepdims=True) + EPSILON)
    normed = (states * first_scale * first_gain).astype(BF16)
    pms = premix.T * (HEAD_DIM**-0.5)
    pos = postmix
    pm = jnp.repeat(pms, HEAD_DIM, axis=1)[:, None]
    po = jnp.repeat(pos, HEAD_DIM, axis=1)[:, None]
    queries, keys, values, attended, probs = attend(spot, picture_start, normed, qkv, pm, po)
    factor = (seq_len * total) / total_valid
    layer_out, mid_grad, attended_grad, sums, *grads = middle_block(
        spot,
        factor.reshape(1, 1),
        rest,
        attended,
        states,
        upstream,
        teacher,
        validity[:, None],
        second_gain[None],
        units,
    )
    if blocked:
        ffn = reduce_blocks(grads[0], grads[1], total)
        half = up_weight.shape[1]
        up_grad, down_grad, output_grad = ffn[:, :half], ffn[:, half : 2 * half].T, ffn[:, 2 * half :]
    else:
        up_grad, down_grad, output_grad = (scatter_whole(g) for g in grads)
        down_grad = down_grad.T
    dq, dk, dv, pre, post, *grads = attend_back(
        spot, blocked, normed.T, queries, keys, values, attended_grad, probs, pm, po, pms, pos
    )
    if blocked:
        attn = reduce_blocks(grads[0], grads[1], total)
        query_grad, key_grad, value_grad = (attn[n * depth : (n + 1) * depth] for n in range(3))
    else:
        query_grad, key_grad, value_grad = (scatter_whole(g) for g in grads)
    input_grad, first_rows = input_block(
        spot, qkv, dq, dk, dv, states, mid_grad, first_gain[None]
    )
    pre = jnp.sum(pre.reshape(HEADS, HEADS, HEAD_DIM), axis=2).T * (HEAD_DIM**-0.5)
    post = jnp.sum(post, axis=2)
    small = jnp.concatenate(
        [
            first_rows[0],
            sums[0],
            pre.reshape(-1),
            post.reshape(-1),
            jnp.sum(sums[1:3], axis=1),
        ]
    )
    if blocked:
        size = small.shape[0]
        small = jnp.pad(small, (0, -size % 1024)).reshape(-1, 128)
        small = reduce_small(small, total).reshape(-1)[:size]
    else:
        small = lax.psum(small, AXES)
    mixes = HEADS * HEADS
    first_grad, second_grad, premix_grad, postmix_grad, losses = jnp.split(
        small, [features, 2 * features, 2 * features + mixes, 2 * features + 2 * mixes]
    )
    return (
        layer_out,
        losses[0] / (total_valid * features),
        losses[1] / total_valid,
        input_grad,
        first_grad,
        query_grad,
        key_grad,
        value_grad,
        premix_grad.reshape(HEADS, HEADS),
        postmix_grad.reshape(HEADS, HEADS),
        output_grad,
        second_grad,
        up_grad,
        down_grad,
    )


def solution(mesh):
    tokens, block = P(AXES, None), P("row", "col")
    return jax.shard_map(
        shards,
        mesh=mesh,
        in_specs=(
            tokens, tokens, tokens, P(AXES), tokens, P(), block, block, block, P(), P(), block,
            P(), block, P("col", "row"),
        ),
        out_specs=(
            tokens, P(), P(), tokens, P(), block, block, block, P(), P(), block, P(), block,
            P("col", "row"),
        ),
        check_vma=False,
    )
```

time: 1290 us -> 395 us (0.31)
  waiting for transfers between devices: 679 us -> 188 us
  matrix products: 343 us -> 0 us
  local copies, waits for them, and re-layouts: 114 us -> 17.9 us
  Pallas kernels: 0 us -> 94.8 us
  blocking collectives: 80.4 us -> 0 us
  starting transfers between devices: 0.94 us -> 57.5 us
  other arithmetic: 42.7 us -> 27.5 us
  between operations: 22 us -> 8.57 us
    reduce_scatter x6 -> x0, waiting for transfers between devices: 477 us -> none  [the longest x1 142 us: shards(): lax.psum_scatter(up_term, ('row', 'col'), scatter_dimension=0, tiled=True)]
    dot_general x31 -> x0, matrix products: 343 us -> none  [the longest x1 51.5 us: one_block(): jnp.einsum('hg,gqk->hqk', postmix, weight_grad, precision=HIGHEST)]
    all_gather x6 -> x0, waiting for transfers between devices: 198 us -> none  [the longest x1 51.4 us: shards(): lax.all_gather(query_weight[None], ('row', 'col'), axis=0, tiled=True)]
    ppermute x0 -> x41, waiting for transfers between devices: none -> 188 us  [exchange(): return lax.ppermute(value, AXES, [(i, i ^ mask) for i in range(total)])]
    pallas_call x0 -> x4, Pallas kernels: none -> 94.8 us  [the longest x1 36 us: middle_block(): pl.pallas_call(functools.partial(middle_kernel, len(pieces), len(grads)),...]
    psum x2 -> x0, blocking collectives: 80.4 us -> none  [shards(): lax.psum((jnp.sum(valid_marks), jnp.sum(valid_marks * jnp.sum(differ * di...]
    ppermute x0 -> x41, starting transfers between devices: none -> 57.5 us  [exchange(): return lax.ppermute(value, AXES, [(i, i ^ mask) for i in range(total)])]
    reshape x15 -> x6, local copies, waits for them, and re-layouts: 58.1 us -> 2.76 us  [the longest x1 0.69 us: shards(): postmix_grad.reshape(HEADS, HEADS)]
  transfers between devices with their start and end apart: 12 -> 41, of which waited for: 9 -> 16; matrix products, arithmetic and copies ran while one was open for 25% -> 10% of each run, Pallas kernels for 0% -> 15%
where the time goes in v1:
time: 395 us; the launch traced here: 394 us
  waiting for transfers between devices  188 us (48%)
  Pallas kernels  94.8 us (24%)
  starting transfers between devices  57.5 us (15%)
  other arithmetic  27.5 us (7%)
  local copies, waits for them, and re-layouts  17.9 us (5%)
  between operations  8.57 us (2%)
    ppermute x41, waiting for transfers between devices, exchange(): return lax.ppermute(value, AXES, [(i, i ^ mask) for i in range(total)])  188 us
    ppermute x41, starting transfers between devices, exchange(): return lax.ppermute(value, AXES, [(i, i ^ mask) for i in range(total)])  57.5 us
    pallas_call x1, Pallas kernels, middle_block(): pl.pallas_call(functools.partial(middle_kernel, len(pieces), len(grads)),...  36 us
    pallas_call x1, Pallas kernels, attend_back(): pl.pallas_call(functools.partial(attend_back_kernel, blocked), grid=(HEAD...  28.5 us
    pallas_call x1, Pallas kernels, attend(): pl.pallas_call(functools.partial(attend_kernel, len(pieces)), grid=(HEADS...  21.1 us
    pallas_call x1, Pallas kernels, input_block(): pl.pallas_call(functools.partial(input_kernel, len(pieces)), in_specs=[SM...  9.14 us
  transfers between devices with their start and end apart: 41, of which 16 were waited for; matrix products, arithmetic and copies ran while one was open for 10% of the time, Pallas kernels for 15%

profile of v1, /device:TPU:0, one launch (start us, length us, event | category | flops | bytes accessed | tf_op | source)
XLA Modules:
  0.0 394.0 jit_solution(5726333676052440558)
XLA Ops:
  5.7 4.1 %collective-permute-start.1 = (bf16[48,3584]{1,0:T(8,128)(2,1)S(1)}, bf16[48,3584]{1,0:T(8,128)(2,1)S(1)}, u32[]{:S(2)}, u32[]{:S(2)}) collective-permute-start(bf16[48,3584]{1,0:T(8,128)(2,1)S(1)} %get-tuple-element.73), channel_id=1, source_target_pairs={{0,16},{1,17},{2,18},{3,19},{4,20},{5,21},{6,22},{7,23},{8,24},{9,... | collective-permute-start | bytes 1032200 | tf_op jit(solution)/shard_map/ppermute | solution.py:506
  13.7 3.8 collective-permute-start.12
  17.6 9.5 %collective-permute-done.1 = bf16[48,3584]{1,0:T(8,128)(2,1)S(1)} collective-permute-done((bf16[48,3584]{1,0:T(8,128)(2,1)S(1)}, bf16[48,3584]{1,0:T(8,128)(2,1)S(1)}, u32[]{:S(2)}, u32[]{:S(2)}) %collective-permute-start.1) | collective-permute-done | bytes 344096 | tf_op jit(solution)/shard_map/ppermute | solution.py:506
  27.0 7.9 %collective-permute-done.2 = bf16[48,3584]{1,0:T(8,128)(2,1)S(1)} collective-permute-done((bf16[48,3584]{1,0:T(8,128)(2,1)S(1)}, bf16[48,3584]{1,0:T(8,128)(2,1)S(1)}, u32[]{:S(2)}, u32[]{:S(2)}) %collective-permute-start.2) | collective-permute-done | bytes 344096 | tf_op jit(solution)/shard_map/ppermute | solution.py:506
  36.2 2.4 collective-permute-start.5
  38.6 10.9 %collective-permute-done.11 = bf16[144,384]{1,0:T(8,128)(2,1)S(1)} collective-permute-done((bf16[144,384]{1,0:T(8,128)(2,1)S(1)}, bf16[144,384]{1,0:T(8,128)(2,1)S(1)}, u32[]{:S(2)}, u32[]{:S(2)}) %collective-permute-start.11) | collective-permute-done | bytes 110624 | tf_op jit(solution)/shard_map/ppermute | solution.py:506
  54.8 51.5 %collective-permute-done.15.rest_3_ = bf16[4,144,384]{2,1,0:T(8,128)(2,1)S(1)} collective-permute-done((bf16[4,144,384]{2,1,0:T(8,128)(2,1)S(1)}, bf16[4,144,384]{2,1,0:T(8,128)(2,1)S(1)}, u32[]{:S(2)}, u32[]{:S(2)}) %collective-permute-start.15) | collective-permute-done | bytes 442400 | tf_op jit(solution)/shard_map/ppermute | solution.py:506
  107.9 7.9 %collective-permute-done.14.rest_2_ = bf16[4,144,384]{2,1,0:T(8,128)(2,1)} collective-permute-done((bf16[4,144,384]{2,1,0:T(8,128)(2,1)S(1)}, bf16[4,144,384]{2,1,0:T(8,128)(2,1)}, u32[]{:S(2)}, u32[]{:S(2)}) %collective-permute-start.14) | collective-permute-done | bytes 442400 | tf_op jit(solution)/shard_map/ppermute | solution.py:506
  127.5 21.1 %attend.1 = (bf16[512,768]{1,0:T(8,128)(2,1)}, bf16[512,768]{1,0:T(8,128)(2,1)}, bf16[512,768]{1,0:T(8,128)(2,1)}, bf16[512,768]{1,0:T(8,128)(2,1)}, bf16[12,256,768]{2,1,0:T(8,128)(2,1)}) custom-call(s32[4]{0:T(128)} %pad_add_fusion.spot, s32[1,2]{1,0:T(1,128)} %starts.1, bf16[512,768]{1,0:T(8,128)(2,1)} %copy.38.normed_ref, ...), custom_call_target="tpu_custom_call" | custom-call | tf_op jit(solution)/shard_map/attend/pallas_call | solution.py:146
  155.7 36.0 %middle.1 = (f32[512,768]{1,0:T(8,128)}, f32[512,768]{1,0:T(8,128)}, bf16[512,768]{1,0:T(8,128)(2,1)}, f32[8,768]{1,0:T(8,128)}, bf16[4,4,48,3456]{3,2,1,0:T(8,128)(2,1)}, /*index=5*/bf16[4,4,48,3456]{3,2,1,0:T(8,128)(2,1)}) custom-call(s32[4]{0:T(128)} %pad_add_fusion.spot, f32[1,1]{1,0:T(1,128)} %bitcast.9.factor, ...), custom_call_target="tpu_custom_call" | custom-call | tf_op jit(solution)/shard_map/middle/pallas_call | solution.py:305
  193.2 28.5 %attend_back.1 = (bf16[512,768]{1,0:T(8,128)(2,1)}, bf16[512,768]{1,0:T(8,128)(2,1)}, bf16[512,768]{1,0:T(8,128)(2,1)}, f32[12,1,768]{2,1,0:T(1,128)}, f32[12,12...) custom-call(s32[4]{0:T(128)} %pad_add_fusion.spot, f32[12,12]{1,0:T(8,128)} %copy-done.8, ...), custom_call_target="tpu_custom_call" | custom-call | tf_op jit(solution)/shard_map/attend_back/pallas_call | solution.py:435
  226.1 9.1 %input_grad.1 = (f32[512,768]{1,0:T(8,128)}, f32[8,768]{1,0:T(8,128)}) custom-call(s32[4]{0:T(128)} %pad_add_fusion.spot, bf16[4,144,384]{2,1,0:T(8,128)(2,1)} %copy-done.1, bf16[4,144,384]{2,1,0:T(8,128)(2,1)} %copy-done.4, bf16[4,144,384]{2,1,0:T(8,128)(2,1)} %collective-permute-done.14.rest_2_, bf16[4,144,384]{2,1,0:T(8,128)(2,1)} %copy-done.3, ...), custom_call_target="tpu_custom_call" | custom-call | tf_op jit(solution)/shard_map/input_grad/pallas_call | solution.py:491
  243.7 2.4 collective-permute-done.23
  246.8 2.5 collective-permute-start.26
  249.2 13.4 %collective-permute-start.25 = (f32[16,128]{1,0:T(8,128)S(1)}, f32[16,128]{1,0:T(8,128)S(1)}, u32[]{:S(2)}, u32[]{:S(2)}) collective-permute-start(f32[16,128]{1,0:T(8,128)S(1)} %add_add_fusion.1), channel_id=1, source_target_pairs={{0,16},{1,17},{2,18},{3,19},{4,20},{5,21},{6,22},{7,23},{8,24},{9,... | collective-permute-start | bytes 24584 | tf_op jit(solution)/shard_map/ppermute | solution.py:506
  265.4 5.7 %fusion.2 = (bf16[4,48,3456]{2,1,0:T(8,128)(2,1)}, bf16[4,48,3456]{2,1,0:T(8,128)(2,1)}, bf16[4,48,3456]{2,1,0:T(8,128)(2,1)}) fusion(bf16[4,4,48,3456]{3,2,1,0:T(8,128)(2,1)} %collective-permute-done.34, bf16[4,4,48,3456]{3,2,1,0:T(8,128)(2,1)} %get-tuple-element.52), kind=kLoop, calls=%fused_computation.9 | loop fusion | flops 7962624 | bytes 11943936 | tf_op jit(solution)/shard_map/convert_element_type | solution.py:522
  281.8 60.2 %collective-permute-done.30 = bf16[4,144,384]{2,1,0:T(8,128)(2,1)} collective-permute-done((bf16[4,144,384]{2,1,0:T(8,128)(2,1)}, bf16[4,144,384]{2,1,0:T(8,128)(2,1)}, u32[]{:S(2)}, u32[]{:S(2)}) %collective-permute-start.30) | collective-permute-done | bytes 442400 | tf_op jit(solution)/shard_map/ppermute | solution.py:506
  342.0 7.5 %collective-permute-done.29 = bf16[4,144,384]{2,1,0:T(8,128)(2,1)} collective-permute-done((bf16[4,144,384]{2,1,0:T(8,128)(2,1)}, bf16[4,144,384]{2,1,0:T(8,128)(2,1)}, u32[]{:S(2)}, u32[]{:S(2)}) %collective-permute-start.29) | collective-permute-done | bytes 442400 | tf_op jit(solution)/shard_map/ppermute | solution.py:506
  352.7 2.6 collective-permute-start.33
  355.3 3.7 fusion.26
  361.0 2.6 collective-permute-start.40
  364.3 6.1 %collective-permute-done.38 = bf16[48,3456]{1,0:T(8,128)(2,1)S(1)} collective-permute-done((bf16[48,3456]{1,0:T(8,128)(2,1)S(1)}, bf16[48,3456]{1,0:T(8,128)(2,1)S(1)}, u32[]{:S(2)}, u32[]{:S(2)}) %collective-permute-start.38) | collective-permute-done | bytes 331808 | tf_op jit(solution)/shard_map/ppermute | solution.py:506
  370.5 7.8 %collective-permute-done.40 = bf16[48,3456]{1,0:T(8,128)(2,1)S(1)} collective-permute-done((bf16[48,3456]{1,0:T(8,128)(2,1)S(1)}, bf16[48,3456]{1,0:T(8,128)(2,1)S(1)}, u32[]{:S(2)}, u32[]{:S(2)}) %collective-permute-start.40) | collective-permute-done | bytes 331808 | tf_op jit(solution)/shard_map/ppermute | solution.py:506
  378.2 11.8 %collective-permute-done.39 = bf16[48,3456]{1,0:T(8,128)(2,1)S(1)} collective-permute-done((bf16[48,3456]{1,0:T(8,128)(2,1)S(1)}, bf16[48,3456]{1,0:T(8,128)(2,1)S(1)}, u32[]{:S(2)}, u32[]{:S(2)}) %collective-permute-start.39) | collective-permute-done | bytes 331808 | tf_op jit(solution)/shard_map/ppermute | solution.py:506
  (158 shorter events, 66.1 us)
Async XLA Ops:
  5.7 21.3 %collective-permute-start.1 = (bf16[48,3584]{1,0:T(8,128)(2,1)S(1)}, bf16[48,3584]{1,0:T(8,128)(2,1)S(1)}, u32[]{:S(2)}, u32[]{:S(2)}) collective-permute-start(bf16[48,3584]{1,0:T(8,128)(2,1)S(1)} %get-tuple-element.73), channel_id=1, source_target_pairs={{0,16},{1,17},{2,18},{3,19},{4,20},{5,21},{6,22},{7,23},{8,24},{9,... | collective-permute-start | bytes 1032200 | tf_op jit(solution)/shard_map/ppermute | solution.py:506
  11.4 23.5 %collective-permute-start.2 = (bf16[48,3584]{1,0:T(8,128)(2,1)S(1)}, bf16[48,3584]{1,0:T(8,128)(2,1)S(1)}, u32[]{:S(2)}, u32[]{:S(2)}) collective-permute-start(bf16[48,3584]{1,0:T(8,128)(2,1)S(1)} %get-tuple-element.73), channel_id=1, source_target_pairs={{0,24},{1,25},{2,26},{3,27},{4,28},{5,29},{6,30},{7,31},{8,16},{9,... | collective-permute-start | bytes 1032200 | tf_op jit(solution)/shard_map/ppermute | solution.py:506
  13.7 24.9 %collective-permute-start.12 = (bf16[144,384]{1,0:T(8,128)(2,1)S(1)}, bf16[144,384]{1,0:T(8,128)(2,1)S(1)}, u32[]{:S(2)}, u32[]{:S(2)}) collective-permute-start(bf16[144,384]{1,0:T(8,128)(2,1)S(1)} %constant_dynamic-update-slice_fusion), channel_id=1, source_target_pairs={{0,24},{1,25},{2,26},{3,27},{4,28},{5,29},{6,30},{7,31},{8,16},{9,... | collective-permute-start | bytes 331784 | tf_op jit(solution)/shard_map/ppermute | solution.py:506
  17.6 32.0 %collective-permute-start.11 = (bf16[144,384]{1,0:T(8,128)(2,1)S(1)}, bf16[144,384]{1,0:T(8,128)(2,1)S(1)}, u32[]{:S(2)}, u32[]{:S(2)}) collective-permute-start(bf16[144,384]{1,0:T(8,128)(2,1)S(1)} %constant_dynamic-update-slice_fusion), channel_id=1, source_target_pairs={{0,16},{1,17},{2,18},{3,19},{4,20},{5,21},{6,22},{7,23},{8,24},{9,... | collective-permute-start | bytes 331784 | tf_op jit(solution)/shard_map/ppermute | solution.py:506
  27.0 22.5 %collective-permute-start.10 = (bf16[144,384]{1,0:T(8,128)(2,1)S(1)}, bf16[144,384]{1,0:T(8,128)(2,1)S(1)}, u32[]{:S(2)}, u32[]{:S(2)}) collective-permute-start(bf16[144,384]{1,0:T(8,128)(2,1)S(1)} %constant_dynamic-update-slice_fusion), channel_id=1, source_target_pairs={{0,8},{1,9},{2,10},{3,11},{4,12},{5,13},{6,14},{7,15},{8,0},{9,1},... | collective-permute-start | bytes 331784 | tf_op jit(solution)/shard_map/ppermute | solution.py:506
  36.2 81.6 %collective-permute-start.5 = (bf16[4,48,3584]{2,1,0:T(8,128)(2,1)}, bf16[4,48,3584]{2,1,0:T(8,128)(2,1)}, u32[]{:S(2)}, u32[]{:S(2)}) collective-permute-start(bf16[4,48,3584]{2,1,0:T(8,128)(2,1)} %pad_maximum_fusion.rest_0_), channel_id=1, source_target_pairs={{0,5},{1,4},{2,7},{3,6},{4,1},{5,0},{6,3},{7,2},{8,13},{9,12},{10,... | collective-permute-start | bytes 4128776 | tf_op jit(solution)/shard_map/ppermute | solution.py:506
  49.7 68.4 %collective-permute-start.4 = (bf16[4,48,3584]{2,1,0:T(8,128)(2,1)}, bf16[4,48,3584]{2,1,0:T(8,128)(2,1)}, u32[]{:S(2)}, u32[]{:S(2)}) collective-permute-start(bf16[4,48,3584]{2,1,0:T(8,128)(2,1)} %pad_maximum_fusion.rest_0_), channel_id=1, source_target_pairs={{0,4},{1,5},{2,6},{3,7},{4,0},{5,1},{6,2},{7,3},{8,12},{9,13},{10,... | collective-permute-start | bytes 4128776 | tf_op jit(solution)/shard_map/ppermute | solution.py:506
  51.3 71.0 %collective-permute-start.3 = (bf16[4,48,3584]{2,1,0:T(8,128)(2,1)}, bf16[4,48,3584]{2,1,0:T(8,128)(2,1)}, u32[]{:S(2)}, u32[]{:S(2)}) collective-permute-start(bf16[4,48,3584]{2,1,0:T(8,128)(2,1)} %pad_maximum_fusion.rest_0_), channel_id=1, source_target_pairs={{0,1},{1,0},{2,3},{3,2},{4,5},{5,4},{6,7},{7,6},{8,9},{9,8},{10,11... | collective-permute-start | bytes 4128776 | tf_op jit(solution)/shard_map/ppermute | solution.py:506
  52.8 53.6 %collective-permute-start.15 = (bf16[4,144,384]{2,1,0:T(8,128)(2,1)S(1)}, bf16[4,144,384]{2,1,0:T(8,128)(2,1)S(1)}, u32[]{:S(2)}, u32[]{:S(2)}) collective-permute-start(bf16[4,144,384]{2,1,0:T(8,128)(2,1)S(1)} %pad_maximum_fusion.1.rest_0_), channel_id=1, source_target_pairs={{0,5},{1,4},{2,7},{3,6},{4,1},{5,0},{6,3},{7,2},{8,13},{9,12},{10,... | collective-permute-start | bytes 1327112 | tf_op jit(solution)/shard_map/ppermute | solution.py:506
  53.3 62.6 %collective-permute-start.14 = (bf16[4,144,384]{2,1,0:T(8,128)(2,1)S(1)}, bf16[4,144,384]{2,1,0:T(8,128)(2,1)}, u32[]{:S(2)}, u32[]{:S(2)}) collective-permute-start(bf16[4,144,384]{2,1,0:T(8,128)(2,1)S(1)} %pad_maximum_fusion.1.rest_0_), channel_id=1, source_target_pairs={{0,4},{1,5},{2,6},{3,7},{4,0},{5,1},{6,2},{7,3},{8,12},{9,13},{10,... | collective-permute-start | bytes 1327112 | tf_op jit(solution)/shard_map/ppermute | solution.py:506
  116.0 34.9 %collective-permute-start.6 = (bf16[4,48,3584]{2,1,0:T(8,128)(2,1)}, bf16[4,48,3584]{2,1,0:T(8,128)(2,1)}, u32[]{:S(2)}, u32[]{:S(2)}) collective-permute-start(bf16[4,48,3584]{2,1,0:T(8,128)(2,1)} %pad_maximum_fusion.rest_0_), channel_id=1, source_target_pairs={{0,2},{1,3},{2,0},{3,1},{4,6},{5,7},{6,4},{7,5},{8,10},{9,11},{10,... | collective-permute-start | bytes 4128776 | tf_op jit(solution)/shard_map/ppermute | solution.py:506
  117.8 33.8 %collective-permute-start.9 = (bf16[4,48,3584]{2,1,0:T(8,128)(2,1)}, bf16[4,48,3584]{2,1,0:T(8,128)(2,1)}, u32[]{:S(2)}, u32[]{:S(2)}) collective-permute-start(bf16[4,48,3584]{2,1,0:T(8,128)(2,1)} %collective-permute-done.5.rest_3_), channel_id=1, source_target_pairs={{0,2},{1,3},{2,0},{3,1},{4,6},{5,7},{6,4},{7,5},{8,10},{9,11},{10,... | collective-permute-start | bytes 4128776 | tf_op jit(solution)/shard_map/ppermute | solution.py:506
  118.1 34.2 %collective-permute-start.8 = (bf16[4,48,3584]{2,1,0:T(8,128)(2,1)}, bf16[4,48,3584]{2,1,0:T(8,128)(2,1)}, u32[]{:S(2)}, u32[]{:S(2)}) collective-permute-start(bf16[4,48,3584]{2,1,0:T(8,128)(2,1)} %collective-permute-done.4.rest_2_), channel_id=1, source_target_pairs={{0,2},{1,3},{2,0},{3,1},{4,6},{5,7},{6,4},{7,5},{8,10},{9,11},{10,... | collective-permute-start | bytes 4128776 | tf_op jit(solution)/shard_map/ppermute | solution.py:506
  122.4 30.7 %collective-permute-start.7 = (bf16[4,48,3584]{2,1,0:T(8,128)(2,1)}, bf16[4,48,3584]{2,1,0:T(8,128)(2,1)}, u32[]{:S(2)}, u32[]{:S(2)}) collective-permute-start(bf16[4,48,3584]{2,1,0:T(8,128)(2,1)} %collective-permute-done.3.rest_1_), channel_id=1, source_target_pairs={{0,2},{1,3},{2,0},{3,1},{4,6},{5,7},{6,4},{7,5},{8,10},{9,11},{10,... | collective-permute-start | bytes 4128776 | tf_op jit(solution)/shard_map/ppermute | solution.py:506
  191.7 73.6 %collective-permute-start.34 = (bf16[4,4,48,3456]{3,2,1,0:T(8,128)(2,1)}, bf16[4,4,48,3456]{3,2,1,0:T(8,128)(2,1)}, u32[]{:S(2)}, u32[]{:S(2)}) collective-permute-start(bf16[4,4,48,3456]{3,2,1,0:T(8,128)(2,1)} %get-tuple-element.53), channel_id=1, source_target_pairs={{0,2},{1,3},{2,0},{3,1},{4,6},{5,7},{6,4},{7,5},{8,10},{9,11},{10,... | collective-permute-start | bytes 15925256 | tf_op jit(solution)/shard_map/ppermute | solution.py:506
  221.6 41.5 %collective-permute-start.27 = (bf16[4,4,144,384]{3,2,1,0:T(8,128)(2,1)}, bf16[4,4,144,384]{3,2,1,0:T(8,128)(2,1)S(1)}, u32[]{:S(2)}, u32[]{:S(2)}) collective-permute-start(bf16[4,4,144,384]{3,2,1,0:T(8,128)(2,1)} %get-tuple-element.51), channel_id=1, source_target_pairs={{0,2},{1,3},{2,0},{3,1},{4,6},{5,7},{6,4},{7,5},{8,10},{9,11},{10,... | collective-permute-start | bytes 5308424 | tf_op jit(solution)/shard_map/ppermute | solution.py:506
  246.8 25.4 %collective-permute-start.26 = (f32[16,128]{1,0:T(8,128)S(1)}, f32[16,128]{1,0:T(8,128)S(1)}, u32[]{:S(2)}, u32[]{:S(2)}) collective-permute-start(f32[16,128]{1,0:T(8,128)S(1)} %add_add_fusion.1), channel_id=1, source_target_pairs={{0,24},{1,25},{2,26},{3,27},{4,28},{5,29},{6,30},{7,31},{8,16},{9,... | collective-permute-start | bytes 24584 | tf_op jit(solution)/shard_map/ppermute | solution.py:506
  249.2 24.4 %collective-permute-start.25 = (f32[16,128]{1,0:T(8,128)S(1)}, f32[16,128]{1,0:T(8,128)S(1)}, u32[]{:S(2)}, u32[]{:S(2)}) collective-permute-start(f32[16,128]{1,0:T(8,128)S(1)} %add_add_fusion.1), channel_id=1, source_target_pairs={{0,16},{1,17},{2,18},{3,19},{4,20},{5,21},{6,22},{7,23},{8,24},{9,... | collective-permute-start | bytes 24584 | tf_op jit(solution)/shard_map/ppermute | solution.py:506
  271.1 84.1 %collective-permute-start.35 = (bf16[4,48,3456]{2,1,0:T(8,128)(2,1)}, bf16[4,48,3456]{2,1,0:T(8,128)(2,1)}, u32[]{:S(2)}, u32[]{:S(2)}) collective-permute-start(bf16[4,48,3456]{2,1,0:T(8,128)(2,1)} %get-tuple-element.58), channel_id=1, source_target_pairs={{0,1},{1,0},{2,3},{3,2},{4,5},{5,4},{6,7},{7,6},{8,9},{9,8},{10,11... | collective-permute-start | bytes 3981320 | tf_op jit(solution)/shard_map/ppermute | solution.py:506
  272.2 83.1 %collective-permute-start.37 = (bf16[4,48,3456]{2,1,0:T(8,128)(2,1)}, bf16[4,48,3456]{2,1,0:T(8,128)(2,1)}, u32[]{:S(2)}, u32[]{:S(2)}) collective-permute-start(bf16[4,48,3456]{2,1,0:T(8,128)(2,1)} %get-tuple-element.59), channel_id=1, source_target_pairs={{0,5},{1,4},{2,7},{3,6},{4,1},{5,0},{6,3},{7,2},{8,13},{9,12},{10,... | collective-permute-start | bytes 3981320 | tf_op jit(solution)/shard_map/ppermute | solution.py:506
  273.7 81.6 %collective-permute-start.36 = (bf16[4,48,3456]{2,1,0:T(8,128)(2,1)}, bf16[4,48,3456]{2,1,0:T(8,128)(2,1)}, u32[]{:S(2)}, u32[]{:S(2)}) collective-permute-start(bf16[4,48,3456]{2,1,0:T(8,128)(2,1)} %get-tuple-element.60), channel_id=1, source_target_pairs={{0,4},{1,5},{2,6},{3,7},{4,0},{5,1},{6,2},{7,3},{8,12},{9,13},{10,... | collective-permute-start | bytes 3981320 | tf_op jit(solution)/shard_map/ppermute | solution.py:506
  275.9 66.1 %collective-permute-start.30 = (bf16[4,144,384]{2,1,0:T(8,128)(2,1)}, bf16[4,144,384]{2,1,0:T(8,128)(2,1)}, u32[]{:S(2)}, u32[]{:S(2)}) collective-permute-start(bf16[4,144,384]{2,1,0:T(8,128)(2,1)} %get-tuple-element.62), channel_id=1, source_target_pairs={{0,5},{1,4},{2,7},{3,6},{4,1},{5,0},{6,3},{7,2},{8,13},{9,12},{10,... | collective-permute-start | bytes 1327112 | tf_op jit(solution)/shard_map/ppermute | solution.py:506
  278.0 71.5 %collective-permute-start.29 = (bf16[4,144,384]{2,1,0:T(8,128)(2,1)}, bf16[4,144,384]{2,1,0:T(8,128)(2,1)}, u32[]{:S(2)}, u32[]{:S(2)}) collective-permute-start(bf16[4,144,384]{2,1,0:T(8,128)(2,1)} %get-tuple-element.63), channel_id=1, source_target_pairs={{0,4},{1,5},{2,6},{3,7},{4,0},{5,1},{6,2},{7,3},{8,12},{9,13},{10,... | collective-permute-start | bytes 1327112 | tf_op jit(solution)/shard_map/ppermute | solution.py:506
  363.6 26.5 %collective-permute-start.39 = (bf16[48,3456]{1,0:T(8,128)(2,1)S(1)}, bf16[48,3456]{1,0:T(8,128)(2,1)S(1)}, u32[]{:S(2)}, u32[]{:S(2)}) collective-permute-start(bf16[48,3456]{1,0:T(8,128)(2,1)S(1)} %get-tuple-element.66), channel_id=1, source_target_pairs={{0,16},{1,17},{2,18},{3,19},{4,20},{5,21},{6,22},{7,23},{8,24},{9,... | collective-permute-start | bytes 995336 | tf_op jit(solution)/shard_map/ppermute | solution.py:506
  (31 other events, 501.3 us)

commit v2 on v1

--- a/solution.py
+++ b/solution.py
@@ -15,9 +15,9 @@
 BF16 = jnp.bfloat16
 AXES = ("row", "col")
 X_BIT, CORE_BIT, Y_BIT, Z_BIT = 1, 2, 4, 8
-PLANE = (X_BIT, Y_BIT, X_BIT | Y_BIT)
-LINE = (Z_BIT, 2 * Z_BIT, 3 * Z_BIT)
+LINES = [[at + Z_BIT // 2 * z for z in range(4)] for at in range(4)]
 EXTRA = 128
+SIDES = ((0, 0), (0, 1), (1, 0))
 PARAMS = pltpu.CompilerParams(vmem_limit_bytes=60000 * 1024)
 SMEM = pl.BlockSpec(memory_space=pltpu.SMEM)
 ANY = pl.BlockSpec(memory_space=pl.ANY)
@@ -30,6 +30,20 @@
 
 def dot_nt(a, b):
     return lax.dot_general(a, b, (((1,), (1,)), ((), ())), preferred_element_type=F32)
+
+
+def cost(micros):
+    return pl.CostEstimate(flops=micros * 10**9, bytes_accessed=10**6, transcendentals=0)
+
+
+def placed(pieces):
+    for core in range(2):
+        lines, halves = pieces[2 * core : 2 * core + 2]
+        for n, (y, x) in enumerate(SIDES):
+            for z in range(4):
+                yield lines, (n, z), core, y, x, z
+        for z in range(4):
+            yield halves, (z // 2, z % 2), core, 1, 1, z
 
 
 def place_copies(spot, pieces, wholes, rows_at, cols_at, widths, sems):
@@ -39,23 +53,21 @@
             for n, (piece, whole) in enumerate(zip(pieces, wholes))
         ]
     copies = []
-    for k, piece in enumerate(pieces):
-        core, y, x = k // 4, (k // 2) % 2, k % 2
-        for z in range(4):
-            r = ((spot[0] ^ z) * 2 + (spot[1] ^ y)) * 2 + (spot[2] ^ core)
-            c = spot[3] ^ x
-            for whole, row, col, width in zip(wholes, rows_at, cols_at, widths):
-                depth = whole.shape[0] // 16
-                copies.append(
-                    pltpu.make_async_copy(
-                        piece.at[z, pl.ds(row, depth), pl.ds(col, width)],
-                        whole.at[
-                            pl.ds(pl.multiple_of(r * depth, 16), depth),
-                            pl.ds(pl.multiple_of(c * width, 128), width),
-                        ],
-                        sems.at[len(copies)],
-                    )
+    for piece, index, core, y, x, z in placed(pieces):
+        r = (z * 2 + (spot[1] ^ y)) * 2 + (spot[2] ^ core)
+        c = spot[3] ^ x
+        for whole, row, col, width in zip(wholes, rows_at, cols_at, widths):
+            depth = whole.shape[0] // 16
+            copies.append(
+                pltpu.make_async_copy(
+                    piece.at[(*index, pl.ds(row, depth), pl.ds(col, width))],
+                    whole.at[
+                        pl.ds(pl.multiple_of(r * depth, 16), depth),
+                        pl.ds(pl.multiple_of(c * width, 128), width),
+                    ],
+                    sems.at[len(copies)],
                 )
+            )
     return copies
 
 
@@ -70,7 +82,7 @@
             copies.append(
                 pltpu.make_async_copy(
                     source.at[pl.ds(start, depth), pl.ds(0, width)],
-                    target.at[plane, spot[0] ^ z, pl.ds(row, depth), pl.ds(col, width)],
+                    target.at[plane, z, pl.ds(row, depth), pl.ds(col, width)],
                     sems.at[2 * j + n],
                 )
             )
@@ -158,40 +170,59 @@
         ],
         compiler_params=PARAMS,
         name="attend",
+        cost_estimate=cost(20),
     )(spot, starts, normed, *pieces, pm, po)
 
 
-def middle_kernel(blocks, outs, spot, factor, *rest):
+def middle_kernel(blocks, outs, tokens, spot, count, *rest):
     pieces, rest = rest[:blocks], rest[blocks:]
     att_ref, states_ref, up_ref, teach_ref, valid_ref, gain_ref = rest[:6]
     layer_ref, mid_ref, agrad_ref, sums_ref = rest[6:10]
     grads, rest = rest[10 : 10 + outs], rest[10 + outs :]
-    wo, wu, wd, hidden, pre, n2t, olt, slots, sems, out_sems = rest
+    wo, wu, wd, hidden, pre, n2t, olt, slots, marks, sems, out_sems, mark_sems = rest
     seq, width = att_ref.shape
     units = wu.shape[1]
-    blocked = blocks == 8
+    blocked = outs == 4
+    mark_copies = []
+    if blocked:
+        for n, (piece, index, *_) in enumerate(placed(pieces)):
+            mark_copies.append(
+                pltpu.make_async_copy(
+                    piece.at[(*index, pl.ds(0, 16), pl.ds((units + width) // 2, EXTRA))],
+                    marks.at[n],
+                    mark_sems.at[n],
+                )
+            )
     copies = place_copies(
         spot,
         pieces,
         (wo, wu, wd),
         (0, 0, 0),
-        (units, 0, units // 2),
+        (units // 2, 0, (units + width) // 2 + EXTRA),
         (width // 2, units // 2, units // 2),
         sems,
     )
-    for copy in copies:
+    for copy in mark_copies + copies[::3] + copies[1::3] + copies[2::3]:
         copy.start()
-    for n, copy in enumerate(copies):
-        if n % 3 == 0:
-            copy.wait()
+    for copy in mark_copies:
+        copy.wait()
+    total_valid = jnp.full((1, 1), count[0, 0], F32)
+    if blocked:
+        digits = jnp.sum(marks[...].astype(F32), axis=0)[:1]
+        lanes = lax.broadcasted_iota(jnp.int32, digits.shape, 1)
+        digits = jnp.where(lanes == 0, digits * 256.0, jnp.where(lanes == 1, digits, 0.0))
+        total_valid += jnp.sum(digits, axis=1, keepdims=True)
+    factor = tokens / total_valid
+    sums_ref[...] = jnp.broadcast_to(total_valid, sums_ref.shape)
+    for copy in copies[::3]:
+        copy.wait()
     mid_ref[...] = states_ref[...] + dot(att_ref[...], wo[...])
     middle = mid_ref[...]
     scale = lax.rsqrt(jnp.mean(middle * middle, axis=1, keepdims=True) + EPSILON)
     n2 = (middle * scale * gain_ref[...]).astype(BF16)
     n2t[...] = n2.T
-    for n, copy in enumerate(copies):
-        if n % 3 != 0:
-            copy.wait()
+    for copy in copies[1::3]:
+        copy.wait()
 
     chunk = 512
     steps = units // chunk
@@ -202,6 +233,8 @@
         return 0
 
     lax.fori_loop(0, steps, up_step, 0)
+    for copy in copies[2::3]:
+        copy.wait()
     layer_ref[...] = mid_ref[...] + dot_nt(hidden[...], wd[...])
     layer = layer_ref[...]
     valid = valid_ref[...].astype(F32)
@@ -209,7 +242,7 @@
     differ = layer - teach_ref[...]
     sums_ref[1:2, :] = jnp.sum(valid * (differ * differ), axis=0, keepdims=True)
     sums_ref[2:3, :] = jnp.sum(valid * (upstream * layer), axis=0, keepdims=True)
-    out_grad = (factor[0, 0] * valid) * (upstream + differ)
+    out_grad = (factor * valid) * (upstream + differ)
     out_low = out_grad.astype(BF16)
     olt[...] = out_low.T
 
@@ -239,11 +272,11 @@
         return send_copies(
             spot,
             slots.at[which],
-            grads[0],
-            grads[1],
+            grads[2 * which],
+            grads[2 * which + 1],
             0,
             j // per,
-            pl.multiple_of(which * (units // 2) + (j % per) * chunk, 128),
+            pl.multiple_of((j % per) * chunk, 128),
             chunk,
             out_sems.at[which],
         )
@@ -256,7 +289,7 @@
     term = gain_ref[...] * grad
     inner = jnp.mean(term * middle, axis=1, keepdims=True)
     layer = layer_ref[...]
-    out_grad = (factor[0, 0] * valid_ref[...].astype(F32)) * (
+    out_grad = (factor * valid_ref[...].astype(F32)) * (
         up_ref[...] + (layer - teach_ref[...])
     )
     mid_grad = out_grad + scale * term - middle * (scale * scale * scale) * inner
@@ -273,7 +306,7 @@
         slots[c, :, :half] = dot(n2t[...], branch[:, c * half : (c + 1) * half]).astype(BF16)
         if blocked:
             made = send_copies(
-                spot, slots.at[c], grads[0], grads[1], 0, c, units, half, out_sems.at[c]
+                spot, slots.at[c], grads[0], grads[1], 0, c, units // 2, half, out_sems.at[c]
             )
         else:
             made = [
@@ -290,12 +323,13 @@
         copy.wait()
 
 
-def middle_block(spot, factor, pieces, attended, states, upstream, teacher, valid, gain, units):
+def middle_block(blocked, spot, count, tokens, pieces, attended, states, upstream, teacher, valid, gain, units):
     seq, width = attended.shape
     full = jax.ShapeDtypeStruct((seq, width), F32)
-    if len(pieces) == 8:
+    if blocked:
         depth = width // 16
-        grads = [jax.ShapeDtypeStruct((4, 4, depth, units + width // 2), BF16)] * 2
+        grads = [jax.ShapeDtypeStruct((4, 4, depth, (units + width) // 2), BF16)] * 2
+        grads += [jax.ShapeDtypeStruct((4, 4, depth, units // 2), BF16)] * 2
     else:
         grads = [
             jax.ShapeDtypeStruct((width, units), BF16),
@@ -303,7 +337,7 @@
             jax.ShapeDtypeStruct((width, width), BF16),
         ]
     return pl.pallas_call(
-        functools.partial(middle_kernel, len(pieces), len(grads)),
+        functools.partial(middle_kernel, len(pieces), len(grads), tokens),
         in_specs=[SMEM, SMEM] + [ANY] * len(pieces) + [VMEM] * 6,
         out_specs=[VMEM] * 4 + [ANY] * len(grads),
         out_shape=[
@@ -322,33 +356,47 @@
             pltpu.VMEM((width, seq), BF16),
             pltpu.VMEM((width, seq), BF16),
             pltpu.VMEM((2, width, 512), BF16),
+            pltpu.VMEM((32, 16, EXTRA), BF16),
             pltpu.SemaphoreType.DMA((96,)),
             pltpu.SemaphoreType.DMA((2, 16)),
+            pltpu.SemaphoreType.DMA((32,)),
         ],
         compiler_params=PARAMS,
         name="middle",
-    )(spot, factor, *pieces, attended, states, upstream, teacher, valid, gain)
-
-
-def attend_back_kernel(
-    blocked, spot, pms, pos, nt_ref, q_ref, k_ref, v_ref, g_ref, p_ref, pm_ref, po_ref,
-    dq_ref, dk_ref, dv_ref, pre_ref, post_ref, *rest,
-):
-    outs = 2 if blocked else 3
-    grads = rest[:outs]
-    vt, qt, gt, dq, dkt, dvt, slots, sems = rest[outs:]
+        cost_estimate=cost(35),
+    )(spot, count, *pieces, attended, states, upstream, teacher, valid, gain)
+
+
+def attend_back_kernel(first, blocked, spot, pms, pos, *refs):
+    turned, refs = (None, refs) if first else (refs[:7], refs[7:])
+    q_ref, k_ref, v_ref, g_ref, p_ref, pm_ref, po_ref = refs[:7]
+    pre_ref, post_ref, *rest = refs[7:]
+    if first:
+        vt, qt, gt, dq, dkt, dvt = rest
+    else:
+        nt_ref, vt, qt, gt, dq_in, dkt_in, dvt_in = turned
+        dq_ref, dk_ref, dv_ref, *rest = rest
+        outs = 2 if blocked else 3
+        grads = rest[:outs]
+        dq, dkt, dvt, slots, sems = rest[outs:]
     step = pl.program_id(0)
+    head = step if first else step + HEADS // 2
     seq, width = q_ref.shape
     half = seq // 2
 
     @pl.when(step == 0)
     def _():
-        vt[...] = v_ref[...].T
-        qt[...] = q_ref[...].T
-        gt[...] = g_ref[...].T
-        dq[...] = jnp.zeros_like(dq)
-        dkt[...] = jnp.zeros_like(dkt)
-        dvt[...] = jnp.zeros_like(dvt)
+        if first:
+            vt[...] = v_ref[...].T
+            qt[...] = q_ref[...].T
+            gt[...] = g_ref[...].T
+            dq[...] = jnp.zeros_like(dq)
+            dkt[...] = jnp.zeros_like(dkt)
+            dvt[...] = jnp.zeros_like(dvt)
+        else:
+            dq[...] = dq_in[...]
+            dkt[...] = dkt_in[...]
+            dvt[...] = dvt_in[...]
 
     pm = pm_ref[0]
     po = po_ref[0]
@@ -376,7 +424,7 @@
     )
     for g in range(HEADS):
         at = slice(g * HEAD_DIM, (g + 1) * HEAD_DIM)
-        b = pos[step, g]
+        b = pos[head, g]
         u0g, u1g = u0[at], u1[at]
         dvt[at, :half] += b * u0g
         dvt[at, half:] += b * u1g
@@ -384,7 +432,7 @@
         post_ref[0, g : g + 1, :] = jnp.sum(both, axis=0, keepdims=True)
     qs = jnp.concatenate(
         [
-            (qt[g * HEAD_DIM : (g + 1) * HEAD_DIM].astype(F32) * pms[step, g]).astype(BF16)
+            (qt[g * HEAD_DIM : (g + 1) * HEAD_DIM].astype(F32) * pms[head, g]).astype(BF16)
             for g in range(HEADS)
         ],
         axis=0,
@@ -392,7 +440,10 @@
     dkt[:, :half] += dot(qs[:, :half], d0) + dot(qs[:, half:], d1)
     dkt[:, half:] += dot(qs[:, half:], d2)
 
-    @pl.when(step == HEADS - 1)
+    if first:
+        return
+
+    @pl.when(step == HEADS // 2 - 1)
     def _():
         dq_ref[...] = dq[...].astype(BF16)
         dk_ref[...] = dkt[...].astype(BF16).T
@@ -422,42 +473,58 @@
             copy.wait()
 
 
-def attend_back(spot, blocked, nt, q, k, v, g, p, pm, po, pms, pos):
+def attend_back(spot, blocked, turned, q, k, v, g, p, pm, po, pms, pos):
     seq, width = q.shape
     half = seq // 2
+    first = turned is None
+    base = 0 if first else HEADS // 2
     whole = pl.BlockSpec((seq, width), lambda h: (0, 0))
-    row = pl.BlockSpec((1, 1, width), lambda h: (h, 0, 0))
+    across = pl.BlockSpec((width, seq), lambda h: (0, 0))
+    row = pl.BlockSpec((1, 1, width), lambda h: (h + base, 0, 0))
     low = jax.ShapeDtypeStruct((seq, width), BF16)
-    if blocked:
-        grads = [jax.ShapeDtypeStruct((4, 4, 3 * (width // 16), width // 2), BF16)] * 2
+    low_across = jax.ShapeDtypeStruct((width, seq), BF16)
+    out_specs = [
+        pl.BlockSpec((1, 1, width), lambda h: (h, 0, 0)),
+        pl.BlockSpec((1, HEADS, half), lambda h: (h, 0, 0)),
+    ]
+    out_shape = [
+        jax.ShapeDtypeStruct((HEADS // 2, 1, width), F32),
+        jax.ShapeDtypeStruct((HEADS // 2, HEADS, half), F32),
+    ]
+    if first:
+        in_specs, scratch = [], []
+        out_specs += [across] * 3 + [whole] + [across] * 2
+        out_shape += [low_across] * 3 + [jax.ShapeDtypeStruct((seq, width), F32)]
+        out_shape += [jax.ShapeDtypeStruct((width, seq), F32)] * 2
     else:
-        grads = [jax.ShapeDtypeStruct((width, width), BF16)] * 3
-    return pl.pallas_call(
-        functools.partial(attend_back_kernel, blocked),
-        grid=(HEADS,),
-        in_specs=[SMEM, SMEM, SMEM, pl.BlockSpec((width, seq), lambda h: (0, 0))]
-        + [whole] * 4
-        + [pl.BlockSpec((1, half, 3 * half), lambda h: (h, 0, 0)), row, row],
-        out_specs=[whole] * 3
-        + [row, pl.BlockSpec((1, HEADS, half), lambda h: (h, 0, 0))]
-        + [ANY] * len(grads),
-        out_shape=[low] * 3
-        + [
-            jax.ShapeDtypeStruct((HEADS, 1, width), F32),
-            jax.ShapeDtypeStruct((HEADS, HEADS, half), F32),
-        ]
-        + grads,
-        scratch_shapes=[pltpu.VMEM((width, seq), BF16)] * 3
-        + [
+        in_specs = [across] * 4 + [whole] + [across] * 2
+        if blocked:
+            grads = [jax.ShapeDtypeStruct((4, 4, 3 * (width // 16), width // 2), BF16)] * 2
+        else:
+            grads = [jax.ShapeDtypeStruct((width, width), BF16)] * 3
+        out_specs += [whole] * 3 + [ANY] * len(grads)
+        out_shape += [low] * 3 + grads
+        scratch = [
             pltpu.VMEM((seq, width), F32),
             pltpu.VMEM((width, seq), F32),
             pltpu.VMEM((width, seq), F32),
             pltpu.VMEM((3, width, width), BF16),
             pltpu.SemaphoreType.DMA((6, 16)),
-        ],
+        ]
+    return pl.pallas_call(
+        functools.partial(attend_back_kernel, first, blocked),
+        grid=(HEADS // 2,),
+        in_specs=[SMEM, SMEM, SMEM]
+        + in_specs
+        + [whole] * 4
+        + [pl.BlockSpec((1, half, 3 * half), lambda h: (h + base, 0, 0)), row, row],
+        out_specs=out_specs,
+        out_shape=out_shape,
+        scratch_shapes=scratch,
         compiler_params=PARAMS,
-        name="attend_back",
-    )(spot, pms, pos, nt, q, k, v, g, p, pm, po)
+        name="attend_back_first" if first else "attend_back",
+        cost_estimate=cost(14),
+    )(spot, pms, pos, *(() if first else turned), q, k, v, g, p, pm, po)
 
 
 def input_kernel(blocks, spot, *rest):
@@ -499,6 +566,7 @@
         scratch_shapes=[pltpu.VMEM((width, width), BF16)] * 3 + [pltpu.SemaphoreType.DMA((96,))],
         compiler_params=PARAMS,
         name="input_grad",
+        cost_estimate=cost(9),
     )(spot, *pieces, dq, dk, dv, states, mid_grad, gain)
 
 
@@ -506,30 +574,61 @@
     return lax.ppermute(value, AXES, [(i, i ^ mask) for i in range(total)])
 
 
-def gather_blocks(packet, total):
-    line = jnp.stack([packet] + [exchange(packet, m, total) for m in LINE])
-    plane = [line] + [exchange(line, m, total) for m in PLANE]
-    return plane + [exchange(part, CORE_BIT, total) for part in plane]
+def after(value, *others):
+    return lax.optimization_barrier((value, *others))[0]
+
+
+def over_lines(blocks):
+    return lax.all_to_all(blocks, "row", 0, 0, axis_index_groups=LINES, tiled=True)
+
+
+def gather_line(packet):
+    return over_lines(jnp.broadcast_to(packet, (4, *packet.shape)))
+
+
+def gather_sides(line, total):
+    return exchange(line, X_BIT, total), exchange(line, Y_BIT, total)
+
+
+def gather_halves(over_x, over_y, total):
+    return exchange(over_x[:2], Y_BIT, total), exchange(over_y[2:], X_BIT, total)
 
 
 def add_low(*terms):
     return functools.reduce(jnp.add, [t.astype(F32) for t in terms])
 
 
-def reduce_blocks(keep, send, total):
-    other = exchange(send, CORE_BIT, total)
-    away = [
-        exchange(add_low(keep[k], other[k]).astype(BF16), m, total) for k, m in enumerate(PLANE, 1)
-    ]
-    line = add_low(keep[0], other[0], *away)
-    far = [exchange(line[k].astype(BF16), m, total) for k, m in enumerate(LINE, 1)]
-    return add_low(line[0], *far)
-
-
-def reduce_small(value, total):
-    value = value + exchange(value, CORE_BIT, total)
-    value = add_low(value, *[exchange(value, m, total) for m in PLANE])
-    return add_low(value, *[exchange(value, m, total) for m in LINE])
+def reduce_core(keep, other):
+    mine = add_low(keep, other).astype(BF16)
+    return mine, mine[2:, :2], mine[1::2, 2:]
+
+
+def reduce_first(over_y, over_x, total):
+    return exchange(over_y, Y_BIT, total), exchange(over_x, X_BIT, total)
+
+
+def reduce_sides(mine, over_y, over_x):
+    return add_low(mine[1, :2], over_y[1]).astype(BF16), add_low(mine[2, 2:], over_x[1]).astype(BF16)
+
+
+def reduce_second(side_x, side_y, total):
+    return exchange(side_x, X_BIT, total), exchange(side_y, Y_BIT, total)
+
+
+def reduce_own(mine, over_y, over_x):
+    return add_low(mine[0, :2], over_y[0]), add_low(mine[0, 2:], over_x[0])
+
+
+def reduce_line(head, tail, side_x, side_y):
+    return over_lines(jnp.concatenate([add_low(head, side_x), add_low(tail, side_y)]).astype(BF16))
+
+
+def pack_small(first_rows, sums, pre, post):
+    pre = jnp.sum(pre.reshape(HEADS, HEADS, HEAD_DIM), axis=2).T * (HEAD_DIM**-0.5)
+    losses = jnp.sum(sums[1:3], axis=1)
+    small = [first_rows[0], sums[0], pre.reshape(-1), jnp.sum(post, axis=2).reshape(-1), losses]
+    small = jnp.concatenate(small)
+    return jnp.pad(small, (0, -small.shape[0] % 1024)).reshape(-1, 128)
 
 
 def gather_whole(block):
@@ -578,16 +677,21 @@
     down_turned = down_weight.T
     if blocked:
         packet = jnp.concatenate([query_weight, key_weight, value_weight], axis=0)
-        qkv = gather_blocks(packet, total)
+        qkv_line = gather_line(packet)
+        qkv_sides = gather_sides(qkv_line, total)
         lanes = lax.broadcasted_iota(jnp.int32, (depth, EXTRA), 1)
         digits = jnp.where(lanes == 0, count // 256, jnp.where(lanes == 1, count % 256, 0))
         packet = jnp.concatenate(
-            [up_weight, down_turned, output_weight, digits.astype(BF16)], axis=1
+            [up_weight, output_weight, digits.astype(BF16), down_turned], axis=1
         )
-        rest = gather_blocks(packet, total)
-        at = 2 * up_weight.shape[1] + width
-        marks = sum(jnp.sum(part[:, 0, at : at + 2].astype(F32), axis=0) for part in rest)
-        total_valid = marks[0] * 256.0 + marks[1]
+        line = gather_line(after(packet, qkv_line))
+        qkv_halves = jnp.stack(gather_halves(*qkv_sides, total))
+        qkv_lines = jnp.stack([qkv_line, *qkv_sides])
+        qkv = [qkv_lines, qkv_halves]
+        qkv += [exchange(part, CORE_BIT, total) for part in qkv]
+        line, *qkv = lax.optimization_barrier((line, *qkv))
+        sides = gather_sides(line, total)
+        total_valid = jnp.zeros((), F32)
     else:
         qkv = [gather_whole(w) for w in (query_weight, key_weight, value_weight)]
         rest = [gather_whole(w) for w in (output_weight, up_weight, down_turned)]
@@ -599,10 +703,15 @@
     pm = jnp.repeat(pms, HEAD_DIM, axis=1)[:, None]
     po = jnp.repeat(pos, HEAD_DIM, axis=1)[:, None]
     queries, keys, values, attended, probs = attend(spot, picture_start, normed, qkv, pm, po)
-    factor = (seq_len * total) / total_valid
+    if blocked:
+        *sides, attended = lax.optimization_barrier((*sides, attended))
+        rest = [jnp.stack([line, *sides]), jnp.stack(gather_halves(*sides, total))]
+        rest += [exchange(part, CORE_BIT, total) for part in rest]
     layer_out, mid_grad, attended_grad, sums, *grads = middle_block(
+        blocked,
         spot,
-        factor.reshape(1, 1),
+        total_valid.reshape(1, 1),
+        seq_len * total,
         rest,
         attended,
         states,
@@ -612,41 +721,72 @@
         second_gain[None],
         units,
     )
+    total_valid = sums[3, 0]
+    heads = queries, keys, values, attended_grad, probs, pm, po, pms, pos
     if blocked:
-        ffn = reduce_blocks(grads[0], grads[1], total)
-        half = up_weight.shape[1]
-        up_grad, down_grad, output_grad = ffn[:, :half], ffn[:, half : 2 * half].T, ffn[:, 2 * half :]
+        down_mine, *first, attended_grad = lax.optimization_barrier(
+            (*reduce_core(grads[2], exchange(grads[3], CORE_BIT, total)), attended_grad)
+        )
+        down_first = reduce_first(*first, total)
+        heads = queries, keys, values, attended_grad, probs, pm, po, pms, pos
+        up_other = exchange(grads[1], CORE_BIT, total)
+        part = attend_back(spot, blocked, None, *heads)
+        up_keep, up_other, *rest = lax.optimization_barrier((grads[0], up_other, *down_first, *part))
+        down_first, part = rest[:2], rest[2:]
+        up_mine, *first = reduce_core(up_keep, up_other)
+        down_sides = reduce_sides(down_mine, *down_first)
+        *rest, up_mine, down_head, down_tail = lax.optimization_barrier(
+            (*first, *down_sides, *part, up_mine, *reduce_own(down_mine, *down_first))
+        )
+        first, down_sides, part = rest[:2], rest[2:4], rest[4:]
+        up_first = reduce_first(*first, total)
+        down_sides = reduce_second(*down_sides, total)
     else:
-        up_grad, down_grad, output_grad = (scatter_whole(g) for g in grads)
+        up_grad, output_grad, down_grad = (scatter_whole(g) for g in (grads[0], grads[2], grads[1]))
         down_grad = down_grad.T
-    dq, dk, dv, pre, post, *grads = attend_back(
-        spot, blocked, normed.T, queries, keys, values, attended_grad, probs, pm, po, pms, pos
-    )
+        part = attend_back(spot, blocked, None, *heads)
+    pre, post, *turned = part
+    pre_last, post_last, dq, dk, dv, *grads = attend_back(spot, blocked, (normed.T, *turned), *heads)
+    pre = jnp.concatenate([pre, pre_last])
+    post = jnp.concatenate([post, post_last])
     if blocked:
-        attn = reduce_blocks(grads[0], grads[1], total)
+        dq, dk, dv, *rest = lax.optimization_barrier((dq, dk, dv, *grads, *up_first, *down_sides))
+        grads, up_first, down_sides = rest[:2], rest[2:4], rest[4:]
+        up_sides = reduce_second(*reduce_sides(up_mine, *up_first), total)
+        down_line = reduce_line(down_head, down_tail, *down_sides)
+        mine, *first, dq, dk, dv = lax.optimization_barrier(
+            (*reduce_core(grads[0], exchange(grads[1], CORE_BIT, total)), dq, dk, dv)
+        )
+        first = reduce_first(*first, total)
+        input_grad, first_rows = input_block(
+            spot, qkv, dq, dk, dv, states, mid_grad, first_gain[None]
+        )
+        input_grad, first_rows, *up_sides = lax.optimization_barrier(
+            (input_grad, first_rows, *up_sides)
+        )
+        up_line = reduce_line(*reduce_own(up_mine, *up_first), *up_sides)
+        sides = reduce_sides(mine, *first)
+        small = pack_small(first_rows, sums, pre, post)
+        small += exchange(small, CORE_BIT, total)
+        small = after(small, *sides)
+        sides = reduce_second(*sides, total)
+        for bit in (X_BIT, Y_BIT):
+            small += exchange(small, bit, total)
+        *sides, down_line, small = lax.optimization_barrier((*sides, down_line, small))
+        for bit in (Z_BIT, 2 * Z_BIT):
+            small += exchange(small, bit, total)
+        line = reduce_line(*reduce_own(mine, *first), *sides)
+        down_grad, ffn, attn = (jnp.sum(w.astype(F32), axis=0) for w in (down_line, up_line, line))
+        down_grad = down_grad.T
+        up_grad, output_grad = ffn[:, : units // col_total], ffn[:, units // col_total :]
         query_grad, key_grad, value_grad = (attn[n * depth : (n + 1) * depth] for n in range(3))
     else:
         query_grad, key_grad, value_grad = (scatter_whole(g) for g in grads)
-    input_grad, first_rows = input_block(
-        spot, qkv, dq, dk, dv, states, mid_grad, first_gain[None]
-    )
-    pre = jnp.sum(pre.reshape(HEADS, HEADS, HEAD_DIM), axis=2).T * (HEAD_DIM**-0.5)
-    post = jnp.sum(post, axis=2)
-    small = jnp.concatenate(
-        [
-            first_rows[0],
-            sums[0],
-            pre.reshape(-1),
-            post.reshape(-1),
-            jnp.sum(sums[1:3], axis=1),
-        ]
-    )
-    if blocked:
-        size = small.shape[0]
-        small = jnp.pad(small, (0, -size % 1024)).reshape(-1, 128)
-        small = reduce_small(small, total).reshape(-1)[:size]
-    else:
-        small = lax.psum(small, AXES)
+        input_grad, first_rows = input_block(
+            spot, qkv, dq, dk, dv, states, mid_grad, first_gain[None]
+        )
+        small = lax.psum(pack_small(first_rows, sums, pre, post), AXES)
+    small = small.reshape(-1)
     mixes = HEADS * HEADS
     first_grad, second_grad, premix_grad, postmix_grad, losses = jnp.split(
         small, [features, 2 * features, 2 * features + mixes, 2 * features + 2 * mixes]

time: 395 us -> 301 us (0.76)
  waiting for transfers between devices: 188 us -> 72 us
  local copies, waits for them, and re-layouts: 17.9 us -> 27.4 us
  other arithmetic: 27.5 us -> 36.7 us
  Pallas kernels: 94.8 us -> 102 us
  starting transfers between devices: 57.5 us -> 52.5 us
    ppermute x41 -> x32, waiting for transfers between devices: 188 us -> 56.6 us  [exchange(): return lax.ppermute(value, AXES, [(i, i ^ mask) for i in range(total)])]
    ppermute x41 -> x32, starting transfers between devices: 57.5 us -> 28.8 us  [exchange(): return lax.ppermute(value, AXES, [(i, i ^ mask) for i in range(total)])]
    all_to_all x0 -> x5, starting transfers between devices: none -> 23.7 us  [over_lines(): lax.all_to_all(blocks, 'row', 0, 0, axis_index_groups=LINES, tiled=True)]
    all_to_all x0 -> x5, waiting for transfers between devices: none -> 15.3 us  [over_lines(): lax.all_to_all(blocks, 'row', 0, 0, axis_index_groups=LINES, tiled=True)]
    pallas_call x2 -> x3, Pallas kernels: 64.5 us -> 72.3 us  [the longest x1 36.5 us: middle_block(): pl.pallas_call(functools.partial(middle_kernel, len(pieces), len(grads),...]
    concatenate x0 -> x6, other arithmetic: none -> 6.85 us  [the longest x3 3.74 us: reduce_line(): jnp.concatenate([add_low(head, side_x), add_low(tail, side_y)]).astype(BF16)]
    unnamed x32 -> x52, local copies, waits for them, and re-layouts: 3.11 us -> 7.4 us
    reduce_sum x11 -> x6, other arithmetic: 8.27 us -> 4.3 us  [the longest x1 1.37 us: pack_small(): losses = jnp.sum(sums[1:3], axis=1)]
  transfers between devices with their start and end apart: 41 -> 37, of which waited for: 16 -> 17; matrix products, arithmetic and copies ran while one was open for 10% -> 15% of each run, Pallas kernels for 15% -> 22%
where the time goes in v2:
time: 301 us; the launch traced here: 300 us
  Pallas kernels  102 us (34%)
  waiting for transfers between devices  72 us (24%)
  starting transfers between devices  52.5 us (17%)
  other arithmetic  36.7 us (12%)
  local copies, waits for them, and re-layouts  27.4 us (9%)
  between operations  8.83 us (3%)
    ppermute x32, waiting for transfers between devices, exchange(): return lax.ppermute(value, AXES, [(i, i ^ mask) for i in range(total)])  56.6 us
    pallas_call x1, Pallas kernels, middle_block(): pl.pallas_call(functools.partial(middle_kernel, len(pieces), len(grads),...  36.5 us
    pallas_call x2, Pallas kernels, attend_back(): pl.pallas_call(functools.partial(attend_back_kernel, first, blocked), gri...  35.8 us
    ppermute x32, starting transfers between devices, exchange(): return lax.ppermute(value, AXES, [(i, i ^ mask) for i in range(total)])  28.8 us
    all_to_all x5, starting transfers between devices, over_lines(): lax.all_to_all(blocks, 'row', 0, 0, axis_index_groups=LINES, tiled=True)  23.7 us
    pallas_call x1, Pallas kernels, attend(): pl.pallas_call(functools.partial(attend_kernel, len(pieces)), grid=(HEADS...  21.1 us
    all_to_all x5, waiting for transfers between devices, over_lines(): lax.all_to_all(blocks, 'row', 0, 0, axis_index_groups=LINES, tiled=True)  15.3 us
    pallas_call x1, Pallas kernels, input_block(): pl.pallas_call(functools.partial(input_kernel, len(pieces)), in_specs=[SM...  9.02 us
  transfers between devices with their start and end apart: 37, of which 17 were waited for; matrix products, arithmetic and copies ran while one was open for 15% of the time, Pallas kernels for 22%

profile of v2, /device:TPU:0, one launch (start us, length us, event | category | flops | bytes accessed | tf_op | source)
XLA Modules:
  0.0 299.8 jit_solution(11269198935298703882)
XLA Ops:
  2.3 6.3 %all-to-all-start = ((bf16[4,144,384]{2,1,0:T(8,128)(2,1)}), bf16[4,144,384]{2,1,0:T(8,128)(2,1)S(1)}, u32[]{:S(2)}, u32[]{:S(2)}) async-start(bf16[4,144,384]{2,1,0:T(8,128)(2,1)} %broadcast_in_dim.35), calls=%async_computation | async-start | bytes 884736 | tf_op jit(solution)/shard_map/all_to_all | solution.py:582
  13.5 7.9 %all-to-all-done = bf16[4,144,384]{2,1,0:T(8,128)(2,1)S(1)} async-done(((bf16[4,144,384]{2,1,0:T(8,128)(2,1)}), bf16[4,144,384]{2,1,0:T(8,128)(2,1)S(1)}, u32[]{:S(2)}, u32[]{:S(2)}) %all-to-all-start) | async-done | bytes 442400 | tf_op jit(solution)/shard_map/all_to_all | solution.py:582
  22.6 4.3 %all-to-all-start.1 = ((bf16[4,48,3584]{2,1,0:T(8,128)(2,1)}), bf16[4,48,3584]{2,1,0:T(8,128)(2,1)}, u32[]{:S(2)}, u32[]{:S(2)}) async-start(bf16[4,48,3584]{2,1,0:T(8,128)(2,1)} %broadcast_in_dim.36), calls=%async_computation.1 | async-start | bytes 2752512 | tf_op jit(solution)/shard_map/all_to_all | solution.py:582
  30.0 8.2 %collective-permute-done.1 = bf16[4,144,384]{2,1,0:T(8,128)(2,1)S(1)} collective-permute-done((bf16[4,144,384]{2,1,0:T(8,128)(2,1)S(1)}, bf16[4,144,384]{2,1,0:T(8,128)(2,1)S(1)}, u32[]{:S(2)}, u32[]{:S(2)}) %collective-permute-start.1) | collective-permute-done | bytes 442400 | tf_op jit(solution)/shard_map/ppermute | solution.py:574
  43.2 5.7 %collective-permute-done.3 = bf16[2,144,384]{2,1,0:T(8,128)(2,1)S(1)} collective-permute-done((bf16[2,144,384]{2,1,0:T(8,128)(2,1)S(1)}, bf16[2,144,384]{2,1,0:T(8,128)(2,1)S(1)}, u32[]{:S(2)}, u32[]{:S(2)}) %collective-permute-start.3) | collective-permute-done | bytes 221216 | tf_op jit(solution)/shard_map/ppermute | solution.py:574
  55.2 4.1 %all-to-all-done.1 = bf16[4,48,3584]{2,1,0:T(8,128)(2,1)} async-done(((bf16[4,48,3584]{2,1,0:T(8,128)(2,1)}), bf16[4,48,3584]{2,1,0:T(8,128)(2,1)}, u32[]{:S(2)}, u32[]{:S(2)}) %all-to-all-start.1) | async-done | bytes 1376288 | tf_op jit(solution)/shard_map/all_to_all | solution.py:582
  62.3 21.1 %attend.1 = (bf16[512,768]{1,0:T(8,128)(2,1)}, bf16[512,768]{1,0:T(8,128)(2,1)}, bf16[512,768]{1,0:T(8,128)(2,1)}, bf16[512,768]{1,0:T(8,128)(2,1)}, bf16[12,256,768]{2,1,0:T(8,128)(2,1)}) custom-call(s32[4]{0:T(128)} %pad_add_fusion.spot, s32[1,2]{1,0:T(1,128)} %starts.1, bf16[512,768]{1,0:T(8,128)(2,1)} %copy.38.normed_ref, ...), custom_call_target="tpu_custom_call" | custom-call | flops 20000000000 | bytes 1000000 | tf_op jit(solution)/shard_map/attend/pallas_call | solution.py:158
  83.4 7.3 %collective-permute-done.7 = bf16[4,48,3584]{2,1,0:T(8,128)(2,1)S(1)} collective-permute-done((bf16[4,48,3584]{2,1,0:T(8,128)(2,1)}, bf16[4,48,3584]{2,1,0:T(8,128)(2,1)S(1)}, u32[]{:S(2)}, u32[]{:S(2)}) %collective-permute-start.7) | collective-permute-done | bytes 1376288 | tf_op jit(solution)/shard_map/ppermute | solution.py:574
  91.9 3.3 %pad_maximum_fusion.rest_0_ = bf16[3,4,48,3584]{3,2,1,0:T(8,128)(2,1)} fusion(bf16[1,4,48,3584]{3,2,1,0:T(8,128)(2,1)S(1)} %bitcast.67, bf16[1,4,48,3584]{3,2,1,0:T(8,128)(2,1)S(1)} %bitcast.68, bf16[1,4,48,3584]{3,2,1,0:T(8,128)(2,1)} %bitcast.10), kind=kLoop, calls=%fused_computation.2 | loop fusion | flops 4128768 | bytes 8257536 | tf_op jit(solution)/shard_map/stack | solution.py:708
  97.4 15.8 %collective-permute-done.9 = bf16[2,48,3584]{2,1,0:T(8,128)(2,1)S(1)} collective-permute-done((bf16[2,48,3584]{2,1,0:T(8,128)(2,1)S(1)}, bf16[2,48,3584]{2,1,0:T(8,128)(2,1)S(1)}, u32[]{:S(2)}, u32[]{:S(2)}) %collective-permute-start.9) | collective-permute-done | bytes 688160 | tf_op jit(solution)/shard_map/ppermute | solution.py:574
  117.9 36.5 %middle.1 = (f32[512,768]{1,0:T(8,128)}, f32[512,768]{1,0:T(8,128)}, bf16[512,768]{1,0:T(8,128)(2,1)}, f32[8,768]{1,0:T(8,128)}, bf16[4,4,48,1920]{3,2,1,0:T(8,1...) custom-call(s32[4]{0:T(128)} %pad_add_fusion.spot, ...), custom_call_target="tpu_custom_call" | custom-call | flops 35000000512 | bytes 1000000 | tf_op jit(solution)/shard_map/middle/pallas_call | solution.py:339
  156.1 3.1 %collective-permute-done.13 = bf16[4,4,48,1536]{3,2,1,0:T(8,128)(2,1)S(1)} collective-permute-done((bf16[4,4,48,1536]{3,2,1,0:T(8,128)(2,1)}, bf16[4,4,48,1536]{3,2,1,0:T(8,128)(2,1)S(1)}, u32[]{:S(2)}, u32[]{:S(2)}) %collective-permute-start.13) | collective-permute-done | bytes 2359328 | tf_op jit(solution)/shard_map/ppermute | solution.py:574
  162.7 15.4 %attend_back_first.1 = (f32[6,1,768]{2,1,0:T(1,128)}, f32[6,12,256]{2,1,0:T(8,128)}, bf16[768,512]{1,0:T(8,128)(2,1)}, bf16[768,512]{1,0:T(8,128)(2,1)}, bf16[76...) custom-call(s32[4]{0:T(128)} %pad_add_fusion.spot, f32[12,12]{1,0:T(8,128)} %copy-done.18, ...), custom_call_target="tpu_custom_call" | custom-call | flops 14000000000 | bytes 1000000 | tf_op jit(solution)/shard_map/attend_back_first/pallas_call | solution.py:514
  179.2 3.4 %add_convert_fusion = bf16[4,4,48,1920]{3,2,1,0:T(8,128)(2,1)S(1)} fusion(bf16[4,4,48,1920]{3,2,1,0:T(8,128)(2,1)} %collective-permute-done.12, bf16[4,4,48,1920]{3,2,1,0:T(8,128)(2,1)} %get-tuple-element.139), kind=kLoop, calls=%fused_computation | loop fusion | flops 5898240 | bytes 8847360 | tf_op jit(solution)/shard_map/convert_element_type | solution.py:602
  184.4 2.2 add_bitcast_fusion
  190.7 20.4 %attend_back.1 = (f32[6,1,768]{2,1,0:T(1,128)}, f32[6,12,256]{2,1,0:T(8,128)}, bf16[512,768]{1,0:T(8,128)(2,1)}, bf16[512,768]{1,0:T(8,128)(2,1)}, bf16[512,768]...) custom-call(s32[4]{0:T(128)} %pad_add_fusion.spot, f32[12,12]{1,0:T(8,128)} %copy-done.18, ...), custom_call_target="tpu_custom_call" | custom-call | flops 14000000000 | bytes 1000000 | tf_op jit(solution)/shard_map/attend_back/pallas_call | solution.py:514
  224.3 3.5 %all-to-all-start.2 = ((bf16[4,48,1536]{2,1,0:T(8,128)(2,1)}), bf16[4,48,1536]{2,1,0:T(8,128)(2,1)S(1)}, u32[]{:S(2)}, u32[]{:S(2)}) async-start(bf16[4,48,1536]{2,1,0:T(8,128)(2,1)} %pad_maximum_fusion.4), calls=%async_computation.2 | async-start | bytes 1179648 | tf_op jit(solution)/shard_map/all_to_all | solution.py:582
  235.8 9.0 %input_grad.1 = (f32[512,768]{1,0:T(8,128)}, f32[8,768]{1,0:T(8,128)}) custom-call(s32[4]{0:T(128)} %pad_add_fusion.spot, bf16[3,4,144,384]{3,2,1,0:T(8,128)(2,1)} %pad_maximum_fusion.2.rest_0_, bf16[2,2,144,384]{3,2,1,0:T(8,128)(2,1)} %pad_maximum_fusion.5.rest_1_, bf16[3,4,144,384]{3,2,1,0:T(8,128)(2,1)} %collective-permute-done.4.rest_2_, ...), custom_call_target="tpu_custom_call" | custom-call | flops 8999999488 | bytes 1000000 | tf_op jit(solution)/shard_map/input_grad/pallas_call | solution.py:558
  246.6 2.3 fusion.1
  252.6 5.0 %all-to-all-start.4 = ((bf16[4,48,1920]{2,1,0:T(8,128)(2,1)}), bf16[4,48,1920]{2,1,0:T(8,128)(2,1)S(1)}, u32[]{:S(2)}, u32[]{:S(2)}) async-start(bf16[4,48,1920]{2,1,0:T(8,128)(2,1)} %pad_maximum_fusion.3), calls=%async_computation.4 | async-start | bytes 1474560 | tf_op jit(solution)/shard_map/all_to_all | solution.py:582
  263.3 5.8 %collective-permute-done.28 = f32[16,128]{1,0:T(8,128)S(1)} collective-permute-done((f32[16,128]{1,0:T(8,128)S(1)}, f32[16,128]{1,0:T(8,128)S(1)}, u32[]{:S(2)}, u32[]{:S(2)}) %collective-permute-start.28) | collective-permute-done | bytes 8224 | tf_op jit(solution)/shard_map/ppermute | solution.py:574
  278.4 2.4 collective-permute-start.31
  282.9 4.5 %all-to-all-start.3 = ((bf16[4,144,384]{2,1,0:T(8,128)(2,1)}), bf16[4,144,384]{2,1,0:T(8,128)(2,1)S(1)}, u32[]{:S(2)}, u32[]{:S(2)}) async-start(bf16[4,144,384]{2,1,0:T(8,128)(2,1)} %pad_maximum_fusion.6), calls=%async_computation.3 | async-start | bytes 884736 | tf_op jit(solution)/shard_map/all_to_all | solution.py:582
  293.5 3.3 %all-to-all-done.3 = bf16[4,144,384]{2,1,0:T(8,128)(2,1)S(1)} async-done(((bf16[4,144,384]{2,1,0:T(8,128)(2,1)}), bf16[4,144,384]{2,1,0:T(8,128)(2,1)S(1)}, u32[]{:S(2)}, u32[]{:S(2)}) %all-to-all-start.3) | async-done | bytes 442400 | tf_op jit(solution)/shard_map/all_to_all | solution.py:582
  (182 shorter events, 90.0 us)
Async XLA Ops:
  2.3 19.1 %all-to-all-start = ((bf16[4,144,384]{2,1,0:T(8,128)(2,1)}), bf16[4,144,384]{2,1,0:T(8,128)(2,1)S(1)}, u32[]{:S(2)}, u32[]{:S(2)}) async-start(bf16[4,144,384]{2,1,0:T(8,128)(2,1)} %broadcast_in_dim.35), calls=%async_computation | async-start | bytes 884736 | tf_op jit(solution)/shard_map/all_to_all | solution.py:582
  22.6 36.7 %all-to-all-start.1 = ((bf16[4,48,3584]{2,1,0:T(8,128)(2,1)}), bf16[4,48,3584]{2,1,0:T(8,128)(2,1)}, u32[]{:S(2)}, u32[]{:S(2)}) async-start(bf16[4,48,3584]{2,1,0:T(8,128)(2,1)} %broadcast_in_dim.36), calls=%async_computation.1 | async-start | bytes 2752512 | tf_op jit(solution)/shard_map/all_to_all | solution.py:582
  40.7 14.5 %collective-permute-start.4 = (bf16[3,4,144,384]{3,2,1,0:T(8,128)(2,1)}, bf16[3,4,144,384]{3,2,1,0:T(8,128)(2,1)}, u32[]{:S(2)}, u32[]{:S(2)}) collective-permute-start(bf16[3,4,144,384]{3,2,1,0:T(8,128)(2,1)} %pad_maximum_fusion.2.rest_0_), channel_id=1, source_target_pairs={{0,2},{1,3},{2,0},{3,1},{4,6},{5,7},{6,4},{7,5},{8,10},{9,11},{10,... | collective-permute-start | bytes 3981320 | tf_op jit(solution)/shard_map/ppermute | solution.py:574
  59.3 31.4 %collective-permute-start.7 = (bf16[4,48,3584]{2,1,0:T(8,128)(2,1)}, bf16[4,48,3584]{2,1,0:T(8,128)(2,1)S(1)}, u32[]{:S(2)}, u32[]{:S(2)}) collective-permute-start(bf16[4,48,3584]{2,1,0:T(8,128)(2,1)} %all-to-all-done.1), channel_id=1, source_target_pairs={{0,4},{1,5},{2,6},{3,7},{4,0},{5,1},{6,2},{7,3},{8,12},{9,13},{10,... | collective-permute-start | bytes 4128776 | tf_op jit(solution)/shard_map/ppermute | solution.py:574
  60.8 31.1 %collective-permute-start.6 = (bf16[4,48,3584]{2,1,0:T(8,128)(2,1)}, bf16[4,48,3584]{2,1,0:T(8,128)(2,1)S(1)}, u32[]{:S(2)}, u32[]{:S(2)}) collective-permute-start(bf16[4,48,3584]{2,1,0:T(8,128)(2,1)} %all-to-all-done.1), channel_id=1, source_target_pairs={{0,1},{1,0},{2,3},{3,2},{4,5},{5,4},{6,7},{7,6},{8,9},{9,8},{10,11... | collective-permute-start | bytes 4128776 | tf_op jit(solution)/shard_map/ppermute | solution.py:574
  95.2 22.7 %collective-permute-start.10 = (bf16[3,4,48,3584]{3,2,1,0:T(8,128)(2,1)}, bf16[3,4,48,3584]{3,2,1,0:T(8,128)(2,1)}, u32[]{:S(2)}, u32[]{:S(2)}) collective-permute-start(bf16[3,4,48,3584]{3,2,1,0:T(8,128)(2,1)} %pad_maximum_fusion.rest_0_), channel_id=1, source_target_pairs={{0,2},{1,3},{2,0},{3,1},{4,6},{5,7},{6,4},{7,5},{8,10},{9,11},{10,... | collective-permute-start | bytes 12386312 | tf_op jit(solution)/shard_map/ppermute | solution.py:574
  95.3 17.9 %collective-permute-start.9 = (bf16[2,48,3584]{2,1,0:T(8,128)(2,1)S(1)}, bf16[2,48,3584]{2,1,0:T(8,128)(2,1)S(1)}, u32[]{:S(2)}, u32[]{:S(2)}) collective-permute-start(bf16[2,48,3584]{2,1,0:T(8,128)(2,1)S(1)} %slice.142), channel_id=1, source_target_pairs={{0,1},{1,0},{2,3},{3,2},{4,5},{5,4},{6,7},{7,6},{8,9},{9,8},{10,11... | collective-permute-start | bytes 2064392 | tf_op jit(solution)/shard_map/ppermute | solution.py:574
  96.9 17.6 %collective-permute-start.8 = (bf16[2,48,3584]{2,1,0:T(8,128)(2,1)S(1)}, bf16[2,48,3584]{2,1,0:T(8,128)(2,1)S(1)}, u32[]{:S(2)}, u32[]{:S(2)}) collective-permute-start(bf16[2,48,3584]{2,1,0:T(8,128)(2,1)S(1)} %slice.141), channel_id=1, source_target_pairs={{0,4},{1,5},{2,6},{3,7},{4,0},{5,1},{6,2},{7,3},{8,12},{9,13},{10,... | collective-permute-start | bytes 2064392 | tf_op jit(solution)/shard_map/ppermute | solution.py:574
  154.6 23.5 %collective-permute-start.12 = (bf16[4,4,48,1920]{3,2,1,0:T(8,128)(2,1)}, bf16[4,4,48,1920]{3,2,1,0:T(8,128)(2,1)}, u32[]{:S(2)}, u32[]{:S(2)}) collective-permute-start(bf16[4,4,48,1920]{3,2,1,0:T(8,128)(2,1)} %get-tuple-element.120), channel_id=1, source_target_pairs={{0,2},{1,3},{2,0},{3,1},{4,6},{5,7},{6,4},{7,5},{8,10},{9,11},{10,... | collective-permute-start | bytes 8847368 | tf_op jit(solution)/shard_map/ppermute | solution.py:574
  161.5 16.6 %collective-permute-start.14 = (bf16[2,2,48,1536]{3,2,1,0:T(8,128)(2,1)S(1)}, bf16[2,2,48,1536]{3,2,1,0:T(8,128)(2,1)S(1)}, u32[]{:S(2)}, u32[]{:S(2)}) collective-permute-start(bf16[2,2,48,1536]{3,2,1,0:T(8,128)(2,1)S(1)} %get-tuple-element.124), channel_id=1, source_target_pairs={{0,4},{1,5},{2,6},{3,7},{4,0},{5,1},{6,2},{7,3},{8,12},{9,13},{10,... | collective-permute-start | bytes 1769480 | tf_op jit(solution)/shard_map/ppermute | solution.py:574
  162.1 16.0 %collective-permute-start.15 = (bf16[2,2,48,1536]{3,2,1,0:T(8,128)(2,1)S(1)}, bf16[2,2,48,1536]{3,2,1,0:T(8,128)(2,1)S(1)}, u32[]{:S(2)}, u32[]{:S(2)}) collective-permute-start(bf16[2,2,48,1536]{3,2,1,0:T(8,128)(2,1)S(1)} %get-tuple-element.125), channel_id=1, source_target_pairs={{0,1},{1,0},{2,3},{3,2},{4,5},{5,4},{6,7},{7,6},{8,9},{9,8},{10,11... | collective-permute-start | bytes 1769480 | tf_op jit(solution)/shard_map/ppermute | solution.py:574
  186.6 24.5 %collective-permute-start.18 = (bf16[2,48,1536]{2,1,0:T(8,128)(2,1)}, bf16[2,48,1536]{2,1,0:T(8,128)(2,1)S(1)}, u32[]{:S(2)}, u32[]{:S(2)}) collective-permute-start(bf16[2,48,1536]{2,1,0:T(8,128)(2,1)} %get-tuple-element.165), channel_id=1, source_target_pairs={{0,1},{1,0},{2,3},{3,2},{4,5},{5,4},{6,7},{7,6},{8,9},{9,8},{10,11... | collective-permute-start | bytes 884744 | tf_op jit(solution)/shard_map/ppermute | solution.py:574
  188.0 23.0 %collective-permute-start.19 = (bf16[2,48,1536]{2,1,0:T(8,128)(2,1)}, bf16[2,48,1536]{2,1,0:T(8,128)(2,1)}, u32[]{:S(2)}, u32[]{:S(2)}) collective-permute-start(bf16[2,48,1536]{2,1,0:T(8,128)(2,1)} %get-tuple-element.166), channel_id=1, source_target_pairs={{0,4},{1,5},{2,6},{3,7},{4,0},{5,1},{6,2},{7,3},{8,12},{9,13},{10,... | collective-permute-start | bytes 884744 | tf_op jit(solution)/shard_map/ppermute | solution.py:574
  189.6 22.8 %collective-permute-start.16 = (bf16[2,2,48,1920]{3,2,1,0:T(8,128)(2,1)S(1)}, bf16[2,2,48,1920]{3,2,1,0:T(8,128)(2,1)}, u32[]{:S(2)}, u32[]{:S(2)}) collective-permute-start(bf16[2,2,48,1920]{3,2,1,0:T(8,128)(2,1)S(1)} %get-tuple-element.163), channel_id=1, source_target_pairs={{0,4},{1,5},{2,6},{3,7},{4,0},{5,1},{6,2},{7,3},{8,12},{9,13},{10,... | collective-permute-start | bytes 2211848 | tf_op jit(solution)/shard_map/ppermute | solution.py:574
  190.1 22.3 %collective-permute-start.17 = (bf16[2,2,48,1920]{3,2,1,0:T(8,128)(2,1)S(1)}, bf16[2,2,48,1920]{3,2,1,0:T(8,128)(2,1)}, u32[]{:S(2)}, u32[]{:S(2)}) collective-permute-start(bf16[2,2,48,1920]{3,2,1,0:T(8,128)(2,1)S(1)} %get-tuple-element.164), channel_id=1, source_target_pairs={{0,1},{1,0},{2,3},{3,2},{4,5},{5,4},{6,7},{7,6},{8,9},{9,8},{10,11... | collective-permute-start | bytes 2211848 | tf_op jit(solution)/shard_map/ppermute | solution.py:574
  212.4 19.2 %collective-permute-start.20 = (bf16[4,4,144,384]{3,2,1,0:T(8,128)(2,1)}, bf16[4,4,144,384]{3,2,1,0:T(8,128)(2,1)}, u32[]{:S(2)}, u32[]{:S(2)}) collective-permute-start(bf16[4,4,144,384]{3,2,1,0:T(8,128)(2,1)} %get-tuple-element.168), channel_id=1, source_target_pairs={{0,2},{1,3},{2,0},{3,1},{4,6},{5,7},{6,4},{7,5},{8,10},{9,11},{10,... | collective-permute-start | bytes 5308424 | tf_op jit(solution)/shard_map/ppermute | solution.py:574
  224.3 28.4 %all-to-all-start.2 = ((bf16[4,48,1536]{2,1,0:T(8,128)(2,1)}), bf16[4,48,1536]{2,1,0:T(8,128)(2,1)S(1)}, u32[]{:S(2)}, u32[]{:S(2)}) async-start(bf16[4,48,1536]{2,1,0:T(8,128)(2,1)} %pad_maximum_fusion.4), calls=%async_computation.2 | async-start | bytes 1179648 | tf_op jit(solution)/shard_map/all_to_all | solution.py:582
  229.2 15.7 %collective-permute-start.26 = (bf16[2,48,1920]{2,1,0:T(8,128)(2,1)S(1)}, bf16[2,48,1920]{2,1,0:T(8,128)(2,1)S(1)}, u32[]{:S(2)}, u32[]{:S(2)}) collective-permute-start(bf16[2,48,1920]{2,1,0:T(8,128)(2,1)S(1)} %get-tuple-element.204), channel_id=1, source_target_pairs={{0,4},{1,5},{2,6},{3,7},{4,0},{5,1},{6,2},{7,3},{8,12},{9,13},{10,... | collective-permute-start | bytes 1105928 | tf_op jit(solution)/shard_map/ppermute | solution.py:574
  230.7 14.1 %collective-permute-start.25 = (bf16[2,48,1920]{2,1,0:T(8,128)(2,1)S(1)}, bf16[2,48,1920]{2,1,0:T(8,128)(2,1)S(1)}, u32[]{:S(2)}, u32[]{:S(2)}) collective-permute-start(bf16[2,48,1920]{2,1,0:T(8,128)(2,1)S(1)} %get-tuple-element.205), channel_id=1, source_target_pairs={{0,1},{1,0},{2,3},{3,2},{4,5},{5,4},{6,7},{7,6},{8,9},{9,8},{10,11... | collective-permute-start | bytes 1105928 | tf_op jit(solution)/shard_map/ppermute | solution.py:574
  244.9 12.8 %collective-permute-start.21 = (bf16[2,2,144,384]{3,2,1,0:T(8,128)(2,1)}, bf16[2,2,144,384]{3,2,1,0:T(8,128)(2,1)}, u32[]{:S(2)}, u32[]{:S(2)}) collective-permute-start(bf16[2,2,144,384]{3,2,1,0:T(8,128)(2,1)} %get-tuple-element.173), channel_id=1, source_target_pairs={{0,4},{1,5},{2,6},{3,7},{4,0},{5,1},{6,2},{7,3},{8,12},{9,13},{10,... | collective-permute-start | bytes 1327112 | tf_op jit(solution)/shard_map/ppermute | solution.py:574
  245.4 12.3 %collective-permute-start.23 = (bf16[2,2,144,384]{3,2,1,0:T(8,128)(2,1)}, bf16[2,2,144,384]{3,2,1,0:T(8,128)(2,1)}, u32[]{:S(2)}, u32[]{:S(2)}) collective-permute-start(bf16[2,2,144,384]{3,2,1,0:T(8,128)(2,1)} %get-tuple-element.174), channel_id=1, source_target_pairs={{0,1},{1,0},{2,3},{3,2},{4,5},{5,4},{6,7},{7,6},{8,9},{9,8},{10,11... | collective-permute-start | bytes 1327112 | tf_op jit(solution)/shard_map/ppermute | solution.py:574
  252.6 30.3 %all-to-all-start.4 = ((bf16[4,48,1920]{2,1,0:T(8,128)(2,1)}), bf16[4,48,1920]{2,1,0:T(8,128)(2,1)S(1)}, u32[]{:S(2)}, u32[]{:S(2)}) async-start(bf16[4,48,1920]{2,1,0:T(8,128)(2,1)} %pad_maximum_fusion.3), calls=%async_computation.4 | async-start | bytes 1474560 | tf_op jit(solution)/shard_map/all_to_all | solution.py:582
  259.6 13.1 %collective-permute-start.24 = (bf16[2,144,384]{2,1,0:T(8,128)(2,1)}, bf16[2,144,384]{2,1,0:T(8,128)(2,1)S(1)}, u32[]{:S(2)}, u32[]{:S(2)}) collective-permute-start(bf16[2,144,384]{2,1,0:T(8,128)(2,1)} %get-tuple-element.218), channel_id=1, source_target_pairs={{0,4},{1,5},{2,6},{3,7},{4,0},{5,1},{6,2},{7,3},{8,12},{9,13},{10,... | collective-permute-start | bytes 663560 | tf_op jit(solution)/shard_map/ppermute | solution.py:574
  282.9 13.9 %all-to-all-start.3 = ((bf16[4,144,384]{2,1,0:T(8,128)(2,1)}), bf16[4,144,384]{2,1,0:T(8,128)(2,1)S(1)}, u32[]{:S(2)}, u32[]{:S(2)}) async-start(bf16[4,144,384]{2,1,0:T(8,128)(2,1)} %pad_maximum_fusion.6), calls=%async_computation.3 | async-start | bytes 884736 | tf_op jit(solution)/shard_map/all_to_all | solution.py:582
  (38 other events, 259.1 us)

commit v3 on v2

--- a/solution.py
+++ b/solution.py
@@ -46,7 +46,7 @@
             yield halves, (z // 2, z % 2), core, 1, 1, z
 
 
-def place_copies(spot, pieces, wholes, rows_at, cols_at, widths, sems):
+def place_copies(spot, pieces, wholes, rows_at, cols_at, widths, sems, near=False):
     if len(pieces) == len(wholes):
         return [
             pltpu.make_async_copy(piece, whole, sems.at[n])
@@ -54,7 +54,7 @@
         ]
     copies = []
     for piece, index, core, y, x, z in placed(pieces):
-        r = (z * 2 + (spot[1] ^ y)) * 2 + (spot[2] ^ core)
+        r = ((spot[0] ^ z if near else z) * 2 + (spot[1] ^ y)) * 2 + (spot[2] ^ core)
         c = spot[3] ^ x
         for whole, row, col, width in zip(wholes, rows_at, cols_at, widths):
             depth = whole.shape[0] // 16
@@ -71,7 +71,7 @@
     return copies
 
 
-def send_copies(spot, source, keep, send, row, half, col, width, sems):
+def send_copies(spot, source, keep, send, row, half, col, width, sems, near=False):
     depth = source.shape[0] // 16
     copies = []
     for j in range(8):
@@ -82,7 +82,7 @@
             copies.append(
                 pltpu.make_async_copy(
                     source.at[pl.ds(start, depth), pl.ds(0, width)],
-                    target.at[plane, z, pl.ds(row, depth), pl.ds(col, width)],
+                    target.at[plane, spot[0] ^ z if near else z, pl.ds(row, depth), pl.ds(col, width)],
                     sems.at[2 * j + n],
                 )
             )
@@ -100,7 +100,7 @@
         width = wq.shape[1] // 2
         depth = wq.shape[0] // 16
         copies = place_copies(
-            spot, pieces, (wq, wk, wv), (0, depth, 2 * depth), (0, 0, 0), (width,) * 3, sems
+            spot, pieces, (wq, wk, wv), (0, depth, 2 * depth), (0, 0, 0), (width,) * 3, sems, True
         )
         for copy in copies:
             copy.start()
@@ -174,15 +174,27 @@
     )(spot, starts, normed, *pieces, pm, po)
 
 
-def middle_kernel(blocks, outs, tokens, spot, count, *rest):
+def up_copies(spot, slots, grads, sems, j, chunk, steps):
+    slot = lax.rem(j, 2)
+    if len(grads) == 1:
+        at = pl.ds(pl.multiple_of(j * chunk, chunk), chunk)
+        return [pltpu.make_async_copy(slots.at[slot], grads[0].at[:, at], sems.at[slot, 0])]
+    per = steps // 2
+    col = pl.multiple_of(lax.rem(j, per) * chunk, 128)
+    return send_copies(
+        spot, slots.at[slot], *grads, 0, lax.div(j, per), col, chunk, sems.at[slot]
+    )
+
+
+def forward_kernel(blocks, outs, tokens, spot, count, *rest):
     pieces, rest = rest[:blocks], rest[blocks:]
     att_ref, states_ref, up_ref, teach_ref, valid_ref, gain_ref = rest[:6]
-    layer_ref, mid_ref, agrad_ref, sums_ref = rest[6:10]
-    grads, rest = rest[10 : 10 + outs], rest[10 + outs :]
-    wo, wu, wd, hidden, pre, n2t, olt, slots, marks, sems, out_sems, mark_sems = rest
+    layer_ref, mid_ref, hidden, n2t, og_ref, sums_ref = rest[6:12]
+    grads, rest = rest[12 : 12 + outs], rest[12 + outs :]
+    wo, wu, wd, olt, slots, marks, sems, out_sems, mark_sems = rest
     seq, width = att_ref.shape
     units = wu.shape[1]
-    blocked = outs == 4
+    blocked = outs == 2
     mark_copies = []
     if blocked:
         for n, (piece, index, *_) in enumerate(placed(pieces)):
@@ -193,16 +205,8 @@
                     mark_sems.at[n],
                 )
             )
-    copies = place_copies(
-        spot,
-        pieces,
-        (wo, wu, wd),
-        (0, 0, 0),
-        (units // 2, 0, (units + width) // 2 + EXTRA),
-        (width // 2, units // 2, units // 2),
-        sems,
-    )
-    for copy in mark_copies + copies[::3] + copies[1::3] + copies[2::3]:
+    copies = weight_copies(spot, pieces, wo, wu, wd, sems)
+    for copy in mark_copies + copies[0] + copies[1] + copies[2]:
         copy.start()
     for copy in mark_copies:
         copy.wait()
@@ -214,14 +218,14 @@
         total_valid += jnp.sum(digits, axis=1, keepdims=True)
     factor = tokens / total_valid
     sums_ref[...] = jnp.broadcast_to(total_valid, sums_ref.shape)
-    for copy in copies[::3]:
+    for copy in copies[0]:
         copy.wait()
     mid_ref[...] = states_ref[...] + dot(att_ref[...], wo[...])
     middle = mid_ref[...]
     scale = lax.rsqrt(jnp.mean(middle * middle, axis=1, keepdims=True) + EPSILON)
     n2 = (middle * scale * gain_ref[...]).astype(BF16)
     n2t[...] = n2.T
-    for copy in copies[1::3]:
+    for copy in copies[1]:
         copy.wait()
 
     chunk = 512
@@ -233,7 +237,7 @@
         return 0
 
     lax.fori_loop(0, steps, up_step, 0)
-    for copy in copies[2::3]:
+    for copy in copies[2]:
         copy.wait()
     layer_ref[...] = mid_ref[...] + dot_nt(hidden[...], wd[...])
     layer = layer_ref[...]
@@ -243,76 +247,152 @@
     sums_ref[1:2, :] = jnp.sum(valid * (differ * differ), axis=0, keepdims=True)
     sums_ref[2:3, :] = jnp.sum(valid * (upstream * layer), axis=0, keepdims=True)
     out_grad = (factor * valid) * (upstream + differ)
-    out_low = out_grad.astype(BF16)
-    olt[...] = out_low.T
+    og_ref[...] = out_grad
+    olt[...] = out_grad.astype(BF16).T
 
     def down_step(j, _):
+        made = up_copies(spot, slots, grads, out_sems, j, chunk, steps)
+
+        @pl.when(j >= 2)
+        def _():
+            for copy in up_copies(spot, slots, grads, out_sems, j - 2, chunk, steps):
+                copy.wait()
+
         at = pl.ds(pl.multiple_of(j * chunk, chunk), chunk)
-        part = hidden[:, at]
-        back = jnp.where(part > 0, dot(out_low, wd[:, at]), 0.0).astype(BF16)
+        slots[lax.rem(j, 2)] = dot(olt[...], hidden[:, at]).astype(BF16)
+        for copy in made:
+            copy.start()
+        return 0
+
+    lax.fori_loop(0, steps, down_step, 0)
+    for j in (steps - 2, steps - 1):
+        for copy in up_copies(spot, slots, grads, out_sems, j, chunk, steps):
+            copy.wait()
+
+
+def weight_copies(spot, pieces, wo, wu, wd, sems):
+    units, width = wu.shape[1], wo.shape[1]
+    copies = place_copies(
+        spot,
+        pieces,
+        (wo, wu, wd),
+        (0, 0, 0),
+        (units // 2, 0, (units + width) // 2 + EXTRA),
+        (width // 2, units // 2, units // 2),
+        sems,
+    )
+    return copies[::3], copies[1::3], copies[2::3]
+
+
+def forward_block(blocked, spot, count, tokens, pieces, attended, states, upstream, teacher, valid, gain, units):
+    seq, width = attended.shape
+    full = jax.ShapeDtypeStruct((seq, width), F32)
+    if blocked:
+        grads = [jax.ShapeDtypeStruct((4, 4, width // 16, units // 2), BF16)] * 2
+    else:
+        grads = [jax.ShapeDtypeStruct((width, units), BF16)]
+    return pl.pallas_call(
+        functools.partial(forward_kernel, len(pieces), len(grads), tokens),
+        in_specs=[SMEM, SMEM] + [ANY] * len(pieces) + [VMEM] * 6,
+        out_specs=[VMEM] * 6 + [ANY] * len(grads),
+        out_shape=[
+            full,
+            full,
+            jax.ShapeDtypeStruct((seq, units), BF16),
+            jax.ShapeDtypeStruct((width, seq), BF16),
+            full,
+            jax.ShapeDtypeStruct((8, width), F32),
+        ]
+        + grads,
+        scratch_shapes=[
+            pltpu.VMEM((width, width), BF16),
+            pltpu.VMEM((width, units), BF16),
+            pltpu.VMEM((width, units), BF16),
+            pltpu.VMEM((width, seq), BF16),
+            pltpu.VMEM((2, width, 512), BF16),
+            pltpu.VMEM((32, 16, EXTRA), BF16),
+            pltpu.SemaphoreType.DMA((96,)),
+            pltpu.SemaphoreType.DMA((2, 16)),
+            pltpu.SemaphoreType.DMA((32,)),
+        ],
+        compiler_params=PARAMS,
+        name="forward",
+        cost_estimate=cost(20),
+    )(spot, count, *pieces, attended, states, upstream, teacher, valid, gain)
+
+
+def back_kernel(blocks, blocked, spot, *rest):
+    pieces, rest = rest[:blocks], rest[blocks:]
+    sources, gain_ref, outs_and_scratch = rest[:5], rest[5], rest[6:]
+    mg_ref, agrad_ref, sum_ref = outs_and_scratch[:3]
+    grads, rest = outs_and_scratch[3:5], outs_and_scratch[5:]
+    wo, wu, wd, hidden, n2t, out_grad, mid_ref, att_ref, pre, attt, slots, sems, in_sems, out_sems = rest
+    seq, width = att_ref.shape
+    units = wu.shape[1]
+    wide = grads if blocked else grads[:1]
+    loads = [
+        pltpu.make_async_copy(source, target, in_sems.at[n])
+        for n, (source, target) in enumerate(zip(sources, (out_grad, hidden, n2t, mid_ref, att_ref)))
+    ]
+    copies = weight_copies(spot, pieces, wo, wu, wd, sems)
+    for copy in [loads[0], *copies[2], *loads[1:3], *copies[1], *loads[3:], *copies[0]]:
+        copy.start()
+    loads[0].wait()
+    out_low = out_grad[...].astype(BF16)
+    for copy in [*copies[2], *loads[1:3]]:
+        copy.wait()
+
+    chunk = 512
+    steps = units // chunk
+
+    def up_step(j, _):
+        made = up_copies(spot, slots, wide, out_sems, j, chunk, steps)
+
+        @pl.when(j >= 2)
+        def _():
+            for copy in up_copies(spot, slots, wide, out_sems, j - 2, chunk, steps):
+                copy.wait()
+
+        at = pl.ds(pl.multiple_of(j * chunk, chunk), chunk)
+        back = jnp.where(hidden[:, at] > 0, dot(out_low, wd[:, at]), 0.0).astype(BF16)
         pre[:, at] = back
-        for which, (left, right) in enumerate(((n2t, back), (olt, part))):
-            slot = slots.at[which]
-
-            @pl.when(j > 0)
-            def _():
-                for copy in grad_copies(which, j - 1):
-                    copy.wait()
-
-            slot[...] = dot(left[...], right).astype(BF16)
-            for copy in grad_copies(which, j):
-                copy.start()
+        slots[lax.rem(j, 2)] = dot(n2t[...], back).astype(BF16)
+        for copy in made:
+            copy.start()
         return 0
 
-    def grad_copies(which, j):
-        if not blocked:
-            at = pl.ds(pl.multiple_of(j * chunk, chunk), chunk)
-            return [pltpu.make_async_copy(slots.at[which], grads[which].at[:, at], out_sems.at[which, 0])]
-        per = steps // 2
-        return send_copies(
-            spot,
-            slots.at[which],
-            grads[2 * which],
-            grads[2 * which + 1],
-            0,
-            j // per,
-            pl.multiple_of((j % per) * chunk, 128),
-            chunk,
-            out_sems.at[which],
-        )
-
-    lax.fori_loop(0, steps, down_step, 0)
+    lax.fori_loop(0, steps, up_step, 0)
+    for copy in [*copies[1], *loads[3:], *copies[0]]:
+        copy.wait()
     grad = dot_nt(pre[...], wu[...])
     middle = mid_ref[...]
     scale = lax.rsqrt(jnp.mean(middle * middle, axis=1, keepdims=True) + EPSILON)
-    sums_ref[0:1, :] = jnp.sum(grad * middle * scale, axis=0, keepdims=True)
+    sum_ref[...] = jnp.broadcast_to(
+        jnp.sum(grad * middle * scale, axis=0, keepdims=True), sum_ref.shape
+    )
     term = gain_ref[...] * grad
     inner = jnp.mean(term * middle, axis=1, keepdims=True)
-    layer = layer_ref[...]
-    out_grad = (factor * valid_ref[...].astype(F32)) * (
-        up_ref[...] + (layer - teach_ref[...])
-    )
-    mid_grad = out_grad + scale * term - middle * (scale * scale * scale) * inner
-    mid_ref[...] = mid_grad
+    mid_grad = out_grad[...] + scale * term - middle * (scale * scale * scale) * inner
+    mg_ref[...] = mid_grad
     branch = mid_grad.astype(BF16)
     agrad_ref[...] = dot_nt(branch, wo[...]).astype(BF16)
-    n2t[...] = att_ref[...].T
-    for which in range(2):
-        for copy in grad_copies(which, steps - 1):
+    attt[...] = att_ref[...].T
+    for j in (steps - 2, steps - 1):
+        for copy in up_copies(spot, slots, wide, out_sems, j, chunk, steps):
             copy.wait()
     half = width // 2
     last = []
     for c in range(2):
-        slots[c, :, :half] = dot(n2t[...], branch[:, c * half : (c + 1) * half]).astype(BF16)
+        slots[c, :, :half] = dot(attt[...], branch[:, c * half : (c + 1) * half]).astype(BF16)
         if blocked:
             made = send_copies(
-                spot, slots.at[c], grads[0], grads[1], 0, c, units // 2, half, out_sems.at[c]
+                spot, slots.at[c], *grads, 0, c, units // 2, half, out_sems.at[c]
             )
         else:
             made = [
                 pltpu.make_async_copy(
                     slots.at[c, :, pl.ds(0, half)],
-                    grads[2].at[:, pl.ds(c * half, half)],
+                    grads[1].at[:, pl.ds(c * half, half)],
                     out_sems.at[c, 0],
                 )
             ]
@@ -323,25 +403,22 @@
         copy.wait()
 
 
-def middle_block(blocked, spot, count, tokens, pieces, attended, states, upstream, teacher, valid, gain, units):
-    seq, width = attended.shape
+def back_block(blocked, spot, pieces, out_grad, hidden, n2t, middle, attended, gain):
+    seq, units = hidden.shape
+    width = attended.shape[1]
     full = jax.ShapeDtypeStruct((seq, width), F32)
     if blocked:
-        depth = width // 16
-        grads = [jax.ShapeDtypeStruct((4, 4, depth, (units + width) // 2), BF16)] * 2
-        grads += [jax.ShapeDtypeStruct((4, 4, depth, units // 2), BF16)] * 2
+        grads = [jax.ShapeDtypeStruct((4, 4, width // 16, (units + width) // 2), BF16)] * 2
     else:
         grads = [
-            jax.ShapeDtypeStruct((width, units), BF16),
             jax.ShapeDtypeStruct((width, units), BF16),
             jax.ShapeDtypeStruct((width, width), BF16),
         ]
     return pl.pallas_call(
-        functools.partial(middle_kernel, len(pieces), len(grads), tokens),
-        in_specs=[SMEM, SMEM] + [ANY] * len(pieces) + [VMEM] * 6,
-        out_specs=[VMEM] * 4 + [ANY] * len(grads),
+        functools.partial(back_kernel, len(pieces), blocked),
+        in_specs=[SMEM] + [ANY] * (len(pieces) + 5) + [VMEM],
+        out_specs=[VMEM] * 3 + [ANY] * len(grads),
         out_shape=[
-            full,
             full,
             jax.ShapeDtypeStruct((seq, width), BF16),
             jax.ShapeDtypeStruct((8, width), F32),
@@ -352,51 +429,42 @@
             pltpu.VMEM((width, units), BF16),
             pltpu.VMEM((width, units), BF16),
             pltpu.VMEM((seq, units), BF16),
+            pltpu.VMEM((width, seq), BF16),
+            pltpu.VMEM((seq, width), F32),
+            pltpu.VMEM((seq, width), F32),
+            pltpu.VMEM((seq, width), BF16),
             pltpu.VMEM((seq, units), BF16),
             pltpu.VMEM((width, seq), BF16),
-            pltpu.VMEM((width, seq), BF16),
             pltpu.VMEM((2, width, 512), BF16),
-            pltpu.VMEM((32, 16, EXTRA), BF16),
             pltpu.SemaphoreType.DMA((96,)),
+            pltpu.SemaphoreType.DMA((5,)),
             pltpu.SemaphoreType.DMA((2, 16)),
-            pltpu.SemaphoreType.DMA((32,)),
         ],
         compiler_params=PARAMS,
-        name="middle",
-        cost_estimate=cost(35),
-    )(spot, count, *pieces, attended, states, upstream, teacher, valid, gain)
-
-
-def attend_back_kernel(first, blocked, spot, pms, pos, *refs):
-    turned, refs = (None, refs) if first else (refs[:7], refs[7:])
-    q_ref, k_ref, v_ref, g_ref, p_ref, pm_ref, po_ref = refs[:7]
-    pre_ref, post_ref, *rest = refs[7:]
-    if first:
-        vt, qt, gt, dq, dkt, dvt = rest
-    else:
-        nt_ref, vt, qt, gt, dq_in, dkt_in, dvt_in = turned
-        dq_ref, dk_ref, dv_ref, *rest = rest
-        outs = 2 if blocked else 3
-        grads = rest[:outs]
-        dq, dkt, dvt, slots, sems = rest[outs:]
+        name="back",
+        cost_estimate=cost(20),
+    )(spot, *pieces, out_grad, hidden, n2t, middle, attended, gain)
+
+
+def attend_back_kernel(
+    blocked, spot, pms, pos, nt_ref, q_ref, k_ref, v_ref, g_ref, p_ref, pm_ref, po_ref,
+    dq_ref, dk_ref, dv_ref, pre_ref, post_ref, *rest,
+):
+    outs = 2 if blocked else 3
+    grads = rest[:outs]
+    vt, qt, gt, dq, dkt, dvt, slots, sems = rest[outs:]
     step = pl.program_id(0)
-    head = step if first else step + HEADS // 2
     seq, width = q_ref.shape
     half = seq // 2
 
     @pl.when(step == 0)
     def _():
-        if first:
-            vt[...] = v_ref[...].T
-            qt[...] = q_ref[...].T
-            gt[...] = g_ref[...].T
-            dq[...] = jnp.zeros_like(dq)
-            dkt[...] = jnp.zeros_like(dkt)
-            dvt[...] = jnp.zeros_like(dvt)
-        else:
-            dq[...] = dq_in[...]
-            dkt[...] = dkt_in[...]
-            dvt[...] = dvt_in[...]
+        vt[...] = v_ref[...].T
+        qt[...] = q_ref[...].T
+        gt[...] = g_ref[...].T
+        dq[...] = jnp.zeros_like(dq)
+        dkt[...] = jnp.zeros_like(dkt)
+        dvt[...] = jnp.zeros_like(dvt)
 
     pm = pm_ref[0]
     po = po_ref[0]
@@ -424,7 +492,7 @@
     )
     for g in range(HEADS):
         at = slice(g * HEAD_DIM, (g + 1) * HEAD_DIM)
-        b = pos[head, g]
+        b = pos[step, g]
         u0g, u1g = u0[at], u1[at]
         dvt[at, :half] += b * u0g
         dvt[at, half:] += b * u1g
@@ -432,7 +500,7 @@
         post_ref[0, g : g + 1, :] = jnp.sum(both, axis=0, keepdims=True)
     qs = jnp.concatenate(
         [
-            (qt[g * HEAD_DIM : (g + 1) * HEAD_DIM].astype(F32) * pms[head, g]).astype(BF16)
+            (qt[g * HEAD_DIM : (g + 1) * HEAD_DIM].astype(F32) * pms[step, g]).astype(BF16)
             for g in range(HEADS)
         ],
         axis=0,
@@ -440,10 +508,7 @@
     dkt[:, :half] += dot(qs[:, :half], d0) + dot(qs[:, half:], d1)
     dkt[:, half:] += dot(qs[:, half:], d2)
 
-    if first:
-        return
-
-    @pl.when(step == HEADS // 2 - 1)
+    @pl.when(step == HEADS - 1)
     def _():
         dq_ref[...] = dq[...].astype(BF16)
         dk_ref[...] = dkt[...].astype(BF16).T
@@ -464,6 +529,7 @@
                         0,
                         part,
                         sems.at[2 * n + c],
+                        True,
                     )
             else:
                 made.append(pltpu.make_async_copy(slots.at[n], grads[n], sems.at[n, 0]))
@@ -473,58 +539,43 @@
             copy.wait()
 
 
-def attend_back(spot, blocked, turned, q, k, v, g, p, pm, po, pms, pos):
+def attend_back(spot, blocked, nt, q, k, v, g, p, pm, po, pms, pos):
     seq, width = q.shape
     half = seq // 2
-    first = turned is None
-    base = 0 if first else HEADS // 2
     whole = pl.BlockSpec((seq, width), lambda h: (0, 0))
-    across = pl.BlockSpec((width, seq), lambda h: (0, 0))
-    row = pl.BlockSpec((1, 1, width), lambda h: (h + base, 0, 0))
+    row = pl.BlockSpec((1, 1, width), lambda h: (h, 0, 0))
     low = jax.ShapeDtypeStruct((seq, width), BF16)
-    low_across = jax.ShapeDtypeStruct((width, seq), BF16)
-    out_specs = [
-        pl.BlockSpec((1, 1, width), lambda h: (h, 0, 0)),
-        pl.BlockSpec((1, HEADS, half), lambda h: (h, 0, 0)),
-    ]
-    out_shape = [
-        jax.ShapeDtypeStruct((HEADS // 2, 1, width), F32),
-        jax.ShapeDtypeStruct((HEADS // 2, HEADS, half), F32),
-    ]
-    if first:
-        in_specs, scratch = [], []
-        out_specs += [across] * 3 + [whole] + [across] * 2
-        out_shape += [low_across] * 3 + [jax.ShapeDtypeStruct((seq, width), F32)]
-        out_shape += [jax.ShapeDtypeStruct((width, seq), F32)] * 2
+    if blocked:
+        grads = [jax.ShapeDtypeStruct((4, 4, 3 * (width // 16), width // 2), BF16)] * 2
     else:
-        in_specs = [across] * 4 + [whole] + [across] * 2
-        if blocked:
-            grads = [jax.ShapeDtypeStruct((4, 4, 3 * (width // 16), width // 2), BF16)] * 2
-        else:
-            grads = [jax.ShapeDtypeStruct((width, width), BF16)] * 3
-        out_specs += [whole] * 3 + [ANY] * len(grads)
-        out_shape += [low] * 3 + grads
-        scratch = [
+        grads = [jax.ShapeDtypeStruct((width, width), BF16)] * 3
+    return pl.pallas_call(
+        functools.partial(attend_back_kernel, blocked),
+        grid=(HEADS,),
+        in_specs=[SMEM, SMEM, SMEM, pl.BlockSpec((width, seq), lambda h: (0, 0))]
+        + [whole] * 4
+        + [pl.BlockSpec((1, half, 3 * half), lambda h: (h, 0, 0)), row, row],
+        out_specs=[whole] * 3
+        + [row, pl.BlockSpec((1, HEADS, half), lambda h: (h, 0, 0))]
+        + [ANY] * len(grads),
+        out_shape=[low] * 3
+        + [
+            jax.ShapeDtypeStruct((HEADS, 1, width), F32),
+            jax.ShapeDtypeStruct((HEADS, HEADS, half), F32),
+        ]
+        + grads,
+        scratch_shapes=[pltpu.VMEM((width, seq), BF16)] * 3
+        + [
             pltpu.VMEM((seq, width), F32),
             pltpu.VMEM((width, seq), F32),
             pltpu.VMEM((width, seq), F32),
             pltpu.VMEM((3, width, width), BF16),
             pltpu.SemaphoreType.DMA((6, 16)),
-        ]
-    return pl.pallas_call(
-        functools.partial(attend_back_kernel, first, blocked),
-        grid=(HEADS // 2,),
-        in_specs=[SMEM, SMEM, SMEM]
-        + in_specs
-        + [whole] * 4
-        + [pl.BlockSpec((1, half, 3 * half), lambda h: (h + base, 0, 0)), row, row],
-        out_specs=out_specs,
-        out_shape=out_shape,
-        scratch_shapes=scratch,
+        ],
         compiler_params=PARAMS,
-        name="attend_back_first" if first else "attend_back",
-        cost_estimate=cost(14),
-    )(spot, pms, pos, *(() if first else turned), q, k, v, g, p, pm, po)
+        name="attend_back",
+        cost_estimate=cost(28),
+    )(spot, pms, pos, nt, q, k, v, g, p, pm, po)
 
 
 def input_kernel(blocks, spot, *rest):
@@ -534,7 +585,7 @@
     width = wq.shape[1] // 2
     depth = wq.shape[0] // 16
     copies = place_copies(
-        spot, pieces, (wq, wk, wv), (0, depth, 2 * depth), (0, 0, 0), (width,) * 3, sems
+        spot, pieces, (wq, wk, wv), (0, depth, 2 * depth), (0, 0, 0), (width,) * 3, sems, True
     )
     for copy in copies:
         copy.start()
@@ -586,6 +637,10 @@
     return over_lines(jnp.broadcast_to(packet, (4, *packet.shape)))
 
 
+def gather_near(packet, total):
+    return jnp.stack([packet, *[exchange(packet, m * Z_BIT, total) for m in (1, 2, 3)]])
+
+
 def gather_sides(line, total):
     return exchange(line, X_BIT, total), exchange(line, Y_BIT, total)
 
@@ -623,10 +678,15 @@
     return over_lines(jnp.concatenate([add_low(head, side_x), add_low(tail, side_y)]).astype(BF16))
 
 
-def pack_small(first_rows, sums, pre, post):
+def reduce_near(head, tail, side_x, side_y, total):
+    line = jnp.concatenate([add_low(head, side_x), add_low(tail, side_y)])
+    return add_low(line[0], *[exchange(line[m].astype(BF16), m * Z_BIT, total) for m in (1, 2, 3)])
+
+
+def pack_small(first_rows, second_rows, sums, pre, post):
     pre = jnp.sum(pre.reshape(HEADS, HEADS, HEAD_DIM), axis=2).T * (HEAD_DIM**-0.5)
     losses = jnp.sum(sums[1:3], axis=1)
-    small = [first_rows[0], sums[0], pre.reshape(-1), jnp.sum(post, axis=2).reshape(-1), losses]
+    small = [first_rows[0], second_rows[0], pre.reshape(-1), jnp.sum(post, axis=2).reshape(-1), losses]
     small = jnp.concatenate(small)
     return jnp.pad(small, (0, -small.shape[0] % 1024)).reshape(-1, 128)
 
@@ -677,14 +737,14 @@
     down_turned = down_weight.T
     if blocked:
         packet = jnp.concatenate([query_weight, key_weight, value_weight], axis=0)
-        qkv_line = gather_line(packet)
+        qkv_line = gather_near(packet, total)
         qkv_sides = gather_sides(qkv_line, total)
         lanes = lax.broadcasted_iota(jnp.int32, (depth, EXTRA), 1)
         digits = jnp.where(lanes == 0, count // 256, jnp.where(lanes == 1, count % 256, 0))
         packet = jnp.concatenate(
             [up_weight, output_weight, digits.astype(BF16), down_turned], axis=1
         )
-        line = gather_line(after(packet, qkv_line))
+        line = gather_line(packet)
         qkv_halves = jnp.stack(gather_halves(*qkv_sides, total))
         qkv_lines = jnp.stack([qkv_line, *qkv_sides])
         qkv = [qkv_lines, qkv_halves]
@@ -707,7 +767,7 @@
         *sides, attended = lax.optimization_barrier((*sides, attended))
         rest = [jnp.stack([line, *sides]), jnp.stack(gather_halves(*sides, total))]
         rest += [exchange(part, CORE_BIT, total) for part in rest]
-    layer_out, mid_grad, attended_grad, sums, *grads = middle_block(
+    layer_out, middle, hidden, n2t, out_grad, sums, *grads = forward_block(
         blocked,
         spot,
         total_valid.reshape(1, 1),
@@ -722,70 +782,72 @@
         units,
     )
     total_valid = sums[3, 0]
-    heads = queries, keys, values, attended_grad, probs, pm, po, pms, pos
-    if blocked:
-        down_mine, *first, attended_grad = lax.optimization_barrier(
-            (*reduce_core(grads[2], exchange(grads[3], CORE_BIT, total)), attended_grad)
+    if blocked:
+        *mine, out_grad = lax.optimization_barrier(
+            (*reduce_core(grads[0], exchange(grads[1], CORE_BIT, total)), out_grad)
         )
-        down_first = reduce_first(*first, total)
-        heads = queries, keys, values, attended_grad, probs, pm, po, pms, pos
-        up_other = exchange(grads[1], CORE_BIT, total)
-        part = attend_back(spot, blocked, None, *heads)
-        up_keep, up_other, *rest = lax.optimization_barrier((grads[0], up_other, *down_first, *part))
-        down_first, part = rest[:2], rest[2:]
-        up_mine, *first = reduce_core(up_keep, up_other)
-        down_sides = reduce_sides(down_mine, *down_first)
-        *rest, up_mine, down_head, down_tail = lax.optimization_barrier(
-            (*first, *down_sides, *part, up_mine, *reduce_own(down_mine, *down_first))
+        down_mine, down_first = mine[0], reduce_first(*mine[1:], total)
+    else:
+        down_grad = scatter_whole(grads[0]).T
+    mid_grad, attended_grad, second_rows, *grads = back_block(
+        blocked, spot, rest, out_grad, hidden, n2t, middle, attended, second_gain[None]
+    )
+    nt = normed.T
+    if blocked:
+        over_y, over_x, attended_grad, *grads = lax.optimization_barrier(
+            (*down_first, attended_grad, *grads)
         )
-        first, down_sides, part = rest[:2], rest[2:4], rest[4:]
-        up_first = reduce_first(*first, total)
-        down_sides = reduce_second(*down_sides, total)
+        down_sides = reduce_sides(down_mine, over_y, over_x)
+        down_own = reduce_own(down_mine, over_y, over_x)
+        *mine, side_x, side_y, attended_grad = lax.optimization_barrier(
+            (*reduce_core(grads[0], exchange(grads[1], CORE_BIT, total)), *down_sides, attended_grad)
+        )
+        up_mine, up_first = mine[0], reduce_first(*mine[1:], total)
+        down_sides = reduce_second(side_x, side_y, total)
     else:
-        up_grad, output_grad, down_grad = (scatter_whole(g) for g in (grads[0], grads[2], grads[1]))
-        down_grad = down_grad.T
-        part = attend_back(spot, blocked, None, *heads)
-    pre, post, *turned = part
-    pre_last, post_last, dq, dk, dv, *grads = attend_back(spot, blocked, (normed.T, *turned), *heads)
-    pre = jnp.concatenate([pre, pre_last])
-    post = jnp.concatenate([post, post_last])
-    if blocked:
-        dq, dk, dv, *rest = lax.optimization_barrier((dq, dk, dv, *grads, *up_first, *down_sides))
+        up_grad, output_grad = (scatter_whole(g) for g in grads)
+    dq, dk, dv, pre, post, *grads = attend_back(
+        spot, blocked, nt, queries, keys, values, attended_grad, probs, pm, po, pms, pos
+    )
+    if blocked:
+        rest = lax.optimization_barrier((dq, dk, dv, *grads, *up_first, *down_sides, pre, post))
+        dq, dk, dv, *rest, pre, post = rest
         grads, up_first, down_sides = rest[:2], rest[2:4], rest[4:]
-        up_sides = reduce_second(*reduce_sides(up_mine, *up_first), total)
-        down_line = reduce_line(down_head, down_tail, *down_sides)
-        mine, *first, dq, dk, dv = lax.optimization_barrier(
+        *mine, dq, dk, dv = lax.optimization_barrier(
             (*reduce_core(grads[0], exchange(grads[1], CORE_BIT, total)), dq, dk, dv)
         )
-        first = reduce_first(*first, total)
+        mine, first = mine[0], reduce_first(*mine[1:], total)
+        up_sides = reduce_second(*reduce_sides(up_mine, *up_first), total)
+        down_line = reduce_line(*down_own, *down_sides)
         input_grad, first_rows = input_block(
             spot, qkv, dq, dk, dv, states, mid_grad, first_gain[None]
         )
-        input_grad, first_rows, *up_sides = lax.optimization_barrier(
-            (input_grad, first_rows, *up_sides)
+        *rest, first_rows, second_rows, pre, post = lax.optimization_barrier(
+            (*first, *up_sides, first_rows, second_rows, pre, post)
         )
-        up_line = reduce_line(*reduce_own(up_mine, *up_first), *up_sides)
+        first, up_sides = rest[:2], rest[2:]
         sides = reduce_sides(mine, *first)
-        small = pack_small(first_rows, sums, pre, post)
+        small = pack_small(first_rows, second_rows, sums, pre, post)
         small += exchange(small, CORE_BIT, total)
         small = after(small, *sides)
         sides = reduce_second(*sides, total)
         for bit in (X_BIT, Y_BIT):
             small += exchange(small, bit, total)
+        up_line = reduce_line(*reduce_own(up_mine, *up_first), *up_sides)
         *sides, down_line, small = lax.optimization_barrier((*sides, down_line, small))
+        line = reduce_near(*reduce_own(mine, *first), *sides, total)
         for bit in (Z_BIT, 2 * Z_BIT):
             small += exchange(small, bit, total)
-        line = reduce_line(*reduce_own(mine, *first), *sides)
-        down_grad, ffn, attn = (jnp.sum(w.astype(F32), axis=0) for w in (down_line, up_line, line))
+        down_grad, ffn = (jnp.sum(w.astype(F32), axis=0) for w in (down_line, up_line))
         down_grad = down_grad.T
         up_grad, output_grad = ffn[:, : units // col_total], ffn[:, units // col_total :]
-        query_grad, key_grad, value_grad = (attn[n * depth : (n + 1) * depth] for n in range(3))
+        query_grad, key_grad, value_grad = (line[n * depth : (n + 1) * depth] for n in range(3))
     else:
         query_grad, key_grad, value_grad = (scatter_whole(g) for g in grads)
         input_grad, first_rows = input_block(
             spot, qkv, dq, dk, dv, states, mid_grad, first_gain[None]
         )
-        small = lax.psum(pack_small(first_rows, sums, pre, post), AXES)
+        small = lax.psum(pack_small(first_rows, second_rows, sums, pre, post), AXES)
     small = small.reshape(-1)
     mixes = HEADS * HEADS
     first_grad, second_grad, premix_grad, postmix_grad, losses = jnp.split(

time: 301 us -> 309 us (1.027)
  waiting for transfers between devices: 72 us -> 79.2 us
  Pallas kernels: 102 us -> 107 us
  local copies, waits for them, and re-layouts: 27.4 us -> 24 us
    ppermute x32 -> x38, waiting for transfers between devices: 56.6 us -> 75.2 us  [exchange(): return lax.ppermute(value, AXES, [(i, i ^ mask) for i in range(total)])]
    ppermute x32 -> x38, starting transfers between devices: 28.8 us -> 41.4 us  [exchange(): return lax.ppermute(value, AXES, [(i, i ^ mask) for i in range(total)])]
    all_to_all x5 -> x3, waiting for transfers between devices: 15.3 us -> 4.03 us  [over_lines(): lax.all_to_all(blocks, 'row', 0, 0, axis_index_groups=LINES, tiled=True)]
    all_to_all x5 -> x3, starting transfers between devices: 23.7 us -> 13.3 us  [over_lines(): lax.all_to_all(blocks, 'row', 0, 0, axis_index_groups=LINES, tiled=True)]
    pallas_call x3, Pallas kernels: 72.3 us -> 76.7 us  [the longest x1 28.7 us: attend_back(): pl.pallas_call(functools.partial(attend_back_kernel, blocked), grid=(HEAD...]
    convert_element_type x2 -> x3, other arithmetic: 3.31 us -> 6.62 us  [reduce_sides(): add_low(mine[2, 2:], over_x[1]).astype(BF16)]
    unnamed x52 -> x40, local copies, waits for them, and re-layouts: 7.4 us -> 6.29 us
  transfers between devices with their start and end apart: 37 -> 41, of which waited for: 17 -> 18; matrix products, arithmetic and copies ran while one was open for 15% -> 14% of each run, Pallas kernels for 22% -> 27%
where the time goes in v3:
time: 309 us; the launch traced here: 307 us
  Pallas kernels  107 us (35%)
  waiting for transfers between devices  79.2 us (26%)
  starting transfers between devices  54.6 us (18%)
  other arithmetic  33.9 us (11%)
  local copies, waits for them, and re-layouts  24 us (8%)
  between operations  8.8 us (3%)
    ppermute x38, waiting for transfers between devices, exchange(): return lax.ppermute(value, AXES, [(i, i ^ mask) for i in range(total)])  75.2 us
    ppermute x38, starting transfers between devices, exchange(): return lax.ppermute(value, AXES, [(i, i ^ mask) for i in range(total)])  41.4 us
    pallas_call x1, Pallas kernels, attend_back(): pl.pallas_call(functools.partial(attend_back_kernel, blocked), grid=(HEAD...  28.7 us
    pallas_call x1, Pallas kernels, forward_block(): pl.pallas_call(functools.partial(forward_kernel, len(pieces), len(grads),...  24.6 us
    pallas_call x1, Pallas kernels, back_block(): pl.pallas_call(functools.partial(back_kernel, len(pieces), blocked), in_s...  23.4 us
    pallas_call x1, Pallas kernels, attend(): pl.pallas_call(functools.partial(attend_kernel, len(pieces)), grid=(HEADS...  21.1 us
    all_to_all x3, starting transfers between devices, over_lines(): lax.all_to_all(blocks, 'row', 0, 0, axis_index_groups=LINES, tiled=True)  13.3 us
    pallas_call x1, Pallas kernels, input_block(): pl.pallas_call(functools.partial(input_kernel, len(pieces)), in_specs=[SM...  9.02 us
  transfers between devices with their start and end apart: 41, of which 18 were waited for; matrix products, arithmetic and copies ran while one was open for 14% of the time, Pallas kernels for 27%

profile of v3, /device:TPU:0, one launch (start us, length us, event | category | flops | bytes accessed | tf_op | source)
XLA Modules:
  0.0 307.4 jit_solution(4437581723627161021)
XLA Ops:
  3.0 5.1 %collective-permute-start.2 = (bf16[144,384]{1,0:T(8,128)(2,1)S(1)}, bf16[144,384]{1,0:T(8,128)(2,1)S(1)}, u32[]{:S(2)}, u32[]{:S(2)}) collective-permute-start(bf16[144,384]{1,0:T(8,128)(2,1)S(1)} %constant_dynamic-update-slice_fusion), channel_id=1, source_target_pairs={{0,24},{1,25},{2,26},{3,27},{4,28},{5,29},{6,30},{7,31},{8,16},{9,... | collective-permute-start | bytes 331784 | tf_op jit(solution)/shard_map/ppermute | solution.py:625
  14.9 5.0 %all-to-all-start = ((bf16[4,48,3584]{2,1,0:T(8,128)(2,1)}), bf16[4,48,3584]{2,1,0:T(8,128)(2,1)}, u32[]{:S(2)}, u32[]{:S(2)}) async-start(bf16[4,48,3584]{2,1,0:T(8,128)(2,1)} %broadcast_in_dim.33), calls=%async_computation | async-start | bytes 2752512 | tf_op jit(solution)/shard_map/all_to_all | solution.py:633
  23.1 7.8 %collective-permute-done.3 = bf16[4,144,384]{2,1,0:T(8,128)(2,1)S(1)} collective-permute-done((bf16[4,144,384]{2,1,0:T(8,128)(2,1)S(1)}, bf16[4,144,384]{2,1,0:T(8,128)(2,1)S(1)}, u32[]{:S(2)}, u32[]{:S(2)}) %collective-permute-start.3) | collective-permute-done | bytes 442400 | tf_op jit(solution)/shard_map/ppermute | solution.py:625
  35.9 5.7 %collective-permute-done.5 = bf16[2,144,384]{2,1,0:T(8,128)(2,1)S(1)} collective-permute-done((bf16[2,144,384]{2,1,0:T(8,128)(2,1)S(1)}, bf16[2,144,384]{2,1,0:T(8,128)(2,1)S(1)}, u32[]{:S(2)}, u32[]{:S(2)}) %collective-permute-start.5) | collective-permute-done | bytes 221216 | tf_op jit(solution)/shard_map/ppermute | solution.py:625
  47.9 4.0 %all-to-all-done = bf16[4,48,3584]{2,1,0:T(8,128)(2,1)} async-done(((bf16[4,48,3584]{2,1,0:T(8,128)(2,1)}), bf16[4,48,3584]{2,1,0:T(8,128)(2,1)}, u32[]{:S(2)}, u32[]{:S(2)}) %all-to-all-start) | async-done | bytes 1376288 | tf_op jit(solution)/shard_map/all_to_all | solution.py:633
  54.9 21.1 %attend.1 = (bf16[512,768]{1,0:T(8,128)(2,1)}, bf16[512,768]{1,0:T(8,128)(2,1)}, bf16[512,768]{1,0:T(8,128)(2,1)}, bf16[512,768]{1,0:T(8,128)(2,1)}, bf16[12,256,768]{2,1,0:T(8,128)(2,1)}) custom-call(s32[4]{0:T(128)} %pad_add_fusion.spot, s32[1,2]{1,0:T(1,128)} %starts.1, bf16[512,768]{1,0:T(8,128)(2,1)} %copy.38.normed_ref, ...), custom_call_target="tpu_custom_call" | custom-call | flops 20000000000 | bytes 1000000 | tf_op jit(solution)/shard_map/attend/pallas_call | solution.py:158
  76.1 7.3 %collective-permute-done.10 = bf16[4,48,3584]{2,1,0:T(8,128)(2,1)S(1)} collective-permute-done((bf16[4,48,3584]{2,1,0:T(8,128)(2,1)}, bf16[4,48,3584]{2,1,0:T(8,128)(2,1)S(1)}, u32[]{:S(2)}, u32[]{:S(2)}) %collective-permute-start.10) | collective-permute-done | bytes 1376288 | tf_op jit(solution)/shard_map/ppermute | solution.py:625
  84.6 3.3 %pad_maximum_fusion.rest_0_ = bf16[3,4,48,3584]{3,2,1,0:T(8,128)(2,1)} fusion(bf16[1,4,48,3584]{3,2,1,0:T(8,128)(2,1)S(1)} %bitcast.88, bf16[1,4,48,3584]{3,2,1,0:T(8,128)(2,1)S(1)} %bitcast.89, bf16[1,4,48,3584]{3,2,1,0:T(8,128)(2,1)} %bitcast.14), kind=kLoop, calls=%fused_computation.2 | loop fusion | flops 4128768 | bytes 8257536 | tf_op jit(solution)/shard_map/stack | solution.py:768
  90.1 15.8 %collective-permute-done.12 = bf16[2,48,3584]{2,1,0:T(8,128)(2,1)S(1)} collective-permute-done((bf16[2,48,3584]{2,1,0:T(8,128)(2,1)S(1)}, bf16[2,48,3584]{2,1,0:T(8,128)(2,1)S(1)}, u32[]{:S(2)}, u32[]{:S(2)}) %collective-permute-start.12) | collective-permute-done | bytes 688160 | tf_op jit(solution)/shard_map/ppermute | solution.py:625
  110.6 24.6 %forward.1 = (f32[512,768]{1,0:T(8,128)}, f32[512,768]{1,0:T(8,128)}, bf16[512,3072]{1,0:T(8,128)(2,1)}, bf16[768,512]{1,0:T(8,128)(2,1)}, f32[512,768]{1,0:T(8,...) custom-call(s32[4]{0:T(128)} %pad_add_fusion.spot, ...), custom_call_target="tpu_custom_call" | custom-call | flops 20000000000 | bytes 1000000 | tf_op jit(solution)/shard_map/forward/pallas_call | solution.py:294
  135.4 4.6 %collective-permute-done.15 = bf16[4,4,48,1536]{3,2,1,0:T(8,128)(2,1)S(1)} collective-permute-done((bf16[4,4,48,1536]{3,2,1,0:T(8,128)(2,1)}, bf16[4,4,48,1536]{3,2,1,0:T(8,128)(2,1)S(1)}, u32[]{:S(2)}, u32[]{:S(2)}) %collective-permute-start.15) | collective-permute-done | bytes 2359328 | tf_op jit(solution)/shard_map/ppermute | solution.py:625
  140.0 2.4 add_convert_fusion.1
  145.0 23.4 %back.1 = (f32[512,768]{1,0:T(8,128)}, bf16[512,768]{1,0:T(8,128)(2,1)}, f32[8,768]{1,0:T(8,128)}, bf16[4,4,48,1920]{3,2,1,0:T(8,128)(2,1)}, bf16[4,4,48,1920]{3,2,1,0:T(8,128)(2,1)}) custom-call(s32[4]{0:T(128)} %pad_add_fusion.spot, bf16[3,4,48,3584]{3,2,1,0:T(8,128)(2,1)} %pad_maximum_fusion.rest_0_, bf16[2,2,48,3584]{3,2,1,0:T(8,128)(2,1)} %copy-done.5, ...), custom_call_target="tpu_custom_call" | custom-call | flops 20000000000 | bytes 1000000 | tf_op jit(solution)/shard_map/back/pallas_call | solution.py:417
  171.8 2.3 collective-permute-done.18
  179.1 28.7 %attend_back.1 = (bf16[512,768]{1,0:T(8,128)(2,1)}, bf16[512,768]{1,0:T(8,128)(2,1)}, bf16[512,768]{1,0:T(8,128)(2,1)}, f32[12,1,768]{2,1,0:T(1,128)}, f32[12,12...) custom-call(s32[4]{0:T(128)} %pad_add_fusion.spot, f32[12,12]{1,0:T(8,128)} %copy-done.13, ...), custom_call_target="tpu_custom_call" | custom-call | flops 28000000000 | bytes 1000000 | tf_op jit(solution)/shard_map/attend_back/pallas_call | solution.py:552
  214.8 3.5 %all-to-all-start.1 = ((bf16[4,48,1536]{2,1,0:T(8,128)(2,1)}), bf16[4,48,1536]{2,1,0:T(8,128)(2,1)S(1)}, u32[]{:S(2)}, u32[]{:S(2)}) async-start(bf16[4,48,1536]{2,1,0:T(8,128)(2,1)} %pad_maximum_fusion.4), calls=%async_computation.1 | async-start | bytes 1179648 | tf_op jit(solution)/shard_map/all_to_all | solution.py:633
  228.0 9.0 %input_grad.1 = (f32[512,768]{1,0:T(8,128)}, f32[8,768]{1,0:T(8,128)}) custom-call(s32[4]{0:T(128)} %pad_add_fusion.spot, bf16[3,4,144,384]{3,2,1,0:T(8,128)(2,1)} %pad_maximum_fusion.2.rest_0_, bf16[2,2,144,384]{3,2,1,0:T(8,128)(2,1)} %pad_maximum_fusion.6.rest_1_, bf16[3,4,144,384]{3,2,1,0:T(8,128)(2,1)} %collective-permute-done.7.rest_2_, ...), custom_call_target="tpu_custom_call" | custom-call | flops 8999999488 | bytes 1000000 | tf_op jit(solution)/shard_map/input_grad/pallas_call | solution.py:609
  237.0 4.2 %collective-permute-done.24 = bf16[2,2,144,384]{3,2,1,0:T(8,128)(2,1)S(1)} collective-permute-done((bf16[2,2,144,384]{3,2,1,0:T(8,128)(2,1)S(1)}, bf16[2,2,144,384]{3,2,1,0:T(8,128)(2,1)S(1)}, u32[]{:S(2)}, u32[]{:S(2)}) %collective-permute-start.24) | collective-permute-done | bytes 442400 | tf_op jit(solution)/shard_map/ppermute | solution.py:625
  258.2 4.2 %collective-permute-done.31 = f32[16,128]{1,0:T(8,128)S(1)} collective-permute-done((f32[16,128]{1,0:T(8,128)S(1)}, f32[16,128]{1,0:T(8,128)S(1)}, u32[]{:S(2)}, u32[]{:S(2)}) %collective-permute-start.31) | collective-permute-done | bytes 8224 | tf_op jit(solution)/shard_map/ppermute | solution.py:625
  266.1 4.8 %all-to-all-start.2 = ((bf16[4,48,1920]{2,1,0:T(8,128)(2,1)}), bf16[4,48,1920]{2,1,0:T(8,128)(2,1)S(1)}, u32[]{:S(2)}, u32[]{:S(2)}) async-start(bf16[4,48,1920]{2,1,0:T(8,128)(2,1)} %pad_maximum_fusion.3), calls=%async_computation.2 | async-start | bytes 1474560 | tf_op jit(solution)/shard_map/all_to_all | solution.py:633
  274.6 2.9 collective-permute-start.36
  279.0 5.3 %collective-permute-done.33 = f32[16,128]{1,0:T(8,128)S(1)} collective-permute-done((f32[16,128]{1,0:T(8,128)S(1)}, f32[16,128]{1,0:T(8,128)S(1)}, u32[]{:S(2)}, u32[]{:S(2)}) %collective-permute-start.33) | collective-permute-done | bytes 8224 | tf_op jit(solution)/shard_map/ppermute | solution.py:625
  284.2 4.9 %collective-permute-start.34 = (f32[16,128]{1,0:T(8,128)S(1)}, f32[16,128]{1,0:T(8,128)S(1)}, u32[]{:S(2)}, u32[]{:S(2)}) collective-permute-start(f32[16,128]{1,0:T(8,128)S(1)} %add.160), channel_id=1, source_target_pairs={{0,16},{1,17},{2,18},{3,19},{4,20},{5,21},{6,22},{7,23},{8,24},{9,... | collective-permute-start | bytes 24584 | tf_op jit(solution)/shard_map/ppermute | solution.py:625
  289.9 8.3 %collective-permute-done.34 = f32[16,128]{1,0:T(8,128)S(1)} collective-permute-done((f32[16,128]{1,0:T(8,128)S(1)}, f32[16,128]{1,0:T(8,128)S(1)}, u32[]{:S(2)}, u32[]{:S(2)}) %collective-permute-start.34) | collective-permute-done | bytes 8224 | tf_op jit(solution)/shard_map/ppermute | solution.py:625
  (178 shorter events, 90.4 us)
Async XLA Ops:
  3.0 17.0 %collective-permute-start.2 = (bf16[144,384]{1,0:T(8,128)(2,1)S(1)}, bf16[144,384]{1,0:T(8,128)(2,1)S(1)}, u32[]{:S(2)}, u32[]{:S(2)}) collective-permute-start(bf16[144,384]{1,0:T(8,128)(2,1)S(1)} %constant_dynamic-update-slice_fusion), channel_id=1, source_target_pairs={{0,24},{1,25},{2,26},{3,27},{4,28},{5,29},{6,30},{7,31},{8,16},{9,... | collective-permute-start | bytes 331784 | tf_op jit(solution)/shard_map/ppermute | solution.py:625
  14.9 37.0 %all-to-all-start = ((bf16[4,48,3584]{2,1,0:T(8,128)(2,1)}), bf16[4,48,3584]{2,1,0:T(8,128)(2,1)}, u32[]{:S(2)}, u32[]{:S(2)}) async-start(bf16[4,48,3584]{2,1,0:T(8,128)(2,1)} %broadcast_in_dim.33), calls=%async_computation | async-start | bytes 2752512 | tf_op jit(solution)/shard_map/all_to_all | solution.py:633
  51.9 31.4 %collective-permute-start.10 = (bf16[4,48,3584]{2,1,0:T(8,128)(2,1)}, bf16[4,48,3584]{2,1,0:T(8,128)(2,1)S(1)}, u32[]{:S(2)}, u32[]{:S(2)}) collective-permute-start(bf16[4,48,3584]{2,1,0:T(8,128)(2,1)} %all-to-all-done), channel_id=1, source_target_pairs={{0,4},{1,5},{2,6},{3,7},{4,0},{5,1},{6,2},{7,3},{8,12},{9,13},{10,... | collective-permute-start | bytes 4128776 | tf_op jit(solution)/shard_map/ppermute | solution.py:625
  53.5 31.1 %collective-permute-start.9 = (bf16[4,48,3584]{2,1,0:T(8,128)(2,1)}, bf16[4,48,3584]{2,1,0:T(8,128)(2,1)S(1)}, u32[]{:S(2)}, u32[]{:S(2)}) collective-permute-start(bf16[4,48,3584]{2,1,0:T(8,128)(2,1)} %all-to-all-done), channel_id=1, source_target_pairs={{0,1},{1,0},{2,3},{3,2},{4,5},{5,4},{6,7},{7,6},{8,9},{9,8},{10,11... | collective-permute-start | bytes 4128776 | tf_op jit(solution)/shard_map/ppermute | solution.py:625
  87.9 22.7 %collective-permute-start.13 = (bf16[3,4,48,3584]{3,2,1,0:T(8,128)(2,1)}, bf16[3,4,48,3584]{3,2,1,0:T(8,128)(2,1)}, u32[]{:S(2)}, u32[]{:S(2)}) collective-permute-start(bf16[3,4,48,3584]{3,2,1,0:T(8,128)(2,1)} %pad_maximum_fusion.rest_0_), channel_id=1, source_target_pairs={{0,2},{1,3},{2,0},{3,1},{4,6},{5,7},{6,4},{7,5},{8,10},{9,11},{10,... | collective-permute-start | bytes 12386312 | tf_op jit(solution)/shard_map/ppermute | solution.py:625
  88.0 17.9 %collective-permute-start.12 = (bf16[2,48,3584]{2,1,0:T(8,128)(2,1)S(1)}, bf16[2,48,3584]{2,1,0:T(8,128)(2,1)S(1)}, u32[]{:S(2)}, u32[]{:S(2)}) collective-permute-start(bf16[2,48,3584]{2,1,0:T(8,128)(2,1)S(1)} %slice.157), channel_id=1, source_target_pairs={{0,1},{1,0},{2,3},{3,2},{4,5},{5,4},{6,7},{7,6},{8,9},{9,8},{10,11... | collective-permute-start | bytes 2064392 | tf_op jit(solution)/shard_map/ppermute | solution.py:625
  89.6 17.6 %collective-permute-start.11 = (bf16[2,48,3584]{2,1,0:T(8,128)(2,1)S(1)}, bf16[2,48,3584]{2,1,0:T(8,128)(2,1)S(1)}, u32[]{:S(2)}, u32[]{:S(2)}) collective-permute-start(bf16[2,48,3584]{2,1,0:T(8,128)(2,1)S(1)} %slice.156), channel_id=1, source_target_pairs={{0,4},{1,5},{2,6},{3,7},{4,0},{5,1},{6,2},{7,3},{8,12},{9,13},{10,... | collective-permute-start | bytes 2064392 | tf_op jit(solution)/shard_map/ppermute | solution.py:625
  143.9 24.5 %collective-permute-start.16 = (bf16[2,2,48,1536]{3,2,1,0:T(8,128)(2,1)S(1)}, bf16[2,2,48,1536]{3,2,1,0:T(8,128)(2,1)S(1)}, u32[]{:S(2)}, u32[]{:S(2)}) collective-permute-start(bf16[2,2,48,1536]{3,2,1,0:T(8,128)(2,1)S(1)} %get-tuple-element.110), channel_id=1, source_target_pairs={{0,4},{1,5},{2,6},{3,7},{4,0},{5,1},{6,2},{7,3},{8,12},{9,13},{10,... | collective-permute-start | bytes 1769480 | tf_op jit(solution)/shard_map/ppermute | solution.py:625
  144.5 24.0 %collective-permute-start.17 = (bf16[2,2,48,1536]{3,2,1,0:T(8,128)(2,1)S(1)}, bf16[2,2,48,1536]{3,2,1,0:T(8,128)(2,1)S(1)}, u32[]{:S(2)}, u32[]{:S(2)}) collective-permute-start(bf16[2,2,48,1536]{3,2,1,0:T(8,128)(2,1)S(1)} %get-tuple-element.111), channel_id=1, source_target_pairs={{0,1},{1,0},{2,3},{3,2},{4,5},{5,4},{6,7},{7,6},{8,9},{9,8},{10,11... | collective-permute-start | bytes 1769480 | tf_op jit(solution)/shard_map/ppermute | solution.py:625
  175.0 32.8 %collective-permute-start.21 = (bf16[2,48,1536]{2,1,0:T(8,128)(2,1)}, bf16[2,48,1536]{2,1,0:T(8,128)(2,1)S(1)}, u32[]{:S(2)}, u32[]{:S(2)}) collective-permute-start(bf16[2,48,1536]{2,1,0:T(8,128)(2,1)} %get-tuple-element.134), channel_id=1, source_target_pairs={{0,1},{1,0},{2,3},{3,2},{4,5},{5,4},{6,7},{7,6},{8,9},{9,8},{10,11... | collective-permute-start | bytes 884744 | tf_op jit(solution)/shard_map/ppermute | solution.py:625
  176.5 31.3 %collective-permute-start.22 = (bf16[2,48,1536]{2,1,0:T(8,128)(2,1)}, bf16[2,48,1536]{2,1,0:T(8,128)(2,1)}, u32[]{:S(2)}, u32[]{:S(2)}) collective-permute-start(bf16[2,48,1536]{2,1,0:T(8,128)(2,1)} %get-tuple-element.135), channel_id=1, source_target_pairs={{0,4},{1,5},{2,6},{3,7},{4,0},{5,1},{6,2},{7,3},{8,12},{9,13},{10,... | collective-permute-start | bytes 884744 | tf_op jit(solution)/shard_map/ppermute | solution.py:625
  178.1 29.8 %collective-permute-start.19 = (bf16[2,2,48,1920]{3,2,1,0:T(8,128)(2,1)S(1)}, bf16[2,2,48,1920]{3,2,1,0:T(8,128)(2,1)}, u32[]{:S(2)}, u32[]{:S(2)}) collective-permute-start(bf16[2,2,48,1920]{3,2,1,0:T(8,128)(2,1)S(1)} %get-tuple-element.132), channel_id=1, source_target_pairs={{0,4},{1,5},{2,6},{3,7},{4,0},{5,1},{6,2},{7,3},{8,12},{9,13},{10,... | collective-permute-start | bytes 2211848 | tf_op jit(solution)/shard_map/ppermute | solution.py:625
  178.6 29.3 %collective-permute-start.20 = (bf16[2,2,48,1920]{3,2,1,0:T(8,128)(2,1)S(1)}, bf16[2,2,48,1920]{3,2,1,0:T(8,128)(2,1)}, u32[]{:S(2)}, u32[]{:S(2)}) collective-permute-start(bf16[2,2,48,1920]{3,2,1,0:T(8,128)(2,1)S(1)} %get-tuple-element.133), channel_id=1, source_target_pairs={{0,1},{1,0},{2,3},{3,2},{4,5},{5,4},{6,7},{7,6},{8,9},{9,8},{10,11... | collective-permute-start | bytes 2211848 | tf_op jit(solution)/shard_map/ppermute | solution.py:625
  208.6 15.0 %collective-permute-start.23 = (bf16[4,4,144,384]{3,2,1,0:T(8,128)(2,1)}, bf16[4,4,144,384]{3,2,1,0:T(8,128)(2,1)}, u32[]{:S(2)}, u32[]{:S(2)}) collective-permute-start(bf16[4,4,144,384]{3,2,1,0:T(8,128)(2,1)} %get-tuple-element.139), channel_id=1, source_target_pairs={{0,2},{1,3},{2,0},{3,1},{4,6},{5,7},{6,4},{7,5},{8,10},{9,11},{10,... | collective-permute-start | bytes 5308424 | tf_op jit(solution)/shard_map/ppermute | solution.py:625
  214.8 51.3 %all-to-all-start.1 = ((bf16[4,48,1536]{2,1,0:T(8,128)(2,1)}), bf16[4,48,1536]{2,1,0:T(8,128)(2,1)S(1)}, u32[]{:S(2)}, u32[]{:S(2)}) async-start(bf16[4,48,1536]{2,1,0:T(8,128)(2,1)} %pad_maximum_fusion.4), calls=%async_computation.1 | async-start | bytes 1179648 | tf_op jit(solution)/shard_map/all_to_all | solution.py:633
  220.6 16.5 %collective-permute-start.27 = (bf16[2,48,1920]{2,1,0:T(8,128)(2,1)}, bf16[2,48,1920]{2,1,0:T(8,128)(2,1)}, u32[]{:S(2)}, u32[]{:S(2)}) collective-permute-start(bf16[2,48,1920]{2,1,0:T(8,128)(2,1)} %get-tuple-element.176), channel_id=1, source_target_pairs={{0,4},{1,5},{2,6},{3,7},{4,0},{5,1},{6,2},{7,3},{8,12},{9,13},{10,... | collective-permute-start | bytes 1105928 | tf_op jit(solution)/shard_map/ppermute | solution.py:625
  222.1 14.9 %collective-permute-start.26 = (bf16[2,48,1920]{2,1,0:T(8,128)(2,1)}, bf16[2,48,1920]{2,1,0:T(8,128)(2,1)}, u32[]{:S(2)}, u32[]{:S(2)}) collective-permute-start(bf16[2,48,1920]{2,1,0:T(8,128)(2,1)} %get-tuple-element.177), channel_id=1, source_target_pairs={{0,1},{1,0},{2,3},{3,2},{4,5},{5,4},{6,7},{7,6},{8,9},{9,8},{10,11... | collective-permute-start | bytes 1105928 | tf_op jit(solution)/shard_map/ppermute | solution.py:625
  227.4 15.1 %collective-permute-start.25 = (bf16[2,2,144,384]{3,2,1,0:T(8,128)(2,1)S(1)}, bf16[2,2,144,384]{3,2,1,0:T(8,128)(2,1)S(1)}, u32[]{:S(2)}, u32[]{:S(2)}) collective-permute-start(bf16[2,2,144,384]{3,2,1,0:T(8,128)(2,1)S(1)} %get-tuple-element.145), channel_id=1, source_target_pairs={{0,1},{1,0},{2,3},{3,2},{4,5},{5,4},{6,7},{7,6},{8,9},{9,8},{10,11... | collective-permute-start | bytes 1327112 | tf_op jit(solution)/shard_map/ppermute | solution.py:625
  253.5 17.4 %collective-permute-start.29 = (bf16[2,144,384]{2,1,0:T(8,128)(2,1)}, bf16[2,144,384]{2,1,0:T(8,128)(2,1)}, u32[]{:S(2)}, u32[]{:S(2)}) collective-permute-start(bf16[2,144,384]{2,1,0:T(8,128)(2,1)} %get-tuple-element.188), channel_id=1, source_target_pairs={{0,4},{1,5},{2,6},{3,7},{4,0},{5,1},{6,2},{7,3},{8,12},{9,13},{10,... | collective-permute-start | bytes 663560 | tf_op jit(solution)/shard_map/ppermute | solution.py:625
  254.5 16.4 %collective-permute-start.28 = (bf16[2,144,384]{2,1,0:T(8,128)(2,1)}, bf16[2,144,384]{2,1,0:T(8,128)(2,1)}, u32[]{:S(2)}, u32[]{:S(2)}) collective-permute-start(bf16[2,144,384]{2,1,0:T(8,128)(2,1)} %get-tuple-element.189), channel_id=1, source_target_pairs={{0,1},{1,0},{2,3},{3,2},{4,5},{5,4},{6,7},{7,6},{8,9},{9,8},{10,11... | collective-permute-start | bytes 663560 | tf_op jit(solution)/shard_map/ppermute | solution.py:625
  266.1 37.5 %all-to-all-start.2 = ((bf16[4,48,1920]{2,1,0:T(8,128)(2,1)}), bf16[4,48,1920]{2,1,0:T(8,128)(2,1)S(1)}, u32[]{:S(2)}, u32[]{:S(2)}) async-start(bf16[4,48,1920]{2,1,0:T(8,128)(2,1)} %pad_maximum_fusion.3), calls=%async_computation.2 | async-start | bytes 1474560 | tf_op jit(solution)/shard_map/all_to_all | solution.py:633
  274.5 28.4 %collective-permute-start.35 = (bf16[144,384]{1,0:T(8,128)(2,1)S(1)}, bf16[144,384]{1,0:T(8,128)(2,1)S(1)}, u32[]{:S(2)}, u32[]{:S(2)}) collective-permute-start(bf16[144,384]{1,0:T(8,128)(2,1)S(1)} %fusion.14), channel_id=1, source_target_pairs={{0,8},{1,9},{2,10},{3,11},{4,12},{5,13},{6,14},{7,15},{8,0},{9,1},... | collective-permute-start | bytes 331784 | tf_op jit(solution)/shard_map/ppermute | solution.py:625
  274.6 28.3 %collective-permute-start.36 = (bf16[144,384]{1,0:T(8,128)(2,1)S(1)}, bf16[144,384]{1,0:T(8,128)(2,1)S(1)}, u32[]{:S(2)}, u32[]{:S(2)}) collective-permute-start(bf16[144,384]{1,0:T(8,128)(2,1)S(1)} %get-tuple-element.197), channel_id=1, source_target_pairs={{0,16},{1,17},{2,18},{3,19},{4,20},{5,21},{6,22},{7,23},{8,24},{9,... | collective-permute-start | bytes 331784 | tf_op jit(solution)/shard_map/ppermute | solution.py:625
  277.5 25.4 %collective-permute-start.37 = (bf16[144,384]{1,0:T(8,128)(2,1)S(1)}, bf16[144,384]{1,0:T(8,128)(2,1)S(1)}, u32[]{:S(2)}, u32[]{:S(2)}) collective-permute-start(bf16[144,384]{1,0:T(8,128)(2,1)S(1)} %get-tuple-element.198), channel_id=1, source_target_pairs={{0,24},{1,25},{2,26},{3,27},{4,28},{5,29},{6,30},{7,31},{8,16},{9,... | collective-permute-start | bytes 331784 | tf_op jit(solution)/shard_map/ppermute | solution.py:625
  (35 other events, 275.2 us)

commit v4 on v2

--- a/solution.py
+++ b/solution.py
@@ -4,6 +4,7 @@
 import jax.numpy as jnp
 from jax import lax
 from jax.experimental import pallas as pl
+from jax.experimental.layout import Layout, with_layout_constraint
 from jax.experimental.pallas import tpu as pltpu
 from jax.sharding import PartitionSpec as P
 
@@ -46,7 +47,7 @@
             yield halves, (z // 2, z % 2), core, 1, 1, z
 
 
-def place_copies(spot, pieces, wholes, rows_at, cols_at, widths, sems):
+def place_copies(spot, pieces, wholes, rows_at, cols_at, widths, sems, near=False):
     if len(pieces) == len(wholes):
         return [
             pltpu.make_async_copy(piece, whole, sems.at[n])
@@ -54,7 +55,7 @@
         ]
     copies = []
     for piece, index, core, y, x, z in placed(pieces):
-        r = (z * 2 + (spot[1] ^ y)) * 2 + (spot[2] ^ core)
+        r = ((spot[0] ^ z if near else z) * 2 + (spot[1] ^ y)) * 2 + (spot[2] ^ core)
         c = spot[3] ^ x
         for whole, row, col, width in zip(wholes, rows_at, cols_at, widths):
             depth = whole.shape[0] // 16
@@ -71,7 +72,7 @@
     return copies
 
 
-def send_copies(spot, source, keep, send, row, half, col, width, sems):
+def send_copies(spot, source, keep, send, row, half, col, width, sems, near=False):
     depth = source.shape[0] // 16
     copies = []
     for j in range(8):
@@ -82,7 +83,7 @@
             copies.append(
                 pltpu.make_async_copy(
                     source.at[pl.ds(start, depth), pl.ds(0, width)],
-                    target.at[plane, z, pl.ds(row, depth), pl.ds(col, width)],
+                    target.at[plane, spot[0] ^ z if near else z, pl.ds(row, depth), pl.ds(col, width)],
                     sems.at[2 * j + n],
                 )
             )
@@ -100,7 +101,7 @@
         width = wq.shape[1] // 2
         depth = wq.shape[0] // 16
         copies = place_copies(
-            spot, pieces, (wq, wk, wv), (0, depth, 2 * depth), (0, 0, 0), (width,) * 3, sems
+            spot, pieces, (wq, wk, wv), (0, depth, 2 * depth), (0, 0, 0), (width,) * 3, sems, True
         )
         for copy in copies:
             copy.start()
@@ -182,7 +183,7 @@
     wo, wu, wd, hidden, pre, n2t, olt, slots, marks, sems, out_sems, mark_sems = rest
     seq, width = att_ref.shape
     units = wu.shape[1]
-    blocked = outs == 4
+    blocked = outs == 2
     mark_copies = []
     if blocked:
         for n, (piece, index, *_) in enumerate(placed(pieces)):
@@ -208,10 +209,8 @@
         copy.wait()
     total_valid = jnp.full((1, 1), count[0, 0], F32)
     if blocked:
-        digits = jnp.sum(marks[...].astype(F32), axis=0)[:1]
-        lanes = lax.broadcasted_iota(jnp.int32, digits.shape, 1)
-        digits = jnp.where(lanes == 0, digits * 256.0, jnp.where(lanes == 1, digits, 0.0))
-        total_valid += jnp.sum(digits, axis=1, keepdims=True)
+        by_lane = jnp.sum(marks[...].astype(F32), axis=0)[:1]
+        total_valid += jnp.sum(by_lane, axis=1, keepdims=True)
     factor = tokens / total_valid
     sums_ref[...] = jnp.broadcast_to(total_valid, sums_ref.shape)
     for copy in copies[::3]:
@@ -272,13 +271,14 @@
         return send_copies(
             spot,
             slots.at[which],
-            grads[2 * which],
-            grads[2 * which + 1],
+            grads[0],
+            grads[1],
             0,
             j // per,
-            pl.multiple_of((j % per) * chunk, 128),
+            pl.multiple_of(which * ((units + width) // 2) + (j % per) * chunk, 128),
             chunk,
             out_sems.at[which],
+            True,
         )
 
     lax.fori_loop(0, steps, down_step, 0)
@@ -306,7 +306,7 @@
         slots[c, :, :half] = dot(n2t[...], branch[:, c * half : (c + 1) * half]).astype(BF16)
         if blocked:
             made = send_copies(
-                spot, slots.at[c], grads[0], grads[1], 0, c, units // 2, half, out_sems.at[c]
+                spot, slots.at[c], grads[0], grads[1], 0, c, units // 2, half, out_sems.at[c], True
             )
         else:
             made = [
@@ -328,8 +328,7 @@
     full = jax.ShapeDtypeStruct((seq, width), F32)
     if blocked:
         depth = width // 16
-        grads = [jax.ShapeDtypeStruct((4, 4, depth, (units + width) // 2), BF16)] * 2
-        grads += [jax.ShapeDtypeStruct((4, 4, depth, units // 2), BF16)] * 2
+        grads = [jax.ShapeDtypeStruct((4, 4, depth, units + width // 2), BF16)] * 2
     else:
         grads = [
             jax.ShapeDtypeStruct((width, units), BF16),
@@ -367,36 +366,27 @@
     )(spot, count, *pieces, attended, states, upstream, teacher, valid, gain)
 
 
-def attend_back_kernel(first, blocked, spot, pms, pos, *refs):
-    turned, refs = (None, refs) if first else (refs[:7], refs[7:])
-    q_ref, k_ref, v_ref, g_ref, p_ref, pm_ref, po_ref = refs[:7]
-    pre_ref, post_ref, *rest = refs[7:]
-    if first:
-        vt, qt, gt, dq, dkt, dvt = rest
-    else:
-        nt_ref, vt, qt, gt, dq_in, dkt_in, dvt_in = turned
-        dq_ref, dk_ref, dv_ref, *rest = rest
-        outs = 2 if blocked else 3
-        grads = rest[:outs]
-        dq, dkt, dvt, slots, sems = rest[outs:]
+def attend_back_kernel(
+    blocked, spot, pms, pos, nt_ref, q_ref, k_ref, v_ref, g_ref, p_ref, pm_ref, po_ref,
+    dq_ref, dk_ref, dv_ref, mix_ref, *rest,
+):
+    outs = 2 if blocked else 3
+    grads = rest[:outs]
+    vt, qt, gt, dq, dkt, dvt, pre, slots, sems = rest[outs:]
     step = pl.program_id(0)
-    head = step if first else step + HEADS // 2
     seq, width = q_ref.shape
     half = seq // 2
 
     @pl.when(step == 0)
     def _():
-        if first:
-            vt[...] = v_ref[...].T
-            qt[...] = q_ref[...].T
-            gt[...] = g_ref[...].T
-            dq[...] = jnp.zeros_like(dq)
-            dkt[...] = jnp.zeros_like(dkt)
-            dvt[...] = jnp.zeros_like(dvt)
-        else:
-            dq[...] = dq_in[...]
-            dkt[...] = dkt_in[...]
-            dvt[...] = dvt_in[...]
+        vt[...] = v_ref[...].T
+        qt[...] = q_ref[...].T
+        gt[...] = g_ref[...].T
+        dq[...] = jnp.zeros_like(dq)
+        dkt[...] = jnp.zeros_like(dkt)
+        dvt[...] = jnp.zeros_like(dvt)
+        pre[...] = jnp.zeros_like(pre)
+        mix_ref[...] = jnp.zeros_like(mix_ref)
 
     pm = pm_ref[0]
     po = po_ref[0]
@@ -419,20 +409,27 @@
     w1 = dot(d1, k_ref[:half]) + dot(d2, k_ref[half:])
     dq[:half] += pm * w0
     dq[half:] += pm * w1
-    pre_ref[0] = jnp.sum(q_ref[:half].astype(F32) * w0, axis=0, keepdims=True) + jnp.sum(
+    row = jnp.sum(q_ref[:half].astype(F32) * w0, axis=0, keepdims=True) + jnp.sum(
         q_ref[half:].astype(F32) * w1, axis=0, keepdims=True
     )
+    pre[...] += jnp.where(lax.broadcasted_iota(jnp.int32, pre.shape, 0) == step, row, 0.0)
+    lane = lax.broadcasted_iota(jnp.int32, (1, 128), 1)
+    posts = jnp.zeros((1, 128), F32)
     for g in range(HEADS):
         at = slice(g * HEAD_DIM, (g + 1) * HEAD_DIM)
-        b = pos[head, g]
+        b = pos[step, g]
         u0g, u1g = u0[at], u1[at]
         dvt[at, :half] += b * u0g
         dvt[at, half:] += b * u1g
         both = u0g * vt[at, :half].astype(F32) + u1g * vt[at, half:].astype(F32)
-        post_ref[0, g : g + 1, :] = jnp.sum(both, axis=0, keepdims=True)
+        post = jnp.sum(jnp.sum(both, axis=0, keepdims=True), axis=1, keepdims=True)
+        posts += jnp.where(lane == 16 + g, post, 0.0)
+    mix_ref[...] += jnp.where(
+        lax.broadcasted_iota(jnp.int32, mix_ref.shape, 0) == step, posts, 0.0
+    )
     qs = jnp.concatenate(
         [
-            (qt[g * HEAD_DIM : (g + 1) * HEAD_DIM].astype(F32) * pms[head, g]).astype(BF16)
+            (qt[g * HEAD_DIM : (g + 1) * HEAD_DIM].astype(F32) * pms[step, g]).astype(BF16)
             for g in range(HEADS)
         ],
         axis=0,
@@ -440,11 +437,19 @@
     dkt[:, :half] += dot(qs[:, :half], d0) + dot(qs[:, half:], d1)
     dkt[:, half:] += dot(qs[:, half:], d2)
 
-    if first:
-        return
-
-    @pl.when(step == HEADS // 2 - 1)
+    @pl.when(step == HEADS - 1)
     def _():
+        feature = lax.broadcasted_iota(jnp.int32, (width, 128), 0)
+        head = lax.broadcasted_iota(jnp.int32, (width, 128), 1)
+        member = (feature >= head * HEAD_DIM) & (feature < (head + 1) * HEAD_DIM)
+        turned = lax.dot_general(
+            member.astype(F32),
+            pre[...],
+            (((0,), (1,)), ((), ())),
+            precision=lax.Precision.HIGHEST,
+            preferred_element_type=F32,
+        )
+        mix_ref[:, :16] += turned[:16]
         dq_ref[...] = dq[...].astype(BF16)
         dk_ref[...] = dkt[...].astype(BF16).T
         dv_ref[...] = dvt[...].astype(BF16).T
@@ -464,6 +469,7 @@
                         0,
                         part,
                         sems.at[2 * n + c],
+                        True,
                     )
             else:
                 made.append(pltpu.make_async_copy(slots.at[n], grads[n], sems.at[n, 0]))
@@ -473,68 +479,52 @@
             copy.wait()
 
 
-def attend_back(spot, blocked, turned, q, k, v, g, p, pm, po, pms, pos):
+def attend_back(spot, blocked, nt, q, k, v, g, p, pm, po, pms, pos):
     seq, width = q.shape
     half = seq // 2
-    first = turned is None
-    base = 0 if first else HEADS // 2
     whole = pl.BlockSpec((seq, width), lambda h: (0, 0))
-    across = pl.BlockSpec((width, seq), lambda h: (0, 0))
-    row = pl.BlockSpec((1, 1, width), lambda h: (h + base, 0, 0))
+    row = pl.BlockSpec((1, 1, width), lambda h: (h, 0, 0))
     low = jax.ShapeDtypeStruct((seq, width), BF16)
-    low_across = jax.ShapeDtypeStruct((width, seq), BF16)
-    out_specs = [
-        pl.BlockSpec((1, 1, width), lambda h: (h, 0, 0)),
-        pl.BlockSpec((1, HEADS, half), lambda h: (h, 0, 0)),
-    ]
-    out_shape = [
-        jax.ShapeDtypeStruct((HEADS // 2, 1, width), F32),
-        jax.ShapeDtypeStruct((HEADS // 2, HEADS, half), F32),
-    ]
-    if first:
-        in_specs, scratch = [], []
-        out_specs += [across] * 3 + [whole] + [across] * 2
-        out_shape += [low_across] * 3 + [jax.ShapeDtypeStruct((seq, width), F32)]
-        out_shape += [jax.ShapeDtypeStruct((width, seq), F32)] * 2
+    if blocked:
+        grads = [jax.ShapeDtypeStruct((4, 4, 3 * (width // 16), width // 2), BF16)] * 2
     else:
-        in_specs = [across] * 4 + [whole] + [across] * 2
-        if blocked:
-            grads = [jax.ShapeDtypeStruct((4, 4, 3 * (width // 16), width // 2), BF16)] * 2
-        else:
-            grads = [jax.ShapeDtypeStruct((width, width), BF16)] * 3
-        out_specs += [whole] * 3 + [ANY] * len(grads)
-        out_shape += [low] * 3 + grads
-        scratch = [
+        grads = [jax.ShapeDtypeStruct((width, width), BF16)] * 3
+    return pl.pallas_call(
+        functools.partial(attend_back_kernel, blocked),
+        grid=(HEADS,),
+        in_specs=[SMEM, SMEM, SMEM, pl.BlockSpec((width, seq), lambda h: (0, 0))]
+        + [whole] * 4
+        + [pl.BlockSpec((1, half, 3 * half), lambda h: (h, 0, 0)), row, row],
+        out_specs=[whole] * 3
+        + [pl.BlockSpec((16, 128), lambda h: (0, 0))]
+        + [ANY] * len(grads),
+        out_shape=[low] * 3
+        + [jax.ShapeDtypeStruct((16, 128), F32)]
+        + grads,
+        scratch_shapes=[pltpu.VMEM((width, seq), BF16)] * 3
+        + [
             pltpu.VMEM((seq, width), F32),
             pltpu.VMEM((width, seq), F32),
             pltpu.VMEM((width, seq), F32),
+            pltpu.VMEM((16, width), F32),
             pltpu.VMEM((3, width, width), BF16),
             pltpu.SemaphoreType.DMA((6, 16)),
-        ]
-    return pl.pallas_call(
-        functools.partial(attend_back_kernel, first, blocked),
-        grid=(HEADS // 2,),
-        in_specs=[SMEM, SMEM, SMEM]
-        + in_specs
-        + [whole] * 4
-        + [pl.BlockSpec((1, half, 3 * half), lambda h: (h + base, 0, 0)), row, row],
-        out_specs=out_specs,
-        out_shape=out_shape,
-        scratch_shapes=scratch,
+        ],
         compiler_params=PARAMS,
-        name="attend_back_first" if first else "attend_back",
-        cost_estimate=cost(14),
-    )(spot, pms, pos, *(() if first else turned), q, k, v, g, p, pm, po)
+        name="attend_back",
+        cost_estimate=cost(28),
+    )(spot, pms, pos, nt, q, k, v, g, p, pm, po)
 
 
 def input_kernel(blocks, spot, *rest):
     pieces, rest = rest[:blocks], rest[blocks:]
-    dq_ref, dk_ref, dv_ref, states_ref, mid_ref, gain_ref, out_ref, first_ref = rest[:8]
-    wq, wk, wv, sems = rest[8:]
-    width = wq.shape[1] // 2
+    dq_ref, dk_ref, dv_ref, states_ref, mid_ref, gain_ref, sums_ref, mix_ref = rest[:8]
+    out_ref, small_ref, wq, wk, wv, sems = rest[8:]
+    features = wq.shape[1]
+    width = features // 2
     depth = wq.shape[0] // 16
     copies = place_copies(
-        spot, pieces, (wq, wk, wv), (0, depth, 2 * depth), (0, 0, 0), (width,) * 3, sems
+        spot, pieces, (wq, wk, wv), (0, depth, 2 * depth), (0, 0, 0), (width,) * 3, sems, True
     )
     for copy in copies:
         copy.start()
@@ -545,29 +535,38 @@
     grad = (
         dot_nt(dq_ref[...], wq[...]) + dot_nt(dk_ref[...], wk[...]) + dot_nt(dv_ref[...], wv[...])
     )
-    first_ref[...] = jnp.broadcast_to(
-        jnp.sum(grad * states * scale, axis=0, keepdims=True), first_ref.shape
+    first = jnp.sum(grad * states * scale, axis=0, keepdims=True)
+    parts = features // 128
+    lane = lax.broadcasted_iota(jnp.int32, (1, 128), 1)
+    losses = [jnp.sum(sums_ref[n : n + 1], axis=1, keepdims=True) for n in (1, 2)]
+    for n in range(parts):
+        at = slice(n * 128, (n + 1) * 128)
+        small_ref[n : n + 1] = first[:, at]
+        small_ref[parts + n : parts + n + 1] = sums_ref[:1, at]
+    small_ref[2 * parts :] = mix_ref[:HEADS]
+    small_ref[2 * parts : 2 * parts + 1] += jnp.where(
+        lane == 32, losses[0], jnp.where(lane == 33, losses[1], 0.0)
     )
     term = gain_ref[...] * grad
     inner = jnp.mean(term * states, axis=1, keepdims=True)
     out_ref[...] = mid_ref[...] + scale * term - states * (scale * scale * scale) * inner
 
 
-def input_block(spot, pieces, dq, dk, dv, states, mid_grad, gain):
+def input_block(spot, pieces, dq, dk, dv, states, mid_grad, gain, sums, mix):
     seq, width = dq.shape
     return pl.pallas_call(
         functools.partial(input_kernel, len(pieces)),
-        in_specs=[SMEM] + [ANY] * len(pieces) + [VMEM] * 6,
+        in_specs=[SMEM] + [ANY] * len(pieces) + [VMEM] * 8,
         out_specs=[VMEM] * 2,
         out_shape=[
             jax.ShapeDtypeStruct((seq, width), F32),
-            jax.ShapeDtypeStruct((8, width), F32),
+            jax.ShapeDtypeStruct((2 * width // 128 + HEADS, 128), F32),
         ],
         scratch_shapes=[pltpu.VMEM((width, width), BF16)] * 3 + [pltpu.SemaphoreType.DMA((96,))],
         compiler_params=PARAMS,
         name="input_grad",
         cost_estimate=cost(9),
-    )(spot, *pieces, dq, dk, dv, states, mid_grad, gain)
+    )(spot, *pieces, dq, dk, dv, states, mid_grad, gain, sums, mix)
 
 
 def exchange(value, mask, total):
@@ -586,12 +585,16 @@
     return over_lines(jnp.broadcast_to(packet, (4, *packet.shape)))
 
 
+def gather_near(packet, total):
+    return jnp.stack([packet, *[exchange(packet, m * Z_BIT, total) for m in (1, 2, 3)]])
+
+
 def gather_sides(line, total):
     return exchange(line, X_BIT, total), exchange(line, Y_BIT, total)
 
 
 def gather_halves(over_x, over_y, total):
-    return exchange(over_x[:2], Y_BIT, total), exchange(over_y[2:], X_BIT, total)
+    return exchange(over_x, Y_BIT, total), exchange(over_y, X_BIT, total)
 
 
 def add_low(*terms):
@@ -620,15 +623,11 @@
 
 
 def reduce_line(head, tail, side_x, side_y):
-    return over_lines(jnp.concatenate([add_low(head, side_x), add_low(tail, side_y)]).astype(BF16))
-
-
-def pack_small(first_rows, sums, pre, post):
-    pre = jnp.sum(pre.reshape(HEADS, HEADS, HEAD_DIM), axis=2).T * (HEAD_DIM**-0.5)
-    losses = jnp.sum(sums[1:3], axis=1)
-    small = [first_rows[0], sums[0], pre.reshape(-1), jnp.sum(post, axis=2).reshape(-1), losses]
-    small = jnp.concatenate(small)
-    return jnp.pad(small, (0, -small.shape[0] % 1024)).reshape(-1, 128)
+    return jnp.concatenate([add_low(head, side_x), add_low(tail, side_y)])
+
+
+def reduce_far(line, total):
+    return [exchange(line[m].astype(BF16), m * Z_BIT, total) for m in (1, 2, 3)]
 
 
 def gather_whole(block):
@@ -673,20 +672,22 @@
     blocked = (row_total, col_total) == (16, 2)
     row = lax.axis_index("row")
     spot = jnp.stack([row // 4, (row // 2) % 2, row % 2, lax.axis_index("col")]).astype(jnp.int32)
-    count = jnp.sum(validity)
     down_turned = down_weight.T
     if blocked:
         packet = jnp.concatenate([query_weight, key_weight, value_weight], axis=0)
-        qkv_line = gather_line(packet)
+        qkv_line = gather_near(packet, total)
         qkv_sides = gather_sides(qkv_line, total)
-        lanes = lax.broadcasted_iota(jnp.int32, (depth, EXTRA), 1)
-        digits = jnp.where(lanes == 0, count // 256, jnp.where(lanes == 1, count % 256, 0))
+        marks = jnp.sum(validity.reshape(-1, EXTRA), axis=0).astype(BF16)
+        marks = jnp.broadcast_to(marks, (depth, EXTRA))
         packet = jnp.concatenate(
-            [up_weight, output_weight, digits.astype(BF16), down_turned], axis=1
-        )
-        line = gather_line(after(packet, qkv_line))
-        qkv_halves = jnp.stack(gather_halves(*qkv_sides, total))
-        qkv_lines = jnp.stack([qkv_line, *qkv_sides])
+            [up_weight, output_weight, marks, down_turned], axis=1
+        )
+        line = gather_line(packet)
+        *halves, qkv_line, side_x, side_y = lax.optimization_barrier(
+            (qkv_sides[0][:2], qkv_sides[1][2:], qkv_line, *qkv_sides)
+        )
+        qkv_halves = jnp.stack(gather_halves(*halves, total))
+        qkv_lines = jnp.stack([qkv_line, side_x, side_y])
         qkv = [qkv_lines, qkv_halves]
         qkv += [exchange(part, CORE_BIT, total) for part in qkv]
         line, *qkv = lax.optimization_barrier((line, *qkv))
@@ -695,7 +696,7 @@
     else:
         qkv = [gather_whole(w) for w in (query_weight, key_weight, value_weight)]
         rest = [gather_whole(w) for w in (output_weight, up_weight, down_turned)]
-        total_valid = lax.psum(count.astype(F32), AXES)
+        total_valid = lax.psum(jnp.sum(validity).astype(F32), AXES)
     first_scale = lax.rsqrt(jnp.mean(states * states, axis=-1, keepdims=True) + EPSILON)
     normed = (states * first_scale * first_gain).astype(BF16)
     pms = premix.T * (HEAD_DIM**-0.5)
@@ -705,7 +706,10 @@
     queries, keys, values, attended, probs = attend(spot, picture_start, normed, qkv, pm, po)
     if blocked:
         *sides, attended = lax.optimization_barrier((*sides, attended))
-        rest = [jnp.stack([line, *sides]), jnp.stack(gather_halves(*sides, total))]
+        *halves, line, side_x, side_y = lax.optimization_barrier(
+            (sides[0][:2], sides[1][2:], line, *sides)
+        )
+        rest = [jnp.stack([line, side_x, side_y]), jnp.stack(gather_halves(*halves, total))]
         rest += [exchange(part, CORE_BIT, total) for part in rest]
     layer_out, mid_grad, attended_grad, sums, *grads = middle_block(
         blocked,
@@ -722,75 +726,65 @@
         units,
     )
     total_valid = sums[3, 0]
-    heads = queries, keys, values, attended_grad, probs, pm, po, pms, pos
+    nt = normed.T
     if blocked:
-        down_mine, *first, attended_grad = lax.optimization_barrier(
-            (*reduce_core(grads[2], exchange(grads[3], CORE_BIT, total)), attended_grad)
-        )
-        down_first = reduce_first(*first, total)
-        heads = queries, keys, values, attended_grad, probs, pm, po, pms, pos
-        up_other = exchange(grads[1], CORE_BIT, total)
-        part = attend_back(spot, blocked, None, *heads)
-        up_keep, up_other, *rest = lax.optimization_barrier((grads[0], up_other, *down_first, *part))
-        down_first, part = rest[:2], rest[2:]
-        up_mine, *first = reduce_core(up_keep, up_other)
-        down_sides = reduce_sides(down_mine, *down_first)
-        *rest, up_mine, down_head, down_tail = lax.optimization_barrier(
-            (*first, *down_sides, *part, up_mine, *reduce_own(down_mine, *down_first))
-        )
-        first, down_sides, part = rest[:2], rest[2:4], rest[4:]
-        up_first = reduce_first(*first, total)
-        down_sides = reduce_second(*down_sides, total)
+        ffn_mine, *first, attended_grad = lax.optimization_barrier(
+            (*reduce_core(grads[0], exchange(grads[1], CORE_BIT, total)), attended_grad)
+        )
+        ffn_first = reduce_first(*first, total)
     else:
-        up_grad, output_grad, down_grad = (scatter_whole(g) for g in (grads[0], grads[2], grads[1]))
+        up_grad, down_grad, output_grad = (scatter_whole(g) for g in grads)
         down_grad = down_grad.T
-        part = attend_back(spot, blocked, None, *heads)
-    pre, post, *turned = part
-    pre_last, post_last, dq, dk, dv, *grads = attend_back(spot, blocked, (normed.T, *turned), *heads)
-    pre = jnp.concatenate([pre, pre_last])
-    post = jnp.concatenate([post, post_last])
+    dq, dk, dv, mix, *grads = attend_back(
+        spot, blocked, nt, queries, keys, values, attended_grad, probs, pm, po, pms, pos
+    )
     if blocked:
-        dq, dk, dv, *rest = lax.optimization_barrier((dq, dk, dv, *grads, *up_first, *down_sides))
-        grads, up_first, down_sides = rest[:2], rest[2:4], rest[4:]
-        up_sides = reduce_second(*reduce_sides(up_mine, *up_first), total)
-        down_line = reduce_line(down_head, down_tail, *down_sides)
-        mine, *first, dq, dk, dv = lax.optimization_barrier(
-            (*reduce_core(grads[0], exchange(grads[1], CORE_BIT, total)), dq, dk, dv)
-        )
+        *ffn_first, dq, dk, dv, mix, keep, send = lax.optimization_barrier(
+            (*ffn_first, dq, dk, dv, mix, *grads)
+        )
+        other = exchange(send, CORE_BIT, total)
+        ffn_sides = reduce_second(*reduce_sides(ffn_mine, *ffn_first), total)
+        mine, *first, dq, dk, dv = lax.optimization_barrier((*reduce_core(keep, other), dq, dk, dv))
         first = reduce_first(*first, total)
-        input_grad, first_rows = input_block(
-            spot, qkv, dq, dk, dv, states, mid_grad, first_gain[None]
-        )
-        input_grad, first_rows, *up_sides = lax.optimization_barrier(
-            (input_grad, first_rows, *up_sides)
-        )
-        up_line = reduce_line(*reduce_own(up_mine, *up_first), *up_sides)
-        sides = reduce_sides(mine, *first)
-        small = pack_small(first_rows, sums, pre, post)
+        input_grad, small = input_block(
+            spot, qkv, dq, dk, dv, states, mid_grad, first_gain[None], sums, mix
+        )
+        *ffn_sides, small = lax.optimization_barrier((*ffn_sides, small))
+        ffn_line = reduce_line(*reduce_own(ffn_mine, *ffn_first), *ffn_sides)
         small += exchange(small, CORE_BIT, total)
-        small = after(small, *sides)
-        sides = reduce_second(*sides, total)
+        near = lax.reduce_precision(small, 8, 7)
+        small = jnp.broadcast_to(jnp.concatenate([near, small - near]), (4, depth, 128))
+        ffn_line = jnp.concatenate([ffn_line, small], axis=2)
+        blocks = [ffn_line[m].astype(BF16) for m in (1, 2, 3)]
+        ffn_far = [exchange(block, m * Z_BIT, total) for m, block in enumerate(blocks, 1)]
+        *first, _, _, _ = lax.optimization_barrier((*first, *blocks))
+        sides = reduce_second(*reduce_sides(mine, *first), total)
+        line = reduce_line(*reduce_own(mine, *first), *sides)
+        ffn_far = [after(far, line) for far in ffn_far]
+        ffn = with_layout_constraint(add_low(ffn_line[0], *ffn_far), Layout((0, 1)))
+        attn = add_low(line[0], *reduce_far(line, total))
+        half = units // col_total
+        up_grad, output_grad, down_grad, small = jnp.split(
+            ffn, [half, half + width, 2 * half + width], axis=1
+        )
+        small = small[: depth // 2] + small[depth // 2 :]
         for bit in (X_BIT, Y_BIT):
             small += exchange(small, bit, total)
-        *sides, down_line, small = lax.optimization_barrier((*sides, down_line, small))
-        for bit in (Z_BIT, 2 * Z_BIT):
-            small += exchange(small, bit, total)
-        line = reduce_line(*reduce_own(mine, *first), *sides)
-        down_grad, ffn, attn = (jnp.sum(w.astype(F32), axis=0) for w in (down_line, up_line, line))
         down_grad = down_grad.T
-        up_grad, output_grad = ffn[:, : units // col_total], ffn[:, units // col_total :]
         query_grad, key_grad, value_grad = (attn[n * depth : (n + 1) * depth] for n in range(3))
     else:
         query_grad, key_grad, value_grad = (scatter_whole(g) for g in grads)
-        input_grad, first_rows = input_block(
-            spot, qkv, dq, dk, dv, states, mid_grad, first_gain[None]
-        )
-        small = lax.psum(pack_small(first_rows, sums, pre, post), AXES)
-    small = small.reshape(-1)
-    mixes = HEADS * HEADS
-    first_grad, second_grad, premix_grad, postmix_grad, losses = jnp.split(
-        small, [features, 2 * features, 2 * features + mixes, 2 * features + 2 * mixes]
-    )
+        input_grad, small = input_block(
+            spot, qkv, dq, dk, dv, states, mid_grad, first_gain[None], sums, mix
+        )
+        small = lax.psum(small, AXES)
+    parts = features // 128
+    first_grad = small[:parts].reshape(-1)
+    second_grad = small[parts : 2 * parts].reshape(-1)
+    small = small[2 * parts :]
+    premix_grad = small[:, :HEADS] * (HEAD_DIM**-0.5)
+    postmix_grad = small[:, 16 : 16 + HEADS]
+    losses = small[0, 32:34]
     return (
         layer_out,
         losses[0] / (total_valid * features),
@@ -800,8 +794,8 @@
         query_grad,
         key_grad,
         value_grad,
-        premix_grad.reshape(HEADS, HEADS),
-        postmix_grad.reshape(HEADS, HEADS),
+        premix_grad,
+        postmix_grad,
         output_grad,
         second_grad,
         up_grad,

time: 301 us -> 279 us (0.927)
  waiting for transfers between devices: 72 us -> 94.4 us
  other arithmetic: 36.7 us -> 20.1 us
  local copies, waits for them, and re-layouts: 27.4 us -> 17.9 us
  starting transfers between devices: 52.5 us -> 43.7 us
  Pallas kernels: 102 us -> 95.6 us
    ppermute x32 -> x34, waiting for transfers between devices: 56.6 us -> 90.3 us  [exchange(): return lax.ppermute(value, AXES, [(i, i ^ mask) for i in range(total)])]
    all_to_all x5 -> x1, starting transfers between devices: 23.7 us -> 5.02 us  [over_lines(): lax.all_to_all(blocks, 'row', 0, 0, axis_index_groups=LINES, tiled=True)]
    all_to_all x5 -> x1, waiting for transfers between devices: 15.3 us -> 4.07 us  [over_lines(): lax.all_to_all(blocks, 'row', 0, 0, axis_index_groups=LINES, tiled=True)]
    ppermute x32 -> x34, starting transfers between devices: 28.8 us -> 38.7 us  [exchange(): return lax.ppermute(value, AXES, [(i, i ^ mask) for i in range(total)])]
    pallas_call x2 -> x1, Pallas kernels: 35.8 us -> 28.9 us  [attend_back(): pl.pallas_call(functools.partial(attend_back_kernel, blocked), grid=(HEAD...]
    concatenate x6 -> x3, other arithmetic: 6.85 us -> 1.35 us  [the longest x1 1.07 us: shards(): jnp.concatenate([up_weight, output_weight, marks, down_turned], axis=1)]
    reduce_sum x7 -> x1, other arithmetic: 5.62 us -> 0.7 us  [shards(): marks = jnp.sum(validity.reshape(-1, EXTRA), axis=0).astype(BF16)]
    another operation x7 -> x6, other arithmetic: 10.5 us -> 5.66 us  [the longest x1 3.23 us: shards(): jnp.stack([line, side_x, side_y])]
  transfers between devices with their start and end apart: 37 -> 35, of which waited for: 17 -> 24; matrix products, arithmetic and copies ran while one was open for 15% -> 9% of each run, Pallas kernels for 22% -> 21%
where the time goes in v4:
time: 279 us; the launch traced here: 278 us
  Pallas kernels  95.6 us (34%)
  waiting for transfers between devices  94.4 us (34%)
  starting transfers between devices  43.7 us (16%)
  other arithmetic  20.1 us (7%)
  local copies, waits for them, and re-layouts  17.9 us (6%)
  between operations  5.93 us (2%)
    ppermute x34, waiting for transfers between devices, exchange(): return lax.ppermute(value, AXES, [(i, i ^ mask) for i in range(total)])  90.3 us
    ppermute x34, starting transfers between devices, exchange(): return lax.ppermute(value, AXES, [(i, i ^ mask) for i in range(total)])  38.7 us
    pallas_call x1, Pallas kernels, middle_block(): pl.pallas_call(functools.partial(middle_kernel, len(pieces), len(grads),...  36.6 us
    pallas_call x1, Pallas kernels, attend_back(): pl.pallas_call(functools.partial(attend_back_kernel, blocked), grid=(HEAD...  28.9 us
    pallas_call x1, Pallas kernels, attend(): pl.pallas_call(functools.partial(attend_kernel, len(pieces)), grid=(HEADS...  21.1 us
    pallas_call x1, Pallas kernels, input_block(): pl.pallas_call(functools.partial(input_kernel, len(pieces)), in_specs=[SM...  9.03 us
  transfers between devices with their start and end apart: 35, of which 24 were waited for; matrix products, arithmetic and copies ran while one was open for 9% of the time, Pallas kernels for 21%

profile of v4, /device:TPU:0, one launch (start us, length us, event | category | flops | bytes accessed | tf_op | source)
XLA Modules:
  0.0 277.6 jit_solution(12593079446160516414)
XLA Ops:
  3.0 5.1 %collective-permute-start.2 = (bf16[144,384]{1,0:T(8,128)(2,1)S(1)}, bf16[144,384]{1,0:T(8,128)(2,1)S(1)}, u32[]{:S(2)}, u32[]{:S(2)}) collective-permute-start(bf16[144,384]{1,0:T(8,128)(2,1)S(1)} %constant_dynamic-update-slice_fusion), channel_id=1, source_target_pairs={{0,24},{1,25},{2,26},{3,27},{4,28},{5,29},{6,30},{7,31},{8,16},{9,... | collective-permute-start | bytes 331784 | tf_op jit(solution)/shard_map/ppermute | solution.py:573
  11.7 5.0 %all-to-all-start = ((bf16[4,48,3584]{2,1,0:T(8,128)(2,1)}), bf16[4,48,3584]{2,1,0:T(8,128)(2,1)}, u32[]{:S(2)}, u32[]{:S(2)}) async-start(bf16[4,48,3584]{2,1,0:T(8,128)(2,1)} %broadcast_in_dim.27), calls=%async_computation | async-start | bytes 2752512 | tf_op jit(solution)/shard_map/all_to_all | solution.py:581
  20.5 8.2 %collective-permute-done.4 = bf16[4,144,384]{2,1,0:T(8,128)(2,1)S(1)} collective-permute-done((bf16[4,144,384]{2,1,0:T(8,128)(2,1)S(1)}, bf16[4,144,384]{2,1,0:T(8,128)(2,1)S(1)}, u32[]{:S(2)}, u32[]{:S(2)}) %collective-permute-start.4) | collective-permute-done | bytes 442400 | tf_op jit(solution)/shard_map/ppermute | solution.py:573
  33.5 5.8 %collective-permute-done.5 = bf16[2,144,384]{2,1,0:T(8,128)(2,1)S(1)} collective-permute-done((bf16[2,144,384]{2,1,0:T(8,128)(2,1)S(1)}, bf16[2,144,384]{2,1,0:T(8,128)(2,1)S(1)}, u32[]{:S(2)}, u32[]{:S(2)}) %collective-permute-start.5) | collective-permute-done | bytes 221216 | tf_op jit(solution)/shard_map/ppermute | solution.py:573
  44.6 4.1 %all-to-all-done = bf16[4,48,3584]{2,1,0:T(8,128)(2,1)} async-done(((bf16[4,48,3584]{2,1,0:T(8,128)(2,1)}), bf16[4,48,3584]{2,1,0:T(8,128)(2,1)}, u32[]{:S(2)}, u32[]{:S(2)}) %all-to-all-start) | async-done | bytes 1376288 | tf_op jit(solution)/shard_map/all_to_all | solution.py:581
  51.7 21.1 %attend.1 = (bf16[512,768]{1,0:T(8,128)(2,1)}, bf16[512,768]{1,0:T(8,128)(2,1)}, bf16[512,768]{1,0:T(8,128)(2,1)}, bf16[512,768]{1,0:T(8,128)(2,1)}, bf16[12,256,768]{2,1,0:T(8,128)(2,1)}) custom-call(s32[4]{0:T(128)} %pad_add_fusion.spot, s32[1,2]{1,0:T(1,128)} %starts.1, bf16[512,768]{1,0:T(8,128)(2,1)} %copy.40.normed_ref, ...), custom_call_target="tpu_custom_call" | custom-call | flops 20000000000 | bytes 1000000 | tf_op jit(solution)/shard_map/attend/pallas_call | solution.py:159
  72.8 7.3 %collective-permute-done.10 = bf16[4,48,3584]{2,1,0:T(8,128)(2,1)S(1)} collective-permute-done((bf16[4,48,3584]{2,1,0:T(8,128)(2,1)}, bf16[4,48,3584]{2,1,0:T(8,128)(2,1)S(1)}, u32[]{:S(2)}, u32[]{:S(2)}) %collective-permute-start.10) | collective-permute-done | bytes 1376288 | tf_op jit(solution)/shard_map/ppermute | solution.py:573
  81.4 3.2 %pad_maximum_fusion.rest_0_ = bf16[3,4,48,3584]{3,2,1,0:T(8,128)(2,1)} fusion(bf16[1,4,48,3584]{3,2,1,0:T(8,128)(2,1)S(1)} %bitcast.78, bf16[1,4,48,3584]{3,2,1,0:T(8,128)(2,1)S(1)} %bitcast.79, bf16[1,4,48,3584]{3,2,1,0:T(8,128)(2,1)} %bitcast.16), kind=kLoop, calls=%fused_computation.1 | loop fusion | flops 4128768 | bytes 8257536 | tf_op jit(solution)/shard_map/stack | solution.py:712
  86.8 15.8 %collective-permute-done.11 = bf16[2,48,3584]{2,1,0:T(8,128)(2,1)S(1)} collective-permute-done((bf16[2,48,3584]{2,1,0:T(8,128)(2,1)S(1)}, bf16[2,48,3584]{2,1,0:T(8,128)(2,1)S(1)}, u32[]{:S(2)}, u32[]{:S(2)}) %collective-permute-start.11) | collective-permute-done | bytes 688160 | tf_op jit(solution)/shard_map/ppermute | solution.py:573
  106.2 36.6 %middle.1 = (f32[512,768]{1,0:T(8,128)}, f32[512,768]{1,0:T(8,128)}, bf16[512,768]{1,0:T(8,128)(2,1)}, f32[8,768]{1,0:T(8,128)}, bf16[4,4,48,3456]{3,2,1,0:T(8,128)(2,1)}, /*index=5*/bf16[4,4,48,3456]{3,2,1,0:T(8,128)(2,1)}) custom-call(s32[4]{0:T(128)} %pad_add_fusion.spot, f32[1,1]{1,0:T(1,128)} %constant.55.clone.1.count, ...), custom_call_target="tpu_custom_call" | custom-call | flops 35000000512 | bytes 1000000 | tf_op jit(solution)/shard_map/middle/pallas_call | solution.py:338
  144.1 7.7 %collective-permute-done.15 = bf16[4,4,48,3456]{3,2,1,0:T(8,128)(2,1)S(1)} collective-permute-done((bf16[4,4,48,3456]{3,2,1,0:T(8,128)(2,1)}, bf16[4,4,48,3456]{3,2,1,0:T(8,128)(2,1)S(1)}, u32[]{:S(2)}, u32[]{:S(2)}) %collective-permute-start.15) | collective-permute-done | bytes 5308448 | tf_op jit(solution)/shard_map/ppermute | solution.py:573
  151.8 3.7 %add_convert_fusion = bf16[4,4,48,3456]{3,2,1,0:T(8,128)(2,1)S(1)} fusion(bf16[4,4,48,3456]{3,2,1,0:T(8,128)(2,1)S(1)} %collective-permute-done.15, bf16[4,4,48,3456]{3,2,1,0:T(8,128)(2,1)} %get-tuple-element.97), kind=kLoop, calls=%fused_computation | loop fusion | flops 10616832 | bytes 15925248 | tf_op jit(solution)/shard_map/convert_element_type | solution.py:605
  160.3 28.9 %attend_back.1 = (bf16[512,768]{1,0:T(8,128)(2,1)}, bf16[512,768]{1,0:T(8,128)(2,1)}, bf16[512,768]{1,0:T(8,128)(2,1)}, f32[16,128]{1,0:T(8,128)}, bf16[4,4,144,...) custom-call(s32[4]{0:T(128)} %pad_add_fusion.spot, f32[12,12]{1,0:T(8,128)} %copy-done.6, f32[12,12]{1,0:T(8,128)} %pos.1, ...), custom_call_target="tpu_custom_call" | custom-call | flops 28000000000 | bytes 1000000 | tf_op jit(solution)/shard_map/attend_back/pallas_call | solution.py:492
  192.5 2.8 %fusion.4 = (bf16[2,48,3456]{2,1,0:T(8,128)(2,1)}, bf16[2,48,3456]{2,1,0:T(8,128)(2,1)}) fusion(bf16[2,2,48,3456]{3,2,1,0:T(8,128)(2,1)} %collective-permute-done.17, bf16[4,4,48,3456]{3,2,1,0:T(8,128)(2,1)S(1)} %add_convert_fusion, bf16[2,2,48,3456]{3,2,1,0:T(8,128)(2,1)} %collective-permute-done.16), kind=kLoop, calls=%fused_computation.18 | loop fusion | flops 2654208 | bytes 3981312 | tf_op jit(solution)/shard_map/convert_element_type | solution.py:614
  200.0 9.0 %input_grad.1 = (f32[512,768]{1,0:T(8,128)}, f32[24,128]{1,0:T(8,128)}) custom-call(s32[4]{0:T(128)} %pad_add_fusion.spot, bf16[3,4,144,384]{3,2,1,0:T(8,128)(2,1)} %pad_maximum_fusion.3.rest_0_, bf16[2,2,144,384]{3,2,1,0:T(8,128)(2,1)} %pad_maximum_fusion.6.rest_1_, bf16[3,4,144,384]{3,2,1,0:T(8,128)(2,1)} %collective-permute-done.7.rest_2_, ...), custom_call_target="tpu_custom_call" | custom-call | flops 8999999488 | bytes 1000000 | tf_op jit(solution)/shard_map/input_grad/pallas_call | solution.py:557
  209.0 3.8 %collective-permute-done.19 = bf16[2,48,3456]{2,1,0:T(8,128)(2,1)} collective-permute-done((bf16[2,48,3456]{2,1,0:T(8,128)(2,1)}, bf16[2,48,3456]{2,1,0:T(8,128)(2,1)}, u32[]{:S(2)}, u32[]{:S(2)}) %collective-permute-start.19) | collective-permute-done | bytes 663584 | tf_op jit(solution)/shard_map/ppermute | solution.py:573
  218.6 7.4 %collective-permute-done.23 = bf16[2,2,144,384]{3,2,1,0:T(8,128)(2,1)S(1)} collective-permute-done((bf16[2,2,144,384]{3,2,1,0:T(8,128)(2,1)}, bf16[2,2,144,384]{3,2,1,0:T(8,128)(2,1)S(1)}, u32[]{:S(2)}, u32[]{:S(2)}) %collective-permute-start.23) | collective-permute-done | bytes 442400 | tf_op jit(solution)/shard_map/ppermute | solution.py:573
  229.5 3.1 %collective-permute-start.22 = (bf16[48,3584]{1,0:T(8,128)(2,1)S(1)}, bf16[48,3584]{1,0:T(8,128)(2,1)S(1)}, u32[]{:S(2)}, u32[]{:S(2)}) collective-permute-start(bf16[48,3584]{1,0:T(8,128)(2,1)S(1)} %get-tuple-element.152), channel_id=1, source_target_pairs={{0,8},{1,9},{2,10},{3,11},{4,12},{5,13},{6,14},{7,15},{8,0},{9,1},... | collective-permute-start | bytes 1032200 | tf_op jit(solution)/shard_map/ppermute | solution.py:573
  234.1 4.5 %collective-permute-done.26 = bf16[2,144,384]{2,1,0:T(8,128)(2,1)S(1)} collective-permute-done((bf16[2,144,384]{2,1,0:T(8,128)(2,1)S(1)}, bf16[2,144,384]{2,1,0:T(8,128)(2,1)S(1)}, u32[]{:S(2)}, u32[]{:S(2)}) %collective-permute-start.26) | collective-permute-done | bytes 221216 | tf_op jit(solution)/shard_map/ppermute | solution.py:573
  238.7 7.3 %collective-permute-done.28 = bf16[48,3584]{1,0:T(8,128)(2,1)S(1)} collective-permute-done((bf16[48,3584]{1,0:T(8,128)(2,1)S(1)}, bf16[48,3584]{1,0:T(8,128)(2,1)S(1)}, u32[]{:S(2)}, u32[]{:S(2)}) %collective-permute-start.28) | collective-permute-done | bytes 344096 | tf_op jit(solution)/shard_map/ppermute | solution.py:573
  245.9 5.6 %collective-permute-done.27 = bf16[48,3584]{1,0:T(8,128)(2,1)S(1)} collective-permute-done((bf16[48,3584]{1,0:T(8,128)(2,1)S(1)}, bf16[48,3584]{1,0:T(8,128)(2,1)S(1)}, u32[]{:S(2)}, u32[]{:S(2)}) %collective-permute-start.27) | collective-permute-done | bytes 344096 | tf_op jit(solution)/shard_map/ppermute | solution.py:573
  255.8 3.1 %collective-permute-done.29 = f32[24,128]{1,0:T(8,128)S(1)} collective-permute-done((f32[24,128]{1,0:T(8,128)S(1)}, f32[24,128]{1,0:T(8,128)S(1)}, u32[]{:S(2)}, u32[]{:S(2)}) %collective-permute-start.29) | collective-permute-done | bytes 12320 | tf_op jit(solution)/shard_map/ppermute | solution.py:573
  260.1 5.3 %collective-permute-start.31 = (bf16[144,384]{1,0:T(8,128)(2,1)S(1)}, bf16[144,384]{1,0:T(8,128)(2,1)S(1)}, u32[]{:S(2)}, u32[]{:S(2)}) collective-permute-start(bf16[144,384]{1,0:T(8,128)(2,1)S(1)} %fusion.10), channel_id=1, source_target_pairs={{0,8},{1,9},{2,10},{3,11},{4,12},{5,13},{6,14},{7,15},{8,0},{9,1},... | collective-permute-start | bytes 331784 | tf_op jit(solution)/shard_map/ppermute | solution.py:573
  271.9 2.7 collective-permute-done.32
  (136 shorter events, 64.5 us)
Async XLA Ops:
  3.0 13.7 %collective-permute-start.2 = (bf16[144,384]{1,0:T(8,128)(2,1)S(1)}, bf16[144,384]{1,0:T(8,128)(2,1)S(1)}, u32[]{:S(2)}, u32[]{:S(2)}) collective-permute-start(bf16[144,384]{1,0:T(8,128)(2,1)S(1)} %constant_dynamic-update-slice_fusion), channel_id=1, source_target_pairs={{0,24},{1,25},{2,26},{3,27},{4,28},{5,29},{6,30},{7,31},{8,16},{9,... | collective-permute-start | bytes 331784 | tf_op jit(solution)/shard_map/ppermute | solution.py:573
  8.1 9.3 %collective-permute-start.1 = (bf16[144,384]{1,0:T(8,128)(2,1)S(1)}, bf16[144,384]{1,0:T(8,128)(2,1)S(1)}, u32[]{:S(2)}, u32[]{:S(2)}) collective-permute-start(bf16[144,384]{1,0:T(8,128)(2,1)S(1)} %constant_dynamic-update-slice_fusion), channel_id=1, source_target_pairs={{0,16},{1,17},{2,18},{3,19},{4,20},{5,21},{6,22},{7,23},{8,24},{9,... | collective-permute-start | bytes 331784 | tf_op jit(solution)/shard_map/ppermute | solution.py:573
  8.1 9.3 %collective-permute-start = (bf16[144,384]{1,0:T(8,128)(2,1)S(1)}, bf16[144,384]{1,0:T(8,128)(2,1)S(1)}, u32[]{:S(2)}, u32[]{:S(2)}) collective-permute-start(bf16[144,384]{1,0:T(8,128)(2,1)S(1)} %constant_dynamic-update-slice_fusion), channel_id=1, source_target_pairs={{0,8},{1,9},{2,10},{3,11},{4,12},{5,13},{6,14},{7,15},{8,0},{9,1},... | collective-permute-start | bytes 331784 | tf_op jit(solution)/shard_map/ppermute | solution.py:573
  11.7 37.0 %all-to-all-start = ((bf16[4,48,3584]{2,1,0:T(8,128)(2,1)}), bf16[4,48,3584]{2,1,0:T(8,128)(2,1)}, u32[]{:S(2)}, u32[]{:S(2)}) async-start(bf16[4,48,3584]{2,1,0:T(8,128)(2,1)} %broadcast_in_dim.27), calls=%async_computation | async-start | bytes 2752512 | tf_op jit(solution)/shard_map/all_to_all | solution.py:581
  17.4 11.3 %collective-permute-start.4 = (bf16[4,144,384]{2,1,0:T(8,128)(2,1)S(1)}, bf16[4,144,384]{2,1,0:T(8,128)(2,1)S(1)}, u32[]{:S(2)}, u32[]{:S(2)}) collective-permute-start(bf16[4,144,384]{2,1,0:T(8,128)(2,1)S(1)} %pad_maximum_fusion.5), channel_id=1, source_target_pairs={{0,4},{1,5},{2,6},{3,7},{4,0},{5,1},{6,2},{7,3},{8,12},{9,13},{10,... | collective-permute-start | bytes 1327112 | tf_op jit(solution)/shard_map/ppermute | solution.py:573
  19.0 11.0 %collective-permute-start.3 = (bf16[4,144,384]{2,1,0:T(8,128)(2,1)S(1)}, bf16[4,144,384]{2,1,0:T(8,128)(2,1)S(1)}, u32[]{:S(2)}, u32[]{:S(2)}) collective-permute-start(bf16[4,144,384]{2,1,0:T(8,128)(2,1)S(1)} %pad_maximum_fusion.5), channel_id=1, source_target_pairs={{0,1},{1,0},{2,3},{3,2},{4,5},{5,4},{6,7},{7,6},{8,9},{9,8},{10,11... | collective-permute-start | bytes 1327112 | tf_op jit(solution)/shard_map/ppermute | solution.py:573
  31.3 13.3 %collective-permute-start.7 = (bf16[3,4,144,384]{3,2,1,0:T(8,128)(2,1)}, bf16[3,4,144,384]{3,2,1,0:T(8,128)(2,1)}, u32[]{:S(2)}, u32[]{:S(2)}) collective-permute-start(bf16[3,4,144,384]{3,2,1,0:T(8,128)(2,1)} %pad_maximum_fusion.3.rest_0_), channel_id=1, source_target_pairs={{0,2},{1,3},{2,0},{3,1},{4,6},{5,7},{6,4},{7,5},{8,10},{9,11},{10,... | collective-permute-start | bytes 3981320 | tf_op jit(solution)/shard_map/ppermute | solution.py:573
  48.7 31.4 %collective-permute-start.10 = (bf16[4,48,3584]{2,1,0:T(8,128)(2,1)}, bf16[4,48,3584]{2,1,0:T(8,128)(2,1)S(1)}, u32[]{:S(2)}, u32[]{:S(2)}) collective-permute-start(bf16[4,48,3584]{2,1,0:T(8,128)(2,1)} %all-to-all-done), channel_id=1, source_target_pairs={{0,4},{1,5},{2,6},{3,7},{4,0},{5,1},{6,2},{7,3},{8,12},{9,13},{10,... | collective-permute-start | bytes 4128776 | tf_op jit(solution)/shard_map/ppermute | solution.py:573
  50.2 31.1 %collective-permute-start.9 = (bf16[4,48,3584]{2,1,0:T(8,128)(2,1)}, bf16[4,48,3584]{2,1,0:T(8,128)(2,1)S(1)}, u32[]{:S(2)}, u32[]{:S(2)}) collective-permute-start(bf16[4,48,3584]{2,1,0:T(8,128)(2,1)} %all-to-all-done), channel_id=1, source_target_pairs={{0,1},{1,0},{2,3},{3,2},{4,5},{5,4},{6,7},{7,6},{8,9},{9,8},{10,11... | collective-permute-start | bytes 4128776 | tf_op jit(solution)/shard_map/ppermute | solution.py:573
  84.7 21.6 %collective-permute-start.13 = (bf16[3,4,48,3584]{3,2,1,0:T(8,128)(2,1)}, bf16[3,4,48,3584]{3,2,1,0:T(8,128)(2,1)}, u32[]{:S(2)}, u32[]{:S(2)}) collective-permute-start(bf16[3,4,48,3584]{3,2,1,0:T(8,128)(2,1)} %pad_maximum_fusion.rest_0_), channel_id=1, source_target_pairs={{0,2},{1,3},{2,0},{3,1},{4,6},{5,7},{6,4},{7,5},{8,10},{9,11},{10,... | collective-permute-start | bytes 12386312 | tf_op jit(solution)/shard_map/ppermute | solution.py:573
  84.7 17.8 %collective-permute-start.11 = (bf16[2,48,3584]{2,1,0:T(8,128)(2,1)S(1)}, bf16[2,48,3584]{2,1,0:T(8,128)(2,1)S(1)}, u32[]{:S(2)}, u32[]{:S(2)}) collective-permute-start(bf16[2,48,3584]{2,1,0:T(8,128)(2,1)S(1)} %slice.151), channel_id=1, source_target_pairs={{0,4},{1,5},{2,6},{3,7},{4,0},{5,1},{6,2},{7,3},{8,12},{9,13},{10,... | collective-permute-start | bytes 2064392 | tf_op jit(solution)/shard_map/ppermute | solution.py:573
  85.3 17.5 %collective-permute-start.12 = (bf16[2,48,3584]{2,1,0:T(8,128)(2,1)S(1)}, bf16[2,48,3584]{2,1,0:T(8,128)(2,1)S(1)}, u32[]{:S(2)}, u32[]{:S(2)}) collective-permute-start(bf16[2,48,3584]{2,1,0:T(8,128)(2,1)S(1)} %slice.152), channel_id=1, source_target_pairs={{0,1},{1,0},{2,3},{3,2},{4,5},{5,4},{6,7},{7,6},{8,9},{9,8},{10,11... | collective-permute-start | bytes 2064392 | tf_op jit(solution)/shard_map/ppermute | solution.py:573
  157.3 31.9 %collective-permute-start.16 = (bf16[2,2,48,3456]{3,2,1,0:T(8,128)(2,1)}, bf16[2,2,48,3456]{3,2,1,0:T(8,128)(2,1)}, u32[]{:S(2)}, u32[]{:S(2)}) collective-permute-start(bf16[2,2,48,3456]{3,2,1,0:T(8,128)(2,1)} %get-tuple-element.101), channel_id=1, source_target_pairs={{0,4},{1,5},{2,6},{3,7},{4,0},{5,1},{6,2},{7,3},{8,12},{9,13},{10,... | collective-permute-start | bytes 3981320 | tf_op jit(solution)/shard_map/ppermute | solution.py:573
  158.8 31.2 %collective-permute-start.17 = (bf16[2,2,48,3456]{3,2,1,0:T(8,128)(2,1)}, bf16[2,2,48,3456]{3,2,1,0:T(8,128)(2,1)}, u32[]{:S(2)}, u32[]{:S(2)}) collective-permute-start(bf16[2,2,48,3456]{3,2,1,0:T(8,128)(2,1)} %get-tuple-element.102), channel_id=1, source_target_pairs={{0,1},{1,0},{2,3},{3,2},{4,5},{5,4},{6,7},{7,6},{8,9},{9,8},{10,11... | collective-permute-start | bytes 3981320 | tf_op jit(solution)/shard_map/ppermute | solution.py:573
  195.3 17.6 %collective-permute-start.19 = (bf16[2,48,3456]{2,1,0:T(8,128)(2,1)}, bf16[2,48,3456]{2,1,0:T(8,128)(2,1)}, u32[]{:S(2)}, u32[]{:S(2)}) collective-permute-start(bf16[2,48,3456]{2,1,0:T(8,128)(2,1)} %get-tuple-element.142), channel_id=1, source_target_pairs={{0,4},{1,5},{2,6},{3,7},{4,0},{5,1},{6,2},{7,3},{8,12},{9,13},{10,... | collective-permute-start | bytes 1990664 | tf_op jit(solution)/shard_map/ppermute | solution.py:573
  195.8 17.4 %collective-permute-start.18 = (bf16[2,48,3456]{2,1,0:T(8,128)(2,1)}, bf16[2,48,3456]{2,1,0:T(8,128)(2,1)}, u32[]{:S(2)}, u32[]{:S(2)}) collective-permute-start(bf16[2,48,3456]{2,1,0:T(8,128)(2,1)} %get-tuple-element.143), channel_id=1, source_target_pairs={{0,1},{1,0},{2,3},{3,2},{4,5},{5,4},{6,7},{7,6},{8,9},{9,8},{10,11... | collective-permute-start | bytes 1990664 | tf_op jit(solution)/shard_map/ppermute | solution.py:573
  213.1 12.8 %collective-permute-start.23 = (bf16[2,2,144,384]{3,2,1,0:T(8,128)(2,1)}, bf16[2,2,144,384]{3,2,1,0:T(8,128)(2,1)S(1)}, u32[]{:S(2)}, u32[]{:S(2)}) collective-permute-start(bf16[2,2,144,384]{3,2,1,0:T(8,128)(2,1)} %get-tuple-element.132), channel_id=1, source_target_pairs={{0,4},{1,5},{2,6},{3,7},{4,0},{5,1},{6,2},{7,3},{8,12},{9,13},{10,... | collective-permute-start | bytes 1327112 | tf_op jit(solution)/shard_map/ppermute | solution.py:573
  214.6 12.5 %collective-permute-start.24 = (bf16[2,2,144,384]{3,2,1,0:T(8,128)(2,1)}, bf16[2,2,144,384]{3,2,1,0:T(8,128)(2,1)S(1)}, u32[]{:S(2)}, u32[]{:S(2)}) collective-permute-start(bf16[2,2,144,384]{3,2,1,0:T(8,128)(2,1)} %get-tuple-element.133), channel_id=1, source_target_pairs={{0,1},{1,0},{2,3},{3,2},{4,5},{5,4},{6,7},{7,6},{8,9},{9,8},{10,11... | collective-permute-start | bytes 1327112 | tf_op jit(solution)/shard_map/ppermute | solution.py:573
  229.1 22.4 %collective-permute-start.27 = (bf16[48,3584]{1,0:T(8,128)(2,1)S(1)}, bf16[48,3584]{1,0:T(8,128)(2,1)S(1)}, u32[]{:S(2)}, u32[]{:S(2)}) collective-permute-start(bf16[48,3584]{1,0:T(8,128)(2,1)S(1)} %get-tuple-element.150), channel_id=1, source_target_pairs={{0,16},{1,17},{2,18},{3,19},{4,20},{5,21},{6,22},{7,23},{8,24},{9,... | collective-permute-start | bytes 1032200 | tf_op jit(solution)/shard_map/ppermute | solution.py:573
  229.2 16.8 %collective-permute-start.28 = (bf16[48,3584]{1,0:T(8,128)(2,1)S(1)}, bf16[48,3584]{1,0:T(8,128)(2,1)S(1)}, u32[]{:S(2)}, u32[]{:S(2)}) collective-permute-start(bf16[48,3584]{1,0:T(8,128)(2,1)S(1)} %get-tuple-element.151), channel_id=1, source_target_pairs={{0,24},{1,25},{2,26},{3,27},{4,28},{5,29},{6,30},{7,31},{8,16},{9,... | collective-permute-start | bytes 1032200 | tf_op jit(solution)/shard_map/ppermute | solution.py:573
  229.5 24.6 %collective-permute-start.22 = (bf16[48,3584]{1,0:T(8,128)(2,1)S(1)}, bf16[48,3584]{1,0:T(8,128)(2,1)S(1)}, u32[]{:S(2)}, u32[]{:S(2)}) collective-permute-start(bf16[48,3584]{1,0:T(8,128)(2,1)S(1)} %get-tuple-element.152), channel_id=1, source_target_pairs={{0,8},{1,9},{2,10},{3,11},{4,12},{5,13},{6,14},{7,15},{8,0},{9,1},... | collective-permute-start | bytes 1032200 | tf_op jit(solution)/shard_map/ppermute | solution.py:573
  258.9 9.1 %collective-permute-start.30 = (f32[24,128]{1,0:T(8,128)S(1)}, f32[24,128]{1,0:T(8,128)S(1)}, u32[]{:S(2)}, u32[]{:S(2)}) collective-permute-start(f32[24,128]{1,0:T(8,128)S(1)} %fusion.17), channel_id=1, source_target_pairs={{0,4},{1,5},{2,6},{3,7},{4,0},{5,1},{6,2},{7,3},{8,12},{9,13},{10,... | collective-permute-start | bytes 36872 | tf_op jit(solution)/shard_map/ppermute | solution.py:573
  260.1 11.8 %collective-permute-start.31 = (bf16[144,384]{1,0:T(8,128)(2,1)S(1)}, bf16[144,384]{1,0:T(8,128)(2,1)S(1)}, u32[]{:S(2)}, u32[]{:S(2)}) collective-permute-start(bf16[144,384]{1,0:T(8,128)(2,1)S(1)} %fusion.10), channel_id=1, source_target_pairs={{0,8},{1,9},{2,10},{3,11},{4,12},{5,13},{6,14},{7,15},{8,0},{9,1},... | collective-permute-start | bytes 331784 | tf_op jit(solution)/shard_map/ppermute | solution.py:573
  265.4 9.3 %collective-permute-start.32 = (bf16[144,384]{1,0:T(8,128)(2,1)S(1)}, bf16[144,384]{1,0:T(8,128)(2,1)S(1)}, u32[]{:S(2)}, u32[]{:S(2)}) collective-permute-start(bf16[144,384]{1,0:T(8,128)(2,1)S(1)} %get-tuple-element.158), channel_id=1, source_target_pairs={{0,16},{1,17},{2,18},{3,19},{4,20},{5,21},{6,22},{7,23},{8,24},{9,... | collective-permute-start | bytes 331784 | tf_op jit(solution)/shard_map/ppermute | solution.py:573
  (23 other events, 142.0 us)

commit v5 on v4

--- a/solution.py
+++ b/solution.py
@@ -18,7 +18,7 @@
 X_BIT, CORE_BIT, Y_BIT, Z_BIT = 1, 2, 4, 8
 LINES = [[at + Z_BIT // 2 * z for z in range(4)] for at in range(4)]
 EXTRA = 128
-SIDES = ((0, 0), (0, 1), (1, 0))
+PIECES = ((0, 0, 0), (0, 1, 0), (1, 0, 0), (1, 1, 0), (1, 1, 2))
 PARAMS = pltpu.CompilerParams(vmem_limit_bytes=60000 * 1024)
 SMEM = pl.BlockSpec(memory_space=pltpu.SMEM)
 ANY = pl.BlockSpec(memory_space=pl.ANY)
@@ -38,13 +38,10 @@
 
 
 def placed(pieces):
-    for core in range(2):
-        lines, halves = pieces[2 * core : 2 * core + 2]
-        for n, (y, x) in enumerate(SIDES):
-            for z in range(4):
-                yield lines, (n, z), core, y, x, z
-        for z in range(4):
-            yield halves, (z // 2, z % 2), core, 1, 1, z
+    for n, piece in enumerate(pieces):
+        y, x, first = PIECES[n % len(PIECES)]
+        for z in range(piece.shape[0]):
+            yield piece, (z,), n // len(PIECES), y, x, first + z
 
 
 def place_copies(spot, pieces, wholes, rows_at, cols_at, widths, sems, near=False):
@@ -581,6 +578,10 @@
     return lax.all_to_all(blocks, "row", 0, 0, axis_index_groups=LINES, tiled=True)
 
 
+def late(value, rank):
+    return 0.0 * value[(0,) * (value.ndim - rank)][(slice(1),) * rank].astype(F32)
+
+
 def gather_line(packet):
     return over_lines(jnp.broadcast_to(packet, (4, *packet.shape)))
 
@@ -686,9 +687,7 @@
         *halves, qkv_line, side_x, side_y = lax.optimization_barrier(
             (qkv_sides[0][:2], qkv_sides[1][2:], qkv_line, *qkv_sides)
         )
-        qkv_halves = jnp.stack(gather_halves(*halves, total))
-        qkv_lines = jnp.stack([qkv_line, side_x, side_y])
-        qkv = [qkv_lines, qkv_halves]
+        qkv = [qkv_line, side_x, side_y, *gather_halves(*halves, total)]
         qkv += [exchange(part, CORE_BIT, total) for part in qkv]
         line, *qkv = lax.optimization_barrier((line, *qkv))
         sides = gather_sides(line, total)
@@ -709,7 +708,7 @@
         *halves, line, side_x, side_y = lax.optimization_barrier(
             (sides[0][:2], sides[1][2:], line, *sides)
         )
-        rest = [jnp.stack([line, side_x, side_y]), jnp.stack(gather_halves(*halves, total))]
+        rest = [line, side_x, side_y, *gather_halves(*halves, total)]
         rest += [exchange(part, CORE_BIT, total) for part in rest]
     layer_out, mid_grad, attended_grad, sums, *grads = middle_block(
         blocked,
@@ -758,16 +757,18 @@
         blocks = [ffn_line[m].astype(BF16) for m in (1, 2, 3)]
         ffn_far = [exchange(block, m * Z_BIT, total) for m, block in enumerate(blocks, 1)]
         *first, _, _, _ = lax.optimization_barrier((*first, *blocks))
-        sides = reduce_second(*reduce_sides(mine, *first), total)
-        line = reduce_line(*reduce_own(mine, *first), *sides)
-        ffn_far = [after(far, line) for far in ffn_far]
-        ffn = with_layout_constraint(add_low(ffn_line[0], *ffn_far), Layout((0, 1)))
+        sides = reduce_sides(mine, *first)
+        sides = reduce_second(*sides, total)
+        ffn = add_low(ffn_line[0], *ffn_far) + late(sides[0], 2)
+        ffn = with_layout_constraint(ffn, Layout((0, 1)))
+        head, tail, ffn = lax.optimization_barrier((*reduce_own(mine, *first), ffn))
+        line = reduce_line(head, tail, *sides)
         attn = add_low(line[0], *reduce_far(line, total))
         half = units // col_total
         up_grad, output_grad, down_grad, small = jnp.split(
             ffn, [half, half + width, 2 * half + width], axis=1
         )
-        small = small[: depth // 2] + small[depth // 2 :]
+        small = small[: depth // 2] + small[depth // 2 :] + late(line, 2)
         for bit in (X_BIT, Y_BIT):
             small += exchange(small, bit, total)
         down_grad = down_grad.T

time: 279 us -> 297 us (1.065)
  waiting for transfers between devices: 94.4 us -> 113 us
  other arithmetic: 20.1 us -> 15.8 us
    ppermute x34 -> x40, waiting for transfers between devices: 90.3 us -> 113 us  [exchange(): return lax.ppermute(value, AXES, [(i, i ^ mask) for i in range(total)])]
    another operation x5 -> x2, other arithmetic: 5.59 us -> 0.21 us  [the longest x1 3.23 us: shards(): jnp.stack([line, side_x, side_y])]
    all_to_all x1, waiting for transfers between devices: 4.07 us -> 0.01 us  [over_lines(): lax.all_to_all(blocks, 'row', 0, 0, axis_index_groups=LINES, tiled=True)]
    ppermute x34 -> x40, starting transfers between devices: 38.7 us -> 37.3 us  [exchange(): return lax.ppermute(value, AXES, [(i, i ^ mask) for i in range(total)])]
  transfers between devices with their start and end apart: 35 -> 41, of which waited for: 24 -> 24; matrix products, arithmetic and copies ran while one was open for 9% -> 8% of each run, Pallas kernels for 21% -> 20%
where the time goes in v5:
time: 297 us; the launch traced here: 296 us
  waiting for transfers between devices  113 us (38%)
  Pallas kernels  95.7 us (32%)
  starting transfers between devices  43.8 us (15%)
  local copies, waits for them, and re-layouts  20.4 us (7%)
  other arithmetic  15.8 us (5%)
  between operations  7.33 us (2%)
    ppermute x40, waiting for transfers between devices, exchange(): return lax.ppermute(value, AXES, [(i, i ^ mask) for i in range(total)])  113 us
    ppermute x40, starting transfers between devices, exchange(): return lax.ppermute(value, AXES, [(i, i ^ mask) for i in range(total)])  37.3 us
    pallas_call x1, Pallas kernels, middle_block(): pl.pallas_call(functools.partial(middle_kernel, len(pieces), len(grads),...  36.5 us
    pallas_call x1, Pallas kernels, attend_back(): pl.pallas_call(functools.partial(attend_back_kernel, blocked), grid=(HEAD...  28.9 us
    pallas_call x1, Pallas kernels, attend(): pl.pallas_call(functools.partial(attend_kernel, len(pieces)), grid=(HEADS...  21.2 us
    pallas_call x1, Pallas kernels, input_block(): pl.pallas_call(functools.partial(input_kernel, len(pieces)), in_specs=[SM...  9.03 us
    all_to_all x1, starting transfers between devices, over_lines(): lax.all_to_all(blocks, 'row', 0, 0, axis_index_groups=LINES, tiled=True)  6.49 us
  transfers between devices with their start and end apart: 41, of which 24 were waited for; matrix products, arithmetic and copies ran while one was open for 8% of the time, Pallas kernels for 20%

profile of v5, /device:TPU:0, one launch (start us, length us, event | category | flops | bytes accessed | tf_op | source)
XLA Modules:
  0.0 296.4 jit_solution(7744899873424710577)
XLA Ops:
  3.6 6.5 %all-to-all-start = ((bf16[4,48,3584]{2,1,0:T(8,128)(2,1)}), bf16[4,48,3584]{2,1,0:T(8,128)(2,1)}, u32[]{:S(2)}, u32[]{:S(2)}) async-start(bf16[4,48,3584]{2,1,0:T(8,128)(2,1)} %broadcast_in_dim.27), calls=%async_computation | async-start | bytes 2752512 | tf_op jit(solution)/shard_map/all_to_all | solution.py:578
  10.2 3.9 %collective-permute-start.2 = (bf16[144,384]{1,0:T(8,128)(2,1)S(1)}, bf16[144,384]{1,0:T(8,128)(2,1)S(1)}, u32[]{:S(2)}, u32[]{:S(2)}) collective-permute-start(bf16[144,384]{1,0:T(8,128)(2,1)S(1)} %constant_dynamic-update-slice_fusion), channel_id=1, source_target_pairs={{0,24},{1,25},{2,26},{3,27},{4,28},{5,29},{6,30},{7,31},{8,16},{9,... | collective-permute-start | bytes 331784 | tf_op jit(solution)/shard_map/ppermute | solution.py:570
  14.7 25.5 %collective-permute-done.2 = bf16[144,384]{1,0:T(8,128)(2,1)S(1)} collective-permute-done((bf16[144,384]{1,0:T(8,128)(2,1)S(1)}, bf16[144,384]{1,0:T(8,128)(2,1)S(1)}, u32[]{:S(2)}, u32[]{:S(2)}) %collective-permute-start.2) | collective-permute-done | bytes 110624 | tf_op jit(solution)/shard_map/ppermute | solution.py:570
  40.2 12.1 %collective-permute-done.1 = bf16[144,384]{1,0:T(8,128)(2,1)S(1)} collective-permute-done((bf16[144,384]{1,0:T(8,128)(2,1)S(1)}, bf16[144,384]{1,0:T(8,128)(2,1)S(1)}, u32[]{:S(2)}, u32[]{:S(2)}) %collective-permute-start.1) | collective-permute-done | bytes 110624 | tf_op jit(solution)/shard_map/ppermute | solution.py:570
  56.9 7.8 %collective-permute-done.4.rest_2_ = bf16[4,144,384]{2,1,0:T(8,128)(2,1)} collective-permute-done((bf16[4,144,384]{2,1,0:T(8,128)(2,1)}, bf16[4,144,384]{2,1,0:T(8,128)(2,1)}, u32[]{:S(2)}, u32[]{:S(2)}) %collective-permute-start.4) | collective-permute-done | bytes 442400 | tf_op jit(solution)/shard_map/ppermute | solution.py:570
  70.5 2.6 collective-permute-done.5.rest_3_
  80.9 21.2 %attend.1 = (bf16[512,768]{1,0:T(8,128)(2,1)}, bf16[512,768]{1,0:T(8,128)(2,1)}, bf16[512,768]{1,0:T(8,128)(2,1)}, bf16[512,768]{1,0:T(8,128)(2,1)}, bf16[12,256,768]{2,1,0:T(8,128)(2,1)}) custom-call(s32[4]{0:T(128)} %pad_add_fusion.spot, s32[1,2]{1,0:T(1,128)} %starts.1, bf16[512,768]{1,0:T(8,128)(2,1)} %copy.40.normed_ref, ...), custom_call_target="tpu_custom_call" | custom-call | flops 20000000000 | bytes 1000000 | tf_op jit(solution)/shard_map/attend/pallas_call | solution.py:156
  102.1 9.3 %collective-permute-done.13.rest_2_ = bf16[4,48,3584]{2,1,0:T(8,128)(2,1)S(1)} collective-permute-done((bf16[4,48,3584]{2,1,0:T(8,128)(2,1)}, bf16[4,48,3584]{2,1,0:T(8,128)(2,1)S(1)}, u32[]{:S(2)}, u32[]{:S(2)}) %collective-permute-start.13) | collective-permute-done | bytes 1376288 | tf_op jit(solution)/shard_map/ppermute | solution.py:570
  116.5 13.8 %collective-permute-done.14.rest_3_ = bf16[2,48,3584]{2,1,0:T(8,128)(2,1)} collective-permute-done((bf16[2,48,3584]{2,1,0:T(8,128)(2,1)S(1)}, bf16[2,48,3584]{2,1,0:T(8,128)(2,1)}, u32[]{:S(2)}, u32[]{:S(2)}) %collective-permute-start.14) | collective-permute-done | bytes 688160 | tf_op jit(solution)/shard_map/ppermute | solution.py:570
  133.8 36.5 %middle.1 = (f32[512,768]{1,0:T(8,128)}, f32[512,768]{1,0:T(8,128)}, bf16[512,768]{1,0:T(8,128)(2,1)}, f32[8,768]{1,0:T(8,128)}, bf16[4,4,48,3456]{3,2,1,0:T(8,128)(2,1)}, /*index=5*/bf16[4,4,48,3456]{3,2,1,0:T(8,128)(2,1)}) custom-call(s32[4]{0:T(128)} %pad_add_fusion.spot, f32[1,1]{1,0:T(1,128)} %constant.55.clone.1.count, ...), custom_call_target="tpu_custom_call" | custom-call | flops 35000000512 | bytes 1000000 | tf_op jit(solution)/shard_map/middle/pallas_call | solution.py:335
  171.8 7.7 %collective-permute-done.21 = bf16[4,4,48,3456]{3,2,1,0:T(8,128)(2,1)S(1)} collective-permute-done((bf16[4,4,48,3456]{3,2,1,0:T(8,128)(2,1)}, bf16[4,4,48,3456]{3,2,1,0:T(8,128)(2,1)S(1)}, u32[]{:S(2)}, u32[]{:S(2)}) %collective-permute-start.21) | collective-permute-done | bytes 5308448 | tf_op jit(solution)/shard_map/ppermute | solution.py:570
  179.4 3.8 %add_convert_fusion = bf16[4,4,48,3456]{3,2,1,0:T(8,128)(2,1)S(1)} fusion(bf16[4,4,48,3456]{3,2,1,0:T(8,128)(2,1)S(1)} %collective-permute-done.21, bf16[4,4,48,3456]{3,2,1,0:T(8,128)(2,1)} %get-tuple-element.109), kind=kLoop, calls=%fused_computation | loop fusion | flops 10616832 | bytes 15925248 | tf_op jit(solution)/shard_map/convert_element_type | solution.py:606
  183.3 1.7 fusion.10
  187.5 28.9 %attend_back.1 = (bf16[512,768]{1,0:T(8,128)(2,1)}, bf16[512,768]{1,0:T(8,128)(2,1)}, bf16[512,768]{1,0:T(8,128)(2,1)}, f32[16,128]{1,0:T(8,128)}, bf16[4,4,144,...) custom-call(s32[4]{0:T(128)} %pad_add_fusion.spot, f32[12,12]{1,0:T(8,128)} %copy-done.9, f32[12,12]{1,0:T(8,128)} %pos.1, ...), custom_call_target="tpu_custom_call" | custom-call | flops 28000000000 | bytes 1000000 | tf_op jit(solution)/shard_map/attend_back/pallas_call | solution.py:489
  219.6 2.9 fusion.5
  227.9 9.0 %input_grad.1 = (f32[512,768]{1,0:T(8,128)}, f32[24,128]{1,0:T(8,128)}) custom-call(s32[4]{0:T(128)} %pad_add_fusion.spot, bf16[4,144,384]{2,1,0:T(8,128)(2,1)} %pad_maximum_fusion.1.rest_0_, bf16[4,144,384]{2,1,0:T(8,128)(2,1)} %collective-permute-done.3.rest_1_, bf16[4,144,384]{2,1,0:T(8,128)(2,1)} %collective-permute-done.4.rest_2_, ...), custom_call_target="tpu_custom_call" | custom-call | flops 8999999488 | bytes 1000000 | tf_op jit(solution)/shard_map/input_grad/pallas_call | solution.py:554
  236.9 3.2 %collective-permute-done.28 = bf16[2,48,3456]{2,1,0:T(8,128)(2,1)} collective-permute-done((bf16[2,48,3456]{2,1,0:T(8,128)(2,1)}, bf16[2,48,3456]{2,1,0:T(8,128)(2,1)}, u32[]{:S(2)}, u32[]{:S(2)}) %collective-permute-start.28) | collective-permute-done | bytes 663584 | tf_op jit(solution)/shard_map/ppermute | solution.py:570
  243.4 2.2 bitcast_add_fusion.1
  246.7 3.7 %collective-permute-start.30 = (bf16[48,3584]{1,0:T(8,128)(2,1)S(1)}, bf16[48,3584]{1,0:T(8,128)(2,1)S(1)}, u32[]{:S(2)}, u32[]{:S(2)}) collective-permute-start(bf16[48,3584]{1,0:T(8,128)(2,1)S(1)} %get-tuple-element.168), channel_id=1, source_target_pairs={{0,8},{1,9},{2,10},{3,11},{4,12},{5,13},{6,14},{7,15},{8,0},{9,1},... | collective-permute-start | bytes 1032200 | tf_op jit(solution)/shard_map/ppermute | solution.py:570
  250.3 3.4 %collective-permute-done.25 = bf16[2,2,144,384]{3,2,1,0:T(8,128)(2,1)S(1)} collective-permute-done((bf16[2,2,144,384]{3,2,1,0:T(8,128)(2,1)}, bf16[2,2,144,384]{3,2,1,0:T(8,128)(2,1)S(1)}, u32[]{:S(2)}, u32[]{:S(2)}) %collective-permute-start.25) | collective-permute-done | bytes 442400 | tf_op jit(solution)/shard_map/ppermute | solution.py:570
  257.6 3.8 %collective-permute-done.33 = bf16[2,144,384]{2,1,0:T(8,128)(2,1)S(1)} collective-permute-done((bf16[2,144,384]{2,1,0:T(8,128)(2,1)S(1)}, bf16[2,144,384]{2,1,0:T(8,128)(2,1)S(1)}, u32[]{:S(2)}, u32[]{:S(2)}) %collective-permute-start.33) | collective-permute-done | bytes 221216 | tf_op jit(solution)/shard_map/ppermute | solution.py:570
  262.6 13.2 %collective-permute-done.31 = bf16[48,3584]{1,0:T(8,128)(2,1)S(1)} collective-permute-done((bf16[48,3584]{1,0:T(8,128)(2,1)S(1)}, bf16[48,3584]{1,0:T(8,128)(2,1)S(1)}, u32[]{:S(2)}, u32[]{:S(2)}) %collective-permute-start.31) | collective-permute-done | bytes 344096 | tf_op jit(solution)/shard_map/ppermute | solution.py:570
  278.7 3.1 %collective-permute-done.34 = f32[24,128]{1,0:T(8,128)S(1)} collective-permute-done((f32[24,128]{1,0:T(8,128)S(1)}, f32[24,128]{1,0:T(8,128)S(1)}, u32[]{:S(2)}, u32[]{:S(2)}) %collective-permute-start.34) | collective-permute-done | bytes 12320 | tf_op jit(solution)/shard_map/ppermute | solution.py:570
  283.5 3.2 %collective-permute-start.38 = (bf16[144,384]{1,0:T(8,128)(2,1)S(1)}, bf16[144,384]{1,0:T(8,128)(2,1)S(1)}, u32[]{:S(2)}, u32[]{:S(2)}) collective-permute-start(bf16[144,384]{1,0:T(8,128)(2,1)S(1)} %get-tuple-element.174), channel_id=1, source_target_pairs={{0,16},{1,17},{2,18},{3,19},{4,20},{5,21},{6,22},{7,23},{8,24},{9,... | collective-permute-start | bytes 331784 | tf_op jit(solution)/shard_map/ppermute | solution.py:570
  (158 shorter events, 60.1 us)
Async XLA Ops:
  3.6 75.0 %all-to-all-start = ((bf16[4,48,3584]{2,1,0:T(8,128)(2,1)}), bf16[4,48,3584]{2,1,0:T(8,128)(2,1)}, u32[]{:S(2)}, u32[]{:S(2)}) async-start(bf16[4,48,3584]{2,1,0:T(8,128)(2,1)} %broadcast_in_dim.27), calls=%async_computation | async-start | bytes 2752512 | tf_op jit(solution)/shard_map/all_to_all | solution.py:578
  10.2 30.0 %collective-permute-start.2 = (bf16[144,384]{1,0:T(8,128)(2,1)S(1)}, bf16[144,384]{1,0:T(8,128)(2,1)S(1)}, u32[]{:S(2)}, u32[]{:S(2)}) collective-permute-start(bf16[144,384]{1,0:T(8,128)(2,1)S(1)} %constant_dynamic-update-slice_fusion), channel_id=1, source_target_pairs={{0,24},{1,25},{2,26},{3,27},{4,28},{5,29},{6,30},{7,31},{8,16},{9,... | collective-permute-start | bytes 331784 | tf_op jit(solution)/shard_map/ppermute | solution.py:570
  14.1 38.3 %collective-permute-start.1 = (bf16[144,384]{1,0:T(8,128)(2,1)S(1)}, bf16[144,384]{1,0:T(8,128)(2,1)S(1)}, u32[]{:S(2)}, u32[]{:S(2)}) collective-permute-start(bf16[144,384]{1,0:T(8,128)(2,1)S(1)} %constant_dynamic-update-slice_fusion), channel_id=1, source_target_pairs={{0,16},{1,17},{2,18},{3,19},{4,20},{5,21},{6,22},{7,23},{8,24},{9,... | collective-permute-start | bytes 331784 | tf_op jit(solution)/shard_map/ppermute | solution.py:570
  14.1 38.3 %collective-permute-start = (bf16[144,384]{1,0:T(8,128)(2,1)S(1)}, bf16[144,384]{1,0:T(8,128)(2,1)S(1)}, u32[]{:S(2)}, u32[]{:S(2)}) collective-permute-start(bf16[144,384]{1,0:T(8,128)(2,1)S(1)} %constant_dynamic-update-slice_fusion), channel_id=1, source_target_pairs={{0,8},{1,9},{2,10},{3,11},{4,12},{5,13},{6,14},{7,15},{8,0},{9,1},... | collective-permute-start | bytes 331784 | tf_op jit(solution)/shard_map/ppermute | solution.py:570
  53.2 11.5 %collective-permute-start.4 = (bf16[4,144,384]{2,1,0:T(8,128)(2,1)}, bf16[4,144,384]{2,1,0:T(8,128)(2,1)}, u32[]{:S(2)}, u32[]{:S(2)}) collective-permute-start(bf16[4,144,384]{2,1,0:T(8,128)(2,1)} %pad_maximum_fusion.1.rest_0_), channel_id=1, source_target_pairs={{0,4},{1,5},{2,6},{3,7},{4,0},{5,1},{6,2},{7,3},{8,12},{9,13},{10,... | collective-permute-start | bytes 1327112 | tf_op jit(solution)/shard_map/ppermute | solution.py:570
  54.7 11.2 %collective-permute-start.3 = (bf16[4,144,384]{2,1,0:T(8,128)(2,1)}, bf16[4,144,384]{2,1,0:T(8,128)(2,1)}, u32[]{:S(2)}, u32[]{:S(2)}) collective-permute-start(bf16[4,144,384]{2,1,0:T(8,128)(2,1)} %pad_maximum_fusion.1.rest_0_), channel_id=1, source_target_pairs={{0,1},{1,0},{2,3},{3,2},{4,5},{5,4},{6,7},{7,6},{8,9},{9,8},{10,11... | collective-permute-start | bytes 1327112 | tf_op jit(solution)/shard_map/ppermute | solution.py:570
  78.7 32.8 %collective-permute-start.13 = (bf16[4,48,3584]{2,1,0:T(8,128)(2,1)}, bf16[4,48,3584]{2,1,0:T(8,128)(2,1)S(1)}, u32[]{:S(2)}, u32[]{:S(2)}) collective-permute-start(bf16[4,48,3584]{2,1,0:T(8,128)(2,1)} %all-to-all-done.rest_0_), channel_id=1, source_target_pairs={{0,4},{1,5},{2,6},{3,7},{4,0},{5,1},{6,2},{7,3},{8,12},{9,13},{10,... | collective-permute-start | bytes 4128776 | tf_op jit(solution)/shard_map/ppermute | solution.py:570
  79.4 32.6 %collective-permute-start.12 = (bf16[4,48,3584]{2,1,0:T(8,128)(2,1)}, bf16[4,48,3584]{2,1,0:T(8,128)(2,1)}, u32[]{:S(2)}, u32[]{:S(2)}) collective-permute-start(bf16[4,48,3584]{2,1,0:T(8,128)(2,1)} %all-to-all-done.rest_0_), channel_id=1, source_target_pairs={{0,1},{1,0},{2,3},{3,2},{4,5},{5,4},{6,7},{7,6},{8,9},{9,8},{10,11... | collective-permute-start | bytes 4128776 | tf_op jit(solution)/shard_map/ppermute | solution.py:570
  113.2 17.1 %collective-permute-start.14 = (bf16[2,48,3584]{2,1,0:T(8,128)(2,1)S(1)}, bf16[2,48,3584]{2,1,0:T(8,128)(2,1)}, u32[]{:S(2)}, u32[]{:S(2)}) collective-permute-start(bf16[2,48,3584]{2,1,0:T(8,128)(2,1)S(1)} %slice.161), channel_id=1, source_target_pairs={{0,4},{1,5},{2,6},{3,7},{4,0},{5,1},{6,2},{7,3},{8,12},{9,13},{10,... | collective-permute-start | bytes 2064392 | tf_op jit(solution)/shard_map/ppermute | solution.py:570
  114.5 16.5 %collective-permute-start.15 = (bf16[2,48,3584]{2,1,0:T(8,128)(2,1)S(1)}, bf16[2,48,3584]{2,1,0:T(8,128)(2,1)}, u32[]{:S(2)}, u32[]{:S(2)}) collective-permute-start(bf16[2,48,3584]{2,1,0:T(8,128)(2,1)S(1)} %slice.162), channel_id=1, source_target_pairs={{0,1},{1,0},{2,3},{3,2},{4,5},{5,4},{6,7},{7,6},{8,9},{9,8},{10,11... | collective-permute-start | bytes 2064392 | tf_op jit(solution)/shard_map/ppermute | solution.py:570
  116.0 17.8 %collective-permute-start.16 = (bf16[4,48,3584]{2,1,0:T(8,128)(2,1)}, bf16[4,48,3584]{2,1,0:T(8,128)(2,1)}, u32[]{:S(2)}, u32[]{:S(2)}) collective-permute-start(bf16[4,48,3584]{2,1,0:T(8,128)(2,1)} %all-to-all-done.rest_0_), channel_id=1, source_target_pairs={{0,2},{1,3},{2,0},{3,1},{4,6},{5,7},{6,4},{7,5},{8,10},{9,11},{10,... | collective-permute-start | bytes 4128776 | tf_op jit(solution)/shard_map/ppermute | solution.py:570
  116.0 17.8 %collective-permute-start.17 = (bf16[4,48,3584]{2,1,0:T(8,128)(2,1)}, bf16[4,48,3584]{2,1,0:T(8,128)(2,1)}, u32[]{:S(2)}, u32[]{:S(2)}) collective-permute-start(bf16[4,48,3584]{2,1,0:T(8,128)(2,1)} %collective-permute-done.12.rest_1_), channel_id=1, source_target_pairs={{0,2},{1,3},{2,0},{3,1},{4,6},{5,7},{6,4},{7,5},{8,10},{9,11},{10,... | collective-permute-start | bytes 4128776 | tf_op jit(solution)/shard_map/ppermute | solution.py:570
  116.5 17.3 %collective-permute-start.18 = (bf16[4,48,3584]{2,1,0:T(8,128)(2,1)S(1)}, bf16[4,48,3584]{2,1,0:T(8,128)(2,1)}, u32[]{:S(2)}, u32[]{:S(2)}) collective-permute-start(bf16[4,48,3584]{2,1,0:T(8,128)(2,1)S(1)} %collective-permute-done.13.rest_2_), channel_id=1, source_target_pairs={{0,2},{1,3},{2,0},{3,1},{4,6},{5,7},{6,4},{7,5},{8,10},{9,11},{10,... | collective-permute-start | bytes 4128776 | tf_op jit(solution)/shard_map/ppermute | solution.py:570
  170.4 9.0 %collective-permute-start.21 = (bf16[4,4,48,3456]{3,2,1,0:T(8,128)(2,1)}, bf16[4,4,48,3456]{3,2,1,0:T(8,128)(2,1)S(1)}, u32[]{:S(2)}, u32[]{:S(2)}) collective-permute-start(bf16[4,4,48,3456]{3,2,1,0:T(8,128)(2,1)} %get-tuple-element.110), channel_id=1, source_target_pairs={{0,2},{1,3},{2,0},{3,1},{4,6},{5,7},{6,4},{7,5},{8,10},{9,11},{10,... | collective-permute-start | bytes 15925256 | tf_op jit(solution)/shard_map/ppermute | solution.py:570
  185.0 31.5 %collective-permute-start.22 = (bf16[2,2,48,3456]{3,2,1,0:T(8,128)(2,1)}, bf16[2,2,48,3456]{3,2,1,0:T(8,128)(2,1)}, u32[]{:S(2)}, u32[]{:S(2)}) collective-permute-start(bf16[2,2,48,3456]{3,2,1,0:T(8,128)(2,1)} %get-tuple-element.112), channel_id=1, source_target_pairs={{0,4},{1,5},{2,6},{3,7},{4,0},{5,1},{6,2},{7,3},{8,12},{9,13},{10,... | collective-permute-start | bytes 3981320 | tf_op jit(solution)/shard_map/ppermute | solution.py:570
  186.0 31.2 %collective-permute-start.23 = (bf16[2,2,48,3456]{3,2,1,0:T(8,128)(2,1)}, bf16[2,2,48,3456]{3,2,1,0:T(8,128)(2,1)}, u32[]{:S(2)}, u32[]{:S(2)}) collective-permute-start(bf16[2,2,48,3456]{3,2,1,0:T(8,128)(2,1)} %get-tuple-element.113), channel_id=1, source_target_pairs={{0,1},{1,0},{2,3},{3,2},{4,5},{5,4},{6,7},{7,6},{8,9},{9,8},{10,11... | collective-permute-start | bytes 3981320 | tf_op jit(solution)/shard_map/ppermute | solution.py:570
  222.5 17.6 %collective-permute-start.28 = (bf16[2,48,3456]{2,1,0:T(8,128)(2,1)}, bf16[2,48,3456]{2,1,0:T(8,128)(2,1)}, u32[]{:S(2)}, u32[]{:S(2)}) collective-permute-start(bf16[2,48,3456]{2,1,0:T(8,128)(2,1)} %get-tuple-element.154), channel_id=1, source_target_pairs={{0,4},{1,5},{2,6},{3,7},{4,0},{5,1},{6,2},{7,3},{8,12},{9,13},{10,... | collective-permute-start | bytes 1990664 | tf_op jit(solution)/shard_map/ppermute | solution.py:570
  223.5 17.4 %collective-permute-start.27 = (bf16[2,48,3456]{2,1,0:T(8,128)(2,1)}, bf16[2,48,3456]{2,1,0:T(8,128)(2,1)}, u32[]{:S(2)}, u32[]{:S(2)}) collective-permute-start(bf16[2,48,3456]{2,1,0:T(8,128)(2,1)} %get-tuple-element.155), channel_id=1, source_target_pairs={{0,1},{1,0},{2,3},{3,2},{4,5},{5,4},{6,7},{7,6},{8,9},{9,8},{10,11... | collective-permute-start | bytes 1990664 | tf_op jit(solution)/shard_map/ppermute | solution.py:570
  240.9 12.8 %collective-permute-start.25 = (bf16[2,2,144,384]{3,2,1,0:T(8,128)(2,1)}, bf16[2,2,144,384]{3,2,1,0:T(8,128)(2,1)S(1)}, u32[]{:S(2)}, u32[]{:S(2)}) collective-permute-start(bf16[2,2,144,384]{3,2,1,0:T(8,128)(2,1)} %get-tuple-element.131), channel_id=1, source_target_pairs={{0,4},{1,5},{2,6},{3,7},{4,0},{5,1},{6,2},{7,3},{8,12},{9,13},{10,... | collective-permute-start | bytes 1327112 | tf_op jit(solution)/shard_map/ppermute | solution.py:570
  241.9 12.5 %collective-permute-start.26 = (bf16[2,2,144,384]{3,2,1,0:T(8,128)(2,1)}, bf16[2,2,144,384]{3,2,1,0:T(8,128)(2,1)S(1)}, u32[]{:S(2)}, u32[]{:S(2)}) collective-permute-start(bf16[2,2,144,384]{3,2,1,0:T(8,128)(2,1)} %get-tuple-element.132), channel_id=1, source_target_pairs={{0,1},{1,0},{2,3},{3,2},{4,5},{5,4},{6,7},{7,6},{8,9},{9,8},{10,11... | collective-permute-start | bytes 1327112 | tf_op jit(solution)/shard_map/ppermute | solution.py:570
  245.9 16.7 %collective-permute-start.32 = (bf16[48,3584]{1,0:T(8,128)(2,1)S(1)}, bf16[48,3584]{1,0:T(8,128)(2,1)S(1)}, u32[]{:S(2)}, u32[]{:S(2)}) collective-permute-start(bf16[48,3584]{1,0:T(8,128)(2,1)S(1)} %get-tuple-element.166), channel_id=1, source_target_pairs={{0,24},{1,25},{2,26},{3,27},{4,28},{5,29},{6,30},{7,31},{8,16},{9,... | collective-permute-start | bytes 1032200 | tf_op jit(solution)/shard_map/ppermute | solution.py:570
  246.7 29.1 %collective-permute-start.31 = (bf16[48,3584]{1,0:T(8,128)(2,1)S(1)}, bf16[48,3584]{1,0:T(8,128)(2,1)S(1)}, u32[]{:S(2)}, u32[]{:S(2)}) collective-permute-start(bf16[48,3584]{1,0:T(8,128)(2,1)S(1)} %get-tuple-element.167), channel_id=1, source_target_pairs={{0,16},{1,17},{2,18},{3,19},{4,20},{5,21},{6,22},{7,23},{8,24},{9,... | collective-permute-start | bytes 1032200 | tf_op jit(solution)/shard_map/ppermute | solution.py:570
  246.7 29.1 %collective-permute-start.30 = (bf16[48,3584]{1,0:T(8,128)(2,1)S(1)}, bf16[48,3584]{1,0:T(8,128)(2,1)S(1)}, u32[]{:S(2)}, u32[]{:S(2)}) collective-permute-start(bf16[48,3584]{1,0:T(8,128)(2,1)S(1)} %get-tuple-element.168), channel_id=1, source_target_pairs={{0,8},{1,9},{2,10},{3,11},{4,12},{5,13},{6,14},{7,15},{8,0},{9,1},... | collective-permute-start | bytes 1032200 | tf_op jit(solution)/shard_map/ppermute | solution.py:570
  256.5 22.1 %collective-permute-start.37 = (bf16[2,144,384]{2,1,0:T(8,128)(2,1)S(1)}, bf16[2,144,384]{2,1,0:T(8,128)(2,1)S(1)}, u32[]{:S(2)}, u32[]{:S(2)}) collective-permute-start(bf16[2,144,384]{2,1,0:T(8,128)(2,1)S(1)} %get-tuple-element.158), channel_id=1, source_target_pairs={{0,4},{1,5},{2,6},{3,7},{4,0},{5,1},{6,2},{7,3},{8,12},{9,13},{10,... | collective-permute-start | bytes 663560 | tf_op jit(solution)/shard_map/ppermute | solution.py:570
  (34 other events, 347.2 us)

commit v6 on v5

--- a/solution.py
+++ b/solution.py
@@ -38,6 +38,8 @@
 
 
 def placed(pieces):
+    if len(pieces) == 4:
+        pieces = [p.at[n] for p, size in zip(pieces, (3, 2, 3, 2)) for n in range(size)]
     for n, piece in enumerate(pieces):
         y, x, first = PIECES[n % len(PIECES)]
         for z in range(piece.shape[0]):
@@ -587,7 +589,7 @@
 
 
 def gather_near(packet, total):
-    return jnp.stack([packet, *[exchange(packet, m * Z_BIT, total) for m in (1, 2, 3)]])
+    return [packet, *[exchange(packet, m * Z_BIT, total) for m in (1, 2, 3)]]
 
 
 def gather_sides(line, total):
@@ -676,10 +678,11 @@
     down_turned = down_weight.T
     if blocked:
         packet = jnp.concatenate([query_weight, key_weight, value_weight], axis=0)
-        qkv_line = gather_near(packet, total)
+        qkv_near = gather_near(packet, total)
+        qkv_line = jnp.stack(qkv_near)
         qkv_sides = gather_sides(qkv_line, total)
-        marks = jnp.sum(validity.reshape(-1, EXTRA), axis=0).astype(BF16)
-        marks = jnp.broadcast_to(marks, (depth, EXTRA))
+        marks = jnp.sum(validity.reshape(-1, EXTRA), axis=0).astype(F32)
+        marks = jnp.broadcast_to(marks, (depth, EXTRA)).astype(BF16)
         packet = jnp.concatenate(
             [up_weight, output_weight, marks, down_turned], axis=1
         )
@@ -687,7 +690,7 @@
         *halves, qkv_line, side_x, side_y = lax.optimization_barrier(
             (qkv_sides[0][:2], qkv_sides[1][2:], qkv_line, *qkv_sides)
         )
-        qkv = [qkv_line, side_x, side_y, *gather_halves(*halves, total)]
+        qkv = [jnp.stack([qkv_line, side_x, side_y]), jnp.stack(gather_halves(*halves, total))]
         qkv += [exchange(part, CORE_BIT, total) for part in qkv]
         line, *qkv = lax.optimization_barrier((line, *qkv))
         sides = gather_sides(line, total)

time: 297 us -> 265 us (0.89)
  waiting for transfers between devices: 113 us -> 82.1 us
    ppermute x40 -> x37, waiting for transfers between devices: 113 us -> 78.1 us  [exchange(): return lax.ppermute(value, AXES, [(i, i ^ mask) for i in range(total)])]
    all_to_all x1, waiting for transfers between devices: 0.01 us -> 4 us  [over_lines(): lax.all_to_all(blocks, 'row', 0, 0, axis_index_groups=LINES, tiled=True)]
    ppermute x40 -> x37, starting transfers between devices: 37.3 us -> 37.2 us  [exchange(): return lax.ppermute(value, AXES, [(i, i ^ mask) for i in range(total)])]
  transfers between devices with their start and end apart: 41 -> 38, of which waited for: 24 -> 24; matrix products, arithmetic and copies ran while one was open for 8% -> 10% of each run, Pallas kernels for 20% -> 22%
where the time goes in v6:
time: 265 us; the launch traced here: 264 us
  Pallas kernels  95.6 us (36%)
  waiting for transfers between devices  82.1 us (31%)
  starting transfers between devices  42.3 us (16%)
  local copies, waits for them, and re-layouts  19.9 us (8%)
  other arithmetic  16.9 us (6%)
  between operations  7.26 us (3%)
    ppermute x37, waiting for transfers between devices, exchange(): return lax.ppermute(value, AXES, [(i, i ^ mask) for i in range(total)])  78.1 us
    ppermute x37, starting transfers between devices, exchange(): return lax.ppermute(value, AXES, [(i, i ^ mask) for i in range(total)])  37.2 us
    pallas_call x1, Pallas kernels, middle_block(): pl.pallas_call(functools.partial(middle_kernel, len(pieces), len(grads),...  36.7 us
    pallas_call x1, Pallas kernels, attend_back(): pl.pallas_call(functools.partial(attend_back_kernel, blocked), grid=(HEAD...  28.8 us
    pallas_call x1, Pallas kernels, attend(): pl.pallas_call(functools.partial(attend_kernel, len(pieces)), grid=(HEADS...  21.1 us
    pallas_call x1, Pallas kernels, input_block(): pl.pallas_call(functools.partial(input_kernel, len(pieces)), in_specs=[SM...  9.03 us
  transfers between devices with their start and end apart: 38, of which 24 were waited for; matrix products, arithmetic and copies ran while one was open for 10% of the time, Pallas kernels for 22%

profile of v6, /device:TPU:0, one launch (start us, length us, event | category | flops | bytes accessed | tf_op | source)
XLA Modules:
  0.0 264.0 jit_solution(1992555358512805285)
XLA Ops:
  3.0 5.1 %collective-permute-start.2 = (bf16[144,384]{1,0:T(8,128)(2,1)S(1)}, bf16[144,384]{1,0:T(8,128)(2,1)S(1)}, u32[]{:S(2)}, u32[]{:S(2)}) collective-permute-start(bf16[144,384]{1,0:T(8,128)(2,1)S(1)} %constant_dynamic-update-slice_fusion), channel_id=1, source_target_pairs={{0,24},{1,25},{2,26},{3,27},{4,28},{5,29},{6,30},{7,31},{8,16},{9,... | collective-permute-start | bytes 331784 | tf_op jit(solution)/shard_map/ppermute | solution.py:572
  11.7 5.0 %all-to-all-start = ((bf16[4,48,3584]{2,1,0:T(8,128)(2,1)}), bf16[4,48,3584]{2,1,0:T(8,128)(2,1)}, u32[]{:S(2)}, u32[]{:S(2)}) async-start(bf16[4,48,3584]{2,1,0:T(8,128)(2,1)} %broadcast_in_dim.27), calls=%async_computation | async-start | bytes 2752512 | tf_op jit(solution)/shard_map/all_to_all | solution.py:580
  17.4 1.6 collective-permute-start.4
  20.5 8.2 %collective-permute-done.4 = bf16[4,144,384]{2,1,0:T(8,128)(2,1)S(1)} collective-permute-done((bf16[4,144,384]{2,1,0:T(8,128)(2,1)S(1)}, bf16[4,144,384]{2,1,0:T(8,128)(2,1)S(1)}, u32[]{:S(2)}, u32[]{:S(2)}) %collective-permute-start.4) | collective-permute-done | bytes 442400 | tf_op jit(solution)/shard_map/ppermute | solution.py:572
  33.6 5.8 %collective-permute-done.5 = bf16[2,144,384]{2,1,0:T(8,128)(2,1)S(1)} collective-permute-done((bf16[2,144,384]{2,1,0:T(8,128)(2,1)S(1)}, bf16[2,144,384]{2,1,0:T(8,128)(2,1)S(1)}, u32[]{:S(2)}, u32[]{:S(2)}) %collective-permute-start.5) | collective-permute-done | bytes 221216 | tf_op jit(solution)/shard_map/ppermute | solution.py:572
  44.7 4.0 %all-to-all-done.rest_0_ = bf16[4,48,3584]{2,1,0:T(8,128)(2,1)} async-done(((bf16[4,48,3584]{2,1,0:T(8,128)(2,1)}), bf16[4,48,3584]{2,1,0:T(8,128)(2,1)}, u32[]{:S(2)}, u32[]{:S(2)}) %all-to-all-start) | async-done | bytes 1376288 | tf_op jit(solution)/shard_map/all_to_all | solution.py:580
  51.7 21.1 %attend.1 = (bf16[512,768]{1,0:T(8,128)(2,1)}, bf16[512,768]{1,0:T(8,128)(2,1)}, bf16[512,768]{1,0:T(8,128)(2,1)}, bf16[512,768]{1,0:T(8,128)(2,1)}, bf16[12,256,768]{2,1,0:T(8,128)(2,1)}) custom-call(s32[4]{0:T(128)} %pad_add_fusion.spot, s32[1,2]{1,0:T(1,128)} %starts.1, bf16[512,768]{1,0:T(8,128)(2,1)} %copy.40.normed_ref, ...), custom_call_target="tpu_custom_call" | custom-call | flops 20000000000 | bytes 1000000 | tf_op jit(solution)/shard_map/attend/pallas_call | solution.py:158
  72.8 7.3 %collective-permute-done.10.rest_2_ = bf16[4,48,3584]{2,1,0:T(8,128)(2,1)S(1)} collective-permute-done((bf16[4,48,3584]{2,1,0:T(8,128)(2,1)}, bf16[4,48,3584]{2,1,0:T(8,128)(2,1)S(1)}, u32[]{:S(2)}, u32[]{:S(2)}) %collective-permute-start.10) | collective-permute-done | bytes 1376288 | tf_op jit(solution)/shard_map/ppermute | solution.py:572
  85.4 12.8 %collective-permute-done.11.rest_3_ = bf16[2,48,3584]{2,1,0:T(8,128)(2,1)} collective-permute-done((bf16[2,48,3584]{2,1,0:T(8,128)(2,1)S(1)}, bf16[2,48,3584]{2,1,0:T(8,128)(2,1)}, u32[]{:S(2)}, u32[]{:S(2)}) %collective-permute-start.11) | collective-permute-done | bytes 688160 | tf_op jit(solution)/shard_map/ppermute | solution.py:572
  101.6 36.7 %middle.1 = (f32[512,768]{1,0:T(8,128)}, f32[512,768]{1,0:T(8,128)}, bf16[512,768]{1,0:T(8,128)(2,1)}, f32[8,768]{1,0:T(8,128)}, bf16[4,4,48,3456]{3,2,1,0:T(8,128)(2,1)}, /*index=5*/bf16[4,4,48,3456]{3,2,1,0:T(8,128)(2,1)}) custom-call(s32[4]{0:T(128)} %pad_add_fusion.spot, f32[1,1]{1,0:T(1,128)} %constant.55.clone.1.count, ...), custom_call_target="tpu_custom_call" | custom-call | flops 35000000512 | bytes 1000000 | tf_op jit(solution)/shard_map/middle/pallas_call | solution.py:337
  139.6 7.7 %collective-permute-done.18 = bf16[4,4,48,3456]{3,2,1,0:T(8,128)(2,1)S(1)} collective-permute-done((bf16[4,4,48,3456]{3,2,1,0:T(8,128)(2,1)}, bf16[4,4,48,3456]{3,2,1,0:T(8,128)(2,1)S(1)}, u32[]{:S(2)}, u32[]{:S(2)}) %collective-permute-start.18) | collective-permute-done | bytes 5308448 | tf_op jit(solution)/shard_map/ppermute | solution.py:572
  147.4 3.7 %add_convert_fusion = bf16[4,4,48,3456]{3,2,1,0:T(8,128)(2,1)S(1)} fusion(bf16[4,4,48,3456]{3,2,1,0:T(8,128)(2,1)S(1)} %collective-permute-done.18, bf16[4,4,48,3456]{3,2,1,0:T(8,128)(2,1)} %get-tuple-element.97), kind=kLoop, calls=%fused_computation | loop fusion | flops 10616832 | bytes 15925248 | tf_op jit(solution)/shard_map/convert_element_type | solution.py:608
  151.1 1.7 fusion.10
  155.3 28.8 %attend_back.1 = (bf16[512,768]{1,0:T(8,128)(2,1)}, bf16[512,768]{1,0:T(8,128)(2,1)}, bf16[512,768]{1,0:T(8,128)(2,1)}, f32[16,128]{1,0:T(8,128)}, bf16[4,4,144,...) custom-call(s32[4]{0:T(128)} %pad_add_fusion.spot, f32[12,12]{1,0:T(8,128)} %copy-done.6, f32[12,12]{1,0:T(8,128)} %pos.1, ...), custom_call_target="tpu_custom_call" | custom-call | flops 28000000000 | bytes 1000000 | tf_op jit(solution)/shard_map/attend_back/pallas_call | solution.py:491
  187.6 2.8 %fusion.5 = (bf16[2,48,3456]{2,1,0:T(8,128)(2,1)}, bf16[2,48,3456]{2,1,0:T(8,128)(2,1)}) fusion(bf16[2,2,48,3456]{3,2,1,0:T(8,128)(2,1)} %collective-permute-done.20, bf16[4,4,48,3456]{3,2,1,0:T(8,128)(2,1)S(1)} %add_convert_fusion, bf16[2,2,48,3456]{3,2,1,0:T(8,128)(2,1)} %collective-permute-done.19), kind=kLoop, calls=%fused_computation.16 | loop fusion | flops 2654208 | bytes 3981312 | tf_op jit(solution)/shard_map/convert_element_type | solution.py:617
  195.5 9.0 %input_grad.1 = (f32[512,768]{1,0:T(8,128)}, f32[24,128]{1,0:T(8,128)}) custom-call(s32[4]{0:T(128)} %pad_add_fusion.spot, bf16[3,4,144,384]{3,2,1,0:T(8,128)(2,1)} %pad_maximum_fusion.1.rest_0_, bf16[2,2,144,384]{3,2,1,0:T(8,128)(2,1)} %pad_maximum_fusion.3.rest_1_, bf16[3,4,144,384]{3,2,1,0:T(8,128)(2,1)} %collective-permute-done.7.rest_2_, ...), custom_call_target="tpu_custom_call" | custom-call | flops 8999999488 | bytes 1000000 | tf_op jit(solution)/shard_map/input_grad/pallas_call | solution.py:556
  204.6 3.4 %collective-permute-done.25 = bf16[2,48,3456]{2,1,0:T(8,128)(2,1)} collective-permute-done((bf16[2,48,3456]{2,1,0:T(8,128)(2,1)}, bf16[2,48,3456]{2,1,0:T(8,128)(2,1)}, u32[]{:S(2)}, u32[]{:S(2)}) %collective-permute-start.25) | collective-permute-done | bytes 663584 | tf_op jit(solution)/shard_map/ppermute | solution.py:572
  211.2 2.1 bitcast_add_fusion.1
  213.8 4.3 %collective-permute-start.27 = (bf16[48,3584]{1,0:T(8,128)(2,1)S(1)}, bf16[48,3584]{1,0:T(8,128)(2,1)S(1)}, u32[]{:S(2)}, u32[]{:S(2)}) collective-permute-start(bf16[48,3584]{1,0:T(8,128)(2,1)S(1)} %get-tuple-element.156), channel_id=1, source_target_pairs={{0,8},{1,9},{2,10},{3,11},{4,12},{5,13},{6,14},{7,15},{8,0},{9,1},... | collective-permute-start | bytes 1032200 | tf_op jit(solution)/shard_map/ppermute | solution.py:572
  218.1 3.4 %collective-permute-done.22 = bf16[2,2,144,384]{3,2,1,0:T(8,128)(2,1)S(1)} collective-permute-done((bf16[2,2,144,384]{3,2,1,0:T(8,128)(2,1)}, bf16[2,2,144,384]{3,2,1,0:T(8,128)(2,1)S(1)}, u32[]{:S(2)}, u32[]{:S(2)}) %collective-permute-start.22) | collective-permute-done | bytes 442400 | tf_op jit(solution)/shard_map/ppermute | solution.py:572
  225.3 3.9 %collective-permute-done.30 = bf16[2,144,384]{2,1,0:T(8,128)(2,1)S(1)} collective-permute-done((bf16[2,144,384]{2,1,0:T(8,128)(2,1)S(1)}, bf16[2,144,384]{2,1,0:T(8,128)(2,1)S(1)}, u32[]{:S(2)}, u32[]{:S(2)}) %collective-permute-start.30) | collective-permute-done | bytes 221216 | tf_op jit(solution)/shard_map/ppermute | solution.py:572
  230.5 13.1 %collective-permute-done.28 = bf16[48,3584]{1,0:T(8,128)(2,1)S(1)} collective-permute-done((bf16[48,3584]{1,0:T(8,128)(2,1)S(1)}, bf16[48,3584]{1,0:T(8,128)(2,1)S(1)}, u32[]{:S(2)}, u32[]{:S(2)}) %collective-permute-start.28) | collective-permute-done | bytes 344096 | tf_op jit(solution)/shard_map/ppermute | solution.py:572
  246.5 3.0 %collective-permute-done.31 = f32[24,128]{1,0:T(8,128)S(1)} collective-permute-done((f32[24,128]{1,0:T(8,128)S(1)}, f32[24,128]{1,0:T(8,128)S(1)}, u32[]{:S(2)}, u32[]{:S(2)}) %collective-permute-start.31) | collective-permute-done | bytes 12320 | tf_op jit(solution)/shard_map/ppermute | solution.py:572
  251.1 3.2 %collective-permute-start.35 = (bf16[144,384]{1,0:T(8,128)(2,1)S(1)}, bf16[144,384]{1,0:T(8,128)(2,1)S(1)}, u32[]{:S(2)}, u32[]{:S(2)}) collective-permute-start(bf16[144,384]{1,0:T(8,128)(2,1)S(1)} %get-tuple-element.162), channel_id=1, source_target_pairs={{0,16},{1,17},{2,18},{3,19},{4,20},{5,21},{6,22},{7,23},{8,24},{9,... | collective-permute-start | bytes 331784 | tf_op jit(solution)/shard_map/ppermute | solution.py:572
  (144 shorter events, 58.9 us)
Async XLA Ops:
  3.0 13.7 %collective-permute-start.2 = (bf16[144,384]{1,0:T(8,128)(2,1)S(1)}, bf16[144,384]{1,0:T(8,128)(2,1)S(1)}, u32[]{:S(2)}, u32[]{:S(2)}) collective-permute-start(bf16[144,384]{1,0:T(8,128)(2,1)S(1)} %constant_dynamic-update-slice_fusion), channel_id=1, source_target_pairs={{0,24},{1,25},{2,26},{3,27},{4,28},{5,29},{6,30},{7,31},{8,16},{9,... | collective-permute-start | bytes 331784 | tf_op jit(solution)/shard_map/ppermute | solution.py:572
  8.1 9.3 %collective-permute-start.1 = (bf16[144,384]{1,0:T(8,128)(2,1)S(1)}, bf16[144,384]{1,0:T(8,128)(2,1)S(1)}, u32[]{:S(2)}, u32[]{:S(2)}) collective-permute-start(bf16[144,384]{1,0:T(8,128)(2,1)S(1)} %constant_dynamic-update-slice_fusion), channel_id=1, source_target_pairs={{0,16},{1,17},{2,18},{3,19},{4,20},{5,21},{6,22},{7,23},{8,24},{9,... | collective-permute-start | bytes 331784 | tf_op jit(solution)/shard_map/ppermute | solution.py:572
  8.1 9.3 %collective-permute-start = (bf16[144,384]{1,0:T(8,128)(2,1)S(1)}, bf16[144,384]{1,0:T(8,128)(2,1)S(1)}, u32[]{:S(2)}, u32[]{:S(2)}) collective-permute-start(bf16[144,384]{1,0:T(8,128)(2,1)S(1)} %constant_dynamic-update-slice_fusion), channel_id=1, source_target_pairs={{0,8},{1,9},{2,10},{3,11},{4,12},{5,13},{6,14},{7,15},{8,0},{9,1},... | collective-permute-start | bytes 331784 | tf_op jit(solution)/shard_map/ppermute | solution.py:572
  11.7 37.0 %all-to-all-start = ((bf16[4,48,3584]{2,1,0:T(8,128)(2,1)}), bf16[4,48,3584]{2,1,0:T(8,128)(2,1)}, u32[]{:S(2)}, u32[]{:S(2)}) async-start(bf16[4,48,3584]{2,1,0:T(8,128)(2,1)} %broadcast_in_dim.27), calls=%async_computation | async-start | bytes 2752512 | tf_op jit(solution)/shard_map/all_to_all | solution.py:580
  17.4 11.3 %collective-permute-start.4 = (bf16[4,144,384]{2,1,0:T(8,128)(2,1)S(1)}, bf16[4,144,384]{2,1,0:T(8,128)(2,1)S(1)}, u32[]{:S(2)}, u32[]{:S(2)}) collective-permute-start(bf16[4,144,384]{2,1,0:T(8,128)(2,1)S(1)} %pad_maximum_fusion.2), channel_id=1, source_target_pairs={{0,4},{1,5},{2,6},{3,7},{4,0},{5,1},{6,2},{7,3},{8,12},{9,13},{10,... | collective-permute-start | bytes 1327112 | tf_op jit(solution)/shard_map/ppermute | solution.py:572
  19.0 11.0 %collective-permute-start.3 = (bf16[4,144,384]{2,1,0:T(8,128)(2,1)S(1)}, bf16[4,144,384]{2,1,0:T(8,128)(2,1)S(1)}, u32[]{:S(2)}, u32[]{:S(2)}) collective-permute-start(bf16[4,144,384]{2,1,0:T(8,128)(2,1)S(1)} %pad_maximum_fusion.2), channel_id=1, source_target_pairs={{0,1},{1,0},{2,3},{3,2},{4,5},{5,4},{6,7},{7,6},{8,9},{9,8},{10,11... | collective-permute-start | bytes 1327112 | tf_op jit(solution)/shard_map/ppermute | solution.py:572
  31.4 13.3 %collective-permute-start.7 = (bf16[3,4,144,384]{3,2,1,0:T(8,128)(2,1)}, bf16[3,4,144,384]{3,2,1,0:T(8,128)(2,1)}, u32[]{:S(2)}, u32[]{:S(2)}) collective-permute-start(bf16[3,4,144,384]{3,2,1,0:T(8,128)(2,1)} %pad_maximum_fusion.1.rest_0_), channel_id=1, source_target_pairs={{0,2},{1,3},{2,0},{3,1},{4,6},{5,7},{6,4},{7,5},{8,10},{9,11},{10,... | collective-permute-start | bytes 3981320 | tf_op jit(solution)/shard_map/ppermute | solution.py:572
  48.7 31.4 %collective-permute-start.10 = (bf16[4,48,3584]{2,1,0:T(8,128)(2,1)}, bf16[4,48,3584]{2,1,0:T(8,128)(2,1)S(1)}, u32[]{:S(2)}, u32[]{:S(2)}) collective-permute-start(bf16[4,48,3584]{2,1,0:T(8,128)(2,1)} %all-to-all-done.rest_0_), channel_id=1, source_target_pairs={{0,4},{1,5},{2,6},{3,7},{4,0},{5,1},{6,2},{7,3},{8,12},{9,13},{10,... | collective-permute-start | bytes 4128776 | tf_op jit(solution)/shard_map/ppermute | solution.py:572
  50.2 31.2 %collective-permute-start.9 = (bf16[4,48,3584]{2,1,0:T(8,128)(2,1)}, bf16[4,48,3584]{2,1,0:T(8,128)(2,1)}, u32[]{:S(2)}, u32[]{:S(2)}) collective-permute-start(bf16[4,48,3584]{2,1,0:T(8,128)(2,1)} %all-to-all-done.rest_0_), channel_id=1, source_target_pairs={{0,1},{1,0},{2,3},{3,2},{4,5},{5,4},{6,7},{7,6},{8,9},{9,8},{10,11... | collective-permute-start | bytes 4128776 | tf_op jit(solution)/shard_map/ppermute | solution.py:572
  82.6 15.5 %collective-permute-start.11 = (bf16[2,48,3584]{2,1,0:T(8,128)(2,1)S(1)}, bf16[2,48,3584]{2,1,0:T(8,128)(2,1)}, u32[]{:S(2)}, u32[]{:S(2)}) collective-permute-start(bf16[2,48,3584]{2,1,0:T(8,128)(2,1)S(1)} %slice.161), channel_id=1, source_target_pairs={{0,4},{1,5},{2,6},{3,7},{4,0},{5,1},{6,2},{7,3},{8,12},{9,13},{10,... | collective-permute-start | bytes 2064392 | tf_op jit(solution)/shard_map/ppermute | solution.py:572
  83.4 15.5 %collective-permute-start.12 = (bf16[2,48,3584]{2,1,0:T(8,128)(2,1)S(1)}, bf16[2,48,3584]{2,1,0:T(8,128)(2,1)}, u32[]{:S(2)}, u32[]{:S(2)}) collective-permute-start(bf16[2,48,3584]{2,1,0:T(8,128)(2,1)S(1)} %slice.162), channel_id=1, source_target_pairs={{0,1},{1,0},{2,3},{3,2},{4,5},{5,4},{6,7},{7,6},{8,9},{9,8},{10,11... | collective-permute-start | bytes 2064392 | tf_op jit(solution)/shard_map/ppermute | solution.py:572
  84.9 16.7 %collective-permute-start.13 = (bf16[4,48,3584]{2,1,0:T(8,128)(2,1)}, bf16[4,48,3584]{2,1,0:T(8,128)(2,1)}, u32[]{:S(2)}, u32[]{:S(2)}) collective-permute-start(bf16[4,48,3584]{2,1,0:T(8,128)(2,1)} %all-to-all-done.rest_0_), channel_id=1, source_target_pairs={{0,2},{1,3},{2,0},{3,1},{4,6},{5,7},{6,4},{7,5},{8,10},{9,11},{10,... | collective-permute-start | bytes 4128776 | tf_op jit(solution)/shard_map/ppermute | solution.py:572
  84.9 16.7 %collective-permute-start.14 = (bf16[4,48,3584]{2,1,0:T(8,128)(2,1)}, bf16[4,48,3584]{2,1,0:T(8,128)(2,1)}, u32[]{:S(2)}, u32[]{:S(2)}) collective-permute-start(bf16[4,48,3584]{2,1,0:T(8,128)(2,1)} %collective-permute-done.9.rest_1_), channel_id=1, source_target_pairs={{0,2},{1,3},{2,0},{3,1},{4,6},{5,7},{6,4},{7,5},{8,10},{9,11},{10,... | collective-permute-start | bytes 4128776 | tf_op jit(solution)/shard_map/ppermute | solution.py:572
  85.4 16.2 %collective-permute-start.15 = (bf16[4,48,3584]{2,1,0:T(8,128)(2,1)S(1)}, bf16[4,48,3584]{2,1,0:T(8,128)(2,1)}, u32[]{:S(2)}, u32[]{:S(2)}) collective-permute-start(bf16[4,48,3584]{2,1,0:T(8,128)(2,1)S(1)} %collective-permute-done.10.rest_2_), channel_id=1, source_target_pairs={{0,2},{1,3},{2,0},{3,1},{4,6},{5,7},{6,4},{7,5},{8,10},{9,11},{10,... | collective-permute-start | bytes 4128776 | tf_op jit(solution)/shard_map/ppermute | solution.py:572
  152.8 31.5 %collective-permute-start.19 = (bf16[2,2,48,3456]{3,2,1,0:T(8,128)(2,1)}, bf16[2,2,48,3456]{3,2,1,0:T(8,128)(2,1)}, u32[]{:S(2)}, u32[]{:S(2)}) collective-permute-start(bf16[2,2,48,3456]{3,2,1,0:T(8,128)(2,1)} %get-tuple-element.100), channel_id=1, source_target_pairs={{0,4},{1,5},{2,6},{3,7},{4,0},{5,1},{6,2},{7,3},{8,12},{9,13},{10,... | collective-permute-start | bytes 3981320 | tf_op jit(solution)/shard_map/ppermute | solution.py:572
  153.9 31.2 %collective-permute-start.20 = (bf16[2,2,48,3456]{3,2,1,0:T(8,128)(2,1)}, bf16[2,2,48,3456]{3,2,1,0:T(8,128)(2,1)}, u32[]{:S(2)}, u32[]{:S(2)}) collective-permute-start(bf16[2,2,48,3456]{3,2,1,0:T(8,128)(2,1)} %get-tuple-element.101), channel_id=1, source_target_pairs={{0,1},{1,0},{2,3},{3,2},{4,5},{5,4},{6,7},{7,6},{8,9},{9,8},{10,11... | collective-permute-start | bytes 3981320 | tf_op jit(solution)/shard_map/ppermute | solution.py:572
  190.4 17.6 %collective-permute-start.25 = (bf16[2,48,3456]{2,1,0:T(8,128)(2,1)}, bf16[2,48,3456]{2,1,0:T(8,128)(2,1)}, u32[]{:S(2)}, u32[]{:S(2)}) collective-permute-start(bf16[2,48,3456]{2,1,0:T(8,128)(2,1)} %get-tuple-element.142), channel_id=1, source_target_pairs={{0,4},{1,5},{2,6},{3,7},{4,0},{5,1},{6,2},{7,3},{8,12},{9,13},{10,... | collective-permute-start | bytes 1990664 | tf_op jit(solution)/shard_map/ppermute | solution.py:572
  191.3 17.4 %collective-permute-start.24 = (bf16[2,48,3456]{2,1,0:T(8,128)(2,1)}, bf16[2,48,3456]{2,1,0:T(8,128)(2,1)}, u32[]{:S(2)}, u32[]{:S(2)}) collective-permute-start(bf16[2,48,3456]{2,1,0:T(8,128)(2,1)} %get-tuple-element.143), channel_id=1, source_target_pairs={{0,1},{1,0},{2,3},{3,2},{4,5},{5,4},{6,7},{7,6},{8,9},{9,8},{10,11... | collective-permute-start | bytes 1990664 | tf_op jit(solution)/shard_map/ppermute | solution.py:572
  208.7 12.8 %collective-permute-start.22 = (bf16[2,2,144,384]{3,2,1,0:T(8,128)(2,1)}, bf16[2,2,144,384]{3,2,1,0:T(8,128)(2,1)S(1)}, u32[]{:S(2)}, u32[]{:S(2)}) collective-permute-start(bf16[2,2,144,384]{3,2,1,0:T(8,128)(2,1)} %get-tuple-element.119), channel_id=1, source_target_pairs={{0,4},{1,5},{2,6},{3,7},{4,0},{5,1},{6,2},{7,3},{8,12},{9,13},{10,... | collective-permute-start | bytes 1327112 | tf_op jit(solution)/shard_map/ppermute | solution.py:572
  209.8 12.5 %collective-permute-start.23 = (bf16[2,2,144,384]{3,2,1,0:T(8,128)(2,1)}, bf16[2,2,144,384]{3,2,1,0:T(8,128)(2,1)S(1)}, u32[]{:S(2)}, u32[]{:S(2)}) collective-permute-start(bf16[2,2,144,384]{3,2,1,0:T(8,128)(2,1)} %get-tuple-element.120), channel_id=1, source_target_pairs={{0,1},{1,0},{2,3},{3,2},{4,5},{5,4},{6,7},{7,6},{8,9},{9,8},{10,11... | collective-permute-start | bytes 1327112 | tf_op jit(solution)/shard_map/ppermute | solution.py:572
  213.7 16.8 %collective-permute-start.29 = (bf16[48,3584]{1,0:T(8,128)(2,1)S(1)}, bf16[48,3584]{1,0:T(8,128)(2,1)S(1)}, u32[]{:S(2)}, u32[]{:S(2)}) collective-permute-start(bf16[48,3584]{1,0:T(8,128)(2,1)S(1)} %get-tuple-element.154), channel_id=1, source_target_pairs={{0,24},{1,25},{2,26},{3,27},{4,28},{5,29},{6,30},{7,31},{8,16},{9,... | collective-permute-start | bytes 1032200 | tf_op jit(solution)/shard_map/ppermute | solution.py:572
  213.7 29.8 %collective-permute-start.28 = (bf16[48,3584]{1,0:T(8,128)(2,1)S(1)}, bf16[48,3584]{1,0:T(8,128)(2,1)S(1)}, u32[]{:S(2)}, u32[]{:S(2)}) collective-permute-start(bf16[48,3584]{1,0:T(8,128)(2,1)S(1)} %get-tuple-element.155), channel_id=1, source_target_pairs={{0,16},{1,17},{2,18},{3,19},{4,20},{5,21},{6,22},{7,23},{8,24},{9,... | collective-permute-start | bytes 1032200 | tf_op jit(solution)/shard_map/ppermute | solution.py:572
  213.8 29.7 %collective-permute-start.27 = (bf16[48,3584]{1,0:T(8,128)(2,1)S(1)}, bf16[48,3584]{1,0:T(8,128)(2,1)S(1)}, u32[]{:S(2)}, u32[]{:S(2)}) collective-permute-start(bf16[48,3584]{1,0:T(8,128)(2,1)S(1)} %get-tuple-element.156), channel_id=1, source_target_pairs={{0,8},{1,9},{2,10},{3,11},{4,12},{5,13},{6,14},{7,15},{8,0},{9,1},... | collective-permute-start | bytes 1032200 | tf_op jit(solution)/shard_map/ppermute | solution.py:572
  224.3 22.1 %collective-permute-start.34 = (bf16[2,144,384]{2,1,0:T(8,128)(2,1)S(1)}, bf16[2,144,384]{2,1,0:T(8,128)(2,1)S(1)}, u32[]{:S(2)}, u32[]{:S(2)}) collective-permute-start(bf16[2,144,384]{2,1,0:T(8,128)(2,1)S(1)} %get-tuple-element.146), channel_id=1, source_target_pairs={{0,4},{1,5},{2,6},{3,7},{4,0},{5,1},{6,2},{7,3},{8,12},{9,13},{10,... | collective-permute-start | bytes 663560 | tf_op jit(solution)/shard_map/ppermute | solution.py:572
  (26 other events, 193.3 us)

commit v7 on v6

--- a/solution.py
+++ b/solution.py
@@ -176,10 +176,11 @@
 
 def middle_kernel(blocks, outs, tokens, spot, count, *rest):
     pieces, rest = rest[:blocks], rest[blocks:]
-    att_ref, states_ref, up_ref, teach_ref, valid_ref, gain_ref = rest[:6]
+    sources, valid_ref, gain_ref = rest[:4], rest[4], rest[5]
     layer_ref, mid_ref, agrad_ref, sums_ref = rest[6:10]
     grads, rest = rest[10 : 10 + outs], rest[10 + outs :]
-    wo, wu, wd, hidden, pre, n2t, olt, slots, marks, sems, out_sems, mark_sems = rest
+    wo, wu, wd, hidden, pre, n2t, olt, slots, marks, sems, out_sems, mark_sems, *rest = rest
+    att_ref, states_ref, up_ref, teach_ref, in_sems = rest
     seq, width = att_ref.shape
     units = wu.shape[1]
     blocked = outs == 2
@@ -202,7 +203,12 @@
         (width // 2, units // 2, units // 2),
         sems,
     )
-    for copy in mark_copies + copies[::3] + copies[1::3] + copies[2::3]:
+    loads = [
+        pltpu.make_async_copy(source, target, in_sems.at[n])
+        for n, (source, target) in enumerate(zip(sources, (att_ref, states_ref, up_ref, teach_ref)))
+    ]
+    early = mark_copies + loads[:1] + copies[::3] + loads[1:2]
+    for copy in early + copies[1::3] + copies[2::3] + loads[2:]:
         copy.start()
     for copy in mark_copies:
         copy.wait()
@@ -212,7 +218,7 @@
         total_valid += jnp.sum(by_lane, axis=1, keepdims=True)
     factor = tokens / total_valid
     sums_ref[...] = jnp.broadcast_to(total_valid, sums_ref.shape)
-    for copy in copies[::3]:
+    for copy in loads[:1] + copies[::3] + loads[1:2]:
         copy.wait()
     mid_ref[...] = states_ref[...] + dot(att_ref[...], wo[...])
     middle = mid_ref[...]
@@ -231,7 +237,7 @@
         return 0
 
     lax.fori_loop(0, steps, up_step, 0)
-    for copy in copies[2::3]:
+    for copy in copies[2::3] + loads[2:]:
         copy.wait()
     layer_ref[...] = mid_ref[...] + dot_nt(hidden[...], wd[...])
     layer = layer_ref[...]
@@ -336,7 +342,7 @@
         ]
     return pl.pallas_call(
         functools.partial(middle_kernel, len(pieces), len(grads), tokens),
-        in_specs=[SMEM, SMEM] + [ANY] * len(pieces) + [VMEM] * 6,
+        in_specs=[SMEM, SMEM] + [ANY] * (len(pieces) + 4) + [VMEM] * 2,
         out_specs=[VMEM] * 4 + [ANY] * len(grads),
         out_shape=[
             full,
@@ -358,6 +364,11 @@
             pltpu.SemaphoreType.DMA((96,)),
             pltpu.SemaphoreType.DMA((2, 16)),
             pltpu.SemaphoreType.DMA((32,)),
+            pltpu.VMEM((seq, width), BF16),
+            pltpu.VMEM((seq, width), F32),
+            pltpu.VMEM((seq, width), F32),
+            pltpu.VMEM((seq, width), F32),
+            pltpu.SemaphoreType.DMA((4,)),
         ],
         compiler_params=PARAMS,
         name="middle",
@@ -604,25 +615,36 @@
     return functools.reduce(jnp.add, [t.astype(F32) for t in terms])
 
 
-def reduce_core(keep, other):
-    mine = add_low(keep, other).astype(BF16)
-    return mine, mine[2:, :2], mine[1::2, 2:]
+def core_sum(terms, *index):
+    return add_low(*[term[index] for term in terms])
+
+
+def reduce_core(terms):
+    low, high = slice(0, 2), slice(2, 4)
+    planes = slice(2, 4), slice(1, 4, 2)
+    return [core_sum(terms, p, z).astype(BF16) for p, z in zip(planes, (low, high))]
 
 
 def reduce_first(over_y, over_x, total):
     return exchange(over_y, Y_BIT, total), exchange(over_x, X_BIT, total)
 
 
-def reduce_sides(mine, over_y, over_x):
-    return add_low(mine[1, :2], over_y[1]).astype(BF16), add_low(mine[2, 2:], over_x[1]).astype(BF16)
+def reduce_sides(terms, over_y, over_x):
+    return [
+        (core_sum(terms, plane, z) + over[1]).astype(BF16)
+        for plane, z, over in ((1, slice(0, 2), over_y), (2, slice(2, 4), over_x))
+    ]
 
 
 def reduce_second(side_x, side_y, total):
     return exchange(side_x, X_BIT, total), exchange(side_y, Y_BIT, total)
 
 
-def reduce_own(mine, over_y, over_x):
-    return add_low(mine[0, :2], over_y[0]), add_low(mine[0, 2:], over_x[0])
+def reduce_own(terms, over_y, over_x):
+    return [
+        core_sum(terms, 0, z) + over[0]
+        for z, over in ((slice(0, 2), over_y), (slice(2, 4), over_x))
+    ]
 
 
 def reduce_line(head, tail, side_x, side_y):
@@ -727,12 +749,10 @@
         second_gain[None],
         units,
     )
-    total_valid = sums[3, 0]
     nt = normed.T
     if blocked:
-        ffn_mine, *first, attended_grad = lax.optimization_barrier(
-            (*reduce_core(grads[0], exchange(grads[1], CORE_BIT, total)), attended_grad)
-        )
+        ffn_mine = grads[0], exchange(grads[1], CORE_BIT, total)
+        *first, attended_grad = lax.optimization_barrier((*reduce_core(ffn_mine), attended_grad))
         ffn_first = reduce_first(*first, total)
     else:
         up_grad, down_grad, output_grad = (scatter_whole(g) for g in grads)
@@ -746,7 +766,8 @@
         )
         other = exchange(send, CORE_BIT, total)
         ffn_sides = reduce_second(*reduce_sides(ffn_mine, *ffn_first), total)
-        mine, *first, dq, dk, dv = lax.optimization_barrier((*reduce_core(keep, other), dq, dk, dv))
+        mine = keep, other
+        *first, dq, dk, dv = lax.optimization_barrier((*reduce_core(mine), dq, dk, dv))
         first = reduce_first(*first, total)
         input_grad, small = input_block(
             spot, qkv, dq, dk, dv, states, mid_grad, first_gain[None], sums, mix
@@ -766,6 +787,7 @@
         ffn = with_layout_constraint(ffn, Layout((0, 1)))
         head, tail, ffn = lax.optimization_barrier((*reduce_own(mine, *first), ffn))
         line = reduce_line(head, tail, *sides)
+        total_valid = sums[3, 0] + late(line, 0)
         attn = add_low(line[0], *reduce_far(line, total))
         half = units // col_total
         up_grad, output_grad, down_grad, small = jnp.split(
@@ -782,6 +804,7 @@
             spot, qkv, dq, dk, dv, states, mid_grad, first_gain[None], sums, mix
         )
         small = lax.psum(small, AXES)
+        total_valid = sums[3, 0]
     parts = features // 128
     first_grad = small[:parts].reshape(-1)
     second_grad = small[parts : 2 * parts].reshape(-1)

time: 265 us -> 265 us (level)
  other arithmetic: 16.9 us -> 20.9 us
    convert_element_type x4, other arithmetic: 7.25 us -> 10.8 us  [the longest x2 7.1 us: reduce_core(): core_sum(terms, p, z).astype(BF16)]
    slice x3 -> x1, local copies, waits for them, and re-layouts: 3.91 us -> 1.2 us  [shards(): total_valid = sums[3, 0] + late(line, 0)]
  transfers between devices with their start and end apart: 38 -> 38, of which waited for: 24 -> 22; matrix products, arithmetic and copies ran while one was open for 10% -> 10% of each run, Pallas kernels for 22% -> 22%
where the time goes in v7:
time: 265 us
  Pallas kernels  94.8 us (36%)
  waiting for transfers between devices  82 us (31%)
  starting transfers between devices  42.3 us (16%)
  other arithmetic  20.9 us (8%)
  local copies, waits for them, and re-layouts  17.3 us (7%)
  between operations  7.22 us (3%)
    ppermute x37, waiting for transfers between devices, exchange(): return lax.ppermute(value, AXES, [(i, i ^ mask) for i in range(total)])  77.9 us
    ppermute x37, starting transfers between devices, exchange(): return lax.ppermute(value, AXES, [(i, i ^ mask) for i in range(total)])  37.3 us
    pallas_call x1, Pallas kernels, middle_block(): pl.pallas_call(functools.partial(middle_kernel, len(pieces), len(grads),...  35.7 us
    pallas_call x1, Pallas kernels, attend_back(): pl.pallas_call(functools.partial(attend_back_kernel, blocked), grid=(HEAD...  28.9 us
    pallas_call x1, Pallas kernels, attend(): pl.pallas_call(functools.partial(attend_kernel, len(pieces)), grid=(HEADS...  21.1 us
    pallas_call x1, Pallas kernels, input_block(): pl.pallas_call(functools.partial(input_kernel, len(pieces)), in_specs=[SM...  9.04 us
    convert_element_type x2, other arithmetic, reduce_core(): core_sum(terms, p, z).astype(BF16)  7.1 us
  transfers between devices with their start and end apart: 38, of which 22 were waited for; matrix products, arithmetic and copies ran while one was open for 10% of the time, Pallas kernels for 22%

profile of v7, /device:TPU:0, one launch (start us, length us, event | category | flops | bytes accessed | tf_op | source)
XLA Modules:
  0.0 264.5 jit_solution(5910290798581012878)
XLA Ops:
  3.0 5.1 %collective-permute-start.2 = (bf16[144,384]{1,0:T(8,128)(2,1)S(1)}, bf16[144,384]{1,0:T(8,128)(2,1)S(1)}, u32[]{:S(2)}, u32[]{:S(2)}) collective-permute-start(bf16[144,384]{1,0:T(8,128)(2,1)S(1)} %constant_dynamic-update-slice_fusion), channel_id=1, source_target_pairs={{0,24},{1,25},{2,26},{3,27},{4,28},{5,29},{6,30},{7,31},{8,16},{9,... | collective-permute-start | bytes 331784 | tf_op jit(solution)/shard_map/ppermute | solution.py:583
  11.7 5.0 %all-to-all-start = ((bf16[4,48,3584]{2,1,0:T(8,128)(2,1)}), bf16[4,48,3584]{2,1,0:T(8,128)(2,1)}, u32[]{:S(2)}, u32[]{:S(2)}) async-start(bf16[4,48,3584]{2,1,0:T(8,128)(2,1)} %broadcast_in_dim.27), calls=%async_computation | async-start | bytes 2752512 | tf_op jit(solution)/shard_map/all_to_all | solution.py:591
  17.4 1.6 collective-permute-start.4
  20.5 8.2 %collective-permute-done.4 = bf16[4,144,384]{2,1,0:T(8,128)(2,1)S(1)} collective-permute-done((bf16[4,144,384]{2,1,0:T(8,128)(2,1)S(1)}, bf16[4,144,384]{2,1,0:T(8,128)(2,1)S(1)}, u32[]{:S(2)}, u32[]{:S(2)}) %collective-permute-start.4) | collective-permute-done | bytes 442400 | tf_op jit(solution)/shard_map/ppermute | solution.py:583
  34.2 5.2 %collective-permute-done.5 = bf16[2,144,384]{2,1,0:T(8,128)(2,1)S(1)} collective-permute-done((bf16[2,144,384]{2,1,0:T(8,128)(2,1)S(1)}, bf16[2,144,384]{2,1,0:T(8,128)(2,1)S(1)}, u32[]{:S(2)}, u32[]{:S(2)}) %collective-permute-start.5) | collective-permute-done | bytes 221216 | tf_op jit(solution)/shard_map/ppermute | solution.py:583
  44.6 4.0 %all-to-all-done.rest_0_ = bf16[4,48,3584]{2,1,0:T(8,128)(2,1)} async-done(((bf16[4,48,3584]{2,1,0:T(8,128)(2,1)}), bf16[4,48,3584]{2,1,0:T(8,128)(2,1)}, u32[]{:S(2)}, u32[]{:S(2)}) %all-to-all-start) | async-done | bytes 1376288 | tf_op jit(solution)/shard_map/all_to_all | solution.py:591
  51.7 21.1 %attend.1 = (bf16[512,768]{1,0:T(8,128)(2,1)}, bf16[512,768]{1,0:T(8,128)(2,1)}, bf16[512,768]{1,0:T(8,128)(2,1)}, bf16[512,768]{1,0:T(8,128)(2,1)}, bf16[12,256,768]{2,1,0:T(8,128)(2,1)}) custom-call(s32[4]{0:T(128)} %pad_add_fusion.spot, s32[1,2]{1,0:T(1,128)} %starts.1, bf16[512,768]{1,0:T(8,128)(2,1)} %copy.40.normed_ref, ...), custom_call_target="tpu_custom_call" | custom-call | flops 20000000000 | bytes 1000000 | tf_op jit(solution)/shard_map/attend/pallas_call | solution.py:158
  72.8 7.3 %collective-permute-done.10.rest_2_ = bf16[4,48,3584]{2,1,0:T(8,128)(2,1)S(1)} collective-permute-done((bf16[4,48,3584]{2,1,0:T(8,128)(2,1)}, bf16[4,48,3584]{2,1,0:T(8,128)(2,1)S(1)}, u32[]{:S(2)}, u32[]{:S(2)}) %collective-permute-start.10) | collective-permute-done | bytes 1376288 | tf_op jit(solution)/shard_map/ppermute | solution.py:583
  85.4 12.8 %collective-permute-done.11.rest_3_ = bf16[2,48,3584]{2,1,0:T(8,128)(2,1)} collective-permute-done((bf16[2,48,3584]{2,1,0:T(8,128)(2,1)S(1)}, bf16[2,48,3584]{2,1,0:T(8,128)(2,1)}, u32[]{:S(2)}, u32[]{:S(2)}) %collective-permute-start.11) | collective-permute-done | bytes 688160 | tf_op jit(solution)/shard_map/ppermute | solution.py:583
  101.7 35.7 %middle.1 = (f32[512,768]{1,0:T(8,128)}, f32[512,768]{1,0:T(8,128)}, bf16[512,768]{1,0:T(8,128)(2,1)}, f32[8,768]{1,0:T(8,128)}, bf16[4,4,48,3456]{3,2,1,0:T(8,128)(2,1)}, /*index=5*/bf16[4,4,48,3456]{3,2,1,0:T(8,128)(2,1)}) custom-call(s32[4]{0:T(128)} %pad_add_fusion.spot, f32[1,1]{1,0:T(1,128)} %constant.55.clone.1.count, ...), custom_call_target="tpu_custom_call" | custom-call | flops 35000000512 | bytes 1000000 | tf_op jit(solution)/shard_map/middle/pallas_call | solution.py:343
  138.7 7.7 %collective-permute-done.18 = bf16[4,4,48,3456]{3,2,1,0:T(8,128)(2,1)S(1)} collective-permute-done((bf16[4,4,48,3456]{3,2,1,0:T(8,128)(2,1)}, bf16[4,4,48,3456]{3,2,1,0:T(8,128)(2,1)S(1)}, u32[]{:S(2)}, u32[]{:S(2)}) %collective-permute-start.18) | collective-permute-done | bytes 5308448 | tf_op jit(solution)/shard_map/ppermute | solution.py:583
  146.4 5.8 %add_convert_fusion = (bf16[2,2,48,3456]{3,2,1,0:T(8,128)(2,1)}, bf16[2,2,48,3456]{3,2,1,0:T(8,128)(2,1)}) fusion(bf16[4,4,48,3456]{3,2,1,0:T(8,128)(2,1)S(1)} %collective-permute-done.18, bf16[4,4,48,3456]{3,2,1,0:T(8,128)(2,1)} %get-tuple-element.95), kind=kLoop, calls=%fused_computation.1 | loop fusion | flops 5308416 | bytes 7962624 | tf_op jit(solution)/shard_map/convert_element_type | solution.py:625
  154.8 28.9 %attend_back.1 = (bf16[512,768]{1,0:T(8,128)(2,1)}, bf16[512,768]{1,0:T(8,128)(2,1)}, bf16[512,768]{1,0:T(8,128)(2,1)}, f32[16,128]{1,0:T(8,128)}, bf16[4,4,144,...) custom-call(s32[4]{0:T(128)} %pad_add_fusion.spot, f32[12,12]{1,0:T(8,128)} %copy-done.8, f32[12,12]{1,0:T(8,128)} %pos.1, ...), custom_call_target="tpu_custom_call" | custom-call | flops 28000000000 | bytes 1000000 | tf_op jit(solution)/shard_map/attend_back/pallas_call | solution.py:502
  186.3 3.4 %fusion.5 = (bf16[2,48,3456]{2,1,0:T(8,128)(2,1)}, bf16[2,48,3456]{2,1,0:T(8,128)(2,1)}) fusion(bf16[4,4,48,3456]{3,2,1,0:T(8,128)(2,1)} %copy-done.1, bf16[2,2,48,3456]{3,2,1,0:T(8,128)(2,1)} %collective-permute-done.20, bf16[4,4,48,3456]{3,2,1,0:T(8,128)(2,1)S(1)} %bitcast.78, bf16[2,2,48,3456]{3,2,1,0:T(8,128)(2,1)} %collective-permute-done.19), kind=kLoop, calls=%fused_computation.18 | loop fusion | flops 3981312 | bytes 5308416 | tf_op jit(solution)/shard_map/convert_element_type | solution.py:634
  193.6 9.0 %input_grad.1 = (f32[512,768]{1,0:T(8,128)}, f32[24,128]{1,0:T(8,128)}) custom-call(s32[4]{0:T(128)} %pad_add_fusion.spot, bf16[3,4,144,384]{3,2,1,0:T(8,128)(2,1)} %pad_maximum_fusion.1.rest_0_, bf16[2,2,144,384]{3,2,1,0:T(8,128)(2,1)} %pad_maximum_fusion.3.rest_1_, bf16[3,4,144,384]{3,2,1,0:T(8,128)(2,1)} %collective-permute-done.7.rest_2_, ...), custom_call_target="tpu_custom_call" | custom-call | flops 8999999488 | bytes 1000000 | tf_op jit(solution)/shard_map/input_grad/pallas_call | solution.py:567
  202.7 4.6 %collective-permute-done.25 = bf16[2,48,3456]{2,1,0:T(8,128)(2,1)} collective-permute-done((bf16[2,48,3456]{2,1,0:T(8,128)(2,1)}, bf16[2,48,3456]{2,1,0:T(8,128)(2,1)}, u32[]{:S(2)}, u32[]{:S(2)}) %collective-permute-start.25) | collective-permute-done | bytes 663584 | tf_op jit(solution)/shard_map/ppermute | solution.py:583
  210.6 2.7 %bitcast_add_fusion.1 = (f32[2,48,3456]{2,1,0:T(8,128)S(1)}, f32[2,48,3456]{2,1,0:T(8,128)S(1)}) fusion(bf16[2,48,3456]{2,1,0:T(8,128)(2,1)} %collective-permute-done.24, bf16[4,4,48,3456]{3,2,1,0:T(8,128)(2,1)} %copy-done.1, bf16[2,2,48,3456]{3,2,1,0:T(8,128)(2,1)} %collective-permute-done.19, bf16[4,4,48,3456]{3,2,1,0:T(8,128)(2,1)S(1)} %bitcast.78, ...), kind=kLoop, calls=%fused_computation.7 | loop fusion | flops 4644864 | bytes 7962624 | tf_op jit(solution)/shard_map/add | solution.py:615
  213.7 4.3 %collective-permute-start.27 = (bf16[48,3584]{1,0:T(8,128)(2,1)S(1)}, bf16[48,3584]{1,0:T(8,128)(2,1)S(1)}, u32[]{:S(2)}, u32[]{:S(2)}) collective-permute-start(bf16[48,3584]{1,0:T(8,128)(2,1)S(1)} %get-tuple-element.152), channel_id=1, source_target_pairs={{0,8},{1,9},{2,10},{3,11},{4,12},{5,13},{6,14},{7,15},{8,0},{9,1},... | collective-permute-start | bytes 1032200 | tf_op jit(solution)/shard_map/ppermute | solution.py:583
  218.0 2.7 %collective-permute-done.22 = bf16[2,2,144,384]{3,2,1,0:T(8,128)(2,1)S(1)} collective-permute-done((bf16[2,2,144,384]{3,2,1,0:T(8,128)(2,1)}, bf16[2,2,144,384]{3,2,1,0:T(8,128)(2,1)S(1)}, u32[]{:S(2)}, u32[]{:S(2)}) %collective-permute-start.22) | collective-permute-done | bytes 442400 | tf_op jit(solution)/shard_map/ppermute | solution.py:583
  221.9 1.6 collective-permute-start.30
  224.8 3.9 %collective-permute-done.30 = bf16[2,144,384]{2,1,0:T(8,128)(2,1)S(1)} collective-permute-done((bf16[2,144,384]{2,1,0:T(8,128)(2,1)S(1)}, bf16[2,144,384]{2,1,0:T(8,128)(2,1)S(1)}, u32[]{:S(2)}, u32[]{:S(2)}) %collective-permute-start.30) | collective-permute-done | bytes 221216 | tf_op jit(solution)/shard_map/ppermute | solution.py:583
  229.9 13.6 %collective-permute-done.28 = bf16[48,3584]{1,0:T(8,128)(2,1)S(1)} collective-permute-done((bf16[48,3584]{1,0:T(8,128)(2,1)S(1)}, bf16[48,3584]{1,0:T(8,128)(2,1)S(1)}, u32[]{:S(2)}, u32[]{:S(2)}) %collective-permute-start.28) | collective-permute-done | bytes 344096 | tf_op jit(solution)/shard_map/ppermute | solution.py:583
  246.4 3.1 %collective-permute-done.31 = f32[24,128]{1,0:T(8,128)S(1)} collective-permute-done((f32[24,128]{1,0:T(8,128)S(1)}, f32[24,128]{1,0:T(8,128)S(1)}, u32[]{:S(2)}, u32[]{:S(2)}) %collective-permute-start.31) | collective-permute-done | bytes 12320 | tf_op jit(solution)/shard_map/ppermute | solution.py:583
  251.6 3.2 %collective-permute-start.35 = (bf16[144,384]{1,0:T(8,128)(2,1)S(1)}, bf16[144,384]{1,0:T(8,128)(2,1)S(1)}, u32[]{:S(2)}, u32[]{:S(2)}) collective-permute-start(bf16[144,384]{1,0:T(8,128)(2,1)S(1)} %get-tuple-element.158), channel_id=1, source_target_pairs={{0,16},{1,17},{2,18},{3,19},{4,20},{5,21},{6,22},{7,23},{8,24},{9,... | collective-permute-start | bytes 331784 | tf_op jit(solution)/shard_map/ppermute | solution.py:583
  (152 shorter events, 56.6 us)
Async XLA Ops:
  3.0 13.7 %collective-permute-start.2 = (bf16[144,384]{1,0:T(8,128)(2,1)S(1)}, bf16[144,384]{1,0:T(8,128)(2,1)S(1)}, u32[]{:S(2)}, u32[]{:S(2)}) collective-permute-start(bf16[144,384]{1,0:T(8,128)(2,1)S(1)} %constant_dynamic-update-slice_fusion), channel_id=1, source_target_pairs={{0,24},{1,25},{2,26},{3,27},{4,28},{5,29},{6,30},{7,31},{8,16},{9,... | collective-permute-start | bytes 331784 | tf_op jit(solution)/shard_map/ppermute | solution.py:583
  8.1 9.3 %collective-permute-start.1 = (bf16[144,384]{1,0:T(8,128)(2,1)S(1)}, bf16[144,384]{1,0:T(8,128)(2,1)S(1)}, u32[]{:S(2)}, u32[]{:S(2)}) collective-permute-start(bf16[144,384]{1,0:T(8,128)(2,1)S(1)} %constant_dynamic-update-slice_fusion), channel_id=1, source_target_pairs={{0,16},{1,17},{2,18},{3,19},{4,20},{5,21},{6,22},{7,23},{8,24},{9,... | collective-permute-start | bytes 331784 | tf_op jit(solution)/shard_map/ppermute | solution.py:583
  8.1 9.3 %collective-permute-start = (bf16[144,384]{1,0:T(8,128)(2,1)S(1)}, bf16[144,384]{1,0:T(8,128)(2,1)S(1)}, u32[]{:S(2)}, u32[]{:S(2)}) collective-permute-start(bf16[144,384]{1,0:T(8,128)(2,1)S(1)} %constant_dynamic-update-slice_fusion), channel_id=1, source_target_pairs={{0,8},{1,9},{2,10},{3,11},{4,12},{5,13},{6,14},{7,15},{8,0},{9,1},... | collective-permute-start | bytes 331784 | tf_op jit(solution)/shard_map/ppermute | solution.py:583
  11.7 37.0 %all-to-all-start = ((bf16[4,48,3584]{2,1,0:T(8,128)(2,1)}), bf16[4,48,3584]{2,1,0:T(8,128)(2,1)}, u32[]{:S(2)}, u32[]{:S(2)}) async-start(bf16[4,48,3584]{2,1,0:T(8,128)(2,1)} %broadcast_in_dim.27), calls=%async_computation | async-start | bytes 2752512 | tf_op jit(solution)/shard_map/all_to_all | solution.py:591
  17.4 11.3 %collective-permute-start.4 = (bf16[4,144,384]{2,1,0:T(8,128)(2,1)S(1)}, bf16[4,144,384]{2,1,0:T(8,128)(2,1)S(1)}, u32[]{:S(2)}, u32[]{:S(2)}) collective-permute-start(bf16[4,144,384]{2,1,0:T(8,128)(2,1)S(1)} %pad_maximum_fusion.2), channel_id=1, source_target_pairs={{0,4},{1,5},{2,6},{3,7},{4,0},{5,1},{6,2},{7,3},{8,12},{9,13},{10,... | collective-permute-start | bytes 1327112 | tf_op jit(solution)/shard_map/ppermute | solution.py:583
  19.0 11.0 %collective-permute-start.3 = (bf16[4,144,384]{2,1,0:T(8,128)(2,1)S(1)}, bf16[4,144,384]{2,1,0:T(8,128)(2,1)S(1)}, u32[]{:S(2)}, u32[]{:S(2)}) collective-permute-start(bf16[4,144,384]{2,1,0:T(8,128)(2,1)S(1)} %pad_maximum_fusion.2), channel_id=1, source_target_pairs={{0,1},{1,0},{2,3},{3,2},{4,5},{5,4},{6,7},{7,6},{8,9},{9,8},{10,11... | collective-permute-start | bytes 1327112 | tf_op jit(solution)/shard_map/ppermute | solution.py:583
  31.3 13.3 %collective-permute-start.7 = (bf16[3,4,144,384]{3,2,1,0:T(8,128)(2,1)}, bf16[3,4,144,384]{3,2,1,0:T(8,128)(2,1)}, u32[]{:S(2)}, u32[]{:S(2)}) collective-permute-start(bf16[3,4,144,384]{3,2,1,0:T(8,128)(2,1)} %pad_maximum_fusion.1.rest_0_), channel_id=1, source_target_pairs={{0,2},{1,3},{2,0},{3,1},{4,6},{5,7},{6,4},{7,5},{8,10},{9,11},{10,... | collective-permute-start | bytes 3981320 | tf_op jit(solution)/shard_map/ppermute | solution.py:583
  48.7 31.4 %collective-permute-start.10 = (bf16[4,48,3584]{2,1,0:T(8,128)(2,1)}, bf16[4,48,3584]{2,1,0:T(8,128)(2,1)S(1)}, u32[]{:S(2)}, u32[]{:S(2)}) collective-permute-start(bf16[4,48,3584]{2,1,0:T(8,128)(2,1)} %all-to-all-done.rest_0_), channel_id=1, source_target_pairs={{0,4},{1,5},{2,6},{3,7},{4,0},{5,1},{6,2},{7,3},{8,12},{9,13},{10,... | collective-permute-start | bytes 4128776 | tf_op jit(solution)/shard_map/ppermute | solution.py:583
  50.2 31.2 %collective-permute-start.9 = (bf16[4,48,3584]{2,1,0:T(8,128)(2,1)}, bf16[4,48,3584]{2,1,0:T(8,128)(2,1)}, u32[]{:S(2)}, u32[]{:S(2)}) collective-permute-start(bf16[4,48,3584]{2,1,0:T(8,128)(2,1)} %all-to-all-done.rest_0_), channel_id=1, source_target_pairs={{0,1},{1,0},{2,3},{3,2},{4,5},{5,4},{6,7},{7,6},{8,9},{9,8},{10,11... | collective-permute-start | bytes 4128776 | tf_op jit(solution)/shard_map/ppermute | solution.py:583
  82.7 15.5 %collective-permute-start.11 = (bf16[2,48,3584]{2,1,0:T(8,128)(2,1)S(1)}, bf16[2,48,3584]{2,1,0:T(8,128)(2,1)}, u32[]{:S(2)}, u32[]{:S(2)}) collective-permute-start(bf16[2,48,3584]{2,1,0:T(8,128)(2,1)S(1)} %slice.200), channel_id=1, source_target_pairs={{0,4},{1,5},{2,6},{3,7},{4,0},{5,1},{6,2},{7,3},{8,12},{9,13},{10,... | collective-permute-start | bytes 2064392 | tf_op jit(solution)/shard_map/ppermute | solution.py:583
  83.4 15.5 %collective-permute-start.12 = (bf16[2,48,3584]{2,1,0:T(8,128)(2,1)S(1)}, bf16[2,48,3584]{2,1,0:T(8,128)(2,1)}, u32[]{:S(2)}, u32[]{:S(2)}) collective-permute-start(bf16[2,48,3584]{2,1,0:T(8,128)(2,1)S(1)} %slice.201), channel_id=1, source_target_pairs={{0,1},{1,0},{2,3},{3,2},{4,5},{5,4},{6,7},{7,6},{8,9},{9,8},{10,11... | collective-permute-start | bytes 2064392 | tf_op jit(solution)/shard_map/ppermute | solution.py:583
  84.9 16.7 %collective-permute-start.13 = (bf16[4,48,3584]{2,1,0:T(8,128)(2,1)}, bf16[4,48,3584]{2,1,0:T(8,128)(2,1)}, u32[]{:S(2)}, u32[]{:S(2)}) collective-permute-start(bf16[4,48,3584]{2,1,0:T(8,128)(2,1)} %all-to-all-done.rest_0_), channel_id=1, source_target_pairs={{0,2},{1,3},{2,0},{3,1},{4,6},{5,7},{6,4},{7,5},{8,10},{9,11},{10,... | collective-permute-start | bytes 4128776 | tf_op jit(solution)/shard_map/ppermute | solution.py:583
  84.9 16.7 %collective-permute-start.14 = (bf16[4,48,3584]{2,1,0:T(8,128)(2,1)}, bf16[4,48,3584]{2,1,0:T(8,128)(2,1)}, u32[]{:S(2)}, u32[]{:S(2)}) collective-permute-start(bf16[4,48,3584]{2,1,0:T(8,128)(2,1)} %collective-permute-done.9.rest_1_), channel_id=1, source_target_pairs={{0,2},{1,3},{2,0},{3,1},{4,6},{5,7},{6,4},{7,5},{8,10},{9,11},{10,... | collective-permute-start | bytes 4128776 | tf_op jit(solution)/shard_map/ppermute | solution.py:583
  85.4 16.2 %collective-permute-start.15 = (bf16[4,48,3584]{2,1,0:T(8,128)(2,1)S(1)}, bf16[4,48,3584]{2,1,0:T(8,128)(2,1)}, u32[]{:S(2)}, u32[]{:S(2)}) collective-permute-start(bf16[4,48,3584]{2,1,0:T(8,128)(2,1)S(1)} %collective-permute-done.10.rest_2_), channel_id=1, source_target_pairs={{0,2},{1,3},{2,0},{3,1},{4,6},{5,7},{6,4},{7,5},{8,10},{9,11},{10,... | collective-permute-start | bytes 4128776 | tf_op jit(solution)/shard_map/ppermute | solution.py:583
  152.2 31.5 %collective-permute-start.19 = (bf16[2,2,48,3456]{3,2,1,0:T(8,128)(2,1)}, bf16[2,2,48,3456]{3,2,1,0:T(8,128)(2,1)}, u32[]{:S(2)}, u32[]{:S(2)}) collective-permute-start(bf16[2,2,48,3456]{3,2,1,0:T(8,128)(2,1)} %get-tuple-element.98), channel_id=1, source_target_pairs={{0,4},{1,5},{2,6},{3,7},{4,0},{5,1},{6,2},{7,3},{8,12},{9,13},{10,... | collective-permute-start | bytes 3981320 | tf_op jit(solution)/shard_map/ppermute | solution.py:583
  153.3 31.2 %collective-permute-start.20 = (bf16[2,2,48,3456]{3,2,1,0:T(8,128)(2,1)}, bf16[2,2,48,3456]{3,2,1,0:T(8,128)(2,1)}, u32[]{:S(2)}, u32[]{:S(2)}) collective-permute-start(bf16[2,2,48,3456]{3,2,1,0:T(8,128)(2,1)} %get-tuple-element.99), channel_id=1, source_target_pairs={{0,1},{1,0},{2,3},{3,2},{4,5},{5,4},{6,7},{7,6},{8,9},{9,8},{10,11... | collective-permute-start | bytes 3981320 | tf_op jit(solution)/shard_map/ppermute | solution.py:583
  189.7 17.6 %collective-permute-start.25 = (bf16[2,48,3456]{2,1,0:T(8,128)(2,1)}, bf16[2,48,3456]{2,1,0:T(8,128)(2,1)}, u32[]{:S(2)}, u32[]{:S(2)}) collective-permute-start(bf16[2,48,3456]{2,1,0:T(8,128)(2,1)} %get-tuple-element.138), channel_id=1, source_target_pairs={{0,4},{1,5},{2,6},{3,7},{4,0},{5,1},{6,2},{7,3},{8,12},{9,13},{10,... | collective-permute-start | bytes 1990664 | tf_op jit(solution)/shard_map/ppermute | solution.py:583
  190.6 17.4 %collective-permute-start.24 = (bf16[2,48,3456]{2,1,0:T(8,128)(2,1)}, bf16[2,48,3456]{2,1,0:T(8,128)(2,1)}, u32[]{:S(2)}, u32[]{:S(2)}) collective-permute-start(bf16[2,48,3456]{2,1,0:T(8,128)(2,1)} %get-tuple-element.139), channel_id=1, source_target_pairs={{0,1},{1,0},{2,3},{3,2},{4,5},{5,4},{6,7},{7,6},{8,9},{9,8},{10,11... | collective-permute-start | bytes 1990664 | tf_op jit(solution)/shard_map/ppermute | solution.py:583
  208.0 12.8 %collective-permute-start.22 = (bf16[2,2,144,384]{3,2,1,0:T(8,128)(2,1)}, bf16[2,2,144,384]{3,2,1,0:T(8,128)(2,1)S(1)}, u32[]{:S(2)}, u32[]{:S(2)}) collective-permute-start(bf16[2,2,144,384]{3,2,1,0:T(8,128)(2,1)} %get-tuple-element.116), channel_id=1, source_target_pairs={{0,4},{1,5},{2,6},{3,7},{4,0},{5,1},{6,2},{7,3},{8,12},{9,13},{10,... | collective-permute-start | bytes 1327112 | tf_op jit(solution)/shard_map/ppermute | solution.py:583
  209.1 12.5 %collective-permute-start.23 = (bf16[2,2,144,384]{3,2,1,0:T(8,128)(2,1)}, bf16[2,2,144,384]{3,2,1,0:T(8,128)(2,1)S(1)}, u32[]{:S(2)}, u32[]{:S(2)}) collective-permute-start(bf16[2,2,144,384]{3,2,1,0:T(8,128)(2,1)} %get-tuple-element.117), channel_id=1, source_target_pairs={{0,1},{1,0},{2,3},{3,2},{4,5},{5,4},{6,7},{7,6},{8,9},{9,8},{10,11... | collective-permute-start | bytes 1327112 | tf_op jit(solution)/shard_map/ppermute | solution.py:583
  213.6 16.3 %collective-permute-start.29 = (bf16[48,3584]{1,0:T(8,128)(2,1)S(1)}, bf16[48,3584]{1,0:T(8,128)(2,1)S(1)}, u32[]{:S(2)}, u32[]{:S(2)}) collective-permute-start(bf16[48,3584]{1,0:T(8,128)(2,1)S(1)} %get-tuple-element.150), channel_id=1, source_target_pairs={{0,24},{1,25},{2,26},{3,27},{4,28},{5,29},{6,30},{7,31},{8,16},{9,... | collective-permute-start | bytes 1032200 | tf_op jit(solution)/shard_map/ppermute | solution.py:583
  213.7 29.8 %collective-permute-start.28 = (bf16[48,3584]{1,0:T(8,128)(2,1)S(1)}, bf16[48,3584]{1,0:T(8,128)(2,1)S(1)}, u32[]{:S(2)}, u32[]{:S(2)}) collective-permute-start(bf16[48,3584]{1,0:T(8,128)(2,1)S(1)} %get-tuple-element.151), channel_id=1, source_target_pairs={{0,16},{1,17},{2,18},{3,19},{4,20},{5,21},{6,22},{7,23},{8,24},{9,... | collective-permute-start | bytes 1032200 | tf_op jit(solution)/shard_map/ppermute | solution.py:583
  213.7 29.8 %collective-permute-start.27 = (bf16[48,3584]{1,0:T(8,128)(2,1)S(1)}, bf16[48,3584]{1,0:T(8,128)(2,1)S(1)}, u32[]{:S(2)}, u32[]{:S(2)}) collective-permute-start(bf16[48,3584]{1,0:T(8,128)(2,1)S(1)} %get-tuple-element.152), channel_id=1, source_target_pairs={{0,8},{1,9},{2,10},{3,11},{4,12},{5,13},{6,14},{7,15},{8,0},{9,1},... | collective-permute-start | bytes 1032200 | tf_op jit(solution)/shard_map/ppermute | solution.py:583
  223.8 22.5 %collective-permute-start.34 = (bf16[2,144,384]{2,1,0:T(8,128)(2,1)S(1)}, bf16[2,144,384]{2,1,0:T(8,128)(2,1)S(1)}, u32[]{:S(2)}, u32[]{:S(2)}) collective-permute-start(bf16[2,144,384]{2,1,0:T(8,128)(2,1)S(1)} %get-tuple-element.142), channel_id=1, source_target_pairs={{0,4},{1,5},{2,6},{3,7},{4,0},{5,1},{6,2},{7,3},{8,12},{9,13},{10,... | collective-permute-start | bytes 663560 | tf_op jit(solution)/shard_map/ppermute | solution.py:583
  (30 other events, 245.5 us)

commit v8 on v7

--- a/solution.py
+++ b/solution.py
@@ -765,15 +765,23 @@
             (*ffn_first, dq, dk, dv, mix, *grads)
         )
         other = exchange(send, CORE_BIT, total)
-        ffn_sides = reduce_second(*reduce_sides(ffn_mine, *ffn_first), total)
+        half = units // col_total
+        ahead = half + width
+        ffn_sides = reduce_sides(ffn_mine, *ffn_first)
+        down_sides = reduce_second(*[side[..., ahead:] for side in ffn_sides], total)
+        ffn_sides = reduce_second(*[side[..., :ahead] for side in ffn_sides], total)
         mine = keep, other
         *first, dq, dk, dv = lax.optimization_barrier((*reduce_core(mine), dq, dk, dv))
         first = reduce_first(*first, total)
         input_grad, small = input_block(
             spot, qkv, dq, dk, dv, states, mid_grad, first_gain[None], sums, mix
         )
-        *ffn_sides, small = lax.optimization_barrier((*ffn_sides, small))
-        ffn_line = reduce_line(*reduce_own(ffn_mine, *ffn_first), *ffn_sides)
+        *down_sides, small, input_grad = lax.optimization_barrier((*down_sides, small, input_grad))
+        own = reduce_own(ffn_mine, *ffn_first)
+        down_line = reduce_line(*[o[..., ahead:] for o in own], *down_sides)
+        down = reduce_far(down_line, total)
+        *ffn_sides, small, tie = lax.optimization_barrier((*ffn_sides, small, down_line[:1, :1, :1]))
+        ffn_line = reduce_line(*[o[..., :ahead] for o in own], *ffn_sides) + late(tie, 3)
         small += exchange(small, CORE_BIT, total)
         near = lax.reduce_precision(small, 8, 7)
         small = jnp.broadcast_to(jnp.concatenate([near, small - near]), (4, depth, 128))
@@ -789,10 +797,8 @@
         line = reduce_line(head, tail, *sides)
         total_valid = sums[3, 0] + late(line, 0)
         attn = add_low(line[0], *reduce_far(line, total))
-        half = units // col_total
-        up_grad, output_grad, down_grad, small = jnp.split(
-            ffn, [half, half + width, 2 * half + width], axis=1
-        )
+        up_grad, output_grad, small = jnp.split(ffn, [half, ahead], axis=1)
+        down_grad = add_low(down_line[0], *down)
         small = small[: depth // 2] + small[depth // 2 :] + late(line, 2)
         for bit in (X_BIT, Y_BIT):
             small += exchange(small, bit, total)

time: 265 us -> 260 us (0.981)
  waiting for transfers between devices: 82 us -> 66.4 us
  starting transfers between devices: 42.3 us -> 49.9 us
  local copies, waits for them, and re-layouts: 17.3 us -> 20.3 us
    ppermute x37 -> x42, waiting for transfers between devices: 77.9 us -> 62.4 us  [exchange(): return lax.ppermute(value, AXES, [(i, i ^ mask) for i in range(total)])]
    ppermute x37 -> x42, starting transfers between devices: 37.3 us -> 44.8 us  [exchange(): return lax.ppermute(value, AXES, [(i, i ^ mask) for i in range(total)])]
    add x0 -> x2, other arithmetic: none -> 3.49 us  [the longest x1 3.39 us: reduce_own(): core_sum(terms, 0, z) + over[0]]
    convert_element_type x2 -> x1, other arithmetic: 3.69 us -> 0.33 us  [reduce_sides(): (core_sum(terms, plane, z) + over[1]).astype(BF16)]
    slice x0 -> x5, local copies, waits for them, and re-layouts: none -> 2.79 us  [the longest x2 1.52 us: shards(): ffn_sides = reduce_second(*[side[..., :ahead] for side in ffn_sides], total)]
  transfers between devices with their start and end apart: 38 -> 43, of which waited for: 22 -> 19; matrix products, arithmetic and copies ran while one was open for 10% -> 12% of each run, Pallas kernels for 22% -> 23%
where the time goes in v8:
time: 260 us; the launch traced here: 259 us
  Pallas kernels  94.8 us (36%)
  waiting for transfers between devices  66.4 us (26%)
  starting transfers between devices  49.9 us (19%)
  local copies, waits for them, and re-layouts  20.3 us (8%)
  other arithmetic  19.4 us (7%)
  between operations  7.96 us (3%)
    ppermute x42, waiting for transfers between devices, exchange(): return lax.ppermute(value, AXES, [(i, i ^ mask) for i in range(total)])  62.4 us
    ppermute x42, starting transfers between devices, exchange(): return lax.ppermute(value, AXES, [(i, i ^ mask) for i in range(total)])  44.8 us
    pallas_call x1, Pallas kernels, middle_block(): pl.pallas_call(functools.partial(middle_kernel, len(pieces), len(grads),...  35.8 us
    pallas_call x1, Pallas kernels, attend_back(): pl.pallas_call(functools.partial(attend_back_kernel, blocked), grid=(HEAD...  28.8 us
    pallas_call x1, Pallas kernels, attend(): pl.pallas_call(functools.partial(attend_kernel, len(pieces)), grid=(HEADS...  21.1 us
    pallas_call x1, Pallas kernels, input_block(): pl.pallas_call(functools.partial(input_kernel, len(pieces)), in_specs=[SM...  9.04 us
  transfers between devices with their start and end apart: 43, of which 19 were waited for; matrix products, arithmetic and copies ran while one was open for 12% of the time, Pallas kernels for 23%

profile of v8, /device:TPU:0, one launch (start us, length us, event | category | flops | bytes accessed | tf_op | source)
XLA Modules:
  0.0 258.7 jit_solution(16636098857429340667)
XLA Ops:
  3.0 5.1 %collective-permute-start.2 = (bf16[144,384]{1,0:T(8,128)(2,1)S(1)}, bf16[144,384]{1,0:T(8,128)(2,1)S(1)}, u32[]{:S(2)}, u32[]{:S(2)}) collective-permute-start(bf16[144,384]{1,0:T(8,128)(2,1)S(1)} %constant_dynamic-update-slice_fusion), channel_id=1, source_target_pairs={{0,24},{1,25},{2,26},{3,27},{4,28},{5,29},{6,30},{7,31},{8,16},{9,... | collective-permute-start | bytes 331784 | tf_op jit(solution)/shard_map/ppermute | solution.py:583
  11.7 5.0 %all-to-all-start = ((bf16[4,48,3584]{2,1,0:T(8,128)(2,1)}), bf16[4,48,3584]{2,1,0:T(8,128)(2,1)}, u32[]{:S(2)}, u32[]{:S(2)}) async-start(bf16[4,48,3584]{2,1,0:T(8,128)(2,1)} %broadcast_in_dim.27), calls=%async_computation | async-start | bytes 2752512 | tf_op jit(solution)/shard_map/all_to_all | solution.py:591
  17.4 1.6 collective-permute-start.4
  20.5 8.2 %collective-permute-done.4 = bf16[4,144,384]{2,1,0:T(8,128)(2,1)S(1)} collective-permute-done((bf16[4,144,384]{2,1,0:T(8,128)(2,1)S(1)}, bf16[4,144,384]{2,1,0:T(8,128)(2,1)S(1)}, u32[]{:S(2)}, u32[]{:S(2)}) %collective-permute-start.4) | collective-permute-done | bytes 442400 | tf_op jit(solution)/shard_map/ppermute | solution.py:583
  33.6 5.8 %collective-permute-done.5 = bf16[2,144,384]{2,1,0:T(8,128)(2,1)S(1)} collective-permute-done((bf16[2,144,384]{2,1,0:T(8,128)(2,1)S(1)}, bf16[2,144,384]{2,1,0:T(8,128)(2,1)S(1)}, u32[]{:S(2)}, u32[]{:S(2)}) %collective-permute-start.5) | collective-permute-done | bytes 221216 | tf_op jit(solution)/shard_map/ppermute | solution.py:583
  44.7 4.0 %all-to-all-done.rest_0_ = bf16[4,48,3584]{2,1,0:T(8,128)(2,1)} async-done(((bf16[4,48,3584]{2,1,0:T(8,128)(2,1)}), bf16[4,48,3584]{2,1,0:T(8,128)(2,1)}, u32[]{:S(2)}, u32[]{:S(2)}) %all-to-all-start) | async-done | bytes 1376288 | tf_op jit(solution)/shard_map/all_to_all | solution.py:591
  51.7 21.1 %attend.1 = (bf16[512,768]{1,0:T(8,128)(2,1)}, bf16[512,768]{1,0:T(8,128)(2,1)}, bf16[512,768]{1,0:T(8,128)(2,1)}, bf16[512,768]{1,0:T(8,128)(2,1)}, bf16[12,256,768]{2,1,0:T(8,128)(2,1)}) custom-call(s32[4]{0:T(128)} %pad_add_fusion.spot, s32[1,2]{1,0:T(1,128)} %starts.1, bf16[512,768]{1,0:T(8,128)(2,1)} %copy.40.normed_ref, ...), custom_call_target="tpu_custom_call" | custom-call | flops 20000000000 | bytes 1000000 | tf_op jit(solution)/shard_map/attend/pallas_call | solution.py:158
  72.8 7.3 %collective-permute-done.10.rest_2_ = bf16[4,48,3584]{2,1,0:T(8,128)(2,1)S(1)} collective-permute-done((bf16[4,48,3584]{2,1,0:T(8,128)(2,1)}, bf16[4,48,3584]{2,1,0:T(8,128)(2,1)S(1)}, u32[]{:S(2)}, u32[]{:S(2)}) %collective-permute-start.10) | collective-permute-done | bytes 1376288 | tf_op jit(solution)/shard_map/ppermute | solution.py:583
  85.4 12.8 %collective-permute-done.11.rest_3_ = bf16[2,48,3584]{2,1,0:T(8,128)(2,1)} collective-permute-done((bf16[2,48,3584]{2,1,0:T(8,128)(2,1)S(1)}, bf16[2,48,3584]{2,1,0:T(8,128)(2,1)}, u32[]{:S(2)}, u32[]{:S(2)}) %collective-permute-start.11) | collective-permute-done | bytes 688160 | tf_op jit(solution)/shard_map/ppermute | solution.py:583
  101.6 35.8 %middle.1 = (f32[512,768]{1,0:T(8,128)}, f32[512,768]{1,0:T(8,128)}, bf16[512,768]{1,0:T(8,128)(2,1)}, f32[8,768]{1,0:T(8,128)}, bf16[4,4,48,3456]{3,2,1,0:T(8,128)(2,1)}, /*index=5*/bf16[4,4,48,3456]{3,2,1,0:T(8,128)(2,1)}) custom-call(s32[4]{0:T(128)} %pad_add_fusion.spot, f32[1,1]{1,0:T(1,128)} %constant.56.clone.1.count, ...), custom_call_target="tpu_custom_call" | custom-call | flops 35000000512 | bytes 1000000 | tf_op jit(solution)/shard_map/middle/pallas_call | solution.py:343
  138.7 7.7 %collective-permute-done.18 = bf16[4,4,48,3456]{3,2,1,0:T(8,128)(2,1)S(1)} collective-permute-done((bf16[4,4,48,3456]{3,2,1,0:T(8,128)(2,1)}, bf16[4,4,48,3456]{3,2,1,0:T(8,128)(2,1)S(1)}, u32[]{:S(2)}, u32[]{:S(2)}) %collective-permute-start.18) | collective-permute-done | bytes 5308448 | tf_op jit(solution)/shard_map/ppermute | solution.py:583
  146.5 4.2 %add_convert_fusion = (bf16[2,2,48,3456]{3,2,1,0:T(8,128)(2,1)S(1)}, bf16[2,2,48,3456]{3,2,1,0:T(8,128)(2,1)S(1)}) fusion(bf16[4,4,48,3456]{3,2,1,0:T(8,128)(2,1)S(1)} %collective-permute-done.18, bf16[4,4,48,3456]{3,2,1,0:T(8,128)(2,1)} %get-tuple-element.100), kind=kLoop, calls=%fused_computation | loop fusion | flops 5308416 | bytes 7962624 | tf_op jit(solution)/shard_map/convert_element_type | solution.py:625
  153.3 28.8 %attend_back.1 = (bf16[512,768]{1,0:T(8,128)(2,1)}, bf16[512,768]{1,0:T(8,128)(2,1)}, bf16[512,768]{1,0:T(8,128)(2,1)}, f32[16,128]{1,0:T(8,128)}, bf16[4,4,144,...) custom-call(s32[4]{0:T(128)} %pad_add_fusion.spot, f32[12,12]{1,0:T(8,128)} %copy-done.7, f32[12,12]{1,0:T(8,128)} %pos.1, ...), custom_call_target="tpu_custom_call" | custom-call | flops 28000000000 | bytes 1000000 | tf_op jit(solution)/shard_map/attend_back/pallas_call | solution.py:502
  184.5 3.4 %add_bitcast_fusion = (f32[2,48,3456]{2,1,0:T(8,128)S(1)}, bf16[2,48,3456]{2,1,0:T(8,128)(2,1)S(1)}, bf16[2,48,3456]{2,1,0:T(8,128)(2,1)S(1)}, f32[2,48,3456]{2,1,0:T(8,128)S(1)}) fusion(bf16[4,4,48,3456]{3,2,1,0:T(8,128)(2,1)} %copy-done.1, bf16[2,2,48,3456]{3,2,1,0:T(8,128)(2,1)S(1)} %collective-permute-done.20, ...), kind=kLoop, calls=%fused_computation.10 | loop fusion | flops 7299072 | bytes 11943936 | tf_op jit(solution)/shard_map/add | solution.py:645
  195.7 9.0 %input_grad.1 = (f32[512,768]{1,0:T(8,128)}, f32[24,128]{1,0:T(8,128)}) custom-call(s32[4]{0:T(128)} %pad_add_fusion.spot, bf16[3,4,144,384]{3,2,1,0:T(8,128)(2,1)} %pad_maximum_fusion.1.rest_0_, bf16[2,2,144,384]{3,2,1,0:T(8,128)(2,1)} %pad_maximum_fusion.3.rest_1_, bf16[3,4,144,384]{3,2,1,0:T(8,128)(2,1)} %collective-permute-done.7.rest_2_, ...), custom_call_target="tpu_custom_call" | custom-call | flops 8999999488 | bytes 1000000 | tf_op jit(solution)/shard_map/input_grad/pallas_call | solution.py:567
  212.1 3.4 %collective-permute-start.39 = (bf16[48,1536]{1,0:T(8,128)(2,1)S(1)}, bf16[48,1536]{1,0:T(8,128)(2,1)S(1)}, u32[]{:S(2)}, u32[]{:S(2)}) collective-permute-start(bf16[48,1536]{1,0:T(8,128)(2,1)S(1)} %fusion.16), channel_id=1, source_target_pairs={{0,8},{1,9},{2,10},{3,11},{4,12},{5,13},{6,14},{7,15},{8,0},{9,1},... | collective-permute-start | bytes 442376 | tf_op jit(solution)/shard_map/ppermute | solution.py:583
  215.7 2.5 collective-permute-done.22
  218.2 2.8 %collective-permute-start.31 = (bf16[48,2048]{1,0:T(8,128)(2,1)S(1)}, bf16[48,2048]{1,0:T(8,128)(2,1)S(1)}, u32[]{:S(2)}, u32[]{:S(2)}) collective-permute-start(bf16[48,2048]{1,0:T(8,128)(2,1)S(1)} %get-tuple-element.162), channel_id=1, source_target_pairs={{0,24},{1,25},{2,26},{3,27},{4,28},{5,29},{6,30},{7,31},{8,16},{9,... | collective-permute-start | bytes 589832 | tf_op jit(solution)/shard_map/ppermute | solution.py:583
  222.7 1.6 collective-permute-start.29
  227.6 2.6 %collective-permute-done.32 = bf16[2,144,384]{2,1,0:T(8,128)(2,1)S(1)} collective-permute-done((bf16[2,144,384]{2,1,0:T(8,128)(2,1)S(1)}, bf16[2,144,384]{2,1,0:T(8,128)(2,1)S(1)}, u32[]{:S(2)}, u32[]{:S(2)}) %collective-permute-start.32) | collective-permute-done | bytes 221216 | tf_op jit(solution)/shard_map/ppermute | solution.py:583
  231.4 5.7 %collective-permute-done.30 = bf16[48,2048]{1,0:T(8,128)(2,1)S(1)} collective-permute-done((bf16[48,2048]{1,0:T(8,128)(2,1)S(1)}, bf16[48,2048]{1,0:T(8,128)(2,1)S(1)}, u32[]{:S(2)}, u32[]{:S(2)}) %collective-permute-start.30) | collective-permute-done | bytes 196640 | tf_op jit(solution)/shard_map/ppermute | solution.py:583
  240.2 2.1 collective-permute-done.33
  245.9 2.0 collective-permute-start.37
  247.9 2.4 collective-permute-start.38
  (165 shorter events, 65.8 us)
Async XLA Ops:
  3.0 13.7 %collective-permute-start.2 = (bf16[144,384]{1,0:T(8,128)(2,1)S(1)}, bf16[144,384]{1,0:T(8,128)(2,1)S(1)}, u32[]{:S(2)}, u32[]{:S(2)}) collective-permute-start(bf16[144,384]{1,0:T(8,128)(2,1)S(1)} %constant_dynamic-update-slice_fusion), channel_id=1, source_target_pairs={{0,24},{1,25},{2,26},{3,27},{4,28},{5,29},{6,30},{7,31},{8,16},{9,... | collective-permute-start | bytes 331784 | tf_op jit(solution)/shard_map/ppermute | solution.py:583
  11.7 37.0 %all-to-all-start = ((bf16[4,48,3584]{2,1,0:T(8,128)(2,1)}), bf16[4,48,3584]{2,1,0:T(8,128)(2,1)}, u32[]{:S(2)}, u32[]{:S(2)}) async-start(bf16[4,48,3584]{2,1,0:T(8,128)(2,1)} %broadcast_in_dim.27), calls=%async_computation | async-start | bytes 2752512 | tf_op jit(solution)/shard_map/all_to_all | solution.py:591
  31.3 13.3 %collective-permute-start.7 = (bf16[3,4,144,384]{3,2,1,0:T(8,128)(2,1)}, bf16[3,4,144,384]{3,2,1,0:T(8,128)(2,1)}, u32[]{:S(2)}, u32[]{:S(2)}) collective-permute-start(bf16[3,4,144,384]{3,2,1,0:T(8,128)(2,1)} %pad_maximum_fusion.1.rest_0_), channel_id=1, source_target_pairs={{0,2},{1,3},{2,0},{3,1},{4,6},{5,7},{6,4},{7,5},{8,10},{9,11},{10,... | collective-permute-start | bytes 3981320 | tf_op jit(solution)/shard_map/ppermute | solution.py:583
  48.7 31.4 %collective-permute-start.10 = (bf16[4,48,3584]{2,1,0:T(8,128)(2,1)}, bf16[4,48,3584]{2,1,0:T(8,128)(2,1)S(1)}, u32[]{:S(2)}, u32[]{:S(2)}) collective-permute-start(bf16[4,48,3584]{2,1,0:T(8,128)(2,1)} %all-to-all-done.rest_0_), channel_id=1, source_target_pairs={{0,4},{1,5},{2,6},{3,7},{4,0},{5,1},{6,2},{7,3},{8,12},{9,13},{10,... | collective-permute-start | bytes 4128776 | tf_op jit(solution)/shard_map/ppermute | solution.py:583
  50.2 31.2 %collective-permute-start.9 = (bf16[4,48,3584]{2,1,0:T(8,128)(2,1)}, bf16[4,48,3584]{2,1,0:T(8,128)(2,1)}, u32[]{:S(2)}, u32[]{:S(2)}) collective-permute-start(bf16[4,48,3584]{2,1,0:T(8,128)(2,1)} %all-to-all-done.rest_0_), channel_id=1, source_target_pairs={{0,1},{1,0},{2,3},{3,2},{4,5},{5,4},{6,7},{7,6},{8,9},{9,8},{10,11... | collective-permute-start | bytes 4128776 | tf_op jit(solution)/shard_map/ppermute | solution.py:583
  82.6 15.5 %collective-permute-start.11 = (bf16[2,48,3584]{2,1,0:T(8,128)(2,1)S(1)}, bf16[2,48,3584]{2,1,0:T(8,128)(2,1)}, u32[]{:S(2)}, u32[]{:S(2)}) collective-permute-start(bf16[2,48,3584]{2,1,0:T(8,128)(2,1)S(1)} %slice.242), channel_id=1, source_target_pairs={{0,4},{1,5},{2,6},{3,7},{4,0},{5,1},{6,2},{7,3},{8,12},{9,13},{10,... | collective-permute-start | bytes 2064392 | tf_op jit(solution)/shard_map/ppermute | solution.py:583
  83.4 15.5 %collective-permute-start.12 = (bf16[2,48,3584]{2,1,0:T(8,128)(2,1)S(1)}, bf16[2,48,3584]{2,1,0:T(8,128)(2,1)}, u32[]{:S(2)}, u32[]{:S(2)}) collective-permute-start(bf16[2,48,3584]{2,1,0:T(8,128)(2,1)S(1)} %slice.243), channel_id=1, source_target_pairs={{0,1},{1,0},{2,3},{3,2},{4,5},{5,4},{6,7},{7,6},{8,9},{9,8},{10,11... | collective-permute-start | bytes 2064392 | tf_op jit(solution)/shard_map/ppermute | solution.py:583
  84.9 16.7 %collective-permute-start.13 = (bf16[4,48,3584]{2,1,0:T(8,128)(2,1)}, bf16[4,48,3584]{2,1,0:T(8,128)(2,1)}, u32[]{:S(2)}, u32[]{:S(2)}) collective-permute-start(bf16[4,48,3584]{2,1,0:T(8,128)(2,1)} %all-to-all-done.rest_0_), channel_id=1, source_target_pairs={{0,2},{1,3},{2,0},{3,1},{4,6},{5,7},{6,4},{7,5},{8,10},{9,11},{10,... | collective-permute-start | bytes 4128776 | tf_op jit(solution)/shard_map/ppermute | solution.py:583
  84.9 16.7 %collective-permute-start.14 = (bf16[4,48,3584]{2,1,0:T(8,128)(2,1)}, bf16[4,48,3584]{2,1,0:T(8,128)(2,1)}, u32[]{:S(2)}, u32[]{:S(2)}) collective-permute-start(bf16[4,48,3584]{2,1,0:T(8,128)(2,1)} %collective-permute-done.9.rest_1_), channel_id=1, source_target_pairs={{0,2},{1,3},{2,0},{3,1},{4,6},{5,7},{6,4},{7,5},{8,10},{9,11},{10,... | collective-permute-start | bytes 4128776 | tf_op jit(solution)/shard_map/ppermute | solution.py:583
  85.4 16.2 %collective-permute-start.15 = (bf16[4,48,3584]{2,1,0:T(8,128)(2,1)S(1)}, bf16[4,48,3584]{2,1,0:T(8,128)(2,1)}, u32[]{:S(2)}, u32[]{:S(2)}) collective-permute-start(bf16[4,48,3584]{2,1,0:T(8,128)(2,1)S(1)} %collective-permute-done.10.rest_2_), channel_id=1, source_target_pairs={{0,2},{1,3},{2,0},{3,1},{4,6},{5,7},{6,4},{7,5},{8,10},{9,11},{10,... | collective-permute-start | bytes 4128776 | tf_op jit(solution)/shard_map/ppermute | solution.py:583
  150.7 31.5 %collective-permute-start.19 = (bf16[2,2,48,3456]{3,2,1,0:T(8,128)(2,1)S(1)}, bf16[2,2,48,3456]{3,2,1,0:T(8,128)(2,1)S(1)}, u32[]{:S(2)}, u32[]{:S(2)}) collective-permute-start(bf16[2,2,48,3456]{3,2,1,0:T(8,128)(2,1)S(1)} %get-tuple-element.103), channel_id=1, source_target_pairs={{0,4},{1,5},{2,6},{3,7},{4,0},{5,1},{6,2},{7,3},{8,12},{9,13},{10,... | collective-permute-start | bytes 3981320 | tf_op jit(solution)/shard_map/ppermute | solution.py:583
  151.8 30.9 %collective-permute-start.20 = (bf16[2,2,48,3456]{3,2,1,0:T(8,128)(2,1)S(1)}, bf16[2,2,48,3456]{3,2,1,0:T(8,128)(2,1)S(1)}, u32[]{:S(2)}, u32[]{:S(2)}) collective-permute-start(bf16[2,2,48,3456]{3,2,1,0:T(8,128)(2,1)S(1)} %get-tuple-element.104), channel_id=1, source_target_pairs={{0,1},{1,0},{2,3},{3,2},{4,5},{5,4},{6,7},{7,6},{8,9},{9,8},{10,11... | collective-permute-start | bytes 3981320 | tf_op jit(solution)/shard_map/ppermute | solution.py:583
  190.2 14.6 %collective-permute-start.26 = (bf16[2,48,1536]{2,1,0:T(8,128)(2,1)}, bf16[2,48,1536]{2,1,0:T(8,128)(2,1)}, u32[]{:S(2)}, u32[]{:S(2)}) collective-permute-start(bf16[2,48,1536]{2,1,0:T(8,128)(2,1)} %slice.324), channel_id=1, source_target_pairs={{0,1},{1,0},{2,3},{3,2},{4,5},{5,4},{6,7},{7,6},{8,9},{9,8},{10,11... | collective-permute-start | bytes 884744 | tf_op jit(solution)/shard_map/ppermute | solution.py:583
  191.7 13.1 %collective-permute-start.27 = (bf16[2,48,1536]{2,1,0:T(8,128)(2,1)S(1)}, bf16[2,48,1536]{2,1,0:T(8,128)(2,1)}, u32[]{:S(2)}, u32[]{:S(2)}) collective-permute-start(bf16[2,48,1536]{2,1,0:T(8,128)(2,1)S(1)} %slice.325), channel_id=1, source_target_pairs={{0,4},{1,5},{2,6},{3,7},{4,0},{5,1},{6,2},{7,3},{8,12},{9,13},{10,... | collective-permute-start | bytes 884744 | tf_op jit(solution)/shard_map/ppermute | solution.py:583
  192.6 16.0 %collective-permute-start.24 = (bf16[2,48,1920]{2,1,0:T(8,128)(2,1)}, bf16[2,48,1920]{2,1,0:T(8,128)(2,1)}, u32[]{:S(2)}, u32[]{:S(2)}) collective-permute-start(bf16[2,48,1920]{2,1,0:T(8,128)(2,1)} %slice.321), channel_id=1, source_target_pairs={{0,1},{1,0},{2,3},{3,2},{4,5},{5,4},{6,7},{7,6},{8,9},{9,8},{10,11... | collective-permute-start | bytes 1105928 | tf_op jit(solution)/shard_map/ppermute | solution.py:583
  193.2 16.9 %collective-permute-start.25 = (bf16[2,48,1920]{2,1,0:T(8,128)(2,1)}, bf16[2,48,1920]{2,1,0:T(8,128)(2,1)}, u32[]{:S(2)}, u32[]{:S(2)}) collective-permute-start(bf16[2,48,1920]{2,1,0:T(8,128)(2,1)} %slice.323), channel_id=1, source_target_pairs={{0,4},{1,5},{2,6},{3,7},{4,0},{5,1},{6,2},{7,3},{8,12},{9,13},{10,... | collective-permute-start | bytes 1105928 | tf_op jit(solution)/shard_map/ppermute | solution.py:583
  205.9 16.8 %collective-permute-start.40 = (bf16[48,1536]{1,0:T(8,128)(2,1)S(1)}, bf16[48,1536]{1,0:T(8,128)(2,1)S(1)}, u32[]{:S(2)}, u32[]{:S(2)}) collective-permute-start(bf16[48,1536]{1,0:T(8,128)(2,1)S(1)} %get-tuple-element.165), channel_id=1, source_target_pairs={{0,16},{1,17},{2,18},{3,19},{4,20},{5,21},{6,22},{7,23},{8,24},{9,... | collective-permute-start | bytes 442376 | tf_op jit(solution)/shard_map/ppermute | solution.py:583
  205.9 18.4 %collective-permute-start.41 = (bf16[48,1536]{1,0:T(8,128)(2,1)S(1)}, bf16[48,1536]{1,0:T(8,128)(2,1)S(1)}, u32[]{:S(2)}, u32[]{:S(2)}) collective-permute-start(bf16[48,1536]{1,0:T(8,128)(2,1)S(1)} %get-tuple-element.166), channel_id=1, source_target_pairs={{0,24},{1,25},{2,26},{3,27},{4,28},{5,29},{6,30},{7,31},{8,16},{9,... | collective-permute-start | bytes 442376 | tf_op jit(solution)/shard_map/ppermute | solution.py:583
  208.6 12.4 %collective-permute-start.23 = (bf16[2,2,144,384]{3,2,1,0:T(8,128)(2,1)S(1)}, bf16[2,2,144,384]{3,2,1,0:T(8,128)(2,1)S(1)}, u32[]{:S(2)}, u32[]{:S(2)}) collective-permute-start(bf16[2,2,144,384]{3,2,1,0:T(8,128)(2,1)S(1)} %get-tuple-element.122), channel_id=1, source_target_pairs={{0,1},{1,0},{2,3},{3,2},{4,5},{5,4},{6,7},{7,6},{8,9},{9,8},{10,11... | collective-permute-start | bytes 1327112 | tf_op jit(solution)/shard_map/ppermute | solution.py:583
  212.1 13.6 %collective-permute-start.39 = (bf16[48,1536]{1,0:T(8,128)(2,1)S(1)}, bf16[48,1536]{1,0:T(8,128)(2,1)S(1)}, u32[]{:S(2)}, u32[]{:S(2)}) collective-permute-start(bf16[48,1536]{1,0:T(8,128)(2,1)S(1)} %fusion.16), channel_id=1, source_target_pairs={{0,8},{1,9},{2,10},{3,11},{4,12},{5,13},{6,14},{7,15},{8,0},{9,1},... | collective-permute-start | bytes 442376 | tf_op jit(solution)/shard_map/ppermute | solution.py:583
  218.2 13.2 %collective-permute-start.31 = (bf16[48,2048]{1,0:T(8,128)(2,1)S(1)}, bf16[48,2048]{1,0:T(8,128)(2,1)S(1)}, u32[]{:S(2)}, u32[]{:S(2)}) collective-permute-start(bf16[48,2048]{1,0:T(8,128)(2,1)S(1)} %get-tuple-element.162), channel_id=1, source_target_pairs={{0,24},{1,25},{2,26},{3,27},{4,28},{5,29},{6,30},{7,31},{8,16},{9,... | collective-permute-start | bytes 589832 | tf_op jit(solution)/shard_map/ppermute | solution.py:583
  221.0 16.1 %collective-permute-start.30 = (bf16[48,2048]{1,0:T(8,128)(2,1)S(1)}, bf16[48,2048]{1,0:T(8,128)(2,1)S(1)}, u32[]{:S(2)}, u32[]{:S(2)}) collective-permute-start(bf16[48,2048]{1,0:T(8,128)(2,1)S(1)} %get-tuple-element.163), channel_id=1, source_target_pairs={{0,16},{1,17},{2,18},{3,19},{4,20},{5,21},{6,22},{7,23},{8,24},{9,... | collective-permute-start | bytes 589832 | tf_op jit(solution)/shard_map/ppermute | solution.py:583
  222.7 14.5 %collective-permute-start.29 = (bf16[48,2048]{1,0:T(8,128)(2,1)S(1)}, bf16[48,2048]{1,0:T(8,128)(2,1)S(1)}, u32[]{:S(2)}, u32[]{:S(2)}) collective-permute-start(bf16[48,2048]{1,0:T(8,128)(2,1)S(1)} %get-tuple-element.164), channel_id=1, source_target_pairs={{0,8},{1,9},{2,10},{3,11},{4,12},{5,13},{6,14},{7,15},{8,0},{9,1},... | collective-permute-start | bytes 589832 | tf_op jit(solution)/shard_map/ppermute | solution.py:583
  226.5 13.5 %collective-permute-start.36 = (bf16[2,144,384]{2,1,0:T(8,128)(2,1)S(1)}, bf16[2,144,384]{2,1,0:T(8,128)(2,1)S(1)}, u32[]{:S(2)}, u32[]{:S(2)}) collective-permute-start(bf16[2,144,384]{2,1,0:T(8,128)(2,1)S(1)} %get-tuple-element.154), channel_id=1, source_target_pairs={{0,4},{1,5},{2,6},{3,7},{4,0},{5,1},{6,2},{7,3},{8,12},{9,13},{10,... | collective-permute-start | bytes 663560 | tf_op jit(solution)/shard_map/ppermute | solution.py:583
  (32 other events, 254.7 us)

commit v9 on v8

--- a/solution.py
+++ b/solution.py
@@ -629,9 +629,10 @@
     return exchange(over_y, Y_BIT, total), exchange(over_x, X_BIT, total)
 
 
-def reduce_sides(terms, over_y, over_x):
+def reduce_sides(terms, over_y, over_x, cols=slice(None)):
+    every = slice(None)
     return [
-        (core_sum(terms, plane, z) + over[1]).astype(BF16)
+        (core_sum(terms, plane, z, every, cols) + over[1, :, :, cols]).astype(BF16)
         for plane, z, over in ((1, slice(0, 2), over_y), (2, slice(2, 4), over_x))
     ]
 
@@ -767,9 +768,10 @@
         other = exchange(send, CORE_BIT, total)
         half = units // col_total
         ahead = half + width
-        ffn_sides = reduce_sides(ffn_mine, *ffn_first)
-        down_sides = reduce_second(*[side[..., ahead:] for side in ffn_sides], total)
-        ffn_sides = reduce_second(*[side[..., :ahead] for side in ffn_sides], total)
+        down_sides = reduce_sides(ffn_mine, *ffn_first, slice(ahead, None))
+        ffn_sides = reduce_sides(ffn_mine, *ffn_first, slice(ahead))
+        down_sides = reduce_second(*down_sides, total)
+        ffn_sides = reduce_second(*ffn_sides, total)
         mine = keep, other
         *first, dq, dk, dv = lax.optimization_barrier((*reduce_core(mine), dq, dk, dv))
         first = reduce_first(*first, total)

time: 260 us -> 259 us (level)
  other arithmetic: 19.4 us -> 23.7 us
  waiting for transfers between devices: 66.4 us -> 63.4 us
    convert_element_type x1 -> x3, other arithmetic: 0.33 us -> 5.43 us  [reduce_sides(): (core_sum(terms, plane, z, every, cols) + over[1, :, :, cols]).astype(BF16)]
    ppermute x42, waiting for transfers between devices: 62.4 us -> 59.3 us  [exchange(): return lax.ppermute(value, AXES, [(i, i ^ mask) for i in range(total)])]
where the time goes in v9:
time: 259 us; the launch traced here: 258 us
  Pallas kernels  94.9 us (37%)
  waiting for transfers between devices  63.4 us (24%)
  starting transfers between devices  49.9 us (19%)
  other arithmetic  23.7 us (9%)
  local copies, waits for them, and re-layouts  18.1 us (7%)
  between operations  7.96 us (3%)
    ppermute x42, waiting for transfers between devices, exchange(): return lax.ppermute(value, AXES, [(i, i ^ mask) for i in range(total)])  59.3 us
    ppermute x42, starting transfers between devices, exchange(): return lax.ppermute(value, AXES, [(i, i ^ mask) for i in range(total)])  44.9 us
    pallas_call x1, Pallas kernels, middle_block(): pl.pallas_call(functools.partial(middle_kernel, len(pieces), len(grads),...  35.8 us
    pallas_call x1, Pallas kernels, attend_back(): pl.pallas_call(functools.partial(attend_back_kernel, blocked), grid=(HEAD...  29 us
    pallas_call x1, Pallas kernels, attend(): pl.pallas_call(functools.partial(attend_kernel, len(pieces)), grid=(HEADS...  21.1 us
    pallas_call x1, Pallas kernels, input_block(): pl.pallas_call(functools.partial(input_kernel, len(pieces)), in_specs=[SM...  9.04 us
    convert_element_type x3, other arithmetic, reduce_sides(): (core_sum(terms, plane, z, every, cols) + over[1, :, :, cols]).astype(BF16)  5.43 us
  transfers between devices with their start and end apart: 43, of which 19 were waited for; matrix products, arithmetic and copies ran while one was open for 12% of the time, Pallas kernels for 23%

profile of v9, /device:TPU:0, one launch (start us, length us, event | category | flops | bytes accessed | tf_op | source)
XLA Modules:
  0.0 257.9 jit_solution(8828233605711037137)
XLA Ops:
  3.0 5.1 %collective-permute-start.2 = (bf16[144,384]{1,0:T(8,128)(2,1)S(1)}, bf16[144,384]{1,0:T(8,128)(2,1)S(1)}, u32[]{:S(2)}, u32[]{:S(2)}) collective-permute-start(bf16[144,384]{1,0:T(8,128)(2,1)S(1)} %constant_dynamic-update-slice_fusion), channel_id=1, source_target_pairs={{0,24},{1,25},{2,26},{3,27},{4,28},{5,29},{6,30},{7,31},{8,16},{9,... | collective-permute-start | bytes 331784 | tf_op jit(solution)/shard_map/ppermute | solution.py:583
  11.7 5.0 %all-to-all-start = ((bf16[4,48,3584]{2,1,0:T(8,128)(2,1)}), bf16[4,48,3584]{2,1,0:T(8,128)(2,1)}, u32[]{:S(2)}, u32[]{:S(2)}) async-start(bf16[4,48,3584]{2,1,0:T(8,128)(2,1)} %broadcast_in_dim.27), calls=%async_computation | async-start | bytes 2752512 | tf_op jit(solution)/shard_map/all_to_all | solution.py:591
  20.5 8.2 %collective-permute-done.4 = bf16[4,144,384]{2,1,0:T(8,128)(2,1)S(1)} collective-permute-done((bf16[4,144,384]{2,1,0:T(8,128)(2,1)S(1)}, bf16[4,144,384]{2,1,0:T(8,128)(2,1)S(1)}, u32[]{:S(2)}, u32[]{:S(2)}) %collective-permute-start.4) | collective-permute-done | bytes 442400 | tf_op jit(solution)/shard_map/ppermute | solution.py:583
  33.5 5.8 %collective-permute-done.5 = bf16[2,144,384]{2,1,0:T(8,128)(2,1)S(1)} collective-permute-done((bf16[2,144,384]{2,1,0:T(8,128)(2,1)S(1)}, bf16[2,144,384]{2,1,0:T(8,128)(2,1)S(1)}, u32[]{:S(2)}, u32[]{:S(2)}) %collective-permute-start.5) | collective-permute-done | bytes 221216 | tf_op jit(solution)/shard_map/ppermute | solution.py:583
  44.7 4.0 %all-to-all-done.rest_0_ = bf16[4,48,3584]{2,1,0:T(8,128)(2,1)} async-done(((bf16[4,48,3584]{2,1,0:T(8,128)(2,1)}), bf16[4,48,3584]{2,1,0:T(8,128)(2,1)}, u32[]{:S(2)}, u32[]{:S(2)}) %all-to-all-start) | async-done | bytes 1376288 | tf_op jit(solution)/shard_map/all_to_all | solution.py:591
  51.7 21.1 %attend.1 = (bf16[512,768]{1,0:T(8,128)(2,1)}, bf16[512,768]{1,0:T(8,128)(2,1)}, bf16[512,768]{1,0:T(8,128)(2,1)}, bf16[512,768]{1,0:T(8,128)(2,1)}, bf16[12,256,768]{2,1,0:T(8,128)(2,1)}) custom-call(s32[4]{0:T(128)} %pad_add_fusion.spot, s32[1,2]{1,0:T(1,128)} %starts.1, bf16[512,768]{1,0:T(8,128)(2,1)} %copy.40.normed_ref, ...), custom_call_target="tpu_custom_call" | custom-call | flops 20000000000 | bytes 1000000 | tf_op jit(solution)/shard_map/attend/pallas_call | solution.py:158
  72.8 7.3 %collective-permute-done.10.rest_2_ = bf16[4,48,3584]{2,1,0:T(8,128)(2,1)S(1)} collective-permute-done((bf16[4,48,3584]{2,1,0:T(8,128)(2,1)}, bf16[4,48,3584]{2,1,0:T(8,128)(2,1)S(1)}, u32[]{:S(2)}, u32[]{:S(2)}) %collective-permute-start.10) | collective-permute-done | bytes 1376288 | tf_op jit(solution)/shard_map/ppermute | solution.py:583
  85.4 12.8 %collective-permute-done.11.rest_3_ = bf16[2,48,3584]{2,1,0:T(8,128)(2,1)} collective-permute-done((bf16[2,48,3584]{2,1,0:T(8,128)(2,1)S(1)}, bf16[2,48,3584]{2,1,0:T(8,128)(2,1)}, u32[]{:S(2)}, u32[]{:S(2)}) %collective-permute-start.11) | collective-permute-done | bytes 688160 | tf_op jit(solution)/shard_map/ppermute | solution.py:583
  101.6 35.8 %middle.1 = (f32[512,768]{1,0:T(8,128)}, f32[512,768]{1,0:T(8,128)}, bf16[512,768]{1,0:T(8,128)(2,1)}, f32[8,768]{1,0:T(8,128)}, bf16[4,4,48,3456]{3,2,1,0:T(8,128)(2,1)}, /*index=5*/bf16[4,4,48,3456]{3,2,1,0:T(8,128)(2,1)}) custom-call(s32[4]{0:T(128)} %pad_add_fusion.spot, f32[1,1]{1,0:T(1,128)} %constant.56.clone.1.count, ...), custom_call_target="tpu_custom_call" | custom-call | flops 35000000512 | bytes 1000000 | tf_op jit(solution)/shard_map/middle/pallas_call | solution.py:343
  140.5 5.9 %collective-permute-done.18 = bf16[4,4,48,3456]{3,2,1,0:T(8,128)(2,1)S(1)} collective-permute-done((bf16[4,4,48,3456]{3,2,1,0:T(8,128)(2,1)}, bf16[4,4,48,3456]{3,2,1,0:T(8,128)(2,1)S(1)}, u32[]{:S(2)}, u32[]{:S(2)}) %collective-permute-start.18) | collective-permute-done | bytes 5308448 | tf_op jit(solution)/shard_map/ppermute | solution.py:583
  146.5 4.2 %add_convert_fusion = (bf16[2,2,48,3456]{3,2,1,0:T(8,128)(2,1)S(1)}, bf16[2,2,48,3456]{3,2,1,0:T(8,128)(2,1)S(1)}) fusion(bf16[4,4,48,3456]{3,2,1,0:T(8,128)(2,1)S(1)} %collective-permute-done.18, bf16[4,4,48,3456]{3,2,1,0:T(8,128)(2,1)} %get-tuple-element.100), kind=kLoop, calls=%fused_computation | loop fusion | flops 5308416 | bytes 7962624 | tf_op jit(solution)/shard_map/convert_element_type | solution.py:625
  153.3 29.0 %attend_back.1 = (bf16[512,768]{1,0:T(8,128)(2,1)}, bf16[512,768]{1,0:T(8,128)(2,1)}, bf16[512,768]{1,0:T(8,128)(2,1)}, f32[16,128]{1,0:T(8,128)}, bf16[4,4,144,...) custom-call(s32[4]{0:T(128)} %pad_add_fusion.spot, f32[12,12]{1,0:T(8,128)} %copy-done.9, f32[12,12]{1,0:T(8,128)} %pos.1, ...), custom_call_target="tpu_custom_call" | custom-call | flops 28000000000 | bytes 1000000 | tf_op jit(solution)/shard_map/attend_back/pallas_call | solution.py:502
  182.8 2.6 %fusion.11 = (bf16[2,48,1536]{2,1,0:T(8,128)(2,1)}, bf16[2,48,1536]{2,1,0:T(8,128)(2,1)S(1)}) fusion(bf16[4,4,48,3456]{3,2,1,0:T(8,128)(2,1)} %copy-done.1, bf16[2,2,48,3456]{3,2,1,0:T(8,128)(2,1)S(1)} %collective-permute-done.20, bf16[4,4,48,3456]{3,2,1,0:T(8,128)(2,1)} %get-tuple-element.100, bf16[2,2,48,3456]{3,2,1,0:T(8,128)(2,1)S(1)} %collective-permute-done.19), kind=kLoop, calls=%fused_computation.41 | loop fusion | flops 1769472 | bytes 2359296 | tf_op jit(solution)/shard_map/convert_element_type | solution.py:635
  187.8 2.5 fusion.9
  192.0 2.5 add_bitcast_fusion
  196.0 9.0 %input_grad.1 = (f32[512,768]{1,0:T(8,128)}, f32[24,128]{1,0:T(8,128)}) custom-call(s32[4]{0:T(128)} %pad_add_fusion.spot, bf16[3,4,144,384]{3,2,1,0:T(8,128)(2,1)} %pad_maximum_fusion.1.rest_0_, bf16[2,2,144,384]{3,2,1,0:T(8,128)(2,1)} %pad_maximum_fusion.3.rest_1_, bf16[3,4,144,384]{3,2,1,0:T(8,128)(2,1)} %collective-permute-done.7.rest_2_, ...), custom_call_target="tpu_custom_call" | custom-call | flops 8999999488 | bytes 1000000 | tf_op jit(solution)/shard_map/input_grad/pallas_call | solution.py:567
  212.4 3.4 %collective-permute-start.39 = (bf16[48,1536]{1,0:T(8,128)(2,1)S(1)}, bf16[48,1536]{1,0:T(8,128)(2,1)S(1)}, u32[]{:S(2)}, u32[]{:S(2)}) collective-permute-start(bf16[48,1536]{1,0:T(8,128)(2,1)S(1)} %fusion.18), channel_id=1, source_target_pairs={{0,8},{1,9},{2,10},{3,11},{4,12},{5,13},{6,14},{7,15},{8,0},{9,1},... | collective-permute-start | bytes 442376 | tf_op jit(solution)/shard_map/ppermute | solution.py:583
  217.5 3.5 %collective-permute-start.31 = (bf16[48,2048]{1,0:T(8,128)(2,1)S(1)}, bf16[48,2048]{1,0:T(8,128)(2,1)S(1)}, u32[]{:S(2)}, u32[]{:S(2)}) collective-permute-start(bf16[48,2048]{1,0:T(8,128)(2,1)S(1)} %get-tuple-element.162), channel_id=1, source_target_pairs={{0,24},{1,25},{2,26},{3,27},{4,28},{5,29},{6,30},{7,31},{8,16},{9,... | collective-permute-start | bytes 589832 | tf_op jit(solution)/shard_map/ppermute | solution.py:583
  222.6 1.6 collective-permute-start.29
  227.4 2.8 %collective-permute-done.32 = bf16[2,144,384]{2,1,0:T(8,128)(2,1)S(1)} collective-permute-done((bf16[2,144,384]{2,1,0:T(8,128)(2,1)S(1)}, bf16[2,144,384]{2,1,0:T(8,128)(2,1)S(1)}, u32[]{:S(2)}, u32[]{:S(2)}) %collective-permute-start.32) | collective-permute-done | bytes 221216 | tf_op jit(solution)/shard_map/ppermute | solution.py:583
  231.3 5.4 %collective-permute-done.30 = bf16[48,2048]{1,0:T(8,128)(2,1)S(1)} collective-permute-done((bf16[48,2048]{1,0:T(8,128)(2,1)S(1)}, bf16[48,2048]{1,0:T(8,128)(2,1)S(1)}, u32[]{:S(2)}, u32[]{:S(2)}) %collective-permute-start.30) | collective-permute-done | bytes 196640 | tf_op jit(solution)/shard_map/ppermute | solution.py:583
  239.4 2.5 collective-permute-done.33
  245.5 2.5 collective-permute-start.37
  248.0 1.9 collective-permute-start.38
  (167 shorter events, 65.4 us)
Async XLA Ops:
  3.0 13.7 %collective-permute-start.2 = (bf16[144,384]{1,0:T(8,128)(2,1)S(1)}, bf16[144,384]{1,0:T(8,128)(2,1)S(1)}, u32[]{:S(2)}, u32[]{:S(2)}) collective-permute-start(bf16[144,384]{1,0:T(8,128)(2,1)S(1)} %constant_dynamic-update-slice_fusion), channel_id=1, source_target_pairs={{0,24},{1,25},{2,26},{3,27},{4,28},{5,29},{6,30},{7,31},{8,16},{9,... | collective-permute-start | bytes 331784 | tf_op jit(solution)/shard_map/ppermute | solution.py:583
  11.7 37.0 %all-to-all-start = ((bf16[4,48,3584]{2,1,0:T(8,128)(2,1)}), bf16[4,48,3584]{2,1,0:T(8,128)(2,1)}, u32[]{:S(2)}, u32[]{:S(2)}) async-start(bf16[4,48,3584]{2,1,0:T(8,128)(2,1)} %broadcast_in_dim.27), calls=%async_computation | async-start | bytes 2752512 | tf_op jit(solution)/shard_map/all_to_all | solution.py:591
  31.3 13.4 %collective-permute-start.7 = (bf16[3,4,144,384]{3,2,1,0:T(8,128)(2,1)}, bf16[3,4,144,384]{3,2,1,0:T(8,128)(2,1)}, u32[]{:S(2)}, u32[]{:S(2)}) collective-permute-start(bf16[3,4,144,384]{3,2,1,0:T(8,128)(2,1)} %pad_maximum_fusion.1.rest_0_), channel_id=1, source_target_pairs={{0,2},{1,3},{2,0},{3,1},{4,6},{5,7},{6,4},{7,5},{8,10},{9,11},{10,... | collective-permute-start | bytes 3981320 | tf_op jit(solution)/shard_map/ppermute | solution.py:583
  48.7 31.4 %collective-permute-start.10 = (bf16[4,48,3584]{2,1,0:T(8,128)(2,1)}, bf16[4,48,3584]{2,1,0:T(8,128)(2,1)S(1)}, u32[]{:S(2)}, u32[]{:S(2)}) collective-permute-start(bf16[4,48,3584]{2,1,0:T(8,128)(2,1)} %all-to-all-done.rest_0_), channel_id=1, source_target_pairs={{0,4},{1,5},{2,6},{3,7},{4,0},{5,1},{6,2},{7,3},{8,12},{9,13},{10,... | collective-permute-start | bytes 4128776 | tf_op jit(solution)/shard_map/ppermute | solution.py:583
  50.2 31.2 %collective-permute-start.9 = (bf16[4,48,3584]{2,1,0:T(8,128)(2,1)}, bf16[4,48,3584]{2,1,0:T(8,128)(2,1)}, u32[]{:S(2)}, u32[]{:S(2)}) collective-permute-start(bf16[4,48,3584]{2,1,0:T(8,128)(2,1)} %all-to-all-done.rest_0_), channel_id=1, source_target_pairs={{0,1},{1,0},{2,3},{3,2},{4,5},{5,4},{6,7},{7,6},{8,9},{9,8},{10,11... | collective-permute-start | bytes 4128776 | tf_op jit(solution)/shard_map/ppermute | solution.py:583
  82.6 15.5 %collective-permute-start.11 = (bf16[2,48,3584]{2,1,0:T(8,128)(2,1)S(1)}, bf16[2,48,3584]{2,1,0:T(8,128)(2,1)}, u32[]{:S(2)}, u32[]{:S(2)}) collective-permute-start(bf16[2,48,3584]{2,1,0:T(8,128)(2,1)S(1)} %slice.248), channel_id=1, source_target_pairs={{0,4},{1,5},{2,6},{3,7},{4,0},{5,1},{6,2},{7,3},{8,12},{9,13},{10,... | collective-permute-start | bytes 2064392 | tf_op jit(solution)/shard_map/ppermute | solution.py:583
  83.4 15.5 %collective-permute-start.12 = (bf16[2,48,3584]{2,1,0:T(8,128)(2,1)S(1)}, bf16[2,48,3584]{2,1,0:T(8,128)(2,1)}, u32[]{:S(2)}, u32[]{:S(2)}) collective-permute-start(bf16[2,48,3584]{2,1,0:T(8,128)(2,1)S(1)} %slice.249), channel_id=1, source_target_pairs={{0,1},{1,0},{2,3},{3,2},{4,5},{5,4},{6,7},{7,6},{8,9},{9,8},{10,11... | collective-permute-start | bytes 2064392 | tf_op jit(solution)/shard_map/ppermute | solution.py:583
  84.9 16.7 %collective-permute-start.13 = (bf16[4,48,3584]{2,1,0:T(8,128)(2,1)}, bf16[4,48,3584]{2,1,0:T(8,128)(2,1)}, u32[]{:S(2)}, u32[]{:S(2)}) collective-permute-start(bf16[4,48,3584]{2,1,0:T(8,128)(2,1)} %all-to-all-done.rest_0_), channel_id=1, source_target_pairs={{0,2},{1,3},{2,0},{3,1},{4,6},{5,7},{6,4},{7,5},{8,10},{9,11},{10,... | collective-permute-start | bytes 4128776 | tf_op jit(solution)/shard_map/ppermute | solution.py:583
  84.9 16.7 %collective-permute-start.14 = (bf16[4,48,3584]{2,1,0:T(8,128)(2,1)}, bf16[4,48,3584]{2,1,0:T(8,128)(2,1)}, u32[]{:S(2)}, u32[]{:S(2)}) collective-permute-start(bf16[4,48,3584]{2,1,0:T(8,128)(2,1)} %collective-permute-done.9.rest_1_), channel_id=1, source_target_pairs={{0,2},{1,3},{2,0},{3,1},{4,6},{5,7},{6,4},{7,5},{8,10},{9,11},{10,... | collective-permute-start | bytes 4128776 | tf_op jit(solution)/shard_map/ppermute | solution.py:583
  85.4 16.2 %collective-permute-start.15 = (bf16[4,48,3584]{2,1,0:T(8,128)(2,1)S(1)}, bf16[4,48,3584]{2,1,0:T(8,128)(2,1)}, u32[]{:S(2)}, u32[]{:S(2)}) collective-permute-start(bf16[4,48,3584]{2,1,0:T(8,128)(2,1)S(1)} %collective-permute-done.10.rest_2_), channel_id=1, source_target_pairs={{0,2},{1,3},{2,0},{3,1},{4,6},{5,7},{6,4},{7,5},{8,10},{9,11},{10,... | collective-permute-start | bytes 4128776 | tf_op jit(solution)/shard_map/ppermute | solution.py:583
  150.7 31.6 %collective-permute-start.19 = (bf16[2,2,48,3456]{3,2,1,0:T(8,128)(2,1)S(1)}, bf16[2,2,48,3456]{3,2,1,0:T(8,128)(2,1)S(1)}, u32[]{:S(2)}, u32[]{:S(2)}) collective-permute-start(bf16[2,2,48,3456]{3,2,1,0:T(8,128)(2,1)S(1)} %get-tuple-element.103), channel_id=1, source_target_pairs={{0,4},{1,5},{2,6},{3,7},{4,0},{5,1},{6,2},{7,3},{8,12},{9,13},{10,... | collective-permute-start | bytes 3981320 | tf_op jit(solution)/shard_map/ppermute | solution.py:583
  151.9 30.9 %collective-permute-start.20 = (bf16[2,2,48,3456]{3,2,1,0:T(8,128)(2,1)S(1)}, bf16[2,2,48,3456]{3,2,1,0:T(8,128)(2,1)S(1)}, u32[]{:S(2)}, u32[]{:S(2)}) collective-permute-start(bf16[2,2,48,3456]{3,2,1,0:T(8,128)(2,1)S(1)} %get-tuple-element.104), channel_id=1, source_target_pairs={{0,1},{1,0},{2,3},{3,2},{4,5},{5,4},{6,7},{7,6},{8,9},{9,8},{10,11... | collective-permute-start | bytes 3981320 | tf_op jit(solution)/shard_map/ppermute | solution.py:583
  185.4 19.6 %collective-permute-start.27 = (bf16[2,48,1536]{2,1,0:T(8,128)(2,1)}, bf16[2,48,1536]{2,1,0:T(8,128)(2,1)}, u32[]{:S(2)}, u32[]{:S(2)}) collective-permute-start(bf16[2,48,1536]{2,1,0:T(8,128)(2,1)} %get-tuple-element.148), channel_id=1, source_target_pairs={{0,4},{1,5},{2,6},{3,7},{4,0},{5,1},{6,2},{7,3},{8,12},{9,13},{10,... | collective-permute-start | bytes 884744 | tf_op jit(solution)/shard_map/ppermute | solution.py:583
  186.4 18.7 %collective-permute-start.26 = (bf16[2,48,1536]{2,1,0:T(8,128)(2,1)S(1)}, bf16[2,48,1536]{2,1,0:T(8,128)(2,1)}, u32[]{:S(2)}, u32[]{:S(2)}) collective-permute-start(bf16[2,48,1536]{2,1,0:T(8,128)(2,1)S(1)} %get-tuple-element.149), channel_id=1, source_target_pairs={{0,1},{1,0},{2,3},{3,2},{4,5},{5,4},{6,7},{7,6},{8,9},{9,8},{10,11... | collective-permute-start | bytes 884744 | tf_op jit(solution)/shard_map/ppermute | solution.py:583
  190.3 18.6 %collective-permute-start.25 = (bf16[2,48,1920]{2,1,0:T(8,128)(2,1)}, bf16[2,48,1920]{2,1,0:T(8,128)(2,1)}, u32[]{:S(2)}, u32[]{:S(2)}) collective-permute-start(bf16[2,48,1920]{2,1,0:T(8,128)(2,1)} %get-tuple-element.150), channel_id=1, source_target_pairs={{0,4},{1,5},{2,6},{3,7},{4,0},{5,1},{6,2},{7,3},{8,12},{9,13},{10,... | collective-permute-start | bytes 1105928 | tf_op jit(solution)/shard_map/ppermute | solution.py:583
  191.4 19.0 %collective-permute-start.24 = (bf16[2,48,1920]{2,1,0:T(8,128)(2,1)}, bf16[2,48,1920]{2,1,0:T(8,128)(2,1)}, u32[]{:S(2)}, u32[]{:S(2)}) collective-permute-start(bf16[2,48,1920]{2,1,0:T(8,128)(2,1)} %get-tuple-element.151), channel_id=1, source_target_pairs={{0,1},{1,0},{2,3},{3,2},{4,5},{5,4},{6,7},{7,6},{8,9},{9,8},{10,11... | collective-permute-start | bytes 1105928 | tf_op jit(solution)/shard_map/ppermute | solution.py:583
  206.1 16.5 %collective-permute-start.40 = (bf16[48,1536]{1,0:T(8,128)(2,1)S(1)}, bf16[48,1536]{1,0:T(8,128)(2,1)S(1)}, u32[]{:S(2)}, u32[]{:S(2)}) collective-permute-start(bf16[48,1536]{1,0:T(8,128)(2,1)S(1)} %get-tuple-element.165), channel_id=1, source_target_pairs={{0,16},{1,17},{2,18},{3,19},{4,20},{5,21},{6,22},{7,23},{8,24},{9,... | collective-permute-start | bytes 442376 | tf_op jit(solution)/shard_map/ppermute | solution.py:583
  206.2 18.0 %collective-permute-start.41 = (bf16[48,1536]{1,0:T(8,128)(2,1)S(1)}, bf16[48,1536]{1,0:T(8,128)(2,1)S(1)}, u32[]{:S(2)}, u32[]{:S(2)}) collective-permute-start(bf16[48,1536]{1,0:T(8,128)(2,1)S(1)} %get-tuple-element.166), channel_id=1, source_target_pairs={{0,24},{1,25},{2,26},{3,27},{4,28},{5,29},{6,30},{7,31},{8,16},{9,... | collective-permute-start | bytes 442376 | tf_op jit(solution)/shard_map/ppermute | solution.py:583
  208.9 12.1 %collective-permute-start.23 = (bf16[2,2,144,384]{3,2,1,0:T(8,128)(2,1)S(1)}, bf16[2,2,144,384]{3,2,1,0:T(8,128)(2,1)S(1)}, u32[]{:S(2)}, u32[]{:S(2)}) collective-permute-start(bf16[2,2,144,384]{3,2,1,0:T(8,128)(2,1)S(1)} %get-tuple-element.122), channel_id=1, source_target_pairs={{0,1},{1,0},{2,3},{3,2},{4,5},{5,4},{6,7},{7,6},{8,9},{9,8},{10,11... | collective-permute-start | bytes 1327112 | tf_op jit(solution)/shard_map/ppermute | solution.py:583
  212.4 13.1 %collective-permute-start.39 = (bf16[48,1536]{1,0:T(8,128)(2,1)S(1)}, bf16[48,1536]{1,0:T(8,128)(2,1)S(1)}, u32[]{:S(2)}, u32[]{:S(2)}) collective-permute-start(bf16[48,1536]{1,0:T(8,128)(2,1)S(1)} %fusion.18), channel_id=1, source_target_pairs={{0,8},{1,9},{2,10},{3,11},{4,12},{5,13},{6,14},{7,15},{8,0},{9,1},... | collective-permute-start | bytes 442376 | tf_op jit(solution)/shard_map/ppermute | solution.py:583
  217.5 13.9 %collective-permute-start.31 = (bf16[48,2048]{1,0:T(8,128)(2,1)S(1)}, bf16[48,2048]{1,0:T(8,128)(2,1)S(1)}, u32[]{:S(2)}, u32[]{:S(2)}) collective-permute-start(bf16[48,2048]{1,0:T(8,128)(2,1)S(1)} %get-tuple-element.162), channel_id=1, source_target_pairs={{0,24},{1,25},{2,26},{3,27},{4,28},{5,29},{6,30},{7,31},{8,16},{9,... | collective-permute-start | bytes 589832 | tf_op jit(solution)/shard_map/ppermute | solution.py:583
  220.9 15.8 %collective-permute-start.30 = (bf16[48,2048]{1,0:T(8,128)(2,1)S(1)}, bf16[48,2048]{1,0:T(8,128)(2,1)S(1)}, u32[]{:S(2)}, u32[]{:S(2)}) collective-permute-start(bf16[48,2048]{1,0:T(8,128)(2,1)S(1)} %get-tuple-element.163), channel_id=1, source_target_pairs={{0,16},{1,17},{2,18},{3,19},{4,20},{5,21},{6,22},{7,23},{8,24},{9,... | collective-permute-start | bytes 589832 | tf_op jit(solution)/shard_map/ppermute | solution.py:583
  222.6 14.2 %collective-permute-start.29 = (bf16[48,2048]{1,0:T(8,128)(2,1)S(1)}, bf16[48,2048]{1,0:T(8,128)(2,1)S(1)}, u32[]{:S(2)}, u32[]{:S(2)}) collective-permute-start(bf16[48,2048]{1,0:T(8,128)(2,1)S(1)} %get-tuple-element.164), channel_id=1, source_target_pairs={{0,8},{1,9},{2,10},{3,11},{4,12},{5,13},{6,14},{7,15},{8,0},{9,1},... | collective-permute-start | bytes 589832 | tf_op jit(solution)/shard_map/ppermute | solution.py:583
  226.3 13.0 %collective-permute-start.36 = (bf16[2,144,384]{2,1,0:T(8,128)(2,1)S(1)}, bf16[2,144,384]{2,1,0:T(8,128)(2,1)S(1)}, u32[]{:S(2)}, u32[]{:S(2)}) collective-permute-start(bf16[2,144,384]{2,1,0:T(8,128)(2,1)S(1)} %get-tuple-element.154), channel_id=1, source_target_pairs={{0,4},{1,5},{2,6},{3,7},{4,0},{5,1},{6,2},{7,3},{8,12},{9,13},{10,... | collective-permute-start | bytes 663560 | tf_op jit(solution)/shard_map/ppermute | solution.py:583
  (34 other events, 264.5 us)
